TPU v7x, 32 devices: a whole 2x2x4 slice. The times are simulated.
32 devices in a mesh: fsdp: 4 (over z), ctx: 2 (over x), tp: 4 (over y, core).
Axes of the slice: x: 2, y: 2, z: 4, core: 2. Of those that a mesh axis runs over, the one named last changes fastest.
Arguments:
- layer_input: bfloat16 [4, 2048, 768], P('fsdp', 'ctx'), may hold values from -6 to 6
- segments: int32 [4, 2048], P('fsdp', 'ctx'), may hold values from 0 to 3, never falling along the last dimension, each value on 1 to 1024 neighbouring positions
- routes: int32 [4, 2048, 2], P('fsdp', 'ctx'), may hold values from 0 to 3, all different within a row; in each aligned block of 1024 rows (0 to 1023, 1024 to 2047, ..., all dimensions but the last counted through in order) at most 1024 rows name the same one
- cotangent: bfloat16 [4, 2048, 768], P('fsdp', 'ctx'), may hold values from -6 to 6
- gains: float32 [2, 768], P(None, ('fsdp', 'ctx')), may hold values from 0.5 to 1.5
- attention_in: float32 [768, 3, 768], P(('fsdp', 'ctx'), None, 'tp'), as said below
- attention_out: float32 [768, 768], P('tp', ('fsdp', 'ctx')), may hold values from -0.3125 to 0.3125
- router_weight: float32 [768, 4], P(('fsdp', 'ctx')), may hold values from -0.21875 to 0.21875
- shared_in: float32 [768, 2, 2048], P(('fsdp', 'ctx'), None, 'tp'), may hold values from -0.21875 to 0.21875
- shared_down: float32 [2048, 768], P('tp', ('fsdp', 'ctx')), may hold values from -0.125 to 0.125
- expert_in: float32 [4, 768, 2, 2048], P('fsdp', 'ctx', None, 'tp'), may hold values from -0.21875 to 0.21875
- expert_down: float32 [4, 2048, 768], P('fsdp', 'tp', 'ctx'), may hold values from -0.125 to 0.125
- model_stats: float32 [6, 768], P(None, ('fsdp', 'ctx')), as said below
- head_stats: float32 [3, 768], P(None, 'tp'), as said below
- value_columns: float32 [768], P('tp'), as said below
- hidden_stats: float32 [3, 2048], P(None, 'tp'), as said below
- router_state: float32 [768, 4], P(('fsdp', 'ctx')), as said below
- expert_model_stats: float32 [4, 2, 768], P('fsdp', None, 'ctx'), as said below
- expert_hidden_stats: float32 [4, 3, 2048], P('fsdp', None, 'tp'), as said below
Outputs:
- layer_output: bfloat16 [4, 2048, 768], P('fsdp', 'ctx')
- input_grad: float32 [4, 2048, 768], P('fsdp', 'ctx')
- grad_gains: float32 [2, 768], P(None, ('fsdp', 'ctx'))
- grad_attention_in: float32 [768, 3, 768], P(('fsdp', 'ctx'), None, 'tp')
- grad_attention_out: float32 [768, 768], P('tp', ('fsdp', 'ctx'))
- grad_router: float32 [768, 4], P(('fsdp', 'ctx'))
- grad_shared_in: float32 [768, 2, 2048], P(('fsdp', 'ctx'), None, 'tp')
- grad_shared_down: float32 [2048, 768], P('tp', ('fsdp', 'ctx'))
- grad_expert_in: float32 [4, 768, 2, 2048], P('fsdp', 'ctx', None, 'tp')
- grad_expert_down: float32 [4, 2048, 768], P('fsdp', 'tp', 'ctx')
- new_gains: float32 [2, 768], P(None, ('fsdp', 'ctx'))
- new_attention_in: float32 [768, 3, 768], P(('fsdp', 'ctx'), None, 'tp')
- new_attention_out: float32 [768, 768], P('tp', ('fsdp', 'ctx'))
- new_router: float32 [768, 4], P(('fsdp', 'ctx'))
- new_shared_in: float32 [768, 2, 2048], P(('fsdp', 'ctx'), None, 'tp')
- new_shared_down: float32 [2048, 768], P('tp', ('fsdp', 'ctx'))
- new_expert_in: float32 [4, 768, 2, 2048], P('fsdp', 'ctx', None, 'tp')
- new_expert_down: float32 [4, 2048, 768], P('fsdp', 'tp', 'ctx')
- new_model_stats: float32 [6, 768], P(None, ('fsdp', 'ctx'))
- new_head_stats: float32 [3, 768], P(None, 'tp')
- new_value_columns: float32 [768], P('tp')
- new_hidden_stats: float32 [3, 2048], P(None, 'tp')
- new_router_state: float32 [768, 4], P(('fsdp', 'ctx'))
- new_expert_model_stats: float32 [4, 2, 768], P('fsdp', None, 'ctx')
- new_expert_hidden_stats: float32 [4, 3, 2048], P('fsdp', None, 'tp')
- update_rms: float32 [8], replicated
Inputs may be any that keep to these rules, and one draw needn't show every extreme that they name: `routes`: each row names two different experts. In each aligned block of 1024 rows (the rows of one device) no expert is named by more than 1024 rows, and in some block one expert is named by exactly 1024. `segments`: within each sequence the ids never fall; each document spans 1 to 1024 positions and one spans exactly that many. `attention_in`: finite real values. `model_stats`: Positive. `head_stats`: Positive. `value_columns`: Positive. `hidden_stats`: Positive. `router_state`: Positive. `expert_model_stats`: Positive. `expert_hidden_stats`: Positive.
All inputs are finite; a program needn't handle non-finite values.
Results may differ from a plain program's by a relative error of at most 0.015.
The roundings to bfloat16 on the way count: a program that leaves them out, or rounds other values in their place, can miss the bound.
Values may be sent and summed in bfloat16 or wider, within the bound.
A program may use at most 256 MiB of HBM per device.

v0:
```python
import jax
import jax.numpy as jnp
from jax import lax
from jax.sharding import PartitionSpec as P

D = 768
HD = 64
FF = 2048
FE = 2048
WINDOW = 1024
HH = 768


EPSILON = 1e-06
TINY_SQUARE = 1e-30
SCALE_FLOOR = 0.001
DECAY_RATE = 0.5
CLIP_LIMIT = 0.5
STEP_RATE = 0.5


def from_behind(value, axis, steps):
    count = lax.axis_size(axis)
    leading, last = (max(0, -steps), min(count, count - steps))
    return lax.ppermute(value, axis, [(source, source + steps) for source in range(leading, last)])


def rms_norm(values, gain_vec):
    inv_rms = lax.rsqrt(jnp.mean(values * values, axis=-1, keepdims=True) + EPSILON)
    return values * inv_rms * gain_vec


def swiglu(gate_up):
    return jax.nn.silu(gate_up[:, 0]) * gate_up[:, 1]


def rotate(values, cosine, sine_tab):
    half_dim = values.shape[-1] // 2
    first_half = values[..., :half_dim]
    second_half = values[..., half_dim:]
    cos_b = cosine[:, None, :]
    sin_b = sine_tab[:, None, :]
    return jnp.concatenate(
        [first_half * cos_b - second_half * sin_b, second_half * cos_b + first_half * sin_b],
        axis=-1,
    )


def slot_tables(block_routes, experts, capacity):
    flat_routes = block_routes.reshape(-1)
    route_count = flat_routes.shape[0]
    onehot = (flat_routes[:, None] == jnp.arange(experts, dtype=jnp.int32)[None, :]).astype(
        jnp.int32
    )
    rank_in = jnp.sum(
        (jnp.cumsum(onehot, axis=0, dtype=jnp.int32) - 1) * onehot, axis=1, dtype=jnp.int32
    )
    slot_index = flat_routes * capacity + rank_in
    owner_route = (
        jnp.zeros((experts * capacity,), jnp.int32)
        .at[slot_index]
        .set(jnp.arange(route_count, dtype=jnp.int32))
    )
    filled = jnp.zeros((experts * capacity,), jnp.int32).at[slot_index].set(1)
    return (slot_index, owner_route, filled)


def block_view(queries, keys_ext, values_ext, seg_own, seg_ext, start_row, base_pos):
    block_len = queries.shape[0]
    block_rows = min(512, block_len)
    query_rows = lax.dynamic_slice_in_dim(queries, start_row, block_rows, 0)
    key_rows = lax.dynamic_slice_in_dim(
        keys_ext, start_row + block_len - WINDOW, block_rows + WINDOW, 0
    )
    value_rows = lax.dynamic_slice_in_dim(
        values_ext, start_row + block_len - WINDOW, block_rows + WINDOW, 0
    )
    scores = (
        jnp.einsum("qhd,khd->hqk", query_rows, key_rows, preferred_element_type=jnp.float32) * 0.125
    )
    query_pos = start_row + jnp.arange(block_rows, dtype=jnp.int32)
    key_pos = start_row - WINDOW + jnp.arange(block_rows + WINDOW, dtype=jnp.int32)
    distance = query_pos[:, None] - key_pos[None, :]
    seg_query = lax.dynamic_slice_in_dim(seg_own, start_row, block_rows, 0)
    seg_key = lax.dynamic_slice_in_dim(
        seg_ext, start_row + block_len - WINDOW, block_rows + WINDOW, 0
    )
    allowed = (
        (distance >= 0)
        & (distance < WINDOW)
        & (seg_query[:, None] == seg_key[None, :])
        & (key_pos[None, :] + base_pos >= 0)
    )
    return (query_rows, key_rows, value_rows, jnp.where(allowed[None], scores, -1e30), allowed)


def factored_update(
    grad_mat, rows_old, cols_old, row_sums, col_sums, row_total, col_total, old_total, square_total
):
    rows_new = DECAY_RATE * rows_old + (1.0 - DECAY_RATE) * row_sums / col_total
    cols_new = DECAY_RATE * cols_old + (1.0 - DECAY_RATE) * col_sums / row_total
    mean_rows = (DECAY_RATE * old_total + (1.0 - DECAY_RATE) * square_total / col_total) / row_total
    second_moment = rows_new[:, None] * cols_new[None, :] / mean_rows
    return (grad_mat * lax.rsqrt(second_moment), rows_new, cols_new)


def apply_update(weight, update, update_root, square_sum, elements):
    param_scale = jnp.maximum(SCALE_FLOOR, jnp.sqrt(square_sum / elements))
    return weight - STEP_RATE * param_scale * update / jnp.maximum(1.0, update_root / CLIP_LIMIT)


def head_sums(partial_sum):
    return lax.psum(partial_sum, "tp")


def grad_sums(partial_sum):
    return lax.psum(partial_sum, "tp")


def to_experts(buffer_rows):
    return lax.all_to_all(buffer_rows, "fsdp", split_axis=0, concat_axis=0, tiled=True)


def to_tokens(buffer_rows):
    return lax.all_to_all(buffer_rows, "fsdp", split_axis=0, concat_axis=0, tiled=True)


def local(
    layer_input,
    segments,
    routes,
    cotangent,
    gains,
    attention_in,
    attention_out,
    router_weight,
    shared_in,
    shared_down,
    expert_in,
    expert_down,
    model_stats,
    head_stats,
    value_columns,
    hidden_stats,
    router_state,
    expert_model_stats,
    expert_hidden_stats,
):
    block_len = layer_input.shape[1]
    model_width = layer_input.shape[2]
    experts = router_weight.shape[1]
    capacity = min(block_len, 4 * block_len // experts)
    ctx_index = lax.axis_index("ctx")
    tp_index = lax.axis_index("tp")
    fsdp_index = lax.axis_index("fsdp")
    shard_index = lax.axis_index(("fsdp", "ctx"))
    base_pos = ctx_index * block_len
    gathered = (
        lax.all_gather(gains.astype(jnp.bfloat16), ("fsdp", "ctx"), axis=1, tiled=True),
        lax.all_gather(attention_in.astype(jnp.bfloat16), ("fsdp", "ctx"), axis=0, tiled=True),
        lax.all_gather(attention_out.astype(jnp.bfloat16), ("fsdp", "ctx"), axis=1, tiled=True),
        lax.all_gather(router_weight.astype(jnp.bfloat16), ("fsdp", "ctx"), axis=0, tiled=True),
        lax.all_gather(shared_in.astype(jnp.bfloat16), ("fsdp", "ctx"), axis=0, tiled=True),
        lax.all_gather(shared_down.astype(jnp.bfloat16), ("fsdp", "ctx"), axis=1, tiled=True),
    )
    gain_low, attn_in_low, attn_out_low, router_low, shared_in_low, shared_down_low = gathered
    expert_full = (
        lax.all_gather(expert_in.astype(jnp.bfloat16), "ctx", axis=1, tiled=True),
        lax.all_gather(expert_down.astype(jnp.bfloat16), "ctx", axis=2, tiled=True),
    )
    expert_in_low = expert_full[0][0]
    expert_down_low = expert_full[1][0]
    residual = layer_input[0].astype(jnp.float32)
    gain_one = gain_low[0].astype(jnp.float32)
    gain_two = gain_low[1].astype(jnp.float32)
    normed_one, norm_one_back = jax.vjp(rms_norm, residual, gain_one)
    normed_one = normed_one.astype(jnp.bfloat16)
    projected = jnp.einsum(
        "td,dgf->tgf", normed_one, attn_in_low, preferred_element_type=jnp.float32
    )
    local_cols = projected.shape[2]
    local_heads = local_cols // HD
    half_dim = HD // 2
    frequency = 10000.0 ** (-jnp.arange(half_dim, dtype=jnp.float32) / half_dim)
    angles = (base_pos + jnp.arange(block_len, dtype=jnp.int32)).astype(jnp.float32)[
        :, None
    ] * frequency[None, :]
    cosine = jnp.cos(angles)
    sine_tab = jnp.sin(angles)
    queries = rotate(projected[:, 0].reshape(block_len, local_heads, HD), cosine, sine_tab).astype(
        jnp.bfloat16
    )
    keys_own = rotate(projected[:, 1].reshape(block_len, local_heads, HD), cosine, sine_tab).astype(
        jnp.bfloat16
    )
    values_own = projected[:, 2].reshape(block_len, local_heads, HD).astype(jnp.bfloat16)
    seg_own = segments[0].astype(jnp.bfloat16)
    keys_prev, values_prev, seg_prev = from_behind((keys_own, values_own, seg_own), "ctx", 1)
    keys_ext = jnp.concatenate([keys_prev, keys_own], axis=0)
    values_ext = jnp.concatenate([values_prev, values_own], axis=0)
    seg_ext = jnp.concatenate([seg_prev, seg_own], axis=0)
    block_rows = min(512, block_len)
    block_total = block_len // block_rows
    starts = jnp.arange(block_total, dtype=jnp.int32) * block_rows

    def forward_block(start_row):
        query_rows, key_rows, value_rows, masked, allowed = block_view(
            queries, keys_ext, values_ext, seg_own, seg_ext, start_row, base_pos
        )
        row_max = jnp.max(masked, axis=-1, keepdims=True)
        exp_terms = jnp.where(allowed[None], jnp.exp(masked - row_max), 0.0)
        row_total = jnp.sum(exp_terms, axis=-1, keepdims=True)
        attn_probs = (exp_terms / row_total).astype(jnp.bfloat16)
        attended = jnp.einsum(
            "hqk,khd->qhd", attn_probs, value_rows, preferred_element_type=jnp.float32
        )
        return (attended, row_max + jnp.log(row_total))

    attended, log_totals = lax.map(forward_block, starts)
    mixed_heads = attended.reshape(block_len, local_cols).astype(jnp.bfloat16)
    attn_total = head_sums(jnp.dot(mixed_heads, attn_out_low, preferred_element_type=jnp.float32))
    after_attn = residual + attn_total
    normed_two, norm_two_back = jax.vjp(rms_norm, after_attn, gain_two)
    normed_two = normed_two.astype(jnp.bfloat16)
    logits = jnp.dot(normed_two, router_low, preferred_element_type=jnp.float32)
    route_rows = routes[0]
    onehot = (route_rows[:, :, None] == jnp.arange(experts, dtype=jnp.int32)[None, None, :]).astype(
        jnp.float32
    )
    picked = jnp.sum(onehot * logits[:, None, :], axis=-1)
    gate_probs = jax.nn.softmax(picked, axis=-1)
    slot_index, owner_route, filled = slot_tables(route_rows, experts, capacity)
    fill_mask = filled.astype(jnp.bfloat16)[:, None]
    send_rows = (normed_two[owner_route // 2] * fill_mask).reshape(experts, capacity, model_width)
    received = to_experts(send_rows).reshape(experts * capacity, model_width)
    expert_gate_up = jnp.einsum(
        "rd,dgf->rgf", received, expert_in_low, preferred_element_type=jnp.float32
    )
    expert_act, expert_act_back = jax.vjp(swiglu, expert_gate_up)
    expert_hidden = expert_act.astype(jnp.bfloat16)
    expert_out = jnp.dot(expert_hidden, expert_down_low, preferred_element_type=jnp.float32)
    returned = to_tokens(expert_out.reshape(experts, capacity, model_width))
    route_out = returned.reshape(experts * capacity, model_width)[slot_index].reshape(
        block_len, 2, model_width
    )
    shared_gate_up = jnp.einsum(
        "td,dgf->tgf", normed_two, shared_in_low, preferred_element_type=jnp.float32
    )
    shared_act, shared_act_back = jax.vjp(swiglu, shared_gate_up)
    shared_hidden = shared_act.astype(jnp.bfloat16)
    shared_out = jnp.dot(shared_hidden, shared_down_low, preferred_element_type=jnp.float32)
    branch_totals = head_sums(jnp.concatenate([shared_out[:, None], route_out], axis=1))
    expert_total = branch_totals[:, 1:]
    layer_out = (
        after_attn + branch_totals[:, 0] + jnp.sum(gate_probs[:, :, None] * expert_total, axis=1)
    )
    upstream = cotangent[0]
    grad_out = upstream.astype(jnp.float32)
    grad_gate = jnp.sum(grad_out[:, None, :] * expert_total, axis=-1)
    grad_picked = gate_probs * (grad_gate - jnp.sum(gate_probs * grad_gate, axis=-1, keepdims=True))
    grad_logits = jnp.sum(grad_picked[:, :, None] * onehot, axis=1).astype(jnp.bfloat16)
    route_grads = (
        (gate_probs[:, :, None] * grad_out[:, None, :])
        .astype(jnp.bfloat16)
        .reshape(2 * block_len, model_width)
    )
    grad_rows = (route_grads[owner_route] * fill_mask).reshape(experts, capacity, model_width)
    grad_received = to_experts(grad_rows).reshape(experts * capacity, model_width)
    rows_again = to_experts(send_rows).reshape(experts * capacity, model_width)
    grad_expert_hidden = jnp.einsum(
        "rd,fd->rf", grad_received, expert_down_low, preferred_element_type=jnp.float32
    )
    grad_expert_gate_up = expert_act_back(grad_expert_hidden)[0].astype(jnp.bfloat16)
    grad_expert_in = jnp.einsum(
        "rd,rgf->dgf", rows_again, grad_expert_gate_up, preferred_element_type=jnp.float32
    )
    grad_expert_down = jnp.einsum(
        "rf,rd->fd", expert_hidden, grad_received, preferred_element_type=jnp.float32
    )
    grad_expert_rows = jnp.einsum(
        "rgf,dgf->rd", grad_expert_gate_up, expert_in_low, preferred_element_type=jnp.float32
    )
    grad_returned = to_tokens(grad_expert_rows.reshape(experts, capacity, model_width))
    grad_routes = grad_returned.reshape(experts * capacity, model_width)[slot_index].reshape(
        block_len, 2, model_width
    )
    grad_shared_hidden = jnp.einsum(
        "td,fd->tf", upstream, shared_down_low, preferred_element_type=jnp.float32
    )
    grad_shared_gate_up = shared_act_back(grad_shared_hidden)[0].astype(jnp.bfloat16)
    grad_shared_in = jnp.einsum(
        "td,tgf->dgf", normed_two, grad_shared_gate_up, preferred_element_type=jnp.float32
    )
    grad_shared_down = jnp.einsum(
        "tf,td->fd", shared_hidden, upstream, preferred_element_type=jnp.float32
    )
    grad_router = jnp.einsum(
        "td,te->de", normed_two, grad_logits, preferred_element_type=jnp.float32
    )
    partial_two = jnp.einsum(
        "tgf,dgf->td", grad_shared_gate_up, shared_in_low, preferred_element_type=jnp.float32
    ) + jnp.sum(grad_routes, axis=1)
    grad_normed_two = grad_sums(partial_two) + jnp.einsum(
        "te,de->td", grad_logits, router_low, preferred_element_type=jnp.float32
    )
    grad_after, grad_gain_two = norm_two_back(grad_normed_two)
    grad_after = grad_after + grad_out
    grad_attn_low = grad_after.astype(jnp.bfloat16)
    grad_attn_out = jnp.einsum(
        "tc,td->cd", mixed_heads, grad_attn_low, preferred_element_type=jnp.float32
    )
    grad_heads = (
        jnp.einsum("td,cd->tc", grad_attn_low, attn_out_low, preferred_element_type=jnp.float32)
        .astype(jnp.bfloat16)
        .reshape(block_len, local_heads, HD)
    )

    def backward_block(block_number, running):
        grad_keys, grad_values, grad_queries = running
        start_row = block_number * block_rows
        query_rows, key_rows, value_rows, masked, allowed = block_view(
            queries, keys_ext, values_ext, seg_own, seg_ext, start_row, base_pos
        )
        log_total = lax.dynamic_index_in_dim(log_totals, block_number, 0, keepdims=False)
        attn_probs = jnp.where(allowed[None], jnp.exp(masked - log_total), 0.0)
        grad_block = lax.dynamic_slice_in_dim(grad_heads, start_row, block_rows, 0)
        grad_probs = jnp.einsum(
            "qhd,khd->hqk", grad_block, value_rows, preferred_element_type=jnp.float32
        )
        inner_sum = jnp.sum(attn_probs * grad_probs, axis=-1, keepdims=True)
        grad_scores = (attn_probs * (grad_probs - inner_sum)).astype(jnp.bfloat16)
        grad_query_rows = (
            jnp.einsum("hqk,khd->qhd", grad_scores, key_rows, preferred_element_type=jnp.float32)
            * 0.125
        )
        grad_key_rows = (
            jnp.einsum("hqk,qhd->khd", grad_scores, query_rows, preferred_element_type=jnp.float32)
            * 0.125
        )
        grad_value_rows = jnp.einsum(
            "hqk,qhd->khd",
            attn_probs.astype(jnp.bfloat16),
            grad_block,
            preferred_element_type=jnp.float32,
        )
        key_offset = start_row + block_len - WINDOW
        grad_keys = lax.dynamic_update_slice_in_dim(
            grad_keys,
            lax.dynamic_slice_in_dim(grad_keys, key_offset, block_rows + WINDOW, 0) + grad_key_rows,
            key_offset,
            0,
        )
        grad_values = lax.dynamic_update_slice_in_dim(
            grad_values,
            lax.dynamic_slice_in_dim(grad_values, key_offset, block_rows + WINDOW, 0)
            + grad_value_rows,
            key_offset,
            0,
        )
        grad_queries = lax.dynamic_update_slice_in_dim(grad_queries, grad_query_rows, start_row, 0)
        return (grad_keys, grad_values, grad_queries)

    zero_ext = jnp.zeros((2 * block_len, local_heads, HD), jnp.float32)
    zero_own = jnp.zeros((block_len, local_heads, HD), jnp.float32)
    grad_keys, grad_values, grad_queries = lax.fori_loop(
        0, block_total, backward_block, (zero_ext, zero_ext, zero_own)
    )
    rim_keys, rim_values = (
        from_behind(grad_keys[:block_len].astype(jnp.bfloat16), "ctx", -1).astype(jnp.float32),
        from_behind(grad_values[:block_len].astype(jnp.bfloat16), "ctx", -1).astype(jnp.float32),
    )
    grad_keys_own = grad_keys[block_len:] + rim_keys
    grad_values_own = grad_values[block_len:] + rim_values
    grad_query_raw = rotate(grad_queries, cosine, -sine_tab)
    grad_key_raw = rotate(grad_keys_own, cosine, -sine_tab)
    grad_projected = (
        jnp.stack([grad_query_raw, grad_key_raw, grad_values_own], axis=1)
        .reshape(block_len, 3, local_cols)
        .astype(jnp.bfloat16)
    )
    grad_attn_in = jnp.einsum(
        "td,tgf->dgf", normed_one, grad_projected, preferred_element_type=jnp.float32
    )
    partial_one = jnp.einsum(
        "tgf,dgf->td", grad_projected, attn_in_low, preferred_element_type=jnp.float32
    )
    grad_residual, grad_gain_one = norm_one_back(grad_sums(partial_one))
    input_grad = grad_after + grad_residual
    dense_grads = (
        lax.psum_scatter(
            jnp.stack([grad_gain_one, grad_gain_two]),
            ("fsdp", "ctx"),
            scatter_dimension=1,
            tiled=True,
        ),
        lax.psum_scatter(grad_attn_in, ("fsdp", "ctx"), scatter_dimension=0, tiled=True),
        lax.psum_scatter(grad_attn_out, ("fsdp", "ctx"), scatter_dimension=1, tiled=True),
        lax.psum_scatter(grad_router, ("fsdp", "ctx"), scatter_dimension=0, tiled=True),
        lax.psum_scatter(grad_shared_in, ("fsdp", "ctx"), scatter_dimension=0, tiled=True),
        lax.psum_scatter(grad_shared_down, ("fsdp", "ctx"), scatter_dimension=1, tiled=True),
    )
    own_gains, own_attn_in, own_attn_out, own_router, own_shared_in, own_shared_down = dense_grads
    expert_grads = (
        lax.psum_scatter(grad_expert_in[None], "ctx", scatter_dimension=1, tiled=True),
        lax.psum_scatter(grad_expert_down[None], "ctx", scatter_dimension=2, tiled=True),
    )
    own_expert_in, own_expert_down = expert_grads
    lead_tp = (tp_index == 0).astype(jnp.float32)
    first_shard = (shard_index == 0).astype(jnp.float32)
    first_ctx = (ctx_index == 0).astype(jnp.float32)
    d_local = gains.shape[1]
    ff_local = shared_down.shape[0]
    fe_local = expert_down.shape[1]
    d_quarter = expert_in.shape[1]
    square_attn_in = own_attn_in * own_attn_in + TINY_SQUARE
    square_attn_out = own_attn_out * own_attn_out + TINY_SQUARE
    square_shared_in = own_shared_in * own_shared_in + TINY_SQUARE
    square_shared_down = own_shared_down * own_shared_down + TINY_SQUARE
    square_expert_in = own_expert_in[0] * own_expert_in[0] + TINY_SQUARE
    square_expert_down = own_expert_down[0] * own_expert_down[0] + TINY_SQUARE
    model_part = lax.dynamic_update_slice(
        jnp.zeros((4, D), jnp.float32),
        jnp.stack(
            [
                jnp.sum(square_attn_in, axis=(1, 2)),
                jnp.sum(square_shared_in, axis=(1, 2)),
                jnp.sum(square_attn_out, axis=0),
                jnp.sum(square_shared_down, axis=0),
            ]
        ),
        (0, shard_index * d_local),
    )
    head_part = lax.dynamic_update_slice(
        jnp.zeros((4, HH), jnp.float32),
        jnp.concatenate(
            [jnp.sum(square_attn_in, axis=0), jnp.sum(square_attn_out, axis=1)[None]], axis=0
        ),
        (0, tp_index * local_cols),
    )
    hidden_part = lax.dynamic_update_slice(
        jnp.zeros((3, FF), jnp.float32),
        jnp.concatenate(
            [jnp.sum(square_shared_in, axis=0), jnp.sum(square_shared_down, axis=1)[None]], axis=0
        ),
        (0, tp_index * ff_local),
    )
    expert_model_part = lax.dynamic_update_slice(
        jnp.zeros((experts, 2, D), jnp.float32),
        jnp.stack([jnp.sum(square_expert_in, axis=(1, 2)), jnp.sum(square_expert_down, axis=0)])[
            None
        ],
        (fsdp_index, 0, ctx_index * d_quarter),
    )
    expert_hidden_part = lax.dynamic_update_slice(
        jnp.zeros((experts, 3, FE), jnp.float32),
        jnp.concatenate(
            [jnp.sum(square_expert_in, axis=0), jnp.sum(square_expert_down, axis=1)[None]], axis=0
        )[None],
        (fsdp_index, 0, tp_index * fe_local),
    )
    scalar_part = jnp.stack(
        [
            lead_tp * jnp.sum(gains * gains),
            jnp.sum(attention_in * attention_in),
            jnp.sum(attention_out * attention_out),
            lead_tp * jnp.sum(router_weight * router_weight),
            jnp.sum(shared_in * shared_in),
            jnp.sum(shared_down * shared_down),
            jnp.sum(expert_in * expert_in),
            jnp.sum(expert_down * expert_down),
            lead_tp * jnp.sum(model_stats[2]),
            first_shard * jnp.sum(head_stats[2]),
            lead_tp * jnp.sum(model_stats[3]),
            first_shard * jnp.sum(hidden_stats[2]),
        ]
    )
    expert_old_part = lax.dynamic_update_slice(
        jnp.zeros((2, experts), jnp.float32),
        jnp.stack(
            [
                lead_tp * jnp.sum(expert_model_stats[0, 0]),
                first_ctx * jnp.sum(expert_hidden_stats[0, 2]),
            ]
        )[:, None],
        (0, fsdp_index),
    )
    global_sums = lax.psum(
        (
            model_part,
            head_part,
            hidden_part,
            expert_model_part,
            expert_hidden_part,
            scalar_part,
            expert_old_part,
        ),
        ("fsdp", "ctx", "tp"),
    )
    (
        model_sum,
        head_sum,
        hidden_sum,
        expert_model_sum,
        expert_hidden_sum,
        scalar_sum,
        expert_old_sum,
    ) = global_sums
    shard_start = shard_index * d_local
    gain_state = DECAY_RATE * model_stats[0:2] + (1.0 - DECAY_RATE) * (
        own_gains * own_gains + TINY_SQUARE
    )
    update_gains = own_gains * lax.rsqrt(gain_state)
    router_new = DECAY_RATE * router_state + (1.0 - DECAY_RATE) * (
        own_router * own_router + TINY_SQUARE
    )
    update_router = own_router * lax.rsqrt(router_new)
    attn_cols_old = jnp.concatenate([head_stats[0:2], value_columns[None]], axis=0).reshape(-1)
    update_attn_in, rows_attn_in, cols_attn_in = factored_update(
        own_attn_in.reshape(d_local, 3 * local_cols),
        model_stats[2],
        attn_cols_old,
        lax.dynamic_slice_in_dim(model_sum[0], shard_start, d_local),
        lax.dynamic_slice_in_dim(head_sum[0:3], tp_index * local_cols, local_cols, 1).reshape(-1),
        D,
        3 * HH,
        scalar_sum[8],
        jnp.sum(model_sum[0]),
    )
    update_attn_out, rows_attn_out, cols_attn_out = factored_update(
        own_attn_out,
        head_stats[2],
        model_stats[4],
        lax.dynamic_slice_in_dim(head_sum[3], tp_index * local_cols, local_cols),
        lax.dynamic_slice_in_dim(model_sum[2], shard_start, d_local),
        HH,
        D,
        scalar_sum[9],
        jnp.sum(head_sum[3]),
    )
    update_shared_in, rows_shared_in, cols_shared_in = factored_update(
        own_shared_in.reshape(d_local, 2 * ff_local),
        model_stats[3],
        hidden_stats[0:2].reshape(-1),
        lax.dynamic_slice_in_dim(model_sum[1], shard_start, d_local),
        lax.dynamic_slice_in_dim(hidden_sum[0:2], tp_index * ff_local, ff_local, 1).reshape(-1),
        D,
        2 * FF,
        scalar_sum[10],
        jnp.sum(model_sum[1]),
    )
    update_shared_down, rows_shared_down, cols_shared_down = factored_update(
        own_shared_down,
        hidden_stats[2],
        model_stats[5],
        lax.dynamic_slice_in_dim(hidden_sum[2], tp_index * ff_local, ff_local),
        lax.dynamic_slice_in_dim(model_sum[3], shard_start, d_local),
        FF,
        D,
        scalar_sum[11],
        jnp.sum(hidden_sum[2]),
    )
    own_expert_model = lax.dynamic_index_in_dim(expert_model_sum, fsdp_index, 0, keepdims=False)
    own_expert_hidden = lax.dynamic_index_in_dim(expert_hidden_sum, fsdp_index, 0, keepdims=False)
    old_expert_totals = lax.dynamic_index_in_dim(expert_old_sum, fsdp_index, 1, keepdims=False)
    update_expert_in, rows_expert_in, cols_expert_in = factored_update(
        own_expert_in[0].reshape(d_quarter, 2 * fe_local),
        expert_model_stats[0, 0],
        expert_hidden_stats[0, 0:2].reshape(-1),
        lax.dynamic_slice_in_dim(own_expert_model[0], ctx_index * d_quarter, d_quarter),
        lax.dynamic_slice_in_dim(own_expert_hidden[0:2], tp_index * fe_local, fe_local, 1).reshape(
            -1
        ),
        D,
        2 * FE,
        old_expert_totals[0],
        jnp.sum(own_expert_model[0]),
    )
    update_expert_down, rows_expert_down, cols_expert_down = factored_update(
        own_expert_down[0],
        expert_hidden_stats[0, 2],
        expert_model_stats[0, 1],
        lax.dynamic_slice_in_dim(own_expert_hidden[2], tp_index * fe_local, fe_local),
        lax.dynamic_slice_in_dim(own_expert_model[1], ctx_index * d_quarter, d_quarter),
        FE,
        D,
        old_expert_totals[1],
        jnp.sum(own_expert_hidden[2]),
    )
    clip_part = jnp.stack(
        [
            lead_tp * jnp.sum(update_gains * update_gains),
            jnp.sum(update_attn_in * update_attn_in),
            jnp.sum(update_attn_out * update_attn_out),
            lead_tp * jnp.sum(update_router * update_router),
            jnp.sum(update_shared_in * update_shared_in),
            jnp.sum(update_shared_down * update_shared_down),
            jnp.sum(update_expert_in * update_expert_in),
            jnp.sum(update_expert_down * update_expert_down),
        ]
    )
    clip_total = lax.psum(clip_part, ("fsdp", "ctx", "tp"))
    elements = jnp.array(
        [
            2 * D,
            D * 3 * HH,
            HH * D,
            D * experts,
            D * 2 * FF,
            FF * D,
            experts * D * 2 * FE,
            experts * FE * D,
        ],
        jnp.float32,
    )
    update_roots = jnp.sqrt(clip_total / elements)
    new_gains = apply_update(gains, update_gains, update_roots[0], scalar_sum[0], elements[0])
    new_attn_in = apply_update(
        attention_in,
        update_attn_in.reshape(attention_in.shape),
        update_roots[1],
        scalar_sum[1],
        elements[1],
    )
    new_attn_out = apply_update(
        attention_out, update_attn_out, update_roots[2], scalar_sum[2], elements[2]
    )
    new_router = apply_update(
        router_weight, update_router, update_roots[3], scalar_sum[3], elements[3]
    )
    new_shared_in = apply_update(
        shared_in,
        update_shared_in.reshape(shared_in.shape),
        update_roots[4],
        scalar_sum[4],
        elements[4],
    )
    new_shared_down = apply_update(
        shared_down, update_shared_down, update_roots[5], scalar_sum[5], elements[5]
    )
    new_expert_in = apply_update(
        expert_in,
        update_expert_in.reshape(expert_in.shape),
        update_roots[6],
        scalar_sum[6],
        elements[6],
    )
    new_expert_down = apply_update(
        expert_down,
        update_expert_down.reshape(expert_down.shape),
        update_roots[7],
        scalar_sum[7],
        elements[7],
    )
    new_model_stats = jnp.concatenate(
        [gain_state, jnp.stack([rows_attn_in, rows_shared_in, cols_attn_out, cols_shared_down])],
        axis=0,
    )
    attn_cols_new = cols_attn_in.reshape(3, local_cols)
    new_head_stats = jnp.concatenate([attn_cols_new[0:2], rows_attn_out[None]], axis=0)
    new_value_columns = attn_cols_new[2]
    new_hidden_stats = jnp.concatenate(
        [cols_shared_in.reshape(2, ff_local), rows_shared_down[None]], axis=0
    )
    new_expert_model_stats = jnp.stack([rows_expert_in, cols_expert_down])[None]
    new_expert_hidden_stats = jnp.concatenate(
        [cols_expert_in.reshape(2, fe_local), rows_expert_down[None]], axis=0
    )[None]
    return (
        layer_out.astype(jnp.bfloat16)[None],
        input_grad[None],
        own_gains,
        own_attn_in,
        own_attn_out,
        own_router,
        own_shared_in,
        own_shared_down,
        own_expert_in,
        own_expert_down,
        new_gains,
        new_attn_in,
        new_attn_out,
        new_router,
        new_shared_in,
        new_shared_down,
        new_expert_in,
        new_expert_down,
        new_model_stats,
        new_head_stats,
        new_value_columns,
        new_hidden_stats,
        router_new,
        new_expert_model_stats,
        new_expert_hidden_stats,
        update_roots,
    )


def solution(mesh):
    in_specs = (
        P("fsdp", "ctx", None),
        P("fsdp", "ctx"),
        P("fsdp", "ctx", None),
        P("fsdp", "ctx", None),
        P(None, ("fsdp", "ctx")),
        P(("fsdp", "ctx"), None, "tp"),
        P("tp", ("fsdp", "ctx")),
        P(("fsdp", "ctx"), None),
        P(("fsdp", "ctx"), None, "tp"),
        P("tp", ("fsdp", "ctx")),
        P("fsdp", "ctx", None, "tp"),
        P("fsdp", "tp", "ctx"),
        P(None, ("fsdp", "ctx")),
        P(None, "tp"),
        P("tp"),
        P(None, "tp"),
        P(("fsdp", "ctx"), None),
        P("fsdp", None, "ctx"),
        P("fsdp", None, "tp"),
    )
    out_specs = (
        P("fsdp", "ctx", None),
        P("fsdp", "ctx", None),
        P(None, ("fsdp", "ctx")),
        P(("fsdp", "ctx"), None, "tp"),
        P("tp", ("fsdp", "ctx")),
        P(("fsdp", "ctx"), None),
        P(("fsdp", "ctx"), None, "tp"),
        P("tp", ("fsdp", "ctx")),
        P("fsdp", "ctx", None, "tp"),
        P("fsdp", "tp", "ctx"),
        P(None, ("fsdp", "ctx")),
        P(("fsdp", "ctx"), None, "tp"),
        P("tp", ("fsdp", "ctx")),
        P(("fsdp", "ctx"), None),
        P(("fsdp", "ctx"), None, "tp"),
        P("tp", ("fsdp", "ctx")),
        P("fsdp", "ctx", None, "tp"),
        P("fsdp", "tp", "ctx"),
        P(None, ("fsdp", "ctx")),
        P(None, "tp"),
        P("tp"),
        P(None, "tp"),
        P(("fsdp", "ctx"), None),
        P("fsdp", None, "ctx"),
        P("fsdp", None, "tp"),
        P(),
    )
    return jax.shard_map(local, mesh=mesh, in_specs=in_specs, out_specs=out_specs, check_vma=False)
```

profile of v0, /device:TPU:0, one launch (start us, length us, event | category | flops | bytes accessed | tf_op | source)
XLA Modules:
  0.0 2331.0 jit_solution(4953208782980414797)
XLA Ops:
  9.5 22.1 all-gather
  35.5 35.3 %all_gather.25 = bf16[768,3,192]{2,1,0:T(4,128)(2,1)S(1)} all-gather(bf16[96,3,192]{2,1,0:T(4,128)(2,1)S(1)} %copy.144), channel_id=1, replica_groups=mesh['fsdp'=4,'ctx'=2,'tp'=4] {'fsdp','ctx'}, dimensions={0}, use_global_device_ids=true | all-gather | bytes 995328 | tf_op jit(solution)/shard_map/all_gather | solution.py:160
  93.0 33.2 %all_gather.26 = bf16[192,768]{0,1:T(8,128)(2,1)} all-gather(bf16[192,96]{0,1:T(8,128)(2,1)} %copy.147), channel_id=1, replica_groups=mesh['fsdp'=4,'ctx'=2,'tp'=4] {'fsdp','ctx'}, dimensions={1}, use_global_device_ids=true | all-gather | bytes 331776 | tf_op jit(solution)/shard_map/all_gather | solution.py:161
  131.6 17.0 all-gather.1
  166.8 32.9 %while.39 = (s32[]{:T(128)}, bf16[2,512,3,64]{1,3,2,0:T(8,128)(2,1)S(1)}, f32[2,3,512,1]{2,1,3,0:T(4,128)}, s32[2]{0:T(128)S(1)}, bf16[2048,3,64]{0,2,1:T(8,128)...) while((s32[]{:T(128)}, ...), condition=%wide.region_4.5_spmd, body=%wide.region_1.4_spmd.sunk | while | flops 644092928 | bytes 33314568 | solution.py:219
  222.4 48.0 %all-reduce.12.cloned.1.call-done = f32[1024,768]{1,0:T(8,128)} async-done(((f32[1024,768]{1,0:T(8,128)}), f32[1024,768]{1,0:T(8,128)}) %all-reduce.12.cloned.1.call-update) | async-done | bytes 3145744 | tf_op jit(solution)/shard_map/psum | solution.py:113
  276.3 17.8 gather_fusion
  299.0 21.4 gather_fusion.2
  328.9 142.5 %all_to_all.21 = bf16[4,1024,768]{2,1,0:T(8,128)(2,1)} all-to-all(bf16[4,1024,768]{2,1,0:T(8,128)(2,1)S(1)} %get-tuple-element.918), channel_id=1, replica_groups=mesh['fsdp'=4,'ctx'=2,'tp'=4] {'fsdp'}, dimensions={0} | all-to-all | bytes 12582912 | tf_op jit(solution)/shard_map/all_to_all | solution.py:121
  480.2 12.1 all_gather.30
  492.3 15.2 all-gather.7.cloned.1.call-done
  507.5 12.5 fusion.86
  520.0 93.9 %all-to-all-done.2 = bf16[4,1024,768]{2,1,0:T(8,128)(2,1)} async-done(((bf16[4,1024,768]{2,1,0:T(8,128)(2,1)}), bf16[4,1024,768]{2,1,0:T(8,128)(2,1)}, u32[]{:S(2)}, u32[]{:S(2)}) %all-to-all-start.2) | async-done | bytes 6291488 | tf_op jit(solution)/shard_map/all_to_all | solution.py:121
  613.9 18.4 fusion.56
  640.2 9.5 convolution_bitcast_fusion
  671.7 256.9 %all-to-all-done.3 = f32[4,1024,768]{2,1,0:T(8,128)} async-done(((f32[4,1024,768]{2,1,0:T(8,128)}), f32[4,1024,768]{2,1,0:T(8,128)}, u32[]{:S(2)}, u32[]{:S(2)}) %all-to-all-start.3) | async-done | bytes 12582944 | tf_op jit(solution)/shard_map/all_to_all | solution.py:125
  936.5 314.4 %all_gather.28 = bf16[512,768]{0,1:T(8,128)(2,1)} all-gather(bf16[512,96]{0,1:T(8,128)(2,1)S(1)} %get-tuple-element.904), channel_id=1, replica_groups=mesh['fsdp'=4,'ctx'=2,'tp'=4] {'fsdp','ctx'}, dimensions={1}, use_global_device_ids=true | all-gather | bytes 884736 | tf_op jit(solution)/shard_map/all_gather | solution.py:164
  1260.5 15.3 gather_fusion.3
  1283.9 15.3 gather_fusion.1
  1313.7 11.9 reduce_sum.547
  1345.9 12.4 convolution_bitcast_fusion.1
  1358.5 198.0 %all-reduce.20.cloned.1.call-done = (f32[1024,3,768]{2,0,1:T(8,128)}, f32[1024,768]{1,0:T(8,128)}) async-done(((f32[1024,3,768]{2,0,1:T(8,128)}, f32[1024,768]{1,0:T(8,128)}), (f32[1024,3,768]{2,0,1:T(8,128)}, f32[1024,768]{1,0:T(8,128)})) %all-reduce.20.cloned.1.call-update) | async-done | bytes 12582928 | tf_op jit(solution)/shard_map/psum | solution.py:113
  1570.8 76.3 %while.40 = (s32[]{:T(128)}, f32[2048,3,64]{0,2,1:T(8,128)}, f32[2048,3,64]{0,2,1:T(8,128)S(1)}, f32[1024,3,64]{0,2,1:T(8,128)}, bf16[1024,3,64]{0,2,1:T(8,128)(...) while((s32[]{:T(128)}, f32[2048,3,64]{0,2,1:T(8,128)}, ...), condition=%wide.region_25.26_spmd, body=%wide.region_23.25_spmd.sunk | while | flops 1541608448 | bytes 106823088 | solution.py:365
  1651.3 11.1 collective-permute-done.3
  1694.4 47.4 %all-reduce.14.cloned.1.call-done = f32[1024,768]{1,0:T(8,128)} async-done(((f32[1024,768]{1,0:T(8,128)}), f32[1024,768]{1,0:T(8,128)}) %all-reduce.14.cloned.1.call-update) | async-done | bytes 3145744 | tf_op jit(solution)/shard_map/psum | solution.py:117
  1769.9 52.0 %reduce-scatter.17.cloned.1.call-done = f32[96,2,512]{2,0,1:T(8,128)} async-done(((f32[768,2,512]{2,0,1:T(8,128)}), f32[96,2,512]{2,0,1:T(8,128)}) %reduce-scatter.17.cloned.1.call-update) | async-done | bytes 393232 | tf_op jit(solution)/shard_map/reduce_scatter | solution.py:399
  1831.9 49.6 %all-reduce.16.cloned.1.call-done = f32[4,3,2048]{2,1,0:T(4,128)} async-done(((f32[4,3,2048]{2,1,0:T(4,128)}), f32[4,3,2048]{2,1,0:T(4,128)}) %all-reduce.16.cloned.1.call-update) | async-done | bytes 98320 | tf_op jit(solution)/shard_map/psum | solution.py:487
  1889.8 62.1 %reduce-scatter.27.cloned.1.call-done = f32[96,192]{1,0:T(8,128)} async-done(((f32[768,192]{1,0:T(8,128)}), f32[96,192]{1,0:T(8,128)}) %reduce-scatter.27.cloned.1.call-update) | async-done | bytes 73744
  1958.4 57.7 %reduce-scatter.25.cloned.1.call-done = f32[96,2]{1,0:T(8,128)} async-done(((f32[768,2]{1,0:T(8,128)}), f32[96,2]{1,0:T(8,128)}) %reduce-scatter.25.cloned.1.call-update) | async-done | bytes 784
  2017.0 71.1 %reduce-scatter.15.cloned.1.call-done = f32[96,3,192]{2,0,1:T(8,128)} async-done(((f32[768,3,192]{2,0,1:T(8,128)}), f32[96,3,192]{2,0,1:T(8,128)}) %reduce-scatter.15.cloned.1.call-update) | async-done | bytes 221200 | tf_op jit(solution)/shard_map/reduce_scatter | solution.py:396
  2097.5 119.9 %all-reduce.18.cloned.1.call-done = (f32[12]{0:T(128)}, f32[4,768]{1,0:T(4,128)}, f32[4,768]{1,0:T(4,128)}, f32[3,2048]{1,0:T(4,128)}, f32[2,4]{0,1:T(4,128)}, /*index=5*/f32[4,2,768]{2,1,0:T(2,128)}) async-done(((f32[12]{0:T(128)}, f32[4,768]{1,0:T(4,128)}, f32[4,768]{1,0:T(4,128)}, f32[3,2048]{1,0:T(4,128)}, f32[2,4]{0,1:T(4,128)}, /*index=5*/f32[4,2,768]{2,1,0:T(2,128)}), (f32[12]{0:T(128)}, ...) | async-done | bytes 73824 | tf_op jit(solution)/shard_map/psum | solution.py:487
  2258.3 41.7 %psum.95 = f32[8]{0:T(128)} all-reduce(f32[8]{0:T(128)} %stack.162), channel_id=1, replica_groups=mesh['fsdp'=4,'ctx'=2,'tp'=4] {'fsdp','ctx','tp'}, use_global_device_ids=true, to_apply=%region_85.86 | all-reduce | flops 8 | bytes 64 | tf_op jit(solution)/shard_map/psum | solution.py:601
  (575 shorter events, 444.6 us)
Async XLA Ops:
  8.0 262.4 %all-reduce.12.cloned.1.call-start = ((), (), s32[]{:S(2)}) async-start(), calls=%async_computation.12 | async-start | bytes 6291456 | tf_op jit(solution)/shard_map/psum | solution.py:113
  31.7 241.2 %copy-start.82 = (f32[768]{0:T(1024)}, f32[768]{0:T(1024)S(1)}, u32[]{:S(2)}) copy-start(f32[768]{0:T(1024)S(1)} %get-tuple-element.813) | copy-start | bytes 9220
  79.1 85.2 %collective-permute-start.2 = (bf16[1024,3,64]{0,2,1:T(8,128)(2,1)}, bf16[1024,3,64]{0,2,1:T(8,128)(2,1)}, u32[]{:S(2)}, u32[]{:S(2)}) collective-permute-start(bf16[1024,3,64]{0,2,1:T(8,128)(2,1)} %pad_maximum_fusion.6), channel_id=1, source_target_pairs={{0,4},{1,5},{2,6},{3,7},{8,12},{9,13},{10,14},{11,15},{16,20},{17,... | collective-permute-start | bytes 1179656 | tf_op jit(solution)/shard_map/ppermute | solution.py:25
  84.2 81.4 %collective-permute-start = (bf16[1024,3,64]{0,2,1:T(8,128)(2,1)}, bf16[1024,3,64]{0,2,1:T(8,128)(2,1)}, u32[]{:S(2)}, u32[]{:S(2)}) collective-permute-start(bf16[1024,3,64]{0,2,1:T(8,128)(2,1)} %bitcast.15), channel_id=1, source_target_pairs={{0,4},{1,5},{2,6},{3,7},{8,12},{9,13},{10,14},{11,15},{16,20},{17,... | collective-permute-start | bytes 1179656 | tf_op jit(solution)/shard_map/ppermute | solution.py:25
  86.4 77.2 %collective-permute-start.1 = (bf16[1024]{0:T(1024)(128)(2,1)S(1)}, bf16[1024]{0:T(1024)(128)(2,1)}, u32[]{:S(2)}, u32[]{:S(2)}) collective-permute-start(bf16[1024]{0:T(1024)(128)(2,1)S(1)} %convert_reduce_fusion), channel_id=1, source_target_pairs={{0,4},{1,5},{2,6},{3,7},{8,12},{9,13},{10,14},{11,15},{16,20},{17,... | collective-permute-start | bytes 6152 | tf_op jit(solution)/shard_map/ppermute | solution.py:25
  273.6 977.4 %copy-start = (bf16[1024,768]{1,0:T(8,128)(2,1)}, bf16[1024,768]{1,0:T(8,128)(2,1)S(1)}, u32[]{:S(2)}) copy-start(bf16[1024,768]{1,0:T(8,128)(2,1)S(1)} %multiply_convert_fusion.3) | copy-start | bytes 4718596
  471.3 142.5 %all-to-all-start.2 = ((bf16[4,1024,768]{2,1,0:T(8,128)(2,1)}), bf16[4,1024,768]{2,1,0:T(8,128)(2,1)}, u32[]{:S(2)}, u32[]{:S(2)}) async-start(bf16[4,1024,768]{2,1,0:T(8,128)(2,1)} %get-tuple-element.917), calls=%async_computation.2 | async-start | bytes 12582912 | tf_op jit(solution)/shard_map/all_to_all | solution.py:121
  476.7 30.8 %all-gather.7.cloned.1.call-start = ((), (), s32[]{:S(2)}) async-start(), calls=%async_computation.14 | async-start | bytes 2359296 | tf_op jit(solution)/shard_map/all_gather | solution.py:168
  649.7 279.0 %all-to-all-start.3 = ((f32[4,1024,768]{2,1,0:T(8,128)}), f32[4,1024,768]{2,1,0:T(8,128)}, u32[]{:S(2)}, u32[]{:S(2)}) async-start(f32[4,1024,768]{2,1,0:T(8,128)} %convolution_bitcast_fusion), calls=%async_computation.3 | async-start | bytes 25165824 | tf_op jit(solution)/shard_map/all_to_all | solution.py:125
  671.7 263.3 %copy-start.29 = (f32[96,2,512]{2,1,0:T(2,128)S(1)}, f32[96,2,512]{2,1,0:T(2,128)}, u32[]{:S(2)}) copy-start(f32[96,2,512]{2,1,0:T(2,128)} %param.32) | copy-start | bytes 1179652
  671.7 264.2 %copy-start.57 = (f32[512,96]{0,1:T(8,128)S(1)}, f32[512,96]{0,1:T(8,128)}, u32[]{:S(2)}) copy-start(f32[512,96]{0,1:T(8,128)} %param.33) | copy-start | bytes 589828
  928.6 355.3 %all-to-all-start.1 = ((f32[4,1024,768]{2,1,0:T(8,128)}), f32[4,1024,768]{2,1,0:T(8,128)}, u32[]{:S(2)}, u32[]{:S(2)}) async-start(f32[4,1024,768]{2,1,0:T(8,128)} %fusion.102), calls=%async_computation.1 | async-start | bytes 25165824 | tf_op jit(solution)/shard_map/all_to_all | solution.py:125
  935.0 315.9 %all-gather.5.cloned.1.call-start = ((), (), s32[]{:S(2)}) async-start(), calls=%async_computation.13 | async-start | bytes 1769472 | tf_op jit(solution)/shard_map/all_gather | solution.py:163
  935.8 620.7 %all-reduce.20.cloned.1.call-start = ((), (), s32[]{:S(2)}) async-start(), calls=%async_computation.26 | async-start | bytes 25165824 | tf_op jit(solution)/shard_map/psum | solution.py:113
  1336.9 348.3 %reduce-scatter.23.cloned.1.call-start = ((), (), s32[]{:S(2)}) async-start(), calls=%async_computation.20 | async-start | bytes 2359296 | tf_op jit(solution)/shard_map/reduce_scatter | solution.py:405
  1345.8 340.8 %reduce-scatter.21.cloned.1.call-start = ((), (), s32[]{:S(2)}) async-start(), calls=%async_computation.19 | async-start | bytes 4718592 | tf_op jit(solution)/shard_map/reduce_scatter | solution.py:404
  1345.9 210.6 %copy-start.79 = (f32[1024,2]{0,1:T(2,128)S(1)}, f32[1024,2]{0,1:T(2,128)}, u32[]{:S(2)}) copy-start(f32[1024,2]{0,1:T(2,128)} %copy-done.78) | copy-start | bytes 24580
  1358.3 383.5 %all-reduce.14.cloned.1.call-start = ((), (), s32[]{:S(2)}) async-start(), calls=%async_computation.15 | async-start | bytes 6291456 | tf_op jit(solution)/shard_map/psum | solution.py:117
  1648.5 13.9 collective-permute-start.3
  1649.8 19.6 collective-permute-start.4
  1673.4 94.9 %reduce-scatter.19.cloned.1.call-start = ((), (), s32[]{:S(2)}) async-start(), calls=%async_computation.18 | async-start | bytes 1769472 | tf_op jit(solution)/shard_map/reduce_scatter | solution.py:400
  1679.3 142.7 %reduce-scatter.17.cloned.1.call-start = ((), (), s32[]{:S(2)}) async-start(), calls=%async_computation.17 | async-start | bytes 3538944 | tf_op jit(solution)/shard_map/reduce_scatter | solution.py:399
  1685.1 196.4 %all-reduce.16.cloned.1.call-start = ((), (), s32[]{:S(2)}) async-start(), calls=%async_computation.21 | async-start | bytes 262144 | tf_op jit(solution)/shard_map/psum | solution.py:487
  1689.1 198.0 %reduce-scatter.29.cloned.1.call-start = ((), (), s32[]{:S(2)}) async-start(), calls=%async_computation.24 | async-start | bytes 442368
  1690.6 261.3 %reduce-scatter.27.cloned.1.call-start = ((), (), s32[]{:S(2)}) async-start(), calls=%async_computation.23 | async-start | bytes 884736
  1694.3 321.8 %reduce-scatter.25.cloned.1.call-start = ((), (), s32[]{:S(2)}) async-start(), calls=%async_computation.22 | async-start | bytes 442368
  1745.8 342.2 %reduce-scatter.15.cloned.1.call-start = ((), (), s32[]{:S(2)}) async-start(), calls=%async_computation.16 | async-start | bytes 2654208 | tf_op jit(solution)/shard_map/reduce_scatter | solution.py:396
  1749.0 468.4 %all-reduce.18.cloned.1.call-start = ((), (), s32[]{:S(2)}) async-start(), calls=%async_computation.25 | async-start | bytes 168960 | tf_op jit(solution)/shard_map/psum | solution.py:487
  1953.6 293.6 %copy-start.28 = (f32[96,2,512]{2,0,1:T(8,128)S(1)}, f32[96,2,512]{2,0,1:T(8,128)}, u32[]{:S(2)}) copy-start(f32[96,2,512]{2,0,1:T(8,128)} %reduce-scatter.17.cloned.1.call-done) | copy-start | bytes 1179652
  1958.4 345.5 %copy-start.12 = (f32[1,384,2,512]{3,1,2,0:T(8,128)S(1)}, f32[1,384,2,512]{3,1,2,0:T(8,128)}, u32[]{:S(2)}) copy-start(f32[1,384,2,512]{3,1,2,0:T(8,128)} %reduce-scatter.21.cloned.1.call-done) | copy-start | bytes 4718596
  1958.4 345.5 %copy-start.19 = (f32[1,384,2,512]{3,2,1,0:T(2,128)S(1)}, f32[1,384,2,512]{3,2,1,0:T(2,128)}, u32[]{:S(2)}) copy-start(f32[1,384,2,512]{3,2,1,0:T(2,128)} %param.34) | copy-start | bytes 4718596
  2017.0 208.5 %copy-start.109 = (f32[2,96]{1,0:T(2,128)}, f32[2,96]{1,0:T(2,128)S(1)}, u32[]{:S(2)}) copy-start(f32[2,96]{1,0:T(2,128)S(1)} %copy.174) | copy-start | bytes 2308
  (132 other events, 2637.6 us)
Sparse Core Ops, SparseCore 0:
  203.5 66.8 all-reduce.11
  938.6 110.5 all-gather.4
  1337.0 219.4 all-reduce.19
  1673.5 68.2 all-reduce.13
  1747.7 133.7 all-reduce.15
  2095.1 122.2 all-reduce.17
Sparse Core Ops, SparseCore 1:
  479.3 28.1 all-gather.6
  1345.9 24.2 reduce-scatter.22
  1372.4 43.3 reduce-scatter.20
  1679.3 64.7 reduce-scatter.18
  1748.2 73.7 reduce-scatter.16
  1825.6 60.5 reduce-scatter.28
  1890.2 61.6 reduce-scatter.26
  1955.5 60.5 reduce-scatter.24
  2020.1 68.0 reduce-scatter.14
where the time goes:
time: 2340 us; the launch traced here: 2330 us
  waiting for transfers between devices  1090 us (47%)
  blocking collectives  618 us (26%)
  local copies, waits for them, and re-layouts  197 us (8%)
  other arithmetic  174 us (7%)
  matrix products  173 us (7%)
  between operations  42.7 us (2%)
  starting transfers between devices  29.3 us (1%)
    all_gather x1, blocking collectives, local(): lax.all_gather(shared_down.astype(jnp.bfloat16), ('fsdp', 'ctx'), axis=1,...  314 us
    all_to_all x2, waiting for transfers between devices, to_tokens(): lax.all_to_all(buffer_rows, 'fsdp', split_axis=0, concat_axis=0, tiled=True)  257 us
    psum x2, waiting for transfers between devices, head_sums(): return lax.psum(partial_sum, 'tp')  246 us
    psum x2, waiting for transfers between devices, local(): lax.psum((model_part, head_part, hidden_part, expert_model_part, expert_h...  170 us
    all_to_all x1, blocking collectives, to_experts(): lax.all_to_all(buffer_rows, 'fsdp', split_axis=0, concat_axis=0, tiled=True)  142 us
    unnamed x18, waiting for transfers between devices  120 us
    all_to_all x1, waiting for transfers between devices, to_experts(): lax.all_to_all(buffer_rows, 'fsdp', split_axis=0, concat_axis=0, tiled=True)  93.9 us
    reduce_scatter x1, waiting for transfers between devices, local(): lax.psum_scatter(grad_attn_in, ('fsdp', 'ctx'), scatter_dimension=0, tile...  71.1 us
  transfers between devices with their start and end apart: 23, of which 14 were waited for; matrix products, arithmetic and copies ran while one was open for 13% of the time, Pallas kernels for 0%

commit v1 on v0

--- a/solution.py
+++ b/solution.py
@@ -109,20 +109,121 @@
     return weight - STEP_RATE * param_scale * update / jnp.maximum(1.0, update_root / CLIP_LIMIT)
 
 
-def head_sums(partial_sum):
-    return lax.psum(partial_sum, "tp")
-
-
-def grad_sums(partial_sum):
-    return lax.psum(partial_sum, "tp")
-
-
-def to_experts(buffer_rows):
-    return lax.all_to_all(buffer_rows, "fsdp", split_axis=0, concat_axis=0, tiled=True)
-
-
-def to_tokens(buffer_rows):
-    return lax.all_to_all(buffer_rows, "fsdp", split_axis=0, concat_axis=0, tiled=True)
+def swiglu_experts(gate_up):
+    return jax.nn.silu(gate_up[:, :, 0]) * gate_up[:, :, 1]
+
+
+def gather_packed(pieces, axes):
+    flat = jnp.concatenate([piece.reshape(-1) for piece, _ in pieces])
+    full = lax.all_gather(flat, axes, axis=0, tiled=False)
+    count = full.shape[0]
+    results = []
+    offset = 0
+    for piece, dim in pieces:
+        size = piece.size
+        part = full[:, offset : offset + size].reshape((count,) + piece.shape)
+        offset += size
+        part = jnp.moveaxis(part, 0, dim)
+        shape = list(piece.shape)
+        shape[dim] *= count
+        results.append(part.reshape(shape))
+    return results
+
+
+def scatter_packed(pieces, axes, count):
+    columns = []
+    local_shapes = []
+    for grad, dim in pieces:
+        shape = grad.shape
+        split = shape[:dim] + (count, shape[dim] // count) + shape[dim + 1 :]
+        local_shapes.append(shape[:dim] + (shape[dim] // count,) + shape[dim + 1 :])
+        part = jnp.moveaxis(grad.reshape(split), dim, 0)
+        columns.append(part.reshape(count, -1))
+    packed = jnp.concatenate(columns, axis=1)
+    width = packed.shape[1]
+    rows = -(-width // 1024) * 8
+    packed = jnp.pad(packed, ((0, 0), (0, rows * 128 - width))).reshape(count * rows, 128)
+    own = lax.psum_scatter(packed, axes, scatter_dimension=0, tiled=True).reshape(-1)
+    results = []
+    offset = 0
+    for local_shape in local_shapes:
+        size = 1
+        for extent in local_shape:
+            size *= extent
+        results.append(own[offset : offset + size].reshape(local_shape))
+        offset += size
+    return results
+
+
+def experts_dense(normed_two, grad_out, weights, expert_in_all, expert_down_all):
+    gate_up = jnp.einsum(
+        "td,edgf->etgf", normed_two, expert_in_all, preferred_element_type=jnp.float32
+    )
+    act, act_back = jax.vjp(swiglu_experts, gate_up)
+    hidden = act.astype(jnp.bfloat16)
+    outs = jnp.einsum("etf,efd->etd", hidden, expert_down_all, preferred_element_type=jnp.float32)
+    weights_e = weights.T[:, :, None]
+    combined = jnp.sum(weights_e * outs, axis=0)
+    gate_dots = jnp.sum(outs * grad_out[None], axis=-1).T
+    grad_outs = (weights_e * grad_out[None]).astype(jnp.bfloat16)
+    grad_hidden = jnp.einsum(
+        "etd,efd->etf", grad_outs, expert_down_all, preferred_element_type=jnp.float32
+    )
+    grad_gate_up = act_back(grad_hidden)[0].astype(jnp.bfloat16)
+    grad_down = jnp.einsum("etf,etd->efd", hidden, grad_outs, preferred_element_type=jnp.float32)
+    grad_in = jnp.einsum(
+        "td,etgf->edgf", normed_two, grad_gate_up, preferred_element_type=jnp.float32
+    )
+    grad_rows = jnp.einsum(
+        "etgf,edgf->td", grad_gate_up, expert_in_all, preferred_element_type=jnp.float32
+    )
+    return combined, gate_dots, grad_rows, grad_in, grad_down
+
+
+def experts_routed(
+    normed_two, grad_out, route_rows, gate_probs, expert_in_low, expert_down_low, capacity
+):
+    block_len, model_width = normed_two.shape
+    experts = lax.axis_size("fsdp")
+    slot_index, owner_route, filled = slot_tables(route_rows, experts, capacity)
+    fill_mask = filled.astype(jnp.bfloat16)[:, None]
+    send_rows = (normed_two[owner_route // 2] * fill_mask).reshape(experts, capacity, model_width)
+    route_grads = (
+        (gate_probs[:, :, None] * grad_out[:, None, :])
+        .astype(jnp.bfloat16)
+        .reshape(2 * block_len, model_width)
+    )
+    grad_rows_sent = (route_grads[owner_route] * fill_mask).reshape(experts, capacity, model_width)
+    exchange = lambda rows: lax.all_to_all(rows, "fsdp", split_axis=0, concat_axis=0, tiled=True)
+    received = exchange(send_rows).reshape(experts * capacity, model_width)
+    grad_received = exchange(grad_rows_sent).reshape(experts * capacity, model_width)
+    gate_up = jnp.einsum("rd,dgf->rgf", received, expert_in_low, preferred_element_type=jnp.float32)
+    act, act_back = jax.vjp(swiglu, gate_up)
+    hidden = act.astype(jnp.bfloat16)
+    outs = jnp.dot(hidden, expert_down_low, preferred_element_type=jnp.float32)
+    grad_hidden = jnp.einsum(
+        "rd,fd->rf", grad_received, expert_down_low, preferred_element_type=jnp.float32
+    )
+    grad_gate_up = act_back(grad_hidden)[0].astype(jnp.bfloat16)
+    grad_in = jnp.einsum("rd,rgf->dgf", received, grad_gate_up, preferred_element_type=jnp.float32)
+    grad_down = jnp.einsum("rf,rd->fd", hidden, grad_received, preferred_element_type=jnp.float32)
+    grad_expert_rows = jnp.einsum(
+        "rgf,dgf->rd", grad_gate_up, expert_in_low, preferred_element_type=jnp.float32
+    )
+    returned = exchange(outs.reshape(experts, capacity, model_width))
+    route_out = returned.reshape(experts * capacity, model_width)[slot_index].reshape(
+        block_len, 2, model_width
+    )
+    grad_returned = exchange(grad_expert_rows.reshape(experts, capacity, model_width))
+    grad_routes = grad_returned.reshape(experts * capacity, model_width)[slot_index].reshape(
+        block_len, 2, model_width
+    )
+    combined = jnp.sum(gate_probs[:, :, None] * route_out, axis=1)
+    gate_dots = jnp.sum(grad_out[:, None, :] * route_out, axis=-1)
+    grad_rows = jnp.sum(grad_routes, axis=1)
+    own_in = lax.psum_scatter(grad_in[None], "ctx", scatter_dimension=1, tiled=True)
+    own_down = lax.psum_scatter(grad_down[None], "ctx", scatter_dimension=2, tiled=True)
+    return combined, gate_dots, grad_rows, own_in, own_down
 
 
 def local(
@@ -149,27 +250,41 @@
     block_len = layer_input.shape[1]
     model_width = layer_input.shape[2]
     experts = router_weight.shape[1]
+    dense_experts = experts <= 4
     capacity = min(block_len, 4 * block_len // experts)
     ctx_index = lax.axis_index("ctx")
     tp_index = lax.axis_index("tp")
     fsdp_index = lax.axis_index("fsdp")
     shard_index = lax.axis_index(("fsdp", "ctx"))
+    shard_count = lax.axis_size(("fsdp", "ctx"))
+    ctx_count = lax.axis_size("ctx")
     base_pos = ctx_index * block_len
-    gathered = (
-        lax.all_gather(gains.astype(jnp.bfloat16), ("fsdp", "ctx"), axis=1, tiled=True),
-        lax.all_gather(attention_in.astype(jnp.bfloat16), ("fsdp", "ctx"), axis=0, tiled=True),
-        lax.all_gather(attention_out.astype(jnp.bfloat16), ("fsdp", "ctx"), axis=1, tiled=True),
-        lax.all_gather(router_weight.astype(jnp.bfloat16), ("fsdp", "ctx"), axis=0, tiled=True),
-        lax.all_gather(shared_in.astype(jnp.bfloat16), ("fsdp", "ctx"), axis=0, tiled=True),
-        lax.all_gather(shared_down.astype(jnp.bfloat16), ("fsdp", "ctx"), axis=1, tiled=True),
-    )
-    gain_low, attn_in_low, attn_out_low, router_low, shared_in_low, shared_down_low = gathered
-    expert_full = (
-        lax.all_gather(expert_in.astype(jnp.bfloat16), "ctx", axis=1, tiled=True),
-        lax.all_gather(expert_down.astype(jnp.bfloat16), "ctx", axis=2, tiled=True),
-    )
-    expert_in_low = expert_full[0][0]
-    expert_down_low = expert_full[1][0]
+    low = lambda v: v.astype(jnp.bfloat16)
+    gain_low, attn_in_low = gather_packed(
+        [(low(gains), 1), (low(attention_in), 0)], ("fsdp", "ctx")
+    )
+    later = [
+        (low(attention_out), 1),
+        (low(router_weight), 0),
+        (low(shared_in), 0),
+        (low(shared_down), 1),
+    ]
+    if dense_experts:
+        later += [(low(expert_in), 0), (low(expert_down), 0)]
+    later_full = gather_packed(later, ("fsdp", "ctx"))
+    attn_out_low, router_low, shared_in_low, shared_down_low = later_full[:4]
+    if dense_experts:
+        fe_local = expert_down.shape[1]
+        expert_in_all = later_full[4].reshape(experts, model_width, 2, fe_local)
+        expert_down_all = (
+            later_full[5]
+            .reshape(experts, ctx_count, fe_local, model_width // ctx_count)
+            .transpose(0, 2, 1, 3)
+            .reshape(experts, fe_local, model_width)
+        )
+    else:
+        expert_in_low = lax.all_gather(low(expert_in), "ctx", axis=1, tiled=True)[0]
+        expert_down_low = lax.all_gather(low(expert_down), "ctx", axis=2, tiled=True)[0]
     residual = layer_input[0].astype(jnp.float32)
     gain_one = gain_low[0].astype(jnp.float32)
     gain_two = gain_low[1].astype(jnp.float32)
@@ -218,7 +333,9 @@
 
     attended, log_totals = lax.map(forward_block, starts)
     mixed_heads = attended.reshape(block_len, local_cols).astype(jnp.bfloat16)
-    attn_total = head_sums(jnp.dot(mixed_heads, attn_out_low, preferred_element_type=jnp.float32))
+    attn_total = lax.psum(
+        jnp.dot(mixed_heads, attn_out_low, preferred_element_type=jnp.float32), "tp"
+    )
     after_attn = residual + attn_total
     normed_two, norm_two_back = jax.vjp(rms_norm, after_attn, gain_two)
     normed_two = normed_two.astype(jnp.bfloat16)
@@ -229,65 +346,48 @@
     )
     picked = jnp.sum(onehot * logits[:, None, :], axis=-1)
     gate_probs = jax.nn.softmax(picked, axis=-1)
-    slot_index, owner_route, filled = slot_tables(route_rows, experts, capacity)
-    fill_mask = filled.astype(jnp.bfloat16)[:, None]
-    send_rows = (normed_two[owner_route // 2] * fill_mask).reshape(experts, capacity, model_width)
-    received = to_experts(send_rows).reshape(experts * capacity, model_width)
-    expert_gate_up = jnp.einsum(
-        "rd,dgf->rgf", received, expert_in_low, preferred_element_type=jnp.float32
-    )
-    expert_act, expert_act_back = jax.vjp(swiglu, expert_gate_up)
-    expert_hidden = expert_act.astype(jnp.bfloat16)
-    expert_out = jnp.dot(expert_hidden, expert_down_low, preferred_element_type=jnp.float32)
-    returned = to_tokens(expert_out.reshape(experts, capacity, model_width))
-    route_out = returned.reshape(experts * capacity, model_width)[slot_index].reshape(
-        block_len, 2, model_width
-    )
+    upstream = cotangent[0]
+    grad_out = upstream.astype(jnp.float32)
+    if dense_experts:
+        weights = jnp.sum(gate_probs[:, :, None] * onehot, axis=1)
+        combined, dots_e, grad_rows, grad_expert_in, grad_expert_down = experts_dense(
+            normed_two, grad_out, weights, expert_in_all, expert_down_all
+        )
+        gate_dots = jnp.sum(onehot * dots_e[:, None, :], axis=-1)
+    else:
+        combined, gate_dots, grad_rows, own_expert_in, own_expert_down = experts_routed(
+            normed_two,
+            grad_out,
+            route_rows,
+            gate_probs,
+            expert_in_low,
+            expert_down_low,
+            capacity,
+        )
     shared_gate_up = jnp.einsum(
         "td,dgf->tgf", normed_two, shared_in_low, preferred_element_type=jnp.float32
     )
     shared_act, shared_act_back = jax.vjp(swiglu, shared_gate_up)
     shared_hidden = shared_act.astype(jnp.bfloat16)
     shared_out = jnp.dot(shared_hidden, shared_down_low, preferred_element_type=jnp.float32)
-    branch_totals = head_sums(jnp.concatenate([shared_out[:, None], route_out], axis=1))
-    expert_total = branch_totals[:, 1:]
-    layer_out = (
-        after_attn + branch_totals[:, 0] + jnp.sum(gate_probs[:, :, None] * expert_total, axis=1)
-    )
-    upstream = cotangent[0]
-    grad_out = upstream.astype(jnp.float32)
-    grad_gate = jnp.sum(grad_out[:, None, :] * expert_total, axis=-1)
-    grad_picked = gate_probs * (grad_gate - jnp.sum(gate_probs * grad_gate, axis=-1, keepdims=True))
-    grad_logits = jnp.sum(grad_picked[:, :, None] * onehot, axis=1).astype(jnp.bfloat16)
-    route_grads = (
-        (gate_probs[:, :, None] * grad_out[:, None, :])
-        .astype(jnp.bfloat16)
-        .reshape(2 * block_len, model_width)
-    )
-    grad_rows = (route_grads[owner_route] * fill_mask).reshape(experts, capacity, model_width)
-    grad_received = to_experts(grad_rows).reshape(experts * capacity, model_width)
-    rows_again = to_experts(send_rows).reshape(experts * capacity, model_width)
-    grad_expert_hidden = jnp.einsum(
-        "rd,fd->rf", grad_received, expert_down_low, preferred_element_type=jnp.float32
-    )
-    grad_expert_gate_up = expert_act_back(grad_expert_hidden)[0].astype(jnp.bfloat16)
-    grad_expert_in = jnp.einsum(
-        "rd,rgf->dgf", rows_again, grad_expert_gate_up, preferred_element_type=jnp.float32
-    )
-    grad_expert_down = jnp.einsum(
-        "rf,rd->fd", expert_hidden, grad_received, preferred_element_type=jnp.float32
-    )
-    grad_expert_rows = jnp.einsum(
-        "rgf,dgf->rd", grad_expert_gate_up, expert_in_low, preferred_element_type=jnp.float32
-    )
-    grad_returned = to_tokens(grad_expert_rows.reshape(experts, capacity, model_width))
-    grad_routes = grad_returned.reshape(experts * capacity, model_width)[slot_index].reshape(
-        block_len, 2, model_width
-    )
     grad_shared_hidden = jnp.einsum(
         "td,fd->tf", upstream, shared_down_low, preferred_element_type=jnp.float32
     )
     grad_shared_gate_up = shared_act_back(grad_shared_hidden)[0].astype(jnp.bfloat16)
+    partial_two = (
+        jnp.einsum(
+            "tgf,dgf->td", grad_shared_gate_up, shared_in_low, preferred_element_type=jnp.float32
+        )
+        + grad_rows
+    )
+    branch_total, grad_normed_part, gate_total = lax.psum(
+        (shared_out + combined, partial_two, gate_dots), "tp"
+    )
+    layer_out = after_attn + branch_total
+    grad_picked = gate_probs * (
+        gate_total - jnp.sum(gate_probs * gate_total, axis=-1, keepdims=True)
+    )
+    grad_logits = jnp.sum(grad_picked[:, :, None] * onehot, axis=1).astype(jnp.bfloat16)
     grad_shared_in = jnp.einsum(
         "td,tgf->dgf", normed_two, grad_shared_gate_up, preferred_element_type=jnp.float32
     )
@@ -297,10 +397,7 @@
     grad_router = jnp.einsum(
         "td,te->de", normed_two, grad_logits, preferred_element_type=jnp.float32
     )
-    partial_two = jnp.einsum(
-        "tgf,dgf->td", grad_shared_gate_up, shared_in_low, preferred_element_type=jnp.float32
-    ) + jnp.sum(grad_routes, axis=1)
-    grad_normed_two = grad_sums(partial_two) + jnp.einsum(
+    grad_normed_two = grad_normed_part + jnp.einsum(
         "te,de->td", grad_logits, router_low, preferred_element_type=jnp.float32
     )
     grad_after, grad_gain_two = norm_two_back(grad_normed_two)
@@ -309,6 +406,29 @@
     grad_attn_out = jnp.einsum(
         "tc,td->cd", mixed_heads, grad_attn_low, preferred_element_type=jnp.float32
     )
+    first_grads = [
+        (grad_attn_out, 1),
+        (grad_router, 0),
+        (grad_shared_in, 0),
+        (grad_shared_down, 1),
+        (grad_gain_two, 0),
+    ]
+    if dense_experts:
+        fe_local = expert_down.shape[1]
+        first_grads += [
+            (grad_expert_in.reshape(shard_count * expert_in.shape[1], 2, fe_local), 0),
+            (
+                grad_expert_down.reshape(experts, fe_local, ctx_count, model_width // ctx_count)
+                .transpose(0, 2, 1, 3)
+                .reshape(shard_count * fe_local, model_width // ctx_count),
+                0,
+            ),
+        ]
+    first_own = scatter_packed(first_grads, ("fsdp", "ctx"), shard_count)
+    own_attn_out, own_router, own_shared_in, own_shared_down, own_gain_two = first_own[:5]
+    if dense_experts:
+        own_expert_in = first_own[5][None]
+        own_expert_down = first_own[6][None]
     grad_heads = (
         jnp.einsum("td,cd->tc", grad_attn_low, attn_out_low, preferred_element_type=jnp.float32)
         .astype(jnp.bfloat16)
@@ -384,27 +504,12 @@
     partial_one = jnp.einsum(
         "tgf,dgf->td", grad_projected, attn_in_low, preferred_element_type=jnp.float32
     )
-    grad_residual, grad_gain_one = norm_one_back(grad_sums(partial_one))
+    grad_residual, grad_gain_one = norm_one_back(lax.psum(partial_one, "tp"))
     input_grad = grad_after + grad_residual
-    dense_grads = (
-        lax.psum_scatter(
-            jnp.stack([grad_gain_one, grad_gain_two]),
-            ("fsdp", "ctx"),
-            scatter_dimension=1,
-            tiled=True,
-        ),
-        lax.psum_scatter(grad_attn_in, ("fsdp", "ctx"), scatter_dimension=0, tiled=True),
-        lax.psum_scatter(grad_attn_out, ("fsdp", "ctx"), scatter_dimension=1, tiled=True),
-        lax.psum_scatter(grad_router, ("fsdp", "ctx"), scatter_dimension=0, tiled=True),
-        lax.psum_scatter(grad_shared_in, ("fsdp", "ctx"), scatter_dimension=0, tiled=True),
-        lax.psum_scatter(grad_shared_down, ("fsdp", "ctx"), scatter_dimension=1, tiled=True),
-    )
-    own_gains, own_attn_in, own_attn_out, own_router, own_shared_in, own_shared_down = dense_grads
-    expert_grads = (
-        lax.psum_scatter(grad_expert_in[None], "ctx", scatter_dimension=1, tiled=True),
-        lax.psum_scatter(grad_expert_down[None], "ctx", scatter_dimension=2, tiled=True),
-    )
-    own_expert_in, own_expert_down = expert_grads
+    own_attn_in, own_gain_one = scatter_packed(
+        [(grad_attn_in, 0), (grad_gain_one, 0)], ("fsdp", "ctx"), shard_count
+    )
+    own_gains = jnp.stack([own_gain_one, own_gain_two])
     lead_tp = (tp_index == 0).astype(jnp.float32)
     first_shard = (shard_index == 0).astype(jnp.float32)
     first_ctx = (ctx_index == 0).astype(jnp.float32)

time: 2340 us -> 2290 us (0.979)
  blocking collectives: 618 us -> 47.6 us
  waiting for transfers between devices: 1090 us -> 1490 us
  local copies, waits for them, and re-layouts: 197 us -> 387 us
  other arithmetic: 174 us -> 137 us
    unnamed x18 -> x10, waiting for transfers between devices: 120 us -> 778 us
    all_gather x6 -> x0, blocking collectives: 434 us -> none  [the longest x1 314 us: local(): lax.all_gather(shared_down.astype(jnp.bfloat16), ('fsdp', 'ctx'), axis=1,...]
    all_to_all x3 -> x0, waiting for transfers between devices: 351 us -> none  [the longest x2 257 us: to_tokens(): lax.all_to_all(buffer_rows, 'fsdp', split_axis=0, concat_axis=0, tiled=True)]
    all_gather x2 -> x1, waiting for transfers between devices: 15.2 us -> 341 us  [gather_packed(): full = lax.all_gather(flat, axes, axis=0, tiled=False)]
    psum x3, waiting for transfers between devices: 293 us -> 36.1 us  [the longest x1 21 us: local(): lax.psum(jnp.dot(mixed_heads, attn_out_low, preferred_element_type=jnp.fl...]
    all_to_all x1 -> x0, blocking collectives: 142 us -> none  [to_experts(): lax.all_to_all(buffer_rows, 'fsdp', split_axis=0, concat_axis=0, tiled=True)]
    reduce_scatter x5 -> x0, waiting for transfers between devices: 123 us -> none  [the longest x1 71.1 us: local(): lax.psum_scatter(grad_attn_in, ('fsdp', 'ctx'), scatter_dimension=0, tile...]
    unnamed x279 -> x188, local copies, waits for them, and re-layouts: 33.8 us -> 120 us
  transfers between devices with their start and end apart: 23 -> 13, of which waited for: 14 -> 10; matrix products, arithmetic and copies ran while one was open for 13% -> 15% of each run, Pallas kernels for 0% -> 0%
where the time goes in v1:
time: 2290 us; the launch traced here: 2280 us
  waiting for transfers between devices  1490 us (65%)
  local copies, waits for them, and re-layouts  387 us (17%)
  matrix products  158 us (7%)
  other arithmetic  137 us (6%)
  blocking collectives  47.6 us (2%)
  between operations  42.5 us (2%)
    unnamed x10, waiting for transfers between devices  778 us
    all_gather x1, waiting for transfers between devices, gather_packed(): full = lax.all_gather(flat, axes, axis=0, tiled=False)  341 us
    psum x2, waiting for transfers between devices, local(): lax.psum((model_part, head_part, hidden_part, expert_model_part, expert_h...  231 us
    unnamed x188, local copies, waits for them, and re-layouts  120 us
    ppermute x5, waiting for transfers between devices, from_behind(): lax.ppermute(value, axis, [(source, source + steps) for source in range(l...  99.1 us
  transfers between devices with their start and end apart: 13, of which 10 were waited for; matrix products, arithmetic and copies ran while one was open for 15% of the time, Pallas kernels for 0%

profile of v1, /device:TPU:0, one launch (start us, length us, event | category | flops | bytes accessed | tf_op | source)
XLA Modules:
  0.0 2275.5 jit_solution(4753559206364376664)
XLA Ops:
  33.1 7.3 dynamic-update-slice.12
  44.1 18.0 reshape.1174
  64.1 32.0 %all-reduce.26.cloned.1.call-done = bf16[443904]{0:T(1024)(128)(2,1)} async-done(((bf16[443904]{0:T(1024)(128)(2,1)}), bf16[443904]{0:T(1024)(128)(2,1)}) %all-reduce.26.cloned.1.call-update) | async-done | bytes 887824
  115.0 71.1 %collective-permute-done.1 = bf16[1024]{0:T(1024)(128)(2,1)S(1)} collective-permute-done((bf16[1024]{0:T(1024)(128)(2,1)S(1)}, bf16[1024]{0:T(1024)(128)(2,1)S(1)}, u32[]{:S(2)}, u32[]{:S(2)}) %collective-permute-start.1) | collective-permute-done | bytes 2080 | tf_op jit(solution)/shard_map/ppermute | solution.py:25
  186.2 16.7 collective-permute-done
  203.0 31.7 %while.39 = (s32[]{:T(128)}, bf16[2,512,3,64]{1,3,2,0:T(8,128)(2,1)S(1)}, f32[2,3,512,1]{2,1,3,0:T(4,128)S(1)}, s32[2]{0:T(128)S(1)}, bf16[2048,3,64]{0,2,1:T(8,...) while((s32[]{:T(128)}, ...), condition=%wide.region_4.5_spmd, body=%wide.region_1.4_spmd.sunk | while | flops 644092928 | bytes 33318164 | solution.py:334
  236.9 341.2 %all-gather.5.cloned.1.call-done = bf16[8,1,756096]{2,1,0:T(2,128)(2,1)} async-done(((bf16[1,1,756096]{2,1,0:T(2,128)(2,1)}), bf16[8,1,756096]{2,1,0:T(2,128)(2,1)}) %all-gather.5.cloned.1.call-update) | async-done | bytes 12097552 | tf_op jit(solution)/shard_map/all_gather | solution.py:118
  578.1 11.2 copy.371
  629.5 11.5 reshape_reshape_reshape.12
  644.8 21.0 all-reduce.20.cloned.1.call-done
  671.1 12.7 convolution_bitcast_fusion
  683.7 15.8 multiply_bitcast_fusion
  699.5 14.4 fusion.57
  713.9 13.3 fusion.65
  755.3 7.1 bitcast_add_fusion
  777.4 19.3 copy.300
  796.8 21.7 reshape_reshape_reshape.14
  864.3 59.7 %while.40 = (s32[]{:T(128)}, f32[2048,3,64]{0,2,1:T(8,128)}, f32[2048,3,64]{0,2,1:T(8,128)S(1)}, f32[1024,3,64]{0,2,1:T(8,128)}, bf16[1024,3,64]{0,2,1:T(8,128)(...) while((s32[]{:T(128)}, f32[2048,3,64]{0,2,1:T(8,128)}, ...), condition=%wide.region_22.23_spmd, body=%wide.region_20.22_spmd.sunk | while | flops 1541608448 | bytes 155581920 | solution.py:485
  869.2 6.7 multiply_reduce_fusion.23
  875.9 9.4 multiply_convert_fusion.10
  898.8 6.7 multiply_reduce_fusion.23
  905.6 9.4 multiply_convert_fusion.10
  935.1 11.2 collective-permute-done.3
  954.9 34.9 %dynamic-update-slice.6 = f32[8,756192]{1,0:T(8,128)} dynamic-update-slice(f32[8,756192]{1,0:T(8,128)} %dynamic-update-slice.5, f32[8,393216]{1,0:T(8,128)} %reshape_reshape_reshape.14, s32[]{} %constant.551, s32[]{} %constant.556) | dynamic-update-slice | bytes 25165828
  989.8 17.9 dynamic-update-slice.7
  1007.7 17.9 pad.25
  1025.5 20.0 reshape.1159
  1054.6 15.2 all-reduce.32.cloned.1.call-done
  1098.7 745.9 %all-reduce.30.cloned.1.call-done = (f32[47296,128]{1,0:T(8,128)}, f32[3520,128]{1,0:T(8,128)}) async-done(((f32[47296,128]{1,0:T(8,128)}, f32[3520,128]{1,0:T(8,128)}), (f32[47296,128]{1,0:T(8,128)}, f32[3520,128]{1,0:T(8,128)})) %all-reduce.30.cloned.1.call-update) | async-done | bytes 26017808
  1893.6 108.9 %all-reduce.24.cloned.1.call-done = f32[4,3,2048]{2,1,0:T(4,128)} async-done(((f32[4,3,2048]{2,1,0:T(4,128)}), f32[4,3,2048]{2,1,0:T(4,128)}) %all-reduce.24.cloned.1.call-update) | async-done | bytes 98320 | tf_op jit(solution)/shard_map/psum | solution.py:592
  2010.9 122.4 %all-reduce.28.cloned.1.call-done = (f32[12]{0:T(128)}, f32[4,768]{1,0:T(4,128)}, f32[4,768]{1,0:T(4,128)}, f32[3,2048]{1,0:T(4,128)}, f32[2,4]{0,1:T(4,128)}, /*index=5*/f32[4,2,768]{2,1,0:T(2,128)}) async-done(((f32[12]{0:T(128)}, f32[4,768]{1,0:T(4,128)}, f32[4,768]{1,0:T(4,128)}, f32[3,2048]{1,0:T(4,128)}, f32[2,4]{0,1:T(4,128)}, /*index=5*/f32[4,2,768]{2,1,0:T(2,128)}), (f32[12]{0:T(128)}, ...) | async-done | bytes 73824 | tf_op jit(solution)/shard_map/psum | solution.py:592
  2203.4 41.6 %psum.103 = f32[8]{0:T(128)S(1)} all-reduce(f32[8]{0:T(128)S(1)} %stack.168), channel_id=1, replica_groups=mesh['fsdp'=4,'ctx'=2,'tp'=4] {'fsdp','ctx','tp'}, use_global_device_ids=true, to_apply=%region_76.77 | all-reduce | flops 8 | bytes 64 | tf_op jit(solution)/shard_map/psum | solution.py:706
  (507 shorter events, 422.3 us)
Async XLA Ops:
  7.2 88.8 %all-reduce.26.cloned.1.call-start = ((), (), s32[]{:S(2)}) async-start(), calls=%async_computation.3 | async-start | bytes 1777664
  17.0 561.1 %all-gather.5.cloned.1.call-start = ((), (), s32[]{:S(2)}) async-start(), calls=%async_computation.4 | async-start | bytes 27219456 | tf_op jit(solution)/shard_map/all_gather | solution.py:118
  62.2 603.6 %all-reduce.20.cloned.1.call-start = ((), (), s32[]{:S(2)}) async-start(), calls=%async_computation | async-start | bytes 6291456 | tf_op jit(solution)/shard_map/psum | solution.py:336
  62.8 41.3 %copy-start.59 = (f32[1024]{0:T(1024)}, f32[1024]{0:T(1024)S(1)}, u32[]{:S(2)}) copy-start(f32[1024]{0:T(1024)S(1)} %fusion.138) | copy-start | bytes 12292
  64.1 42.7 %copy-start.43 = (f32[1024,32]{0,1:T(8,128)}, f32[1024,32]{0,1:T(8,128)S(1)}, u32[]{:S(2)}) copy-start(f32[1024,32]{0,1:T(8,128)S(1)} %get-tuple-element.936) | copy-start | bytes 393220
  108.1 78.0 %collective-permute-start.2 = (bf16[1024,3,64]{0,2,1:T(8,128)(2,1)S(1)}, bf16[1024,3,64]{0,2,1:T(8,128)(2,1)S(1)}, u32[]{:S(2)}, u32[]{:S(2)}) collective-permute-start(bf16[1024,3,64]{0,2,1:T(8,128)(2,1)S(1)} %pad_maximum_fusion.3), channel_id=1, source_target_pairs={{0,4},{1,5},{2,6},{3,7},{8,12},{9,13},{10,14},{11,15},{16,20},{17,... | collective-permute-start | bytes 1179656 | tf_op jit(solution)/shard_map/ppermute | solution.py:25
  110.9 75.2 %collective-permute-start.1 = (bf16[1024]{0:T(1024)(128)(2,1)S(1)}, bf16[1024]{0:T(1024)(128)(2,1)S(1)}, u32[]{:S(2)}, u32[]{:S(2)}) collective-permute-start(bf16[1024]{0:T(1024)(128)(2,1)S(1)} %convert_reduce_fusion), channel_id=1, source_target_pairs={{0,4},{1,5},{2,6},{3,7},{8,12},{9,13},{10,14},{11,15},{16,20},{17,... | collective-permute-start | bytes 6152 | tf_op jit(solution)/shard_map/ppermute | solution.py:25
  113.4 89.5 %collective-permute-start = (bf16[1024,3,64]{0,2,1:T(8,128)(2,1)S(1)}, bf16[1024,3,64]{0,2,1:T(8,128)(2,1)S(1)}, u32[]{:S(2)}, u32[]{:S(2)}) collective-permute-start(bf16[1024,3,64]{0,2,1:T(8,128)(2,1)S(1)} %bitcast.409), channel_id=1, source_target_pairs={{0,4},{1,5},{2,6},{3,7},{8,12},{9,13},{10,14},{11,15},{16,20},{17,... | collective-permute-start | bytes 1179656 | tf_op jit(solution)/shard_map/ppermute | solution.py:25
  236.5 352.9 %copy-start.4 = (bf16[2048,3,64]{0,2,1:T(8,128)(2,1)}, bf16[2048,3,64]{0,2,1:T(8,128)(2,1)S(1)}, u32[]{:S(2)}) copy-start(bf16[2048,3,64]{0,2,1:T(8,128)(2,1)S(1)} %get-tuple-element.1244) | copy-start | bytes 2359300
  236.5 352.9 %copy-start.12 = (bf16[2048,3,64]{0,2,1:T(8,128)(2,1)}, bf16[2048,3,64]{0,2,1:T(8,128)(2,1)S(1)}, u32[]{:S(2)}) copy-start(bf16[2048,3,64]{0,2,1:T(8,128)(2,1)S(1)} %get-tuple-element.1246) | copy-start | bytes 2359300
  236.5 352.9 %copy-start.19 = (bf16[1024,3,64]{0,2,1:T(8,128)(2,1)}, bf16[1024,3,64]{0,2,1:T(8,128)(2,1)S(1)}, u32[]{:S(2)}) copy-start(bf16[1024,3,64]{0,2,1:T(8,128)(2,1)S(1)} %get-tuple-element.1247) | copy-start | bytes 1179652
  597.2 250.5 %all-reduce.22.cloned.1.call-start = ((), (), s32[]{:S(2)}) async-start(), calls=%async_computation.1 | async-start | bytes 6291456 | tf_op jit(solution)/shard_map/psum | solution.py:383
  668.6 182.9 %copy-start.2 = (f32[1024,768]{1,0:T(8,128)}, f32[1024,768]{1,0:T(8,128)S(1)}, u32[]{:S(2)}) copy-start(f32[1024,768]{1,0:T(8,128)S(1)} %get-tuple-element.880) | copy-start | bytes 9437188
  762.5 307.3 %all-reduce.32.cloned.1.call-start = ((), (), s32[]{:S(2)}) async-start(), calls=%async_computation.7 | async-start | bytes 12582912 | tf_op jit(solution)/shard_map/psum | solution.py:383
  925.3 21.5 collective-permute-start.4
  926.6 19.7 collective-permute-start.3
  950.7 894.0 %all-reduce.30.cloned.1.call-start = ((), (), s32[]{:S(2)}) async-start(), calls=%async_computation.6 | async-start | bytes 52035584
  1076.0 926.5 %all-reduce.24.cloned.1.call-start = ((), (), s32[]{:S(2)}) async-start(), calls=%async_computation.2 | async-start | bytes 262144 | tf_op jit(solution)/shard_map/psum | solution.py:592
  1854.5 26.4 %copy-start.67 = (f32[96,4]{0,1:T(4,128)}, f32[96,4]{0,1:T(4,128)S(1)}, u32[]{:S(2)}) copy-start(f32[96,4]{0,1:T(4,128)S(1)} %copy.313) | copy-start | bytes 4612
  1854.6 403.8 %copy-start.47 = (f32[192,96]{1,0:T(8,128)}, f32[192,96]{1,0:T(8,128)S(1)}, u32[]{:S(2)}) copy-start(f32[192,96]{1,0:T(8,128)S(1)} %reshape.1162) | copy-start | bytes 221188
  1880.8 252.5 %all-reduce.28.cloned.1.call-start = ((), (), s32[]{:S(2)}) async-start(), calls=%async_computation.5 | async-start | bytes 168960 | tf_op jit(solution)/shard_map/psum | solution.py:592
  1883.3 123.6 %copy-start.54 = (f32[3,2048]{1,0:T(4,128)}, f32[3,2048]{1,0:T(4,128)S(1)}, u32[]{:S(2)}) copy-start(f32[3,2048]{1,0:T(4,128)S(1)} %maximum_dynamic-update-slice_fusion) | copy-start | bytes 73732
  2194.5 50.5 %copy-start.84 = (f32[8]{0:T(128)S(1)}, f32[8]{0:T(128)}, u32[]{:S(2)}) copy-start(f32[8]{0:T(128)} %constant.500) | copy-start | bytes 100
  2194.5 56.3 %copy-start.26 = (f32[512,96]{1,0:T(8,128)S(1)}, f32[512,96]{1,0:T(8,128)}, u32[]{:S(2)}) copy-start(f32[512,96]{1,0:T(8,128)} %copy-done.25) | copy-start | bytes 589828
  2194.5 56.3 %copy-start.45 = (f32[512,96]{1,0:T(8,128)S(1)}, f32[512,96]{1,0:T(8,128)}, u32[]{:S(2)}) copy-start(f32[512,96]{1,0:T(8,128)} %copy.311) | copy-start | bytes 589828
  2194.6 56.3 %copy-start.77 = (f32[1,96]{1,0:T(1,128)S(1)}, f32[1,96]{1,0:T(1,128)}, u32[]{:S(2)}) copy-start(f32[1,96]{1,0:T(1,128)} %get-tuple-element.937) | copy-start | bytes 1156
  2196.4 60.7 %copy-start.74 = (f32[2,96]{1,0:T(2,128)S(1)}, f32[2,96]{1,0:T(2,128)}, u32[]{:S(2)}) copy-start(f32[2,96]{1,0:T(2,128)} %copy-done.73) | copy-start | bytes 2308
  2200.4 59.6 %copy-start.29 = (f32[96,2,512]{2,1,0:T(2,128)S(1)}, f32[96,2,512]{2,1,0:T(2,128)}, u32[]{:S(2)}) copy-start(f32[96,2,512]{2,1,0:T(2,128)} %reshape.1164) | copy-start | bytes 1179652
  2200.4 59.6 %copy-start.76 = (f32[1,96]{1,0:T(1,128)S(1)}, f32[1,96]{1,0:T(1,128)}, u32[]{:S(2)}) copy-start(f32[1,96]{1,0:T(1,128)} %copy-done.75) | copy-start | bytes 1156
  2200.4 61.8 %copy-start.68 = (f32[96,4]{0,1:T(4,128)S(1)}, f32[96,4]{0,1:T(4,128)}, u32[]{:S(2)}) copy-start(f32[96,4]{0,1:T(4,128)} %copy-done.67) | copy-start | bytes 4612
  2200.4 63.1 %copy-start.32 = (f32[1,512,384]{2,1,0:T(8,128)S(1)}, f32[1,512,384]{2,1,0:T(8,128)}, u32[]{:S(2)}) copy-start(f32[1,512,384]{2,1,0:T(8,128)} %broadcast_in_dim_reshape.7) | copy-start | bytes 2359300
  2200.4 63.0 %copy-start.66 = (f32[384]{0:T(512)S(1)}, f32[384]{0:T(512)}, u32[]{:S(2)}) copy-start(f32[384]{0:T(512)} %get-tuple-element.871) | copy-start | bytes 4612
  (73 other events, 532.8 us)
Sparse Core Ops, SparseCore 0:
  17.1 78.9 all-reduce.25
  98.2 479.8 all-gather.4
  597.3 68.4 all-reduce.19
  762.6 68.5 all-reduce.21
  950.8 118.9 all-reduce.31
  1076.1 768.4 all-reduce.29
  1880.9 121.5 all-reduce.23
  2011.2 122.0 all-reduce.27

commit v2 on v1

--- a/solution.py
+++ b/solution.py
@@ -187,16 +187,18 @@
     experts = lax.axis_size("fsdp")
     slot_index, owner_route, filled = slot_tables(route_rows, experts, capacity)
     fill_mask = filled.astype(jnp.bfloat16)[:, None]
-    send_rows = (normed_two[owner_route // 2] * fill_mask).reshape(experts, capacity, model_width)
     route_grads = (
         (gate_probs[:, :, None] * grad_out[:, None, :])
         .astype(jnp.bfloat16)
         .reshape(2 * block_len, model_width)
     )
-    grad_rows_sent = (route_grads[owner_route] * fill_mask).reshape(experts, capacity, model_width)
+    send_rows = jnp.concatenate(
+        [normed_two[owner_route // 2] * fill_mask, route_grads[owner_route] * fill_mask], axis=1
+    ).reshape(experts, capacity, 2 * model_width)
     exchange = lambda rows: lax.all_to_all(rows, "fsdp", split_axis=0, concat_axis=0, tiled=True)
-    received = exchange(send_rows).reshape(experts * capacity, model_width)
-    grad_received = exchange(grad_rows_sent).reshape(experts * capacity, model_width)
+    received_both = exchange(send_rows).reshape(experts * capacity, 2 * model_width)
+    received = received_both[:, :model_width]
+    grad_received = received_both[:, model_width:]
     gate_up = jnp.einsum("rd,dgf->rgf", received, expert_in_low, preferred_element_type=jnp.float32)
     act, act_back = jax.vjp(swiglu, gate_up)
     hidden = act.astype(jnp.bfloat16)
@@ -210,20 +212,17 @@
     grad_expert_rows = jnp.einsum(
         "rgf,dgf->rd", grad_gate_up, expert_in_low, preferred_element_type=jnp.float32
     )
-    returned = exchange(outs.reshape(experts, capacity, model_width))
-    route_out = returned.reshape(experts * capacity, model_width)[slot_index].reshape(
-        block_len, 2, model_width
-    )
-    grad_returned = exchange(grad_expert_rows.reshape(experts, capacity, model_width))
-    grad_routes = grad_returned.reshape(experts * capacity, model_width)[slot_index].reshape(
-        block_len, 2, model_width
-    )
+    returned = exchange(
+        jnp.concatenate([outs, grad_expert_rows], axis=1).reshape(
+            experts, capacity, 2 * model_width
+        )
+    ).reshape(experts * capacity, 2 * model_width)[slot_index]
+    route_out = returned[:, :model_width].reshape(block_len, 2, model_width)
+    grad_routes = returned[:, model_width:].reshape(block_len, 2, model_width)
     combined = jnp.sum(gate_probs[:, :, None] * route_out, axis=1)
     gate_dots = jnp.sum(grad_out[:, None, :] * route_out, axis=-1)
     grad_rows = jnp.sum(grad_routes, axis=1)
-    own_in = lax.psum_scatter(grad_in[None], "ctx", scatter_dimension=1, tiled=True)
-    own_down = lax.psum_scatter(grad_down[None], "ctx", scatter_dimension=2, tiled=True)
-    return combined, gate_dots, grad_rows, own_in, own_down
+    return combined, gate_dots, grad_rows, grad_in, grad_down
 
 
 def local(
@@ -250,7 +249,7 @@
     block_len = layer_input.shape[1]
     model_width = layer_input.shape[2]
     experts = router_weight.shape[1]
-    dense_experts = experts <= 4
+    dense_experts = False
     capacity = min(block_len, 4 * block_len // experts)
     ctx_index = lax.axis_index("ctx")
     tp_index = lax.axis_index("tp")
@@ -355,7 +354,7 @@
         )
         gate_dots = jnp.sum(onehot * dots_e[:, None, :], axis=-1)
     else:
-        combined, gate_dots, grad_rows, own_expert_in, own_expert_down = experts_routed(
+        combined, gate_dots, grad_rows, grad_expert_in, grad_expert_down = experts_routed(
             normed_two,
             grad_out,
             route_rows,
@@ -424,6 +423,11 @@
                 0,
             ),
         ]
+    if not dense_experts:
+        own_expert_in = lax.psum_scatter(grad_expert_in[None], "ctx", scatter_dimension=1, tiled=True)
+        own_expert_down = lax.psum_scatter(
+            grad_expert_down[None], "ctx", scatter_dimension=2, tiled=True
+        )
     first_own = scatter_packed(first_grads, ("fsdp", "ctx"), shard_count)
     own_attn_out, own_router, own_shared_in, own_shared_down, own_gain_two = first_own[:5]
     if dense_experts:

time: 2290 us -> 2260 us (0.987)
  local copies, waits for them, and re-layouts: 387 us -> 307 us
  waiting for transfers between devices: 1490 us -> 1420 us
  other arithmetic: 137 us -> 191 us
  matrix products: 158 us -> 188 us
    all_to_all x0 -> x2, waiting for transfers between devices: none -> 769 us  [experts_routed(): lax.all_to_all(rows, 'fsdp', split_axis=0, concat_axis=0, tiled=True)]
    unnamed x10 -> x13, waiting for transfers between devices: 778 us -> 291 us
    all_gather x1, waiting for transfers between devices: 341 us -> 0.01 us  [gather_packed(): full = lax.all_gather(flat, axes, axis=0, tiled=False)]
    unnamed x188 -> x265, local copies, waits for them, and re-layouts: 120 us -> 42.2 us
    ppermute x5, waiting for transfers between devices: 99.1 us -> 27.9 us  [from_behind(): lax.ppermute(value, axis, [(source, source + steps) for source in range(l...]
    gather x0 -> x3, local copies, waits for them, and re-layouts: none -> 61.6 us  [the longest x1 22.4 us: experts_routed(): exchange(jnp.concatenate([outs, grad_expert_rows], axis=1).reshape(expert...]
    psum x2, waiting for transfers between devices: 15.2 us -> 55.7 us  [local(): lax.psum((shared_out + combined, partial_two, gate_dots), 'tp')]
    reduce_sum x2 -> x4, other arithmetic: 0.06 us -> 33.7 us  [the longest x1 11.8 us: experts_routed(): gate_dots = jnp.sum(grad_out[:, None, :] * route_out, axis=-1)]
  transfers between devices with their start and end apart: 13 -> 18, of which waited for: 10 -> 13; matrix products, arithmetic and copies ran while one was open for 15% -> 16% of each run, Pallas kernels for 0% -> 0%
where the time goes in v2:
time: 2260 us; the launch traced here: 2250 us
  waiting for transfers between devices  1420 us (63%)
  local copies, waits for them, and re-layouts  307 us (14%)
  other arithmetic  191 us (8%)
  matrix products  188 us (8%)
  blocking collectives  60.7 us (3%)
  between operations  44.6 us (2%)
  starting transfers between devices  28.9 us (1%)
    all_to_all x2, waiting for transfers between devices, experts_routed(): lax.all_to_all(rows, 'fsdp', split_axis=0, concat_axis=0, tiled=True)  769 us
    unnamed x13, waiting for transfers between devices  291 us
    psum x2, waiting for transfers between devices, local(): lax.psum((model_part, head_part, hidden_part, expert_model_part, expert_h...  216 us
    psum x2, waiting for transfers between devices, local(): lax.psum((shared_out + combined, partial_two, gate_dots), 'tp')  55.7 us
    psum x1, waiting for transfers between devices, local(): lax.psum(jnp.dot(mixed_heads, attn_out_low, preferred_element_type=jnp.fl...  47.9 us
  transfers between devices with their start and end apart: 18, of which 13 were waited for; matrix products, arithmetic and copies ran while one was open for 16% of the time, Pallas kernels for 0%

profile of v2, /device:TPU:0, one launch (start us, length us, event | category | flops | bytes accessed | tf_op | source)
XLA Modules:
  0.0 2251.1 jit_solution(10345769687586566409)
XLA Ops:
  31.2 63.9 %all-reduce.26.cloned.1.call-done = bf16[443904]{0:T(1024)(128)(2,1)} async-done(((bf16[443904]{0:T(1024)(128)(2,1)}), bf16[443904]{0:T(1024)(128)(2,1)}) %all-reduce.26.cloned.1.call-update) | async-done | bytes 887824
  135.8 15.2 collective-permute-done
  151.0 39.3 %while.39 = (s32[]{:T(128)}, bf16[2,512,3,64]{1,3,2,0:T(8,128)(2,1)}, f32[2,3,512,1]{2,1,3,0:T(4,128)}, s32[2]{0:T(128)}, bf16[2048,3,64]{0,2,1:T(8,128)(2,1)S(1...) while((s32[]{:T(128)}, ...), condition=%wide.region_4.5_spmd, body=%wide.region_1.4_spmd.sunk | while | flops 644092928 | bytes 33331516 | solution.py:333
  222.8 47.9 %all-reduce.20.cloned.1.call-done = f32[1024,768]{1,0:T(8,128)} async-done(((f32[1024,768]{1,0:T(8,128)}), f32[1024,768]{1,0:T(8,128)}) %all-reduce.20.cloned.1.call-update) | async-done | bytes 3145744 | tf_op jit(solution)/shard_map/psum | solution.py:335
  276.6 17.8 gather_fusion
  299.2 21.4 gather_fusion.1
  339.9 13.0 all_gather.23
  352.9 15.5 all-gather.6.cloned.1.call-done
  368.4 242.6 %all-to-all-done = bf16[4,1024,1536]{2,1,0:T(8,128)(2,1)} async-done(((bf16[4,1024,1536]{2,1,0:T(8,128)(2,1)}), bf16[4,1024,1536]{2,1,0:T(8,128)(2,1)}, u32[]{:S(2)}, u32[]{:S(2)}) %all-to-all-start) | async-done | bytes 12582944 | tf_op jit(solution)/shard_map/all_to_all | solution.py:198
  611.0 12.4 fusion.61
  623.4 14.3 multiply_bitcast_fusion
  645.7 15.4 convolution_bitcast_fusion
  661.0 9.1 pad_maximum_fusion
  678.8 8.9 all-to-all-start.1
  703.9 525.9 %all-to-all-done.1 = f32[4,1024,1536]{1,2,0:T(8,128)} async-done(((f32[4,1024,1536]{1,2,0:T(8,128)}), f32[4,1024,1536]{1,2,0:T(8,128)}, u32[]{:S(2)}, u32[]{:S(2)}) %all-to-all-start.1) | async-done | bytes 25165856 | tf_op jit(solution)/shard_map/all_to_all | solution.py:198
  1229.8 24.7 %copy.207 = f32[4,1024,1536]{2,1,0:T(8,128)} copy(f32[4,1024,1536]{1,2,0:T(8,128)} %all-to-all-done.1) | data formatting | bytes 50331648 | tf_op jit(solution)/shard_map/all_to_all | solution.py:198
  1254.5 22.4 gather_fusion.2
  1276.9 11.8 multiply_reduce_fusion.1
  1297.3 10.3 reduce_sum.549
  1314.0 13.3 fusion.107
  1331.3 13.8 fusion.88
  1360.6 11.6 multiply_reduce_fusion.2
  1390.7 77.0 %while.40 = (s32[]{:T(128)}, f32[2048,3,64]{0,2,1:T(8,128)}, f32[2048,3,64]{0,2,1:T(8,128)S(1)}, f32[1024,3,64]{0,2,1:T(8,128)}, bf16[1024,3,64]{0,2,1:T(8,128)(...) while((s32[]{:T(128)}, f32[2048,3,64]{0,2,1:T(8,128)}, ...), condition=%wide.region_26.27_spmd, body=%wide.region_24.26_spmd.sunk | while | flops 1541608448 | bytes 106823088 | solution.py:489
  1399.0 8.9 multiply_reduce_fusion.22
  1407.9 9.4 multiply_convert_fusion.7
  1437.4 8.9 multiply_reduce_fusion.22
  1446.3 9.4 multiply_convert_fusion.7
  1566.2 47.2 %all-reduce.32.cloned.1.call-done = (f32[1024,768]{1,0:T(8,128)}, f32[1024,768]{1,0:T(8,128)}) async-done(((f32[1024,768]{1,0:T(8,128)}, f32[1024,768]{1,0:T(8,128)}), (f32[1024,768]{1,0:T(8,128)}, f32[1024,768]{1,0:T(8,128)})) %all-reduce.32.cloned.1.call-update) | async-done | bytes 6291472 | tf_op jit(solution)/shard_map/psum | solution.py:382
  1643.3 98.7 %all-reduce.24.cloned.1.call-done = f32[4,3,2048]{2,1,0:T(4,128)} async-done(((f32[4,3,2048]{2,1,0:T(4,128)}), f32[4,3,2048]{2,1,0:T(4,128)}) %all-reduce.24.cloned.1.call-update) | async-done | bytes 98320 | tf_op jit(solution)/shard_map/psum | solution.py:596
  1755.6 226.5 %all-reduce.30.cloned.1.call-done = (f32[10432,128]{1,0:T(8,128)}, f32[3520,128]{1,0:T(8,128)}) async-done(((f32[10432,128]{1,0:T(8,128)}, f32[3520,128]{1,0:T(8,128)}), (f32[10432,128]{1,0:T(8,128)}, f32[3520,128]{1,0:T(8,128)})) %all-reduce.30.cloned.1.call-update) | async-done | bytes 7143440
  1999.7 117.8 %all-reduce.28.cloned.1.call-done = (f32[12]{0:T(128)}, f32[4,768]{1,0:T(4,128)}, f32[4,768]{1,0:T(4,128)}, f32[3,2048]{1,0:T(4,128)}, f32[2,4]{0,1:T(4,128)}, /*index=5*/f32[4,2,768]{2,1,0:T(2,128)}) async-done(((f32[12]{0:T(128)}, f32[4,768]{1,0:T(4,128)}, f32[4,768]{1,0:T(4,128)}, f32[3,2048]{1,0:T(4,128)}, f32[2,4]{0,1:T(4,128)}, /*index=5*/f32[4,2,768]{2,1,0:T(2,128)}), (f32[12]{0:T(128)}, ...) | async-done | bytes 73824 | tf_op jit(solution)/shard_map/psum | solution.py:596
  2174.3 41.6 %psum.103 = f32[8]{0:T(128)} all-reduce(f32[8]{0:T(128)} %stack.168), channel_id=1, replica_groups=mesh['fsdp'=4,'ctx'=2,'tp'=4] {'fsdp','ctx','tp'}, use_global_device_ids=true, to_apply=%region_82.83 | all-reduce | flops 8 | bytes 64 | tf_op jit(solution)/shard_map/psum | solution.py:710
  (619 shorter events, 498.7 us)
Async XLA Ops:
  8.1 87.0 %all-reduce.26.cloned.1.call-start = ((), (), s32[]{:S(2)}) async-start(), calls=%async_computation.10 | async-start | bytes 1777664
  16.1 177.6 %all-gather.8.cloned.1.call-start = ((), (), s32[]{:S(2)}) async-start(), calls=%async_computation.11 | async-start | bytes 5985792 | tf_op jit(solution)/shard_map/all_gather | solution.py:118
  16.2 118.4 %collective-permute-start.1 = (bf16[1024]{0:T(1024)(128)(2,1)S(1)}, bf16[1024]{0:T(1024)(128)(2,1)S(1)}, u32[]{:S(2)}, u32[]{:S(2)}) collective-permute-start(bf16[1024]{0:T(1024)(128)(2,1)S(1)} %convert_reduce_fusion), channel_id=1, source_target_pairs={{0,4},{1,5},{2,6},{3,7},{8,12},{9,13},{10,14},{11,15},{16,20},{17,... | collective-permute-start | bytes 6152 | tf_op jit(solution)/shard_map/ppermute | solution.py:25
  29.5 241.2 %all-reduce.20.cloned.1.call-start = ((), (), s32[]{:S(2)}) async-start(), calls=%async_computation.4 | async-start | bytes 6291456 | tf_op jit(solution)/shard_map/psum | solution.py:335
  30.0 73.0 %copy-start.102 = (f32[1024]{0:T(1024)}, f32[1024]{0:T(1024)S(1)}, u32[]{:S(2)}) copy-start(f32[1024]{0:T(1024)S(1)} %fusion.74) | copy-start | bytes 12292
  30.0 75.6 %copy-start.98 = (f32[1024]{0:T(1024)}, f32[1024]{0:T(1024)S(1)}, u32[]{:S(2)}) copy-start(f32[1024]{0:T(1024)S(1)} %fusion.162) | copy-start | bytes 12292
  31.2 75.8 %copy-start.61 = (f32[1024,32]{0,1:T(8,128)}, f32[1024,32]{0,1:T(8,128)S(1)}, u32[]{:S(2)}) copy-start(f32[1024,32]{0,1:T(8,128)S(1)} %get-tuple-element.932) | copy-start | bytes 393220
  108.5 26.1 %collective-permute-start.2 = (bf16[1024,3,64]{0,2,1:T(8,128)(2,1)}, bf16[1024,3,64]{0,2,1:T(8,128)(2,1)}, u32[]{:S(2)}, u32[]{:S(2)}) collective-permute-start(bf16[1024,3,64]{0,2,1:T(8,128)(2,1)} %pad_maximum_fusion.5), channel_id=1, source_target_pairs={{0,4},{1,5},{2,6},{3,7},{8,12},{9,13},{10,14},{11,15},{16,20},{17,... | collective-permute-start | bytes 1179656 | tf_op jit(solution)/shard_map/ppermute | solution.py:25
  133.2 17.8 collective-permute-start
  205.2 67.9 %copy-start.108 = (s32[2048,1]{0,1:T(1,128)}, s32[2048,1]{0,1:T(1,128)S(1)}, u32[]{:S(2)}) copy-start(s32[2048,1]{0,1:T(1,128)S(1)} %compare_select_fusion) | copy-start | bytes 24580
  221.7 51.5 %copy-start.88 = (f32[768]{0:T(1024)}, f32[768]{0:T(1024)S(1)}, u32[]{:S(2)}) copy-start(f32[768]{0:T(1024)S(1)} %reshape.1210) | copy-start | bytes 9220
  222.8 50.7 %copy-start.49 = (bf16[768,4]{1,0:T(8,128)(2,1)}, bf16[768,4]{1,0:T(8,128)(2,1)S(1)}, u32[]{:S(2)}) copy-start(bf16[768,4]{1,0:T(8,128)(2,1)S(1)} %reshape_reshape.22) | copy-start | bytes 18436
  331.4 279.6 %all-to-all-start = ((bf16[4,1024,1536]{2,1,0:T(8,128)(2,1)}), bf16[4,1024,1536]{2,1,0:T(8,128)(2,1)}, u32[]{:S(2)}, u32[]{:S(2)}) async-start(bf16[4,1024,1536]{2,1,0:T(8,128)(2,1)} %pad_maximum_fusion.1), calls=%async_computation | async-start | bytes 25165824 | tf_op jit(solution)/shard_map/all_to_all | solution.py:198
  337.9 30.5 %all-gather.6.cloned.1.call-start = ((), (), s32[]{:S(2)}) async-start(), calls=%async_computation.5 | async-start | bytes 2359296 | tf_op jit(solution)/shard_map/all_gather | solution.py:285
  678.8 551.0 %all-to-all-start.1 = ((f32[4,1024,1536]{1,2,0:T(8,128)}), f32[4,1024,1536]{1,2,0:T(8,128)}, u32[]{:S(2)}, u32[]{:S(2)}) async-start(f32[4,1024,1536]{1,2,0:T(8,128)} %bitcast.408), calls=%async_computation.1 | async-start | bytes 50331648 | tf_op jit(solution)/shard_map/all_to_all | solution.py:198
  687.7 693.2 %all-reduce.22.cloned.1.call-start = ((), (), s32[]{:S(2)}) async-start(), calls=%async_computation.6 | async-start | bytes 6291456 | tf_op jit(solution)/shard_map/psum | solution.py:382
  1313.8 210.4 %reduce-scatter.5.cloned.1.call-start = ((), (), s32[]{:S(2)}) async-start(), calls=%async_computation.8 | async-start | bytes 2359296 | tf_op jit(solution)/shard_map/reduce_scatter | solution.py:428
  1327.3 198.9 %reduce-scatter.3.cloned.1.call-start = ((), (), s32[]{:S(2)}) async-start(), calls=%async_computation.7 | async-start | bytes 4718592 | tf_op jit(solution)/shard_map/reduce_scatter | solution.py:427
  1345.2 268.2 %all-reduce.32.cloned.1.call-start = ((), (), s32[]{:S(2)}) async-start(), calls=%async_computation.14 | async-start | bytes 12582912 | tf_op jit(solution)/shard_map/psum | solution.py:382
  1468.9 14.0 collective-permute-start.3
  1475.5 14.6 collective-permute-start.4
  1494.0 248.0 %all-reduce.24.cloned.1.call-start = ((), (), s32[]{:S(2)}) async-start(), calls=%async_computation.9 | async-start | bytes 262144 | tf_op jit(solution)/shard_map/psum | solution.py:596
  1529.8 452.3 %all-reduce.30.cloned.1.call-start = ((), (), s32[]{:S(2)}) async-start(), calls=%async_computation.13 | async-start | bytes 14286848
  1619.6 122.4 %copy-start.113 = (f32[1,3,512]{2,0,1:T(1,128)S(1)}, f32[1,3,512]{2,0,1:T(1,128)}, u32[]{:S(2)}) copy-start(f32[1,3,512]{2,0,1:T(1,128)} %param.42) | copy-start | bytes 18436
  1619.6 123.8 %slice-start = ((f32[1,3,512]{2,0,1:T(1,128)}), f32[1,2,512]{2,0,1:T(1,128)S(1)}, s32[]{:S(2)}) async-start(f32[1,3,512]{2,0,1:T(1,128)} %param.42), calls=%async_computation.15 | async-start | bytes 8192 | tf_op jit(solution)/shard_map/slice | solution.py:677
  1619.6 127.9 %copy-start.103 = (f32[1024]{0:T(1024)S(1)}, f32[1024]{0:T(1024)}, u32[]{:S(2)}) copy-start(f32[1024]{0:T(1024)} %copy-done.102) | copy-start | bytes 12292
  1619.6 128.0 %copy-start.6 = (f32[1024,768]{1,0:T(8,128)S(1)}, f32[1024,768]{1,0:T(8,128)}, u32[]{:S(2)}) copy-start(f32[1024,768]{1,0:T(8,128)} %copy-done.4) | copy-start | bytes 9437188
  1619.6 497.9 %all-reduce.28.cloned.1.call-start = ((), (), s32[]{:S(2)}) async-start(), calls=%async_computation.12 | async-start | bytes 168960 | tf_op jit(solution)/shard_map/psum | solution.py:596
  1985.1 135.7 %slice-start.1 = ((f32[3,192]{1,0:T(4,128)}), f32[2,192]{1,0:T(2,128)S(1)}, s32[]{:S(2)}) async-start(f32[3,192]{1,0:T(4,128)} %param.37), calls=%async_computation.16 | async-start | bytes 4096 | tf_op jit(solution)/shard_map/slice | solution.py:626
  1990.1 174.6 %copy-start.13 = (f32[1,384,2,512]{3,1,2,0:T(8,128)S(1)}, f32[1,384,2,512]{3,1,2,0:T(8,128)}, u32[]{:S(2)}) copy-start(f32[1,384,2,512]{3,1,2,0:T(8,128)} %reduce-scatter.3.cloned.1.call-done) | copy-start | bytes 4718596
  1992.2 132.6 %copy-start.111 = (f32[96,4]{0,1:T(4,128)}, f32[96,4]{0,1:T(4,128)S(1)}, u32[]{:S(2)}) copy-start(f32[96,4]{0,1:T(4,128)S(1)} %copy.229) | copy-start | bytes 4612
  1996.5 223.3 %copy-start.21 = (f32[1,384,2,512]{3,2,1,0:T(2,128)S(1)}, f32[1,384,2,512]{3,2,1,0:T(2,128)}, u32[]{:S(2)}) copy-start(f32[1,384,2,512]{3,2,1,0:T(2,128)} %param.34) | copy-start | bytes 4718596
  (122 other events, 887.8 us)
Sparse Core Ops, SparseCore 0:
  16.2 78.8 all-reduce.25
  97.9 86.3 all-gather.7
  203.0 67.6 all-reduce.19
  1313.9 66.9 all-reduce.21
  1494.1 119.1 all-reduce.31
  1619.3 122.6 all-reduce.23
  1746.1 235.9 all-reduce.29
  1995.3 122.1 all-reduce.27
Sparse Core Ops, SparseCore 1:
  340.5 27.8 all-gather.5
  1327.4 24.5 reduce-scatter.4
  1354.1 43.3 reduce-scatter.2

commit v3 on v2

--- a/solution.py
+++ b/solution.py
@@ -2,6 +2,8 @@
 import jax.numpy as jnp
 from jax import lax
 from jax.sharding import PartitionSpec as P
+from jax.experimental import pallas as pl
+from jax.experimental.pallas import tpu as pltpu
 
 D = 768
 HD = 64
@@ -107,6 +109,75 @@
 def apply_update(weight, update, update_root, square_sum, elements):
     param_scale = jnp.maximum(SCALE_FLOOR, jnp.sqrt(square_sum / elements))
     return weight - STEP_RATE * param_scale * update / jnp.maximum(1.0, update_root / CLIP_LIMIT)
+
+
+def butterfly_partners():
+    partners = []
+    here = [lax.axis_index(name) for name in ("fsdp", "ctx", "tp")]
+    for axis_number, name in enumerate(("fsdp", "ctx", "tp")):
+        size = lax.axis_size(name)
+        step = 1
+        while step < size:
+            bit = (here[axis_number] // step) % 2
+            other = list(here)
+            other[axis_number] = here[axis_number] + step * (1 - 2 * bit)
+            partners.append(tuple(other))
+            step *= 2
+    return partners
+
+
+def butterfly_kernel(x_ref, o_ref, stage, inbox, send_sems, recv_sems):
+    partners = butterfly_partners()
+    barrier = pltpu.get_barrier_semaphore()
+    for partner in partners:
+        pl.semaphore_signal(
+            barrier, 1, device_id=partner, device_id_type=pl.DeviceIdType.MESH
+        )
+    pl.semaphore_wait(barrier, len(partners))
+    acc = x_ref[...]
+    for round_number, partner in enumerate(partners):
+        stage[round_number] = acc
+        copy = pltpu.make_async_remote_copy(
+            src_ref=stage.at[round_number],
+            dst_ref=inbox.at[round_number],
+            send_sem=send_sems.at[round_number],
+            recv_sem=recv_sems.at[round_number],
+            device_id=partner,
+            device_id_type=pl.DeviceIdType.MESH,
+        )
+        copy.start()
+        copy.wait()
+        acc = stage[round_number] + inbox[round_number]
+    o_ref[...] = acc
+
+
+def butterfly_sum(values, collective_id):
+    flat = jnp.concatenate([v.reshape(-1).astype(jnp.float32) for v in values])
+    size = flat.shape[0]
+    rows = -(-size // 1024) * 8
+    block = jnp.pad(flat, (0, rows * 128 - size)).reshape(rows, 128)
+    rounds = sum(
+        max(1, lax.axis_size(name)).bit_length() - 1 for name in ("fsdp", "ctx", "tp")
+    )
+    total = pl.pallas_call(
+        butterfly_kernel,
+        out_shape=jax.ShapeDtypeStruct((rows, 128), jnp.float32),
+        in_specs=[pl.BlockSpec(memory_space=pltpu.VMEM)],
+        out_specs=pl.BlockSpec(memory_space=pltpu.VMEM),
+        scratch_shapes=[
+            pltpu.VMEM((rounds, rows, 128), jnp.float32),
+            pltpu.VMEM((rounds, rows, 128), jnp.float32),
+            pltpu.SemaphoreType.DMA((rounds,)),
+            pltpu.SemaphoreType.DMA((rounds,)),
+        ],
+        compiler_params=pltpu.CompilerParams(collective_id=collective_id, has_side_effects=True),
+    )(block).reshape(-1)
+    results = []
+    offset = 0
+    for v in values:
+        results.append(total[offset : offset + v.size].reshape(v.shape))
+        offset += v.size
+    return results
 
 
 def swiglu_experts(gate_up):
@@ -593,8 +664,8 @@
         )[:, None],
         (0, fsdp_index),
     )
-    global_sums = lax.psum(
-        (
+    global_sums = butterfly_sum(
+        [
             model_part,
             head_part,
             hidden_part,
@@ -602,8 +673,8 @@
             expert_hidden_part,
             scalar_part,
             expert_old_part,
-        ),
-        ("fsdp", "ctx", "tp"),
+        ],
+        1,
     )
     (
         model_sum,
@@ -707,7 +778,7 @@
             jnp.sum(update_expert_down * update_expert_down),
         ]
     )
-    clip_total = lax.psum(clip_part, ("fsdp", "ctx", "tp"))
+    clip_total = butterfly_sum([clip_part], 2)[0]
     elements = jnp.array(
         [
             2 * D,

time: 2260 us -> 2050 us (0.907)
  waiting for transfers between devices: 1420 us -> 1190 us
  Pallas kernels: 0 us -> 44.6 us
  blocking collectives: 60.7 us -> 20.2 us
    psum x2 -> x0, waiting for transfers between devices: 216 us -> none  [local(): lax.psum((model_part, head_part, hidden_part, expert_model_part, expert_h...]
    pallas_call x0 -> x2, Pallas kernels: none -> 44.6 us  [butterfly_sum(): pl.pallas_call(butterfly_kernel, out_shape=jax.ShapeDtypeStruct((rows, 12...]
    psum x1 -> x0, blocking collectives: 41.6 us -> none  [local(): clip_total = lax.psum(clip_part, ('fsdp', 'ctx', 'tp'))]
    unnamed x13 -> x11, waiting for transfers between devices: 291 us -> 268 us
  transfers between devices with their start and end apart: 18 -> 16, of which waited for: 13 -> 11; matrix products, arithmetic and copies ran while one was open for 16% -> 13% of each run, Pallas kernels for 0% -> 0%
where the time goes in v3:
time: 2050 us; the launch traced here: 2040 us
  waiting for transfers between devices  1190 us (58%)
  local copies, waits for them, and re-layouts  326 us (16%)
  matrix products  188 us (9%)
  other arithmetic  187 us (9%)
  Pallas kernels  44.6 us (2%)
  between operations  44.5 us (2%)
  starting transfers between devices  29.4 us (1%)
    all_to_all x2, waiting for transfers between devices, experts_routed(): lax.all_to_all(rows, 'fsdp', split_axis=0, concat_axis=0, tiled=True)  769 us
    unnamed x11, waiting for transfers between devices  268 us
    psum x2, waiting for transfers between devices, local(): lax.psum((shared_out + combined, partial_two, gate_dots), 'tp')  62.4 us
    psum x1, waiting for transfers between devices, local(): lax.psum(jnp.dot(mixed_heads, attn_out_low, preferred_element_type=jnp.fl...  47.9 us
    pallas_call x2, Pallas kernels, butterfly_sum(): pl.pallas_call(butterfly_kernel, out_shape=jax.ShapeDtypeStruct((rows, 12...  44.6 us
    unnamed x266, local copies, waits for them, and re-layouts  43.6 us
  transfers between devices with their start and end apart: 16, of which 11 were waited for; matrix products, arithmetic and copies ran while one was open for 13% of the time, Pallas kernels for 0%

profile of v3, /device:TPU:0, one launch (start us, length us, event | category | flops | bytes accessed | tf_op | source)
XLA Modules:
  0.0 2039.4 jit_solution(1970840261362090880)
XLA Ops:
  31.2 63.9 %all-reduce.23.cloned.1.call-done = bf16[443904]{0:T(1024)(128)(2,1)} async-done(((bf16[443904]{0:T(1024)(128)(2,1)}), bf16[443904]{0:T(1024)(128)(2,1)}) %all-reduce.23.cloned.1.call-update) | async-done | bytes 887824
  135.8 15.2 collective-permute-done
  151.1 39.3 %while.39 = (s32[]{:T(128)}, bf16[2,512,3,64]{1,3,2,0:T(8,128)(2,1)}, f32[2,3,512,1]{2,1,3,0:T(4,128)}, s32[2]{0:T(128)}, bf16[2048,3,64]{0,2,1:T(8,128)(2,1)S(1...) while((s32[]{:T(128)}, ...), condition=%wide.region_4.5_spmd, body=%wide.region_1.4_spmd.sunk | while | flops 644092928 | bytes 33331516 | solution.py:404
  222.9 47.9 %all-reduce.19.cloned.1.call-done = f32[1024,768]{1,0:T(8,128)} async-done(((f32[1024,768]{1,0:T(8,128)}), f32[1024,768]{1,0:T(8,128)}) %all-reduce.19.cloned.1.call-update) | async-done | bytes 3145744 | tf_op jit(solution)/shard_map/psum | solution.py:406
  276.6 17.8 gather_fusion
  299.2 21.4 %gather_fusion.1 = bf16[4096,768]{1,0:T(8,128)(2,1)} fusion(bf16[2048,768]{1,0:T(8,128)(2,1)} %multiply_convert_fusion.2, s32[4096]{0:T(1024)S(1)} %get-tuple-element.931), kind=kCustom, calls=%fused_computation.1 | custom fusion | bytes 12599296 | tf_op jit(solution)/shard_map/gather | solution.py:267
  339.9 13.0 all_gather.23
  352.9 15.5 all-gather.6.cloned.1.call-done
  368.4 242.6 %all-to-all-done = bf16[4,1024,1536]{2,1,0:T(8,128)(2,1)} async-done(((bf16[4,1024,1536]{2,1,0:T(8,128)(2,1)}), bf16[4,1024,1536]{2,1,0:T(8,128)(2,1)}, u32[]{:S(2)}, u32[]{:S(2)}) %all-to-all-start) | async-done | bytes 12582944 | tf_op jit(solution)/shard_map/all_to_all | solution.py:269
  611.0 12.4 fusion.61
  623.5 14.3 multiply_bitcast_fusion
  645.7 15.4 convolution_bitcast_fusion
  661.1 9.1 pad_maximum_fusion
  678.8 9.1 all-to-all-start.1
  704.1 525.9 %all-to-all-done.1 = f32[4,1024,1536]{1,2,0:T(8,128)} async-done(((f32[4,1024,1536]{1,2,0:T(8,128)}), f32[4,1024,1536]{1,2,0:T(8,128)}, u32[]{:S(2)}, u32[]{:S(2)}) %all-to-all-start.1) | async-done | bytes 25165856 | tf_op jit(solution)/shard_map/all_to_all | solution.py:269
  1230.0 24.7 %copy.214 = f32[4,1024,1536]{2,1,0:T(8,128)} copy(f32[4,1024,1536]{1,2,0:T(8,128)} %all-to-all-done.1) | data formatting | bytes 50331648 | tf_op jit(solution)/shard_map/all_to_all | solution.py:269
  1254.7 22.4 %gather_fusion.2 = f32[2048,1536]{1,0:T(8,128)} fusion(f32[4096,1536]{1,0:T(8,128)} %bitcast.436, s32[2048]{0:T(1024)S(1)} %broadcast_clamp_fusion), kind=kCustom, calls=%fused_computation.2 | custom fusion | bytes 25174016 | tf_op jit(solution)/shard_map/gather | solution.py:286
  1277.1 11.8 multiply_reduce_fusion.1
  1297.3 10.3 reduce_sum.549
  1334.1 11.4 multiply_reduce_fusion.2
  1345.5 35.6 %all-reduce.21.cloned.1.call-done = f32[1024,768]{1,0:T(8,128)} async-done(((f32[1024,768]{1,0:T(8,128)}), f32[1024,768]{1,0:T(8,128)}) %all-reduce.21.cloned.1.call-update) | async-done | bytes 3145744 | tf_op jit(solution)/shard_map/psum | solution.py:453
  1390.9 76.7 %while.40 = (s32[]{:T(128)}, f32[2048,3,64]{0,2,1:T(8,128)}, f32[2048,3,64]{0,2,1:T(8,128)S(1)}, f32[1024,3,64]{0,2,1:T(8,128)}, bf16[1024,3,64]{0,2,1:T(8,128)(...) while((s32[]{:T(128)}, f32[2048,3,64]{0,2,1:T(8,128)}, ...), condition=%wide.region_26.27_spmd, body=%wide.region_24.26_spmd.sunk | while | flops 1541608448 | bytes 106823088 | solution.py:560
  1399.1 8.9 multiply_reduce_fusion.22
  1407.9 9.4 multiply_convert_fusion.7
  1437.4 8.9 multiply_reduce_fusion.22
  1446.3 9.4 multiply_convert_fusion.7
  1494.1 14.0 fusion.107
  1535.8 13.4 fusion.88
  1586.6 26.8 %all-reduce.27.cloned.1.call-done = (f32[1024,768]{1,0:T(8,128)}, f32[1024,768]{1,0:T(8,128)}) async-done(((f32[1024,768]{1,0:T(8,128)}, f32[1024,768]{1,0:T(8,128)}), (f32[1024,768]{1,0:T(8,128)}, f32[1024,768]{1,0:T(8,128)})) %all-reduce.27.cloned.1.call-update) | async-done | bytes 6291472 | tf_op jit(solution)/shard_map/psum | solution.py:453
  1652.5 204.4 %all-reduce.25.cloned.1.call-done = (f32[10432,128]{1,0:T(8,128)}, f32[3520,128]{1,0:T(8,128)}) async-done(((f32[10432,128]{1,0:T(8,128)}, f32[3520,128]{1,0:T(8,128)}), (f32[10432,128]{1,0:T(8,128)}, f32[3520,128]{1,0:T(8,128)})) %all-reduce.25.cloned.1.call-update) | async-done | bytes 7143440
  1868.6 29.8 %shard_map.395 = f32[344,128]{1,0:T(8,128)} custom-call(f32[344,128]{1,0:T(8,128)} %pad_bitcast_fusion.x_ref), custom_call_target="tpu_custom_call" | custom-call | tf_op jit(solution)/shard_map/pallas_call | solution.py:162
  1986.7 14.9 shard_map.396
  (635 shorter events, 507.2 us)
Async XLA Ops:
  8.1 87.0 %all-reduce.23.cloned.1.call-start = ((), (), s32[]{:S(2)}) async-start(), calls=%async_computation.9 | async-start | bytes 1777664
  16.1 177.6 %all-gather.8.cloned.1.call-start = ((), (), s32[]{:S(2)}) async-start(), calls=%async_computation.10 | async-start | bytes 5985792 | tf_op jit(solution)/shard_map/all_gather | solution.py:189
  16.2 118.4 %collective-permute-start.1 = (bf16[1024]{0:T(1024)(128)(2,1)S(1)}, bf16[1024]{0:T(1024)(128)(2,1)S(1)}, u32[]{:S(2)}, u32[]{:S(2)}) collective-permute-start(bf16[1024]{0:T(1024)(128)(2,1)S(1)} %convert_reduce_fusion), channel_id=1, source_target_pairs={{0,4},{1,5},{2,6},{3,7},{8,12},{9,13},{10,14},{11,15},{16,20},{17,... | collective-permute-start | bytes 6152 | tf_op jit(solution)/shard_map/ppermute | solution.py:27
  29.5 241.3 %all-reduce.19.cloned.1.call-start = ((), (), s32[]{:S(2)}) async-start(), calls=%async_computation.4 | async-start | bytes 6291456 | tf_op jit(solution)/shard_map/psum | solution.py:406
  30.0 73.0 %copy-start.106 = (f32[1024]{0:T(1024)}, f32[1024]{0:T(1024)S(1)}, u32[]{:S(2)}) copy-start(f32[1024]{0:T(1024)S(1)} %fusion.74) | copy-start | bytes 12292
  30.0 75.7 %copy-start.102 = (f32[1024]{0:T(1024)}, f32[1024]{0:T(1024)S(1)}, u32[]{:S(2)}) copy-start(f32[1024]{0:T(1024)S(1)} %fusion.162) | copy-start | bytes 12292
  31.2 75.9 %copy-start.65 = (f32[1024,32]{0,1:T(8,128)}, f32[1024,32]{0,1:T(8,128)S(1)}, u32[]{:S(2)}) copy-start(f32[1024,32]{0,1:T(8,128)S(1)} %get-tuple-element.938) | copy-start | bytes 393220
  108.5 26.1 %collective-permute-start.2 = (bf16[1024,3,64]{0,2,1:T(8,128)(2,1)}, bf16[1024,3,64]{0,2,1:T(8,128)(2,1)}, u32[]{:S(2)}, u32[]{:S(2)}) collective-permute-start(bf16[1024,3,64]{0,2,1:T(8,128)(2,1)} %pad_maximum_fusion.5), channel_id=1, source_target_pairs={{0,4},{1,5},{2,6},{3,7},{8,12},{9,13},{10,14},{11,15},{16,20},{17,... | collective-permute-start | bytes 1179656 | tf_op jit(solution)/shard_map/ppermute | solution.py:27
  133.3 17.8 collective-permute-start
  205.2 67.9 %copy-start.112 = (s32[2048,1]{0,1:T(1,128)}, s32[2048,1]{0,1:T(1,128)S(1)}, u32[]{:S(2)}) copy-start(s32[2048,1]{0,1:T(1,128)S(1)} %compare_select_fusion) | copy-start | bytes 24580
  221.7 51.5 %copy-start.94 = (f32[768]{0:T(1024)}, f32[768]{0:T(1024)S(1)}, u32[]{:S(2)}) copy-start(f32[768]{0:T(1024)S(1)} %reshape.1234) | copy-start | bytes 9220
  222.9 50.7 %copy-start.53 = (bf16[768,4]{1,0:T(8,128)(2,1)}, bf16[768,4]{1,0:T(8,128)(2,1)S(1)}, u32[]{:S(2)}) copy-start(bf16[768,4]{1,0:T(8,128)(2,1)S(1)} %reshape_reshape.22) | copy-start | bytes 18436
  331.4 279.6 %all-to-all-start = ((bf16[4,1024,1536]{2,1,0:T(8,128)(2,1)}), bf16[4,1024,1536]{2,1,0:T(8,128)(2,1)}, u32[]{:S(2)}, u32[]{:S(2)}) async-start(bf16[4,1024,1536]{2,1,0:T(8,128)(2,1)} %pad_maximum_fusion.1), calls=%async_computation | async-start | bytes 25165824 | tf_op jit(solution)/shard_map/all_to_all | solution.py:269
  337.9 30.5 %all-gather.6.cloned.1.call-start = ((), (), s32[]{:S(2)}) async-start(), calls=%async_computation.5 | async-start | bytes 2359296 | tf_op jit(solution)/shard_map/all_gather | solution.py:356
  678.8 551.2 %all-to-all-start.1 = ((f32[4,1024,1536]{1,2,0:T(8,128)}), f32[4,1024,1536]{1,2,0:T(8,128)}, u32[]{:S(2)}, u32[]{:S(2)}) async-start(f32[4,1024,1536]{1,2,0:T(8,128)} %bitcast.437), calls=%async_computation.1 | async-start | bytes 50331648 | tf_op jit(solution)/shard_map/all_to_all | solution.py:269
  687.9 693.2 %all-reduce.21.cloned.1.call-start = ((), (), s32[]{:S(2)}) async-start(), calls=%async_computation.6 | async-start | bytes 6291456 | tf_op jit(solution)/shard_map/psum | solution.py:453
  1313.8 299.6 %all-reduce.27.cloned.1.call-start = ((), (), s32[]{:S(2)}) async-start(), calls=%async_computation.12 | async-start | bytes 12582912 | tf_op jit(solution)/shard_map/psum | solution.py:453
  1334.0 47.1 %copy-start.92 = (bf16[1024,4]{0,1:T(4,128)(2,1)}, bf16[1024,4]{0,1:T(4,128)(2,1)S(1)}, u32[]{:S(2)}) copy-start(bf16[1024,4]{0,1:T(4,128)(2,1)S(1)} %select_reduce_fusion) | copy-start | bytes 24580
  1334.0 47.1 %copy-start.5 = (f32[1024,768]{1,0:T(8,128)S(1)}, f32[1024,768]{1,0:T(8,128)}, u32[]{:S(2)}) copy-start(f32[1024,768]{1,0:T(8,128)} %copy-done.4) | copy-start | bytes 9437188
  1334.0 47.1 %copy-start.54 = (bf16[768,4]{1,0:T(8,128)(2,1)S(1)}, bf16[768,4]{1,0:T(8,128)(2,1)}, u32[]{:S(2)}) copy-start(bf16[768,4]{1,0:T(8,128)(2,1)} %copy-done.53) | copy-start | bytes 18436
  1334.0 47.1 %copy-start.95 = (f32[768]{0:T(1024)S(1)}, f32[768]{0:T(1024)}, u32[]{:S(2)}) copy-start(f32[768]{0:T(1024)} %copy-done.94) | copy-start | bytes 9220
  1468.9 14.0 collective-permute-start.3
  1475.7 14.4 collective-permute-start.4
  1494.0 142.5 %reduce-scatter.5.cloned.1.call-start = ((), (), s32[]{:S(2)}) async-start(), calls=%async_computation.8 | async-start | bytes 2359296 | tf_op jit(solution)/shard_map/reduce_scatter | solution.py:499
  1508.1 130.0 %reduce-scatter.3.cloned.1.call-start = ((), (), s32[]{:S(2)}) async-start(), calls=%async_computation.7 | async-start | bytes 4718592 | tf_op jit(solution)/shard_map/reduce_scatter | solution.py:498
  1549.2 307.7 %all-reduce.25.cloned.1.call-start = ((), (), s32[]{:S(2)}) async-start(), calls=%async_computation.11 | async-start | bytes 14286848
  1652.5 211.5 %copy-start.78 = (f32[24576]{0:T(1024)S(1)}, f32[24576]{0:T(1024)}, u32[]{:S(2)}) copy-start(f32[24576]{0:T(1024)} %reshape.1224) | copy-start | bytes 294916
  1652.5 211.6 %copy-start.91 = (f32[6144]{0:T(1024)S(1)}, f32[6144]{0:T(1024)}, u32[]{:S(2)}) copy-start(f32[6144]{0:T(1024)} %reshape.1223) | copy-start | bytes 73732
  1859.0 49.6 %copy-start.41 = (f32[96,2,512]{2,1,0:T(2,128)}, f32[96,2,512]{2,1,0:T(2,128)S(1)}, u32[]{:S(2)}) copy-start(f32[96,2,512]{2,1,0:T(2,128)S(1)} %reshape.1218) | copy-start | bytes 1179652
  1860.9 59.7 %copy-start.37 = (f32[512,96]{1,0:T(8,128)}, f32[512,96]{1,0:T(8,128)S(1)}, u32[]{:S(2)}) copy-start(f32[512,96]{1,0:T(8,128)S(1)} %reshape.1219) | copy-start | bytes 589828
  1916.5 60.6 %copy-start.12 = (f32[1,384,2,512]{3,1,2,0:T(8,128)S(1)}, f32[1,384,2,512]{3,1,2,0:T(8,128)}, u32[]{:S(2)}) copy-start(f32[1,384,2,512]{3,1,2,0:T(8,128)} %reduce-scatter.3.cloned.1.call-done) | copy-start | bytes 4718596
  1921.4 84.1 %copy-start.24 = (f32[1,384,2,512]{3,2,1,0:T(2,128)S(1)}, f32[1,384,2,512]{3,2,1,0:T(2,128)}, u32[]{:S(2)}) copy-start(f32[1,384,2,512]{3,2,1,0:T(2,128)} %param.34) | copy-start | bytes 4718596
  (121 other events, 966.5 us)
Sparse Core Ops, SparseCore 0:
  16.2 78.9 all-reduce.22
  97.9 86.3 all-gather.7
  203.0 67.6 all-reduce.18
  1313.9 67.1 all-reduce.20
  1494.1 119.1 all-reduce.26
  1619.7 237.1 all-reduce.24
Sparse Core Ops, SparseCore 1:
  340.5 27.8 all-gather.5
  1508.2 25.4 reduce-scatter.4
  1549.3 42.7 reduce-scatter.2

commit v4 on v3

--- a/solution.py
+++ b/solution.py
@@ -267,7 +267,16 @@
         [normed_two[owner_route // 2] * fill_mask, route_grads[owner_route] * fill_mask], axis=1
     ).reshape(experts, capacity, 2 * model_width)
     exchange = lambda rows: lax.all_to_all(rows, "fsdp", split_axis=0, concat_axis=0, tiled=True)
-    received_both = exchange(send_rows).reshape(experts * capacity, 2 * model_width)
+    pair_count = lax.axis_size("tp")
+    swap = lambda rows: lax.ppermute(
+        rows, "tp", [(index, index + 1 - 2 * (index % 2)) for index in range(pair_count)]
+    )
+    half = capacity // 2
+    side = lax.axis_index("tp") % 2
+    mine = exchange(lax.dynamic_slice_in_dim(send_rows, side * half, half, 1))
+    received_both = jnp.concatenate([mine, swap(mine)], axis=1).reshape(
+        experts * capacity, 2 * model_width
+    )
     received = received_both[:, :model_width]
     grad_received = received_both[:, model_width:]
     gate_up = jnp.einsum("rd,dgf->rgf", received, expert_in_low, preferred_element_type=jnp.float32)
@@ -283,11 +292,16 @@
     grad_expert_rows = jnp.einsum(
         "rgf,dgf->rd", grad_gate_up, expert_in_low, preferred_element_type=jnp.float32
     )
-    returned = exchange(
-        jnp.concatenate([outs, grad_expert_rows], axis=1).reshape(
-            experts, capacity, 2 * model_width
-        )
-    ).reshape(experts * capacity, 2 * model_width)[slot_index]
+    results = jnp.concatenate([outs, grad_expert_rows], axis=1).reshape(
+        experts, capacity, 2 * model_width
+    )
+    pair_sum = results[:, :half] + swap(results[:, half:])
+    held = exchange(pair_sum).reshape(experts * half, 2 * model_width)
+    slot_expert = slot_index // capacity
+    slot_rank = slot_index % capacity
+    in_side = (slot_rank // half) == side
+    local_slot = slot_expert * half + slot_rank % half
+    returned = jnp.where(in_side[:, None], held[local_slot], 0.0)
     route_out = returned[:, :model_width].reshape(block_len, 2, model_width)
     grad_routes = returned[:, model_width:].reshape(block_len, 2, model_width)
     combined = jnp.sum(gate_probs[:, :, None] * route_out, axis=1)

time: 2050 us -> 1760 us (0.86)
  waiting for transfers between devices: 1190 us -> 685 us
  blocking collectives: 20.2 us -> 166 us
  other arithmetic: 187 us -> 228 us
  local copies, waits for them, and re-layouts: 326 us -> 364 us
    all_to_all x2 -> x1, waiting for transfers between devices: 769 us -> 257 us  [experts_routed(): lax.all_to_all(rows, 'fsdp', split_axis=0, concat_axis=0, tiled=True)]
    all_to_all x0 -> x1, blocking collectives: none -> 143 us  [experts_routed(): lax.all_to_all(rows, 'fsdp', split_axis=0, concat_axis=0, tiled=True)]
    reshape x1, local copies, waits for them, and re-layouts: 8.62 us -> 30 us  [experts_routed(): jnp.concatenate([outs, grad_expert_rows], axis=1)]
    unnamed x266 -> x271, local copies, waits for them, and re-layouts: 43.6 us -> 56.8 us
  transfers between devices with their start and end apart: 16 -> 17, of which waited for: 11 -> 11; matrix products, arithmetic and copies ran while one was open for 13% -> 16% of each run, Pallas kernels for 0% -> 0%
where the time goes in v4:
time: 1760 us; the launch traced here: 1750 us
  waiting for transfers between devices  685 us (39%)
  local copies, waits for them, and re-layouts  364 us (21%)
  other arithmetic  228 us (13%)
  matrix products  188 us (11%)
  blocking collectives  166 us (9%)
  Pallas kernels  44.6 us (3%)
  between operations  44.6 us (3%)
  starting transfers between devices  20.5 us (1%)
    unnamed x11, waiting for transfers between devices  268 us
    all_to_all x1, waiting for transfers between devices, experts_routed(): lax.all_to_all(rows, 'fsdp', split_axis=0, concat_axis=0, tiled=True)  257 us
    all_to_all x1, blocking collectives, experts_routed(): lax.all_to_all(rows, 'fsdp', split_axis=0, concat_axis=0, tiled=True)  143 us
    psum x2, waiting for transfers between devices, local(): lax.psum((shared_out + combined, partial_two, gate_dots), 'tp')  62.5 us
    unnamed x271, local copies, waits for them, and re-layouts  56.8 us
    psum x1, waiting for transfers between devices, local(): lax.psum(jnp.dot(mixed_heads, attn_out_low, preferred_element_type=jnp.fl...  47.1 us
    pallas_call x2, Pallas kernels, butterfly_sum(): pl.pallas_call(butterfly_kernel, out_shape=jax.ShapeDtypeStruct((rows, 12...  44.6 us
  transfers between devices with their start and end apart: 17, of which 11 were waited for; matrix products, arithmetic and copies ran while one was open for 16% of the time, Pallas kernels for 0%

profile of v4, /device:TPU:0, one launch (start us, length us, event | category | flops | bytes accessed | tf_op | source)
XLA Modules:
  0.0 1748.8 jit_solution(14966860576198955056)
XLA Ops:
  31.3 63.8 %all-reduce.23.cloned.1.call-done = bf16[443904]{0:T(1024)(128)(2,1)} async-done(((bf16[443904]{0:T(1024)(128)(2,1)}), bf16[443904]{0:T(1024)(128)(2,1)}) %all-reduce.23.cloned.1.call-update) | async-done | bytes 887824
  135.8 15.2 collective-permute-done
  151.1 39.3 %while.39 = (s32[]{:T(128)}, bf16[2,512,3,64]{1,3,2,0:T(8,128)(2,1)}, f32[2,3,512,1]{2,1,3,0:T(4,128)}, s32[2]{0:T(128)}, bf16[2048,3,64]{0,2,1:T(8,128)(2,1)S(1...) while((s32[]{:T(128)}, ...), condition=%wide.region_4.5_spmd, body=%wide.region_1.4_spmd.sunk | while | flops 644092928 | bytes 33331516 | solution.py:418
  223.6 47.1 %all-reduce.19.cloned.1.call-done = f32[1024,768]{1,0:T(8,128)} async-done(((f32[1024,768]{1,0:T(8,128)}), f32[1024,768]{1,0:T(8,128)}) %all-reduce.19.cloned.1.call-update) | async-done | bytes 3145744 | tf_op jit(solution)/shard_map/psum | solution.py:420
  276.6 17.8 %gather_fusion = bf16[4096,768]{1,0:T(8,128)(2,1)} fusion(bf16[1024,768]{1,0:T(8,128)(2,1)S(1)} %multiply_convert_fusion.4, s32[4096]{0:T(1024)S(1)} %get-tuple-element.935), kind=kCustom, calls=%fused_computation | custom fusion | bytes 12599296 | tf_op jit(solution)/shard_map/gather | solution.py:267
  299.2 21.4 %gather_fusion.1 = bf16[4096,768]{1,0:T(8,128)(2,1)} fusion(bf16[2048,768]{1,0:T(8,128)(2,1)} %multiply_convert_fusion.2, s32[4096]{0:T(1024)S(1)} %get-tuple-element.934), kind=kCustom, calls=%fused_computation.1 | custom fusion | bytes 12599296 | tf_op jit(solution)/shard_map/gather | solution.py:267
  331.4 142.6 %all_to_all.10 = bf16[4,512,1536]{2,1,0:T(8,128)(2,1)} all-to-all(bf16[4,512,1536]{2,1,0:T(8,128)(2,1)S(1)} %fusion.56), channel_id=1, replica_groups=mesh['fsdp'=4,'ctx'=2,'tp'=4] {'fsdp'}, dimensions={0} | all-to-all | bytes 12582912 | tf_op jit(solution)/shard_map/all_to_all | solution.py:269
  476.0 16.5 all_gather.23
  492.5 10.4 pad_maximum_fusion.1
  505.2 12.4 fusion.62
  517.7 14.3 multiply_bitcast_fusion
  540.0 15.4 convolution_bitcast_fusion
  555.4 14.6 pad_maximum_fusion
  570.0 30.0 %reshape.1340 = f32[4,1024,1536]{1,0,2:T(4,128)} reshape(f32[4096,1536]{0,1:T(8,128)} %pad_maximum_fusion) | data formatting | bytes 50331648 | tf_op jit(solution)/shard_map/reshape | solution.py:295
  599.9 18.6 %fusion.188 = (f32[4,512,1536]{1,0,2:T(4,128)}, f32[4,512,1536]{1,0,2:T(4,128)}) fusion(f32[4,1024,1536]{1,0,2:T(4,128)} %reshape.1340), kind=kLoop, calls=%fused_computation.424 | loop fusion | bytes 50331648 | tf_op jit(solution)/shard_map/slice | solution.py:298
  618.5 13.2 copy.254
  631.7 19.3 %collective-permute-done.4 = f32[4,512,1536]{1,2,0:T(8,128)S(1)} collective-permute-done((f32[4,512,1536]{1,2,0:T(8,128)}, f32[4,512,1536]{1,2,0:T(8,128)S(1)}, u32[]{:S(2)}, u32[]{:S(2)}) %collective-permute-start.4) | collective-permute-done | bytes 12582944 | tf_op jit(solution)/shard_map/ppermute | solution.py:271
  651.0 13.8 copy_add_fusion
  687.6 257.4 %all-to-all-done.1 = f32[4,512,1536]{1,2,0:T(8,128)} async-done(((f32[4,512,1536]{1,2,0:T(8,128)}), f32[4,512,1536]{1,2,0:T(8,128)}, u32[]{:S(2)}, u32[]{:S(2)}) %all-to-all-start.1) | async-done | bytes 12582944 | tf_op jit(solution)/shard_map/all_to_all | solution.py:269
  945.0 12.6 copy.217
  957.6 18.8 %gather_fusion.2 = f32[2048,1536]{1,0:T(8,128)} fusion(f32[2048,1536]{1,0:T(8,128)} %bitcast.435, s32[2048]{0:T(1024)S(1)} %broadcast_clamp_fusion), kind=kCustom, calls=%fused_computation.2 | custom fusion | bytes 25174016 | tf_op jit(solution)/shard_map/gather | solution.py:304
  986.5 11.8 multiply_reduce_fusion.1
  1006.7 10.3 reduce_sum.549
  1043.4 11.4 multiply_reduce_fusion.2
  1054.8 35.7 %all-reduce.21.cloned.1.call-done = f32[1024,768]{1,0:T(8,128)} async-done(((f32[1024,768]{1,0:T(8,128)}), f32[1024,768]{1,0:T(8,128)}) %all-reduce.21.cloned.1.call-update) | async-done | bytes 3145744 | tf_op jit(solution)/shard_map/psum | solution.py:467
  1100.2 76.7 %while.40 = (s32[]{:T(128)}, f32[2048,3,64]{0,2,1:T(8,128)}, f32[2048,3,64]{0,2,1:T(8,128)S(1)}, f32[1024,3,64]{0,2,1:T(8,128)}, bf16[1024,3,64]{0,2,1:T(8,128)(...) while((s32[]{:T(128)}, f32[2048,3,64]{0,2,1:T(8,128)}, ...), condition=%wide.region_26.27_spmd, body=%wide.region_24.26_spmd.sunk | while | flops 1541608448 | bytes 106823088 | solution.py:574
  1203.4 13.9 fusion.108
  1245.0 13.4 fusion.89
  1295.8 26.9 %all-reduce.27.cloned.1.call-done = (f32[1024,768]{1,0:T(8,128)}, f32[1024,768]{1,0:T(8,128)}) async-done(((f32[1024,768]{1,0:T(8,128)}, f32[1024,768]{1,0:T(8,128)}), (f32[1024,768]{1,0:T(8,128)}, f32[1024,768]{1,0:T(8,128)})) %all-reduce.27.cloned.1.call-update) | async-done | bytes 6291472 | tf_op jit(solution)/shard_map/psum | solution.py:467
  1361.9 204.3 %all-reduce.25.cloned.1.call-done = (f32[10432,128]{1,0:T(8,128)}, f32[3520,128]{1,0:T(8,128)}) async-done(((f32[10432,128]{1,0:T(8,128)}, f32[3520,128]{1,0:T(8,128)}), (f32[10432,128]{1,0:T(8,128)}, f32[3520,128]{1,0:T(8,128)})) %all-reduce.25.cloned.1.call-update) | async-done | bytes 7143440
  1578.0 29.8 %shard_map.395 = f32[344,128]{1,0:T(8,128)} custom-call(f32[344,128]{1,0:T(8,128)} %pad_bitcast_fusion.x_ref), custom_call_target="tpu_custom_call" | custom-call | tf_op jit(solution)/shard_map/pallas_call | solution.py:162
  1696.1 14.9 shard_map.396
  (648 shorter events, 548.7 us)
Async XLA Ops:
  8.1 87.0 %all-reduce.23.cloned.1.call-start = ((), (), s32[]{:S(2)}) async-start(), calls=%async_computation.9 | async-start | bytes 1777664
  16.1 177.6 %all-gather.8.cloned.1.call-start = ((), (), s32[]{:S(2)}) async-start(), calls=%async_computation.10 | async-start | bytes 5985792 | tf_op jit(solution)/shard_map/all_gather | solution.py:189
  16.2 118.4 %collective-permute-start.1 = (bf16[1024]{0:T(1024)(128)(2,1)S(1)}, bf16[1024]{0:T(1024)(128)(2,1)S(1)}, u32[]{:S(2)}, u32[]{:S(2)}) collective-permute-start(bf16[1024]{0:T(1024)(128)(2,1)S(1)} %convert_reduce_fusion), channel_id=1, source_target_pairs={{0,4},{1,5},{2,6},{3,7},{8,12},{9,13},{10,14},{11,15},{16,20},{17,... | collective-permute-start | bytes 6152 | tf_op jit(solution)/shard_map/ppermute | solution.py:27
  29.6 241.2 %all-reduce.19.cloned.1.call-start = ((), (), s32[]{:S(2)}) async-start(), calls=%async_computation.4 | async-start | bytes 6291456 | tf_op jit(solution)/shard_map/psum | solution.py:420
  30.0 72.9 %copy-start.110 = (f32[1024]{0:T(1024)}, f32[1024]{0:T(1024)S(1)}, u32[]{:S(2)}) copy-start(f32[1024]{0:T(1024)S(1)} %fusion.75) | copy-start | bytes 12292
  30.1 75.6 %copy-start.106 = (f32[1024]{0:T(1024)}, f32[1024]{0:T(1024)S(1)}, u32[]{:S(2)}) copy-start(f32[1024]{0:T(1024)S(1)} %fusion.169) | copy-start | bytes 12292
  31.3 75.8 %copy-start.65 = (f32[1024,32]{0,1:T(8,128)}, f32[1024,32]{0,1:T(8,128)S(1)}, u32[]{:S(2)}) copy-start(f32[1024,32]{0,1:T(8,128)S(1)} %get-tuple-element.942) | copy-start | bytes 393220
  108.5 26.1 %collective-permute-start.2 = (bf16[1024,3,64]{0,2,1:T(8,128)(2,1)}, bf16[1024,3,64]{0,2,1:T(8,128)(2,1)}, u32[]{:S(2)}, u32[]{:S(2)}) collective-permute-start(bf16[1024,3,64]{0,2,1:T(8,128)(2,1)} %pad_maximum_fusion.5), channel_id=1, source_target_pairs={{0,4},{1,5},{2,6},{3,7},{8,12},{9,13},{10,14},{11,15},{16,20},{17,... | collective-permute-start | bytes 1179656 | tf_op jit(solution)/shard_map/ppermute | solution.py:27
  133.2 17.8 %collective-permute-start = (bf16[1024,3,64]{0,2,1:T(8,128)(2,1)S(1)}, bf16[1024,3,64]{0,2,1:T(8,128)(2,1)S(1)}, u32[]{:S(2)}, u32[]{:S(2)}) collective-permute-start(bf16[1024,3,64]{0,2,1:T(8,128)(2,1)S(1)} %bitcast.467), channel_id=1, source_target_pairs={{0,4},{1,5},{2,6},{3,7},{8,12},{9,13},{10,14},{11,15},{16,20},{17,... | collective-permute-start | bytes 1179656 | tf_op jit(solution)/shard_map/ppermute | solution.py:27
  202.9 302.3 %all-gather.6.cloned.1.call-start = ((), (), s32[]{:S(2)}) async-start(), calls=%async_computation.5 | async-start | bytes 2359296 | tf_op jit(solution)/shard_map/all_gather | solution.py:370
  205.3 67.9 %copy-start.94 = (s32[2048]{0:T(1024)}, s32[2048]{0:T(1024)S(1)}, u32[]{:S(2)}) copy-start(s32[2048]{0:T(1024)S(1)} %fusion.142) | copy-start | bytes 24580
  222.4 51.3 %copy-start.98 = (f32[768]{0:T(1024)}, f32[768]{0:T(1024)S(1)}, u32[]{:S(2)}) copy-start(f32[768]{0:T(1024)S(1)} %reshape.1372) | copy-start | bytes 9220
  223.6 50.5 %copy-start.53 = (bf16[768,4]{1,0:T(8,128)(2,1)}, bf16[768,4]{1,0:T(8,128)(2,1)S(1)}, u32[]{:S(2)}) copy-start(bf16[768,4]{1,0:T(8,128)(2,1)S(1)} %reshape_reshape.22) | copy-start | bytes 18436
  331.4 142.6 %copy-start.22 = (f32[1,384,2,512]{3,2,1,0:T(2,128)S(1)}, f32[1,384,2,512]{3,2,1,0:T(2,128)}, u32[]{:S(2)}) copy-start(f32[1,384,2,512]{3,2,1,0:T(2,128)} %param.34) | copy-start | bytes 4718596
  474.0 18.5 %collective-permute-start.3 = (bf16[4,512,1536]{2,1,0:T(8,128)(2,1)}, bf16[4,512,1536]{2,1,0:T(8,128)(2,1)}, u32[]{:S(2)}, u32[]{:S(2)}) collective-permute-start(bf16[4,512,1536]{2,1,0:T(8,128)(2,1)} %all_to_all.10), channel_id=1, source_target_pairs={{0,1},{1,0},{2,3},{3,2},{4,5},{5,4},{6,7},{7,6},{8,9},{9,8},{10,11... | collective-permute-start | bytes 18874376 | tf_op jit(solution)/shard_map/ppermute | solution.py:271
  631.7 19.4 %collective-permute-start.4 = (f32[4,512,1536]{1,2,0:T(8,128)}, f32[4,512,1536]{1,2,0:T(8,128)S(1)}, u32[]{:S(2)}, u32[]{:S(2)}) collective-permute-start(f32[4,512,1536]{1,2,0:T(8,128)} %copy.254), channel_id=1, source_target_pairs={{0,1},{1,0},{2,3},{3,2},{4,5},{5,4},{6,7},{7,6},{8,9},{9,8},{10,11... | collective-permute-start | bytes 37748744 | tf_op jit(solution)/shard_map/ppermute | solution.py:271
  664.8 280.2 %all-to-all-start.1 = ((f32[4,512,1536]{1,2,0:T(8,128)}), f32[4,512,1536]{1,2,0:T(8,128)}, u32[]{:S(2)}, u32[]{:S(2)}) async-start(f32[4,512,1536]{1,2,0:T(8,128)} %copy_add_fusion), calls=%async_computation.1 | async-start | bytes 25165824 | tf_op jit(solution)/shard_map/all_to_all | solution.py:269
  671.4 419.0 %all-reduce.21.cloned.1.call-start = ((), (), s32[]{:S(2)}) async-start(), calls=%async_computation.6 | async-start | bytes 6291456 | tf_op jit(solution)/shard_map/psum | solution.py:467
  1023.1 299.6 %all-reduce.27.cloned.1.call-start = ((), (), s32[]{:S(2)}) async-start(), calls=%async_computation.12 | async-start | bytes 12582912 | tf_op jit(solution)/shard_map/psum | solution.py:467
  1043.3 47.1 %copy-start.96 = (bf16[1024,4]{0,1:T(4,128)(2,1)}, bf16[1024,4]{0,1:T(4,128)(2,1)S(1)}, u32[]{:S(2)}) copy-start(bf16[1024,4]{0,1:T(4,128)(2,1)S(1)} %select_reduce_fusion) | copy-start | bytes 24580
  1043.3 47.1 %copy-start.5 = (f32[1024,768]{1,0:T(8,128)S(1)}, f32[1024,768]{1,0:T(8,128)}, u32[]{:S(2)}) copy-start(f32[1024,768]{1,0:T(8,128)} %copy-done.4) | copy-start | bytes 9437188
  1178.2 14.0 collective-permute-start.5
  1185.0 14.4 collective-permute-start.6
  1203.4 142.6 %reduce-scatter.5.cloned.1.call-start = ((), (), s32[]{:S(2)}) async-start(), calls=%async_computation.8 | async-start | bytes 2359296 | tf_op jit(solution)/shard_map/reduce_scatter | solution.py:513
  1217.4 130.1 %reduce-scatter.3.cloned.1.call-start = ((), (), s32[]{:S(2)}) async-start(), calls=%async_computation.7 | async-start | bytes 4718592 | tf_op jit(solution)/shard_map/reduce_scatter | solution.py:512
  1258.5 307.7 %all-reduce.25.cloned.1.call-start = ((), (), s32[]{:S(2)}) async-start(), calls=%async_computation.11 | async-start | bytes 14286848
  1361.9 211.5 %copy-start.78 = (f32[24576]{0:T(1024)S(1)}, f32[24576]{0:T(1024)}, u32[]{:S(2)}) copy-start(f32[24576]{0:T(1024)} %reshape.1362) | copy-start | bytes 294916
  1361.9 211.5 %copy-start.91 = (f32[6144]{0:T(1024)S(1)}, f32[6144]{0:T(1024)}, u32[]{:S(2)}) copy-start(f32[6144]{0:T(1024)} %reshape.1361) | copy-start | bytes 73732
  1568.4 49.7 %copy-start.41 = (f32[96,2,512]{2,1,0:T(2,128)}, f32[96,2,512]{2,1,0:T(2,128)S(1)}, u32[]{:S(2)}) copy-start(f32[96,2,512]{2,1,0:T(2,128)S(1)} %reshape.1356) | copy-start | bytes 1179652
  1570.2 59.8 %copy-start.37 = (f32[512,96]{1,0:T(8,128)}, f32[512,96]{1,0:T(8,128)S(1)}, u32[]{:S(2)}) copy-start(f32[512,96]{1,0:T(8,128)S(1)} %reshape.1357) | copy-start | bytes 589828
  1625.9 60.6 %copy-start.12 = (f32[1,384,2,512]{3,1,2,0:T(8,128)S(1)}, f32[1,384,2,512]{3,1,2,0:T(8,128)}, u32[]{:S(2)}) copy-start(f32[1,384,2,512]{3,1,2,0:T(8,128)} %reduce-scatter.3.cloned.1.call-done) | copy-start | bytes 4718596
  1630.9 84.1 %copy-start.24 = (f32[1,384,2,512]{3,2,1,0:T(2,128)S(1)}, f32[1,384,2,512]{3,2,1,0:T(2,128)}, u32[]{:S(2)}) copy-start(f32[1,384,2,512]{3,2,1,0:T(2,128)} %param.34) | copy-start | bytes 4718596
  (124 other events, 1061.8 us)
Sparse Core Ops, SparseCore 0:
  16.2 78.8 all-reduce.22
  97.9 86.3 all-gather.7
  203.0 67.6 all-reduce.18
  1023.2 67.1 all-reduce.20
  1203.5 119.1 all-reduce.26
  1329.0 237.1 all-reduce.24
Sparse Core Ops, SparseCore 1:
  475.3 29.9 all-gather.5
  1217.5 25.4 reduce-scatter.4
  1258.6 42.7 reduce-scatter.2

commit v5 on v4

--- a/solution.py
+++ b/solution.py
@@ -296,12 +296,12 @@
         experts, capacity, 2 * model_width
     )
     pair_sum = results[:, :half] + swap(results[:, half:])
-    held = exchange(pair_sum).reshape(experts * half, 2 * model_width)
+    held = exchange(pair_sum.astype(jnp.bfloat16)).reshape(experts * half, 2 * model_width)
     slot_expert = slot_index // capacity
     slot_rank = slot_index % capacity
     in_side = (slot_rank // half) == side
     local_slot = slot_expert * half + slot_rank % half
-    returned = jnp.where(in_side[:, None], held[local_slot], 0.0)
+    returned = jnp.where(in_side[:, None], held[local_slot].astype(jnp.float32), 0.0)
     route_out = returned[:, :model_width].reshape(block_len, 2, model_width)
     grad_routes = returned[:, model_width:].reshape(block_len, 2, model_width)
     combined = jnp.sum(gate_probs[:, :, None] * route_out, axis=1)

time: 1760 us -> 1610 us (0.915)
  waiting for transfers between devices: 685 us -> 550 us
    all_to_all x1, waiting for transfers between devices: 257 us -> 122 us  [experts_routed(): lax.all_to_all(rows, 'fsdp', split_axis=0, concat_axis=0, tiled=True)]
  transfers between devices with their start and end apart: 17 -> 17, of which waited for: 11 -> 11; matrix products, arithmetic and copies ran while one was open for 16% -> 17% of each run, Pallas kernels for 0% -> 0%
where the time goes in v5:
time: 1610 us; the launch traced here: 1590 us
  waiting for transfers between devices  550 us (34%)
  local copies, waits for them, and re-layouts  358 us (22%)
  other arithmetic  214 us (13%)
  matrix products  188 us (12%)
  blocking collectives  166 us (10%)
  Pallas kernels  44.6 us (3%)
  between operations  44.6 us (3%)
  starting transfers between devices  19.4 us (1%)
    unnamed x11, waiting for transfers between devices  268 us
    all_to_all x1, blocking collectives, experts_routed(): lax.all_to_all(rows, 'fsdp', split_axis=0, concat_axis=0, tiled=True)  143 us
    all_to_all x1, waiting for transfers between devices, experts_routed(): lax.all_to_all(rows, 'fsdp', split_axis=0, concat_axis=0, tiled=True)  122 us
    psum x2, waiting for transfers between devices, local(): lax.psum((shared_out + combined, partial_two, gate_dots), 'tp')  62.5 us
    unnamed x271, local copies, waits for them, and re-layouts  57 us
    psum x1, waiting for transfers between devices, local(): lax.psum(jnp.dot(mixed_heads, attn_out_low, preferred_element_type=jnp.fl...  47.1 us
    pallas_call x2, Pallas kernels, butterfly_sum(): pl.pallas_call(butterfly_kernel, out_shape=jax.ShapeDtypeStruct((rows, 12...  44.6 us
  transfers between devices with their start and end apart: 17, of which 11 were waited for; matrix products, arithmetic and copies ran while one was open for 17% of the time, Pallas kernels for 0%

profile of v5, /device:TPU:0, one launch (start us, length us, event | category | flops | bytes accessed | tf_op | source)
XLA Modules:
  0.0 1593.0 jit_solution(5345113674352943426)
XLA Ops:
  31.3 63.8 %all-reduce.23.cloned.1.call-done = bf16[443904]{0:T(1024)(128)(2,1)} async-done(((bf16[443904]{0:T(1024)(128)(2,1)}), bf16[443904]{0:T(1024)(128)(2,1)}) %all-reduce.23.cloned.1.call-update) | async-done | bytes 887824
  135.8 15.2 collective-permute-done
  151.1 39.3 %while.39 = (s32[]{:T(128)}, bf16[2,512,3,64]{1,3,2,0:T(8,128)(2,1)}, f32[2,3,512,1]{2,1,3,0:T(4,128)}, s32[2]{0:T(128)}, bf16[2048,3,64]{0,2,1:T(8,128)(2,1)S(1...) while((s32[]{:T(128)}, ...), condition=%wide.region_4.5_spmd, body=%wide.region_1.4_spmd.sunk | while | flops 644092928 | bytes 33331516 | solution.py:418
  223.6 47.1 %all-reduce.19.cloned.1.call-done = f32[1024,768]{1,0:T(8,128)} async-done(((f32[1024,768]{1,0:T(8,128)}), f32[1024,768]{1,0:T(8,128)}) %all-reduce.19.cloned.1.call-update) | async-done | bytes 3145744 | tf_op jit(solution)/shard_map/psum | solution.py:420
  276.6 17.8 %gather_fusion = bf16[4096,768]{1,0:T(8,128)(2,1)} fusion(bf16[1024,768]{1,0:T(8,128)(2,1)S(1)} %multiply_convert_fusion.4, s32[4096]{0:T(1024)S(1)} %get-tuple-element.935), kind=kCustom, calls=%fused_computation | custom fusion | bytes 12599296 | tf_op jit(solution)/shard_map/gather | solution.py:267
  299.2 21.4 %gather_fusion.1 = bf16[4096,768]{1,0:T(8,128)(2,1)} fusion(bf16[2048,768]{1,0:T(8,128)(2,1)} %multiply_convert_fusion.2, s32[4096]{0:T(1024)S(1)} %get-tuple-element.934), kind=kCustom, calls=%fused_computation.1 | custom fusion | bytes 12599296 | tf_op jit(solution)/shard_map/gather | solution.py:267
  331.4 142.6 %all_to_all.10 = bf16[4,512,1536]{2,1,0:T(8,128)(2,1)} all-to-all(bf16[4,512,1536]{2,1,0:T(8,128)(2,1)S(1)} %fusion.57), channel_id=1, replica_groups=mesh['fsdp'=4,'ctx'=2,'tp'=4] {'fsdp'}, dimensions={0} | all-to-all | bytes 12582912 | tf_op jit(solution)/shard_map/all_to_all | solution.py:269
  476.0 16.5 %all_gather.23 = bf16[1,512,768]{2,1,0:T(8,128)(2,1)S(1)} all-gather(bf16[1,512,384]{2,1,0:T(8,128)(2,1)S(1)} %get-tuple-element.898), channel_id=1, replica_groups=mesh['fsdp'=4,'ctx'=2,'tp'=4] {'ctx'}, dimensions={2}, use_global_device_ids=true | all-gather | bytes 1179648 | tf_op jit(solution)/shard_map/all_gather | solution.py:371
  492.5 10.4 pad_maximum_fusion.1
  505.2 12.4 fusion.63
  517.7 14.3 multiply_bitcast_fusion
  540.0 15.4 convolution_bitcast_fusion
  555.4 14.6 pad_maximum_fusion
  570.0 30.0 %reshape.1340 = f32[4,1024,1536]{1,0,2:T(4,128)} reshape(f32[4096,1536]{0,1:T(8,128)} %pad_maximum_fusion) | data formatting | bytes 50331648 | tf_op jit(solution)/shard_map/reshape | solution.py:295
  599.9 18.6 %fusion.189 = (f32[4,512,1536]{1,0,2:T(4,128)}, f32[4,512,1536]{1,0,2:T(4,128)}) fusion(f32[4,1024,1536]{1,0,2:T(4,128)} %reshape.1340), kind=kLoop, calls=%fused_computation.425 | loop fusion | bytes 50331648 | tf_op jit(solution)/shard_map/slice | solution.py:298
  618.5 13.2 copy.254
  631.7 19.3 %collective-permute-done.4 = f32[4,512,1536]{1,2,0:T(8,128)S(1)} collective-permute-done((f32[4,512,1536]{1,2,0:T(8,128)}, f32[4,512,1536]{1,2,0:T(8,128)S(1)}, u32[]{:S(2)}, u32[]{:S(2)}) %collective-permute-start.4) | collective-permute-done | bytes 12582944 | tf_op jit(solution)/shard_map/ppermute | solution.py:271
  651.0 10.6 fusion.49
  683.7 122.2 %all-to-all-done.1 = bf16[4,512,1536]{1,2,0:T(8,128)(2,1)} async-done(((bf16[4,512,1536]{1,2,0:T(8,128)(2,1)}), bf16[4,512,1536]{1,2,0:T(8,128)(2,1)}, u32[]{:S(2)}, u32[]{:S(2)}) %all-to-all-start.1) | async-done | bytes 6291488 | tf_op jit(solution)/shard_map/all_to_all | solution.py:269
  814.5 16.9 %gather_fusion.2 = bf16[2048,1536]{1,0:T(8,128)(2,1)} fusion(bf16[2048,1536]{1,0:T(8,128)(2,1)} %bitcast.435, s32[2048]{0:T(1024)S(1)} %broadcast_clamp_fusion), kind=kCustom, calls=%fused_computation.2 | custom fusion | bytes 12591104 | tf_op jit(solution)/shard_map/gather | solution.py:304
  850.8 10.3 reduce_sum.549
  887.5 11.4 multiply_reduce_fusion.2
  898.9 35.7 %all-reduce.21.cloned.1.call-done = f32[1024,768]{1,0:T(8,128)} async-done(((f32[1024,768]{1,0:T(8,128)}), f32[1024,768]{1,0:T(8,128)}) %all-reduce.21.cloned.1.call-update) | async-done | bytes 3145744 | tf_op jit(solution)/shard_map/psum | solution.py:467
  944.4 76.7 %while.40 = (s32[]{:T(128)}, f32[2048,3,64]{0,2,1:T(8,128)}, f32[2048,3,64]{0,2,1:T(8,128)S(1)}, f32[1024,3,64]{0,2,1:T(8,128)}, bf16[1024,3,64]{0,2,1:T(8,128)(...) while((s32[]{:T(128)}, f32[2048,3,64]{0,2,1:T(8,128)}, ...), condition=%wide.region_26.27_spmd, body=%wide.region_24.26_spmd.sunk | while | flops 1541608448 | bytes 106823088 | solution.py:574
  961.4 9.4 multiply_convert_fusion.7
  999.8 9.4 multiply_convert_fusion.7
  1047.6 13.9 fusion.109
  1089.2 13.4 fusion.90
  1140.0 26.9 %all-reduce.27.cloned.1.call-done = (f32[1024,768]{1,0:T(8,128)}, f32[1024,768]{1,0:T(8,128)}) async-done(((f32[1024,768]{1,0:T(8,128)}, f32[1024,768]{1,0:T(8,128)}), (f32[1024,768]{1,0:T(8,128)}, f32[1024,768]{1,0:T(8,128)})) %all-reduce.27.cloned.1.call-update) | async-done | bytes 6291472 | tf_op jit(solution)/shard_map/psum | solution.py:467
  1206.0 204.3 %all-reduce.25.cloned.1.call-done = (f32[10432,128]{1,0:T(8,128)}, f32[3520,128]{1,0:T(8,128)}) async-done(((f32[10432,128]{1,0:T(8,128)}, f32[3520,128]{1,0:T(8,128)}), (f32[10432,128]{1,0:T(8,128)}, f32[3520,128]{1,0:T(8,128)})) %all-reduce.25.cloned.1.call-update) | async-done | bytes 7143440
  1422.2 29.8 %shard_map.395 = f32[344,128]{1,0:T(8,128)} custom-call(f32[344,128]{1,0:T(8,128)} %pad_bitcast_fusion.x_ref), custom_call_target="tpu_custom_call" | custom-call | tf_op jit(solution)/shard_map/pallas_call | solution.py:162
  1540.3 14.9 shard_map.396
  (648 shorter events, 538.7 us)
Async XLA Ops:
  8.1 87.0 %all-reduce.23.cloned.1.call-start = ((), (), s32[]{:S(2)}) async-start(), calls=%async_computation.9 | async-start | bytes 1777664
  16.1 177.6 %all-gather.8.cloned.1.call-start = ((), (), s32[]{:S(2)}) async-start(), calls=%async_computation.10 | async-start | bytes 5985792 | tf_op jit(solution)/shard_map/all_gather | solution.py:189
  16.2 118.4 %collective-permute-start.1 = (bf16[1024]{0:T(1024)(128)(2,1)S(1)}, bf16[1024]{0:T(1024)(128)(2,1)S(1)}, u32[]{:S(2)}, u32[]{:S(2)}) collective-permute-start(bf16[1024]{0:T(1024)(128)(2,1)S(1)} %convert_reduce_fusion), channel_id=1, source_target_pairs={{0,4},{1,5},{2,6},{3,7},{8,12},{9,13},{10,14},{11,15},{16,20},{17,... | collective-permute-start | bytes 6152 | tf_op jit(solution)/shard_map/ppermute | solution.py:27
  29.6 241.2 %all-reduce.19.cloned.1.call-start = ((), (), s32[]{:S(2)}) async-start(), calls=%async_computation.4 | async-start | bytes 6291456 | tf_op jit(solution)/shard_map/psum | solution.py:420
  30.0 72.9 %copy-start.110 = (f32[1024]{0:T(1024)}, f32[1024]{0:T(1024)S(1)}, u32[]{:S(2)}) copy-start(f32[1024]{0:T(1024)S(1)} %fusion.76) | copy-start | bytes 12292
  30.1 75.6 %copy-start.106 = (f32[1024]{0:T(1024)}, f32[1024]{0:T(1024)S(1)}, u32[]{:S(2)}) copy-start(f32[1024]{0:T(1024)S(1)} %fusion.170) | copy-start | bytes 12292
  31.3 75.8 %copy-start.65 = (f32[1024,32]{0,1:T(8,128)}, f32[1024,32]{0,1:T(8,128)S(1)}, u32[]{:S(2)}) copy-start(f32[1024,32]{0,1:T(8,128)S(1)} %get-tuple-element.942) | copy-start | bytes 393220
  108.5 26.1 %collective-permute-start.2 = (bf16[1024,3,64]{0,2,1:T(8,128)(2,1)}, bf16[1024,3,64]{0,2,1:T(8,128)(2,1)}, u32[]{:S(2)}, u32[]{:S(2)}) collective-permute-start(bf16[1024,3,64]{0,2,1:T(8,128)(2,1)} %pad_maximum_fusion.5), channel_id=1, source_target_pairs={{0,4},{1,5},{2,6},{3,7},{8,12},{9,13},{10,14},{11,15},{16,20},{17,... | collective-permute-start | bytes 1179656 | tf_op jit(solution)/shard_map/ppermute | solution.py:27
  133.2 17.8 %collective-permute-start = (bf16[1024,3,64]{0,2,1:T(8,128)(2,1)S(1)}, bf16[1024,3,64]{0,2,1:T(8,128)(2,1)S(1)}, u32[]{:S(2)}, u32[]{:S(2)}) collective-permute-start(bf16[1024,3,64]{0,2,1:T(8,128)(2,1)S(1)} %bitcast.467), channel_id=1, source_target_pairs={{0,4},{1,5},{2,6},{3,7},{8,12},{9,13},{10,14},{11,15},{16,20},{17,... | collective-permute-start | bytes 1179656 | tf_op jit(solution)/shard_map/ppermute | solution.py:27
  202.9 302.3 %all-gather.6.cloned.1.call-start = ((), (), s32[]{:S(2)}) async-start(), calls=%async_computation.5 | async-start | bytes 2359296 | tf_op jit(solution)/shard_map/all_gather | solution.py:370
  205.3 67.9 %copy-start.94 = (s32[2048]{0:T(1024)}, s32[2048]{0:T(1024)S(1)}, u32[]{:S(2)}) copy-start(s32[2048]{0:T(1024)S(1)} %fusion.143) | copy-start | bytes 24580
  222.4 51.3 %copy-start.98 = (f32[768]{0:T(1024)}, f32[768]{0:T(1024)S(1)}, u32[]{:S(2)}) copy-start(f32[768]{0:T(1024)S(1)} %reshape.1372) | copy-start | bytes 9220
  223.6 50.5 %copy-start.53 = (bf16[768,4]{1,0:T(8,128)(2,1)}, bf16[768,4]{1,0:T(8,128)(2,1)S(1)}, u32[]{:S(2)}) copy-start(bf16[768,4]{1,0:T(8,128)(2,1)S(1)} %reshape_reshape.22) | copy-start | bytes 18436
  331.4 142.6 %copy-start.22 = (f32[1,384,2,512]{3,2,1,0:T(2,128)S(1)}, f32[1,384,2,512]{3,2,1,0:T(2,128)}, u32[]{:S(2)}) copy-start(f32[1,384,2,512]{3,2,1,0:T(2,128)} %param.34) | copy-start | bytes 4718596
  474.0 18.5 %collective-permute-start.3 = (bf16[4,512,1536]{2,1,0:T(8,128)(2,1)}, bf16[4,512,1536]{2,1,0:T(8,128)(2,1)}, u32[]{:S(2)}, u32[]{:S(2)}) collective-permute-start(bf16[4,512,1536]{2,1,0:T(8,128)(2,1)} %all_to_all.10), channel_id=1, source_target_pairs={{0,1},{1,0},{2,3},{3,2},{4,5},{5,4},{6,7},{7,6},{8,9},{9,8},{10,11... | collective-permute-start | bytes 18874376 | tf_op jit(solution)/shard_map/ppermute | solution.py:271
  631.7 19.4 %collective-permute-start.4 = (f32[4,512,1536]{1,2,0:T(8,128)}, f32[4,512,1536]{1,2,0:T(8,128)S(1)}, u32[]{:S(2)}, u32[]{:S(2)}) collective-permute-start(f32[4,512,1536]{1,2,0:T(8,128)} %copy.254), channel_id=1, source_target_pairs={{0,1},{1,0},{2,3},{3,2},{4,5},{5,4},{6,7},{7,6},{8,9},{9,8},{10,11... | collective-permute-start | bytes 37748744 | tf_op jit(solution)/shard_map/ppermute | solution.py:271
  661.7 144.2 %all-to-all-start.1 = ((bf16[4,512,1536]{1,2,0:T(8,128)(2,1)}), bf16[4,512,1536]{1,2,0:T(8,128)(2,1)}, u32[]{:S(2)}, u32[]{:S(2)}) async-start(bf16[4,512,1536]{1,2,0:T(8,128)(2,1)} %fusion.49), calls=%async_computation.1 | async-start | bytes 12582912 | tf_op jit(solution)/shard_map/all_to_all | solution.py:269
  667.2 267.4 %all-reduce.21.cloned.1.call-start = ((), (), s32[]{:S(2)}) async-start(), calls=%async_computation.6 | async-start | bytes 6291456 | tf_op jit(solution)/shard_map/psum | solution.py:467
  867.2 299.6 %all-reduce.27.cloned.1.call-start = ((), (), s32[]{:S(2)}) async-start(), calls=%async_computation.12 | async-start | bytes 12582912 | tf_op jit(solution)/shard_map/psum | solution.py:467
  887.5 47.1 %copy-start.96 = (bf16[1024,4]{0,1:T(4,128)(2,1)}, bf16[1024,4]{0,1:T(4,128)(2,1)S(1)}, u32[]{:S(2)}) copy-start(bf16[1024,4]{0,1:T(4,128)(2,1)S(1)} %select_reduce_fusion) | copy-start | bytes 24580
  887.5 47.1 %copy-start.5 = (f32[1024,768]{1,0:T(8,128)S(1)}, f32[1024,768]{1,0:T(8,128)}, u32[]{:S(2)}) copy-start(f32[1024,768]{1,0:T(8,128)} %copy-done.4) | copy-start | bytes 9437188
  1022.4 14.0 collective-permute-start.5
  1029.2 14.4 collective-permute-start.6
  1047.5 142.6 %reduce-scatter.5.cloned.1.call-start = ((), (), s32[]{:S(2)}) async-start(), calls=%async_computation.8 | async-start | bytes 2359296 | tf_op jit(solution)/shard_map/reduce_scatter | solution.py:513
  1061.5 130.1 %reduce-scatter.3.cloned.1.call-start = ((), (), s32[]{:S(2)}) async-start(), calls=%async_computation.7 | async-start | bytes 4718592 | tf_op jit(solution)/shard_map/reduce_scatter | solution.py:512
  1102.6 307.7 %all-reduce.25.cloned.1.call-start = ((), (), s32[]{:S(2)}) async-start(), calls=%async_computation.11 | async-start | bytes 14286848
  1206.0 211.5 %copy-start.78 = (f32[24576]{0:T(1024)S(1)}, f32[24576]{0:T(1024)}, u32[]{:S(2)}) copy-start(f32[24576]{0:T(1024)} %reshape.1362) | copy-start | bytes 294916
  1206.0 211.5 %copy-start.91 = (f32[6144]{0:T(1024)S(1)}, f32[6144]{0:T(1024)}, u32[]{:S(2)}) copy-start(f32[6144]{0:T(1024)} %reshape.1361) | copy-start | bytes 73732
  1412.5 49.7 %copy-start.41 = (f32[96,2,512]{2,1,0:T(2,128)}, f32[96,2,512]{2,1,0:T(2,128)S(1)}, u32[]{:S(2)}) copy-start(f32[96,2,512]{2,1,0:T(2,128)S(1)} %reshape.1356) | copy-start | bytes 1179652
  1414.4 59.8 %copy-start.37 = (f32[512,96]{1,0:T(8,128)}, f32[512,96]{1,0:T(8,128)S(1)}, u32[]{:S(2)}) copy-start(f32[512,96]{1,0:T(8,128)S(1)} %reshape.1357) | copy-start | bytes 589828
  1470.0 60.6 %copy-start.12 = (f32[1,384,2,512]{3,1,2,0:T(8,128)S(1)}, f32[1,384,2,512]{3,1,2,0:T(8,128)}, u32[]{:S(2)}) copy-start(f32[1,384,2,512]{3,1,2,0:T(8,128)} %reduce-scatter.3.cloned.1.call-done) | copy-start | bytes 4718596
  1475.0 84.1 %copy-start.24 = (f32[1,384,2,512]{3,2,1,0:T(2,128)S(1)}, f32[1,384,2,512]{3,2,1,0:T(2,128)}, u32[]{:S(2)}) copy-start(f32[1,384,2,512]{3,2,1,0:T(2,128)} %param.34) | copy-start | bytes 4718596
  (124 other events, 1057.9 us)
Sparse Core Ops, SparseCore 0:
  16.2 78.8 all-reduce.22
  97.9 86.3 all-gather.7
  203.0 67.6 all-reduce.18
  867.4 67.1 all-reduce.20
  1047.6 119.1 all-reduce.26
  1173.2 237.1 all-reduce.24
Sparse Core Ops, SparseCore 1:
  475.3 29.9 all-gather.5
  1061.6 25.4 reduce-scatter.4
  1102.7 42.7 reduce-scatter.2

commit v6 on v5

--- a/solution.py
+++ b/solution.py
@@ -180,6 +180,87 @@
     return results
 
 
+def halving_kernel(x_ref, o_ref, stage_one, stage_two, inbox_one, inbox_two, inbox_three, sems):
+    rows = o_ref.shape[0]
+    chunk = 64
+    fsdp_here = lax.axis_index("fsdp")
+    ctx_here = lax.axis_index("ctx")
+    tp_here = lax.axis_index("tp")
+    bit_low = fsdp_here % 2
+    bit_high = (fsdp_here // 2) % 2
+    partners = [
+        (fsdp_here, 1 - ctx_here, tp_here),
+        (fsdp_here + 1 - 2 * bit_low, ctx_here, tp_here),
+        (fsdp_here + 2 - 4 * bit_high, ctx_here, tp_here),
+    ]
+    barrier = pltpu.get_barrier_semaphore()
+    for partner in partners:
+        pl.semaphore_signal(barrier, 1, device_id=partner, device_id_type=pl.DeviceIdType.MESH)
+    pl.semaphore_wait(barrier, len(partners))
+
+    def swap(src, dst, number, partner):
+        copy = pltpu.make_async_remote_copy(
+            src_ref=src,
+            dst_ref=dst,
+            send_sem=sems.at[0, number],
+            recv_sem=sems.at[1, number],
+            device_id=partner,
+            device_id_type=pl.DeviceIdType.MESH,
+        )
+        copy.start()
+        copy.wait()
+
+    swap(x_ref.at[:, pl.ds(1 - ctx_here, 1)], inbox_one, 0, partners[0])
+
+    @pl.loop(0, rows // chunk)
+    def _(step):
+        part = pl.ds(pl.multiple_of(step * chunk, chunk), chunk)
+        for high in range(2):
+            for low in range(2):
+                stage_one[high, low, part] = (
+                    x_ref[2 * high + low, ctx_here, part] + inbox_one[2 * high + low, 0, part]
+                )
+
+    swap(stage_one.at[:, pl.ds(1 - bit_low, 1)], inbox_two, 1, partners[1])
+
+    @pl.loop(0, rows // chunk)
+    def _(step):
+        part = pl.ds(pl.multiple_of(step * chunk, chunk), chunk)
+        for high in range(2):
+            stage_two[high, part] = stage_one[high, bit_low, part] + inbox_two[high, 0, part]
+
+    swap(stage_two.at[pl.ds(1 - bit_high, 1)], inbox_three, 2, partners[2])
+
+    @pl.loop(0, rows // chunk)
+    def _(step):
+        part = pl.ds(pl.multiple_of(step * chunk, chunk), chunk)
+        o_ref[part] = stage_two[bit_high, part] + inbox_three[0, part]
+
+
+def halving_scatter(packed, collective_id):
+    count, width = packed.shape
+    rows = -(-width // (128 * 64)) * 64
+    block = jnp.pad(packed, ((0, 0), (0, rows * 128 - width))).reshape(count // 2, 2, rows, 128)
+    own = pl.pallas_call(
+        halving_kernel,
+        out_shape=jax.ShapeDtypeStruct((rows, 128), jnp.float32),
+        in_specs=[pl.BlockSpec(memory_space=pltpu.VMEM)],
+        out_specs=pl.BlockSpec(memory_space=pltpu.VMEM),
+        scratch_shapes=[
+            pltpu.VMEM((2, 2, rows, 128), jnp.float32),
+            pltpu.VMEM((2, rows, 128), jnp.float32),
+            pltpu.VMEM((count // 2, 1, rows, 128), jnp.float32),
+            pltpu.VMEM((2, 1, rows, 128), jnp.float32),
+            pltpu.VMEM((1, rows, 128), jnp.float32),
+            pltpu.SemaphoreType.DMA((2, 3)),
+        ],
+        compiler_params=pltpu.CompilerParams(
+            collective_id=collective_id, has_side_effects=True, vmem_limit_bytes=60 * 1024 * 1024
+        ),
+    )(block)
+    return own.reshape(-1)[:width]
+
+
 def swiglu_experts(gate_up):
     return jax.nn.silu(gate_up[:, :, 0]) * gate_up[:, :, 1]
 
@@ -201,7 +282,7 @@
     return results
 
 
-def scatter_packed(pieces, axes, count):
+def scatter_packed(pieces, axes, count, use_kernel=False):
     columns = []
     local_shapes = []
     for grad, dim in pieces:
@@ -211,10 +292,13 @@
         part = jnp.moveaxis(grad.reshape(split), dim, 0)
         columns.append(part.reshape(count, -1))
     packed = jnp.concatenate(columns, axis=1)
-    width = packed.shape[1]
-    rows = -(-width // 1024) * 8
-    packed = jnp.pad(packed, ((0, 0), (0, rows * 128 - width))).reshape(count * rows, 128)
-    own = lax.psum_scatter(packed, axes, scatter_dimension=0, tiled=True).reshape(-1)
+    if use_kernel:
+        own = halving_scatter(packed, 3)
+    else:
+        width = packed.shape[1]
+        rows = -(-width // 1024) * 8
+        packed = jnp.pad(packed, ((0, 0), (0, rows * 128 - width))).reshape(count * rows, 128)
+        own = lax.psum_scatter(packed, axes, scatter_dimension=0, tiled=True).reshape(-1)
     results = []
     offset = 0
     for local_shape in local_shapes:
@@ -513,11 +597,6 @@
         own_expert_down = lax.psum_scatter(
             grad_expert_down[None], "ctx", scatter_dimension=2, tiled=True
         )
-    first_own = scatter_packed(first_grads, ("fsdp", "ctx"), shard_count)
-    own_attn_out, own_router, own_shared_in, own_shared_down, own_gain_two = first_own[:5]
-    if dense_experts:
-        own_expert_in = first_own[5][None]
-        own_expert_down = first_own[6][None]
     grad_heads = (
         jnp.einsum("td,cd->tc", grad_attn_low, attn_out_low, preferred_element_type=jnp.float32)
         .astype(jnp.bfloat16)
@@ -595,9 +674,18 @@
     )
     grad_residual, grad_gain_one = norm_one_back(lax.psum(partial_one, "tp"))
     input_grad = grad_after + grad_residual
-    own_attn_in, own_gain_one = scatter_packed(
-        [(grad_attn_in, 0), (grad_gain_one, 0)], ("fsdp", "ctx"), shard_count
-    )
+    halving = lax.axis_size("fsdp") == 4 and ctx_count == 2
+    all_own = scatter_packed(
+        first_grads + [(grad_attn_in, 0), (grad_gain_one, 0)],
+        ("fsdp", "ctx"),
+        shard_count,
+        halving,
+    )
+    own_attn_out, own_router, own_shared_in, own_shared_down, own_gain_two = all_own[:5]
+    own_attn_in, own_gain_one = all_own[-2:]
+    if dense_experts:
+        own_expert_in = all_own[5][None]
+        own_expert_down = all_own[6][None]
     own_gains = jnp.stack([own_gain_one, own_gain_two])
     lead_tp = (tp_index == 0).astype(jnp.float32)
     first_shard = (shard_index == 0).astype(jnp.float32)

time: 1610 us -> 1560 us (0.969)
  waiting for transfers between devices: 550 us -> 311 us
  Pallas kernels: 44.6 us -> 212 us
  other arithmetic: 214 us -> 244 us
    unnamed x11 -> x9, waiting for transfers between devices: 268 us -> 64.3 us
    pallas_call x0 -> x1, Pallas kernels: none -> 167 us  [halving_scatter(): pl.pallas_call(halving_kernel, out_shape=jax.ShapeDtypeStruct((rows, 128)...]
    all_to_all x1, waiting for transfers between devices: 122 us -> 44 us  [experts_routed(): lax.all_to_all(rows, 'fsdp', split_axis=0, concat_axis=0, tiled=True)]
    psum x2, waiting for transfers between devices: 62.5 us -> 123 us  [local(): lax.psum((shared_out + combined, partial_two, gate_dots), 'tp')]
    reduce_sum x1, other arithmetic: 11.4 us -> 31.2 us  [experts_routed(): combined = jnp.sum(gate_probs[:, :, None] * route_out, axis=1)]
    unnamed x271 -> x297, local copies, waits for them, and re-layouts: 57 us -> 71.7 us
  transfers between devices with their start and end apart: 17 -> 16, of which waited for: 11 -> 10; matrix products, arithmetic and copies ran while one was open for 17% -> 19% of each run, Pallas kernels for 0% -> 0%
where the time goes in v6:
time: 1560 us; the launch traced here: 1540 us
  local copies, waits for them, and re-layouts  366 us (23%)
  waiting for transfers between devices  311 us (20%)
  other arithmetic  244 us (16%)
  Pallas kernels  212 us (14%)
  matrix products  176 us (11%)
  blocking collectives  165 us (11%)
  between operations  43 us (3%)
  starting transfers between devices  18 us (1%)
    pallas_call x1, Pallas kernels, halving_scatter(): pl.pallas_call(halving_kernel, out_shape=jax.ShapeDtypeStruct((rows, 128)...  167 us
    all_to_all x1, blocking collectives, experts_routed(): lax.all_to_all(rows, 'fsdp', split_axis=0, concat_axis=0, tiled=True)  143 us
    psum x2, waiting for transfers between devices, local(): lax.psum((shared_out + combined, partial_two, gate_dots), 'tp')  123 us
    unnamed x297, local copies, waits for them, and re-layouts  71.7 us
    unnamed x9, waiting for transfers between devices  64.3 us
    psum x1, waiting for transfers between devices, local(): lax.psum(jnp.dot(mixed_heads, attn_out_low, preferred_element_type=jnp.fl...  46.9 us
    pallas_call x2, Pallas kernels, butterfly_sum(): pl.pallas_call(butterfly_kernel, out_shape=jax.ShapeDtypeStruct((rows, 12...  45.1 us
    all_to_all x1, waiting for transfers between devices, experts_routed(): lax.all_to_all(rows, 'fsdp', split_axis=0, concat_axis=0, tiled=True)  44 us
  transfers between devices with their start and end apart: 16, of which 10 were waited for; matrix products, arithmetic and copies ran while one was open for 19% of the time, Pallas kernels for 0%

profile of v6, /device:TPU:0, one launch (start us, length us, event | category | flops | bytes accessed | tf_op | source)
XLA Modules:
  0.0 1543.1 jit_solution(18039616421557669607)
XLA Ops:
  31.0 64.2 %all-reduce.18.cloned.1.call-done = bf16[443904]{0:T(1024)(128)(2,1)} async-done(((bf16[443904]{0:T(1024)(128)(2,1)}), bf16[443904]{0:T(1024)(128)(2,1)}) %all-reduce.18.cloned.1.call-update) | async-done | bytes 887824
  135.4 15.3 collective-permute-done
  150.8 39.3 %while.39 = (s32[]{:T(128)}, bf16[2,512,3,64]{1,3,2,0:T(8,128)(2,1)}, f32[2,3,512,1]{2,1,3,0:T(4,128)}, s32[2]{0:T(128)}, bf16[2048,3,64]{0,2,1:T(8,128)(2,1)S(1...) while((s32[]{:T(128)}, ...), condition=%wide.region_4.5_spmd, body=%wide.region_1.4_spmd.sunk | while | flops 644092928 | bytes 33331516 | solution.py:502
  223.6 46.9 %all-reduce.14.cloned.1.call-done = f32[1024,768]{1,0:T(8,128)} async-done(((f32[1024,768]{1,0:T(8,128)}), f32[1024,768]{1,0:T(8,128)}) %all-reduce.14.cloned.1.call-update) | async-done | bytes 3145744 | tf_op jit(solution)/shard_map/psum | solution.py:504
  276.4 17.8 %gather_fusion = bf16[4096,768]{1,0:T(8,128)(2,1)} fusion(bf16[1024,768]{1,0:T(8,128)(2,1)S(1)} %multiply_convert_fusion.4, s32[4096]{0:T(1024)S(1)} %get-tuple-element.935), kind=kCustom, calls=%fused_computation | custom fusion | bytes 12599296 | tf_op jit(solution)/shard_map/gather | solution.py:351
  299.0 21.5 %gather_fusion.1 = bf16[4096,768]{1,0:T(8,128)(2,1)} fusion(bf16[2048,768]{1,0:T(8,128)(2,1)} %multiply_convert_fusion.2, s32[4096]{0:T(1024)S(1)} %get-tuple-element.934), kind=kCustom, calls=%fused_computation.1 | custom fusion | bytes 12599296 | tf_op jit(solution)/shard_map/gather | solution.py:351
  331.3 142.6 %all_to_all.10 = bf16[4,512,1536]{2,1,0:T(8,128)(2,1)} all-to-all(bf16[4,512,1536]{2,1,0:T(8,128)(2,1)S(1)} %fusion.57), channel_id=1, replica_groups=mesh['fsdp'=4,'ctx'=2,'tp'=4] {'fsdp'}, dimensions={0} | all-to-all | bytes 12582912 | tf_op jit(solution)/shard_map/all_to_all | solution.py:353
  475.9 16.6 %all_gather.23 = bf16[1,512,768]{2,1,0:T(8,128)(2,1)S(1)} all-gather(bf16[1,512,384]{2,1,0:T(8,128)(2,1)S(1)} %get-tuple-element.898), channel_id=1, replica_groups=mesh['fsdp'=4,'ctx'=2,'tp'=4] {'ctx'}, dimensions={2}, use_global_device_ids=true | all-gather | bytes 1179648 | tf_op jit(solution)/shard_map/all_gather | solution.py:455
  492.4 10.4 pad_maximum_fusion.1
  505.1 12.4 fusion.63
  517.6 14.4 multiply_bitcast_fusion
  539.9 15.3 convolution_bitcast_fusion
  555.3 14.6 pad_maximum_fusion
  569.9 30.0 %reshape.1334 = f32[4,1024,1536]{1,0,2:T(4,128)} reshape(f32[4096,1536]{0,1:T(8,128)} %pad_maximum_fusion) | data formatting | bytes 50331648 | tf_op jit(solution)/shard_map/reshape | solution.py:379
  599.9 18.3 %fusion.189 = (f32[4,512,1536]{1,0,2:T(4,128)}, f32[4,512,1536]{1,0,2:T(4,128)}) fusion(f32[4,1024,1536]{1,0,2:T(4,128)} %reshape.1334), kind=kLoop, calls=%fused_computation.416 | loop fusion | bytes 50331648 | tf_op jit(solution)/shard_map/slice | solution.py:382
  618.2 13.1 copy.261
  631.4 12.7 fusion.109
  650.9 14.0 fusion.49
  670.1 13.6 fusion.90
  764.8 44.0 %all-to-all-done.1 = bf16[4,512,1536]{1,2,0:T(8,128)(2,1)} async-done(((bf16[4,512,1536]{1,2,0:T(8,128)(2,1)}), bf16[4,512,1536]{1,2,0:T(8,128)(2,1)}, u32[]{:S(2)}, u32[]{:S(2)}) %all-to-all-start.1) | async-done | bytes 6291488 | tf_op jit(solution)/shard_map/all_to_all | solution.py:353
  817.5 16.9 %gather_fusion.2 = bf16[2048,1536]{1,0:T(8,128)(2,1)} fusion(bf16[2048,1536]{1,0:T(8,128)(2,1)} %bitcast.435, s32[2048]{0:T(1024)S(1)} %copy-done.112), kind=kCustom, calls=%fused_computation.2 | custom fusion | bytes 12591104 | tf_op jit(solution)/shard_map/gather | solution.py:388
  860.3 12.0 reduce_sum.549
  889.7 31.2 %multiply_reduce_fusion.2 = f32[1024,768]{1,0:T(8,128)S(1)} fusion(f32[1024,2,768]{2,1,0:T(2,128)} %reshape.1336, f32[1024,2]{1,0:T(8,128)S(1)} %copy-done.30), kind=kLoop, calls=%fused_computation.96 | loop fusion | flops 2359296 | bytes 9445376 | tf_op jit(solution)/shard_map/reduce_sum | solution.py:391
  923.6 22.7 %all-reduce.16.cloned.1.call-done = f32[1024,768]{1,0:T(8,128)} async-done(((f32[1024,768]{1,0:T(8,128)}), f32[1024,768]{1,0:T(8,128)}) %all-reduce.16.cloned.1.call-update) | async-done | bytes 3145744 | tf_op jit(solution)/shard_map/psum | solution.py:551
  956.1 77.1 %while.40 = (s32[]{:T(128)}, f32[2048,3,64]{0,2,1:T(8,128)}, f32[2048,3,64]{0,2,1:T(8,128)S(1)}, f32[1024,3,64]{0,2,1:T(8,128)}, bf16[1024,3,64]{0,2,1:T(8,128)(...) while((s32[]{:T(128)}, f32[2048,3,64]{0,2,1:T(8,128)}, ...), condition=%wide.region_26.27_spmd, body=%wide.region_24.26_spmd.sunk | while | flops 1541608448 | bytes 106823088 | solution.py:653
  973.5 9.4 multiply_convert_fusion.7
  1003.0 8.9 multiply_reduce_fusion.22
  1011.9 9.4 multiply_convert_fusion.7
  1078.7 100.6 %all-reduce.20.cloned.1.call-done = (f32[1024,768]{1,0:T(8,128)}, f32[1024,768]{1,0:T(8,128)}) async-done(((f32[1024,768]{1,0:T(8,128)}, f32[1024,768]{1,0:T(8,128)}), (f32[1024,768]{1,0:T(8,128)}, f32[1024,768]{1,0:T(8,128)})) %all-reduce.20.cloned.1.call-update) | async-done | bytes 6291472 | tf_op jit(solution)/shard_map/psum | solution.py:551
  1192.2 166.8 %shard_map.395 = f32[1792,128]{1,0:T(8,128)} custom-call(f32[4,2,1792,128]{3,2,1,0:T(8,128)} %bitcast.436), custom_call_target="tpu_custom_call" | custom-call | tf_op jit(solution)/shard_map/pallas_call | solution.py:244
  1370.6 29.5 %shard_map.396 = f32[344,128]{1,0:T(8,128)} custom-call(f32[344,128]{1,0:T(8,128)} %pad_bitcast_fusion.1.x_ref), custom_call_target="tpu_custom_call" | custom-call | tf_op jit(solution)/shard_map/pallas_call | solution.py:162
  1485.9 15.6 %shard_map.397 = f32[8,128]{1,0:T(8,128)} custom-call(f32[8,128]{1,0:T(8,128)} %pad_bitcast_fusion.2.x_ref), custom_call_target="tpu_custom_call" | custom-call | tf_op jit(solution)/shard_map/pallas_call | solution.py:162
  (666 shorter events, 530.9 us)
Async XLA Ops:
  8.1 87.1 %all-reduce.18.cloned.1.call-start = ((), (), s32[]{:S(2)}) async-start(), calls=%async_computation.9 | async-start | bytes 1777664
  16.0 177.4 %all-gather.8.cloned.1.call-start = ((), (), s32[]{:S(2)}) async-start(), calls=%async_computation.10 | async-start | bytes 5985792 | tf_op jit(solution)/shard_map/all_gather | solution.py:270
  16.1 118.3 %collective-permute-start.1 = (bf16[1024]{0:T(1024)(128)(2,1)S(1)}, bf16[1024]{0:T(1024)(128)(2,1)S(1)}, u32[]{:S(2)}, u32[]{:S(2)}) collective-permute-start(bf16[1024]{0:T(1024)(128)(2,1)S(1)} %convert_reduce_fusion), channel_id=1, source_target_pairs={{0,4},{1,5},{2,6},{3,7},{8,12},{9,13},{10,14},{11,15},{16,20},{17,... | collective-permute-start | bytes 6152 | tf_op jit(solution)/shard_map/ppermute | solution.py:27
  29.3 241.3 %all-reduce.14.cloned.1.call-start = ((), (), s32[]{:S(2)}) async-start(), calls=%async_computation.4 | async-start | bytes 6291456 | tf_op jit(solution)/shard_map/psum | solution.py:504
  29.7 73.3 %copy-start.106 = (f32[1024]{0:T(1024)}, f32[1024]{0:T(1024)S(1)}, u32[]{:S(2)}) copy-start(f32[1024]{0:T(1024)S(1)} %fusion.76) | copy-start | bytes 12292
  29.7 75.9 %copy-start.101 = (f32[1024]{0:T(1024)}, f32[1024]{0:T(1024)S(1)}, u32[]{:S(2)}) copy-start(f32[1024]{0:T(1024)S(1)} %fusion.170) | copy-start | bytes 12292
  31.0 76.1 %copy-start.61 = (f32[1024,32]{0,1:T(8,128)}, f32[1024,32]{0,1:T(8,128)S(1)}, u32[]{:S(2)}) copy-start(f32[1024,32]{0,1:T(8,128)S(1)} %get-tuple-element.942) | copy-start | bytes 393220
  108.5 25.8 %collective-permute-start.2 = (bf16[1024,3,64]{0,2,1:T(8,128)(2,1)}, bf16[1024,3,64]{0,2,1:T(8,128)(2,1)}, u32[]{:S(2)}, u32[]{:S(2)}) collective-permute-start(bf16[1024,3,64]{0,2,1:T(8,128)(2,1)} %pad_maximum_fusion.5), channel_id=1, source_target_pairs={{0,4},{1,5},{2,6},{3,7},{8,12},{9,13},{10,14},{11,15},{16,20},{17,... | collective-permute-start | bytes 1179656 | tf_op jit(solution)/shard_map/ppermute | solution.py:27
  133.0 17.7 %collective-permute-start = (bf16[1024,3,64]{0,2,1:T(8,128)(2,1)S(1)}, bf16[1024,3,64]{0,2,1:T(8,128)(2,1)S(1)}, u32[]{:S(2)}, u32[]{:S(2)}) collective-permute-start(bf16[1024,3,64]{0,2,1:T(8,128)(2,1)S(1)} %bitcast.471), channel_id=1, source_target_pairs={{0,4},{1,5},{2,6},{3,7},{8,12},{9,13},{10,14},{11,15},{16,20},{17,... | collective-permute-start | bytes 1179656 | tf_op jit(solution)/shard_map/ppermute | solution.py:27
  202.7 302.4 %all-gather.6.cloned.1.call-start = ((), (), s32[]{:S(2)}) async-start(), calls=%async_computation.5 | async-start | bytes 2359296 | tf_op jit(solution)/shard_map/all_gather | solution.py:454
  205.1 67.9 %copy-start.89 = (s32[2048]{0:T(1024)}, s32[2048]{0:T(1024)S(1)}, u32[]{:S(2)}) copy-start(s32[2048]{0:T(1024)S(1)} %fusion.143) | copy-start | bytes 24580
  222.5 51.1 %copy-start.91 = (f32[768]{0:T(1024)}, f32[768]{0:T(1024)S(1)}, u32[]{:S(2)}) copy-start(f32[768]{0:T(1024)S(1)} %reshape.1363) | copy-start | bytes 9220
  223.6 50.3 %copy-start.51 = (bf16[768,4]{1,0:T(8,128)(2,1)}, bf16[768,4]{1,0:T(8,128)(2,1)S(1)}, u32[]{:S(2)}) copy-start(bf16[768,4]{1,0:T(8,128)(2,1)S(1)} %reshape_reshape.22) | copy-start | bytes 18436
  331.3 142.6 %copy-start.19 = (f32[1,384,2,512]{3,2,1,0:T(2,128)S(1)}, f32[1,384,2,512]{3,2,1,0:T(2,128)}, u32[]{:S(2)}) copy-start(f32[1,384,2,512]{3,2,1,0:T(2,128)} %param.34) | copy-start | bytes 4718596
  473.9 18.6 %collective-permute-start.3 = (bf16[4,512,1536]{2,1,0:T(8,128)(2,1)}, bf16[4,512,1536]{2,1,0:T(8,128)(2,1)}, u32[]{:S(2)}, u32[]{:S(2)}) collective-permute-start(bf16[4,512,1536]{2,1,0:T(8,128)(2,1)} %all_to_all.10), channel_id=1, source_target_pairs={{0,1},{1,0},{2,3},{3,2},{4,5},{5,4},{6,7},{7,6},{8,9},{9,8},{10,11... | collective-permute-start | bytes 18874376 | tf_op jit(solution)/shard_map/ppermute | solution.py:355
  475.0 281.6 %reduce-scatter.5.cloned.1.call-start = ((), (), s32[]{:S(2)}) async-start(), calls=%async_computation.8 | async-start | bytes 2359296 | tf_op jit(solution)/shard_map/reduce_scatter | solution.py:597
  631.4 19.5 %collective-permute-start.4 = (f32[4,512,1536]{1,2,0:T(8,128)}, f32[4,512,1536]{1,2,0:T(8,128)}, u32[]{:S(2)}, u32[]{:S(2)}) collective-permute-start(f32[4,512,1536]{1,2,0:T(8,128)} %copy.261), channel_id=1, source_target_pairs={{0,1},{1,0},{2,3},{3,2},{4,5},{5,4},{6,7},{7,6},{8,9},{9,8},{10,11... | collective-permute-start | bytes 37748744 | tf_op jit(solution)/shard_map/ppermute | solution.py:355
  664.8 144.0 %all-to-all-start.1 = ((bf16[4,512,1536]{1,2,0:T(8,128)(2,1)}), bf16[4,512,1536]{1,2,0:T(8,128)(2,1)}, u32[]{:S(2)}, u32[]{:S(2)}) async-start(bf16[4,512,1536]{1,2,0:T(8,128)(2,1)} %fusion.49), calls=%async_computation.1 | async-start | bytes 12582912 | tf_op jit(solution)/shard_map/all_to_all | solution.py:353
  670.1 87.9 %reduce-scatter.3.cloned.1.call-start = ((), (), s32[]{:S(2)}) async-start(), calls=%async_computation.7 | async-start | bytes 4718592 | tf_op jit(solution)/shard_map/reduce_scatter | solution.py:596
  683.8 262.5 %all-reduce.16.cloned.1.call-start = ((), (), s32[]{:S(2)}) async-start(), calls=%async_computation.6 | async-start | bytes 6291456 | tf_op jit(solution)/shard_map/psum | solution.py:551
  764.8 52.6 %copy-start.112 = (s32[2048]{0:T(1024)S(1)}, s32[2048]{0:T(1024)}, u32[]{:S(2)}) copy-start(s32[2048]{0:T(1024)} %broadcast_clamp_fusion) | copy-start | bytes 24580
  879.1 300.1 %all-reduce.20.cloned.1.call-start = ((), (), s32[]{:S(2)}) async-start(), calls=%async_computation.11 | async-start | bytes 12582912 | tf_op jit(solution)/shard_map/psum | solution.py:551
  889.7 31.2 %copy-start.35 = (bf16[1024,1,512]{2,0,1:T(8,128)(2,1)S(1)}, bf16[1024,1,512]{2,0,1:T(8,128)(2,1)}, u32[]{:S(2)}) copy-start(bf16[1024,1,512]{2,0,1:T(8,128)(2,1)} %copy-done.34) | copy-start | bytes 3145732
  889.7 31.2 %copy-start.48 = (bf16[512,8,96]{0,2,1:T(8,128)(2,1)S(1)}, bf16[512,8,96]{0,2,1:T(8,128)(2,1)}, u32[]{:S(2)}) copy-start(bf16[512,8,96]{0,2,1:T(8,128)(2,1)} %copy.215) | copy-start | bytes 2359300
  1034.5 14.0 collective-permute-start.5
  1036.6 19.1 %collective-permute-start.6 = (bf16[1024,3,64]{0,2,1:T(8,128)(2,1)}, bf16[1024,3,64]{0,2,1:T(8,128)(2,1)}, u32[]{:S(2)}, u32[]{:S(2)}) collective-permute-start(bf16[1024,3,64]{0,2,1:T(8,128)(2,1)} %slice.662), channel_id=1, source_target_pairs={{4,0},{5,1},{6,2},{7,3},{12,8},{13,9},{14,10},{15,11},{20,16},{21,... | collective-permute-start | bytes 1179656 | tf_op jit(solution)/shard_map/ppermute | solution.py:27
  1362.2 45.9 %copy-start.37 = (f32[96,2,512]{2,1,0:T(2,128)}, f32[96,2,512]{2,1,0:T(2,128)S(1)}, u32[]{:S(2)}) copy-start(f32[96,2,512]{2,1,0:T(2,128)S(1)} %reshape.1347) | copy-start | bytes 1179652
  1363.1 58.3 %copy-start.32 = (f32[512,96]{1,0:T(8,128)}, f32[512,96]{1,0:T(8,128)S(1)}, u32[]{:S(2)}) copy-start(f32[512,96]{1,0:T(8,128)S(1)} %reshape.1348) | copy-start | bytes 589828
  1365.5 42.6 %copy-start.66 = (f32[192,96]{1,0:T(8,128)}, f32[192,96]{1,0:T(8,128)S(1)}, u32[]{:S(2)}) copy-start(f32[192,96]{1,0:T(8,128)S(1)} %reshape.1346) | copy-start | bytes 221188
  1415.9 60.4 %copy-start.11 = (f32[1,384,2,512]{3,1,2,0:T(8,128)S(1)}, f32[1,384,2,512]{3,1,2,0:T(8,128)}, u32[]{:S(2)}) copy-start(f32[1,384,2,512]{3,1,2,0:T(8,128)} %reduce-scatter.3.cloned.1.call-done) | copy-start | bytes 4718596
  1418.2 99.9 %copy-start.97 = (f32[3,192]{1,0:T(4,128)}, f32[3,192]{1,0:T(4,128)S(1)}, u32[]{:S(2)}) copy-start(f32[3,192]{1,0:T(4,128)S(1)} %fusion.166) | copy-start | bytes 6916
  1422.2 83.2 %copy-start.21 = (f32[1,384,2,512]{3,2,1,0:T(2,128)S(1)}, f32[1,384,2,512]{3,2,1,0:T(2,128)}, u32[]{:S(2)}) copy-start(f32[1,384,2,512]{3,2,1,0:T(2,128)} %param.34) | copy-start | bytes 4718596
  (135 other events, 982.8 us)
Sparse Core Ops, SparseCore 0:
  16.1 79.0 all-reduce.17
  97.9 86.3 all-gather.7
  202.8 67.6 all-reduce.13
  879.2 67.0 all-reduce.15
  1060.0 119.1 all-reduce.19
Sparse Core Ops, SparseCore 1:
  475.1 30.0 all-gather.5
  644.2 24.9 reduce-scatter.4
  683.9 44.0 reduce-scatter.2

commit v7 on v6

--- a/solution.py
+++ b/solution.py
@@ -261,13 +261,79 @@
     return own.reshape(-1)[:width]
 
 
+def gather_kernel(x_ref, o_ref, inbox, send_sems, recv_sems):
+    fsdp_here = lax.axis_index("fsdp")
+    ctx_here = lax.axis_index("ctx")
+    tp_here = lax.axis_index("tp")
+    ctx_count = lax.axis_size("ctx")
+    count = lax.axis_size("fsdp") * ctx_count
+    me = fsdp_here * ctx_count + ctx_here
+    peers = []
+    for offset in range(1, count):
+        other = (me + offset) % count
+        peers.append((other // ctx_count, other % ctx_count, tp_here))
+    barrier = pltpu.get_barrier_semaphore()
+    for peer in peers:
+        pl.semaphore_signal(barrier, 1, device_id=peer, device_id_type=pl.DeviceIdType.MESH)
+    pl.semaphore_wait(barrier, len(peers))
+    copies = []
+    for number, peer in enumerate(peers):
+        copy = pltpu.make_async_remote_copy(
+            src_ref=x_ref,
+            dst_ref=inbox.at[me],
+            send_sem=send_sems.at[number],
+            recv_sem=recv_sems.at[me],
+            device_id=peer,
+            device_id_type=pl.DeviceIdType.MESH,
+        )
+        copy.start()
+        copies.append(copy)
+    o_ref[me] = x_ref[...]
+    for copy in copies:
+        copy.wait_send()
+    for offset in range(1, count):
+        source = (me + count - offset) % count
+        pltpu.make_async_remote_copy(
+            src_ref=x_ref,
+            dst_ref=inbox.at[source],
+            send_sem=send_sems.at[0],
+            recv_sem=recv_sems.at[source],
+            device_id=peers[0],
+            device_id_type=pl.DeviceIdType.MESH,
+        ).wait_recv()
+        o_ref[source] = inbox[source]
+
+
+def gather_shards(flat, collective_id):
+    size = flat.shape[0]
+    rows = -(-size // 2048) * 16
+    block = jnp.pad(flat, (0, rows * 128 - size)).reshape(rows, 128)
+    count = lax.axis_size("fsdp") * lax.axis_size("ctx")
+    full = pl.pallas_call(
+        gather_kernel,
+        out_shape=jax.ShapeDtypeStruct((count, rows, 128), flat.dtype),
+        in_specs=[pl.BlockSpec(memory_space=pltpu.VMEM)],
+        out_specs=pl.BlockSpec(memory_space=pltpu.VMEM),
+        scratch_shapes=[
+            pltpu.VMEM((count, rows, 128), flat.dtype),
+            pltpu.SemaphoreType.DMA((count - 1,)),
+            pltpu.SemaphoreType.DMA((count,)),
+        ],
+        compiler_params=pltpu.CompilerParams(collective_id=collective_id, has_side_effects=True),
+    )(block)
+    return full.reshape(count, rows * 128)[:, :size]
+
+
 def swiglu_experts(gate_up):
     return jax.nn.silu(gate_up[:, :, 0]) * gate_up[:, :, 1]
 
 
-def gather_packed(pieces, axes):
+def gather_packed(pieces, axes, use_kernel=False):
     flat = jnp.concatenate([piece.reshape(-1) for piece, _ in pieces])
-    full = lax.all_gather(flat, axes, axis=0, tiled=False)
+    if use_kernel:
+        full = gather_shards(flat, 4)
+    else:
+        full = lax.all_gather(flat, axes, axis=0, tiled=False)
     count = full.shape[0]
     results = []
     offset = 0
@@ -429,7 +495,7 @@
     base_pos = ctx_index * block_len
     low = lambda v: v.astype(jnp.bfloat16)
     gain_low, attn_in_low = gather_packed(
-        [(low(gains), 1), (low(attention_in), 0)], ("fsdp", "ctx")
+        [(low(gains), 1), (low(attention_in), 0)], ("fsdp", "ctx"), shard_count <= 8
     )
     later = [
         (low(attention_out), 1),
@@ -672,21 +738,21 @@
     partial_one = jnp.einsum(
         "tgf,dgf->td", grad_projected, attn_in_low, preferred_element_type=jnp.float32
     )
-    grad_residual, grad_gain_one = norm_one_back(lax.psum(partial_one, "tp"))
-    input_grad = grad_after + grad_residual
+    tp_one = lax.psum(partial_one, "tp")
     halving = lax.axis_size("fsdp") == 4 and ctx_count == 2
     all_own = scatter_packed(
-        first_grads + [(grad_attn_in, 0), (grad_gain_one, 0)],
+        first_grads + [(grad_attn_in, 0)],
         ("fsdp", "ctx"),
         shard_count,
         halving,
     )
     own_attn_out, own_router, own_shared_in, own_shared_down, own_gain_two = all_own[:5]
-    own_attn_in, own_gain_one = all_own[-2:]
+    own_attn_in = all_own[-1]
+    grad_residual, grad_gain_one = norm_one_back(tp_one + 0.0 * own_attn_in[0, 0, 0])
+    input_grad = grad_after + grad_residual
     if dense_experts:
         own_expert_in = all_own[5][None]
         own_expert_down = all_own[6][None]
-    own_gains = jnp.stack([own_gain_one, own_gain_two])
     lead_tp = (tp_index == 0).astype(jnp.float32)
     first_shard = (shard_index == 0).astype(jnp.float32)
     first_ctx = (ctx_index == 0).astype(jnp.float32)
@@ -775,6 +841,7 @@
             expert_hidden_part,
             scalar_part,
             expert_old_part,
+            lead_tp * grad_gain_one,
         ],
         1,
     )
@@ -786,7 +853,10 @@
         expert_hidden_sum,
         scalar_sum,
         expert_old_sum,
+        gain_one_sum,
     ) = global_sums
+    own_gain_one = lax.dynamic_slice_in_dim(gain_one_sum, shard_index * d_local, d_local)
+    own_gains = jnp.stack([own_gain_one, own_gain_two])
     shard_start = shard_index * d_local
     gain_state = DECAY_RATE * model_stats[0:2] + (1.0 - DECAY_RATE) * (
         own_gains * own_gains + TINY_SQUARE

time: 1560 us -> 1420 us (0.910)
  waiting for transfers between devices: 311 us -> 153 us
  Pallas kernels: 212 us -> 231 us
    psum x2, waiting for transfers between devices: 123 us -> 22.7 us  [local(): lax.psum((shared_out + combined, partial_two, gate_dots), 'tp')]
    unnamed x9 -> x7, waiting for transfers between devices: 64.3 us -> 0.12 us
    all_gather x1, waiting for transfers between devices: 0.01 us -> 24.2 us  [gather_packed(): full = lax.all_gather(flat, axes, axis=0, tiled=False)]
    pallas_call x0 -> x1, Pallas kernels: none -> 22.7 us  [gather_shards(): pl.pallas_call(gather_kernel, out_shape=jax.ShapeDtypeStruct((count, rows...]
    unnamed x297 -> x310, local copies, waits for them, and re-layouts: 71.7 us -> 65.4 us
  transfers between devices with their start and end apart: 16 -> 15, of which waited for: 10 -> 8; matrix products, arithmetic and copies ran while one was open for 19% -> 22% of each run, Pallas kernels for 0% -> 12%
where the time goes in v7:
time: 1420 us; the launch traced here: 1410 us
  local copies, waits for them, and re-layouts  367 us (26%)
  other arithmetic  249 us (18%)
  Pallas kernels  231 us (16%)
  matrix products  176 us (12%)
  blocking collectives  165 us (12%)
  waiting for transfers between devices  153 us (11%)
  between operations  42.9 us (3%)
  starting transfers between devices  16.7 us (1%)
    pallas_call x1, Pallas kernels, halving_scatter(): pl.pallas_call(halving_kernel, out_shape=jax.ShapeDtypeStruct((rows, 128)...  165 us
    all_to_all x1, blocking collectives, experts_routed(): lax.all_to_all(rows, 'fsdp', split_axis=0, concat_axis=0, tiled=True)  143 us
    unnamed x310, local copies, waits for them, and re-layouts  65.4 us
    psum x1, waiting for transfers between devices, local(): lax.psum(jnp.dot(mixed_heads, attn_out_low, preferred_element_type=jnp.fl...  46.2 us
    pallas_call x2, Pallas kernels, butterfly_sum(): pl.pallas_call(butterfly_kernel, out_shape=jax.ShapeDtypeStruct((rows, 12...  43.6 us
    all_to_all x1, waiting for transfers between devices, experts_routed(): lax.all_to_all(rows, 'fsdp', split_axis=0, concat_axis=0, tiled=True)  42.5 us
    reduce_sum x1, other arithmetic, experts_routed(): combined = jnp.sum(gate_probs[:, :, None] * route_out, axis=1)  31.2 us
    reshape x1, local copies, waits for them, and re-layouts, experts_routed(): jnp.concatenate([outs, grad_expert_rows], axis=1)  30 us
  transfers between devices with their start and end apart: 15, of which 8 were waited for; matrix products, arithmetic and copies ran while one was open for 22% of the time, Pallas kernels for 12%

profile of v7, /device:TPU:0, one launch (start us, length us, event | category | flops | bytes accessed | tf_op | source)
XLA Modules:
  0.0 1409.0 jit_solution(15703423070212700374)
XLA Ops:
  12.4 22.7 %shard_map.395 = bf16[8,448,128]{2,1,0:T(8,128)(2,1)} custom-call(bf16[448,128]{1,0:T(8,128)(2,1)} %fusion.142.x_ref), custom_call_target="tpu_custom_call" | custom-call | tf_op jit(solution)/shard_map/pallas_call | solution.py:312
  93.4 39.3 %while.39 = (s32[]{:T(128)}, bf16[2,512,3,64]{1,3,2,0:T(8,128)(2,1)}, f32[2,3,512,1]{2,1,3,0:T(4,128)}, s32[2]{0:T(128)}, bf16[2048,3,64]{0,2,1:T(8,128)(2,1)S(1...) while((s32[]{:T(128)}, ...), condition=%wide.region_4.5_spmd, body=%wide.region_1.4_spmd.sunk | while | flops 644092928 | bytes 33331516 | solution.py:568
  136.0 24.2 %all-gather.7.cloned.1.call-done = bf16[8,1,166272]{2,1,0:T(2,128)(2,1)} async-done(((bf16[1,1,166272]{2,1,0:T(2,128)(2,1)}), bf16[8,1,166272]{2,1,0:T(2,128)(2,1)}) %all-gather.7.cloned.1.call-update) | async-done | bytes 2660368 | tf_op jit(solution)/shard_map/all_gather | solution.py:336
  190.1 46.2 %all-reduce.13.cloned.1.call-done = f32[1024,768]{1,0:T(8,128)} async-done(((f32[1024,768]{1,0:T(8,128)}), f32[1024,768]{1,0:T(8,128)}) %all-reduce.13.cloned.1.call-update) | async-done | bytes 3145744 | tf_op jit(solution)/shard_map/psum | solution.py:570
  242.1 17.8 %gather_fusion = bf16[4096,768]{1,0:T(8,128)(2,1)} fusion(bf16[1024,768]{1,0:T(8,128)(2,1)S(1)} %multiply_convert_fusion.4, s32[4096]{0:T(1024)S(1)} %get-tuple-element.933), kind=kCustom, calls=%fused_computation | custom fusion | bytes 12599296 | tf_op jit(solution)/shard_map/gather | solution.py:417
  264.7 21.4 %gather_fusion.1 = bf16[4096,768]{1,0:T(8,128)(2,1)} fusion(bf16[2048,768]{1,0:T(8,128)(2,1)} %multiply_convert_fusion.2, s32[4096]{0:T(1024)S(1)} %get-tuple-element.932), kind=kCustom, calls=%fused_computation.1 | custom fusion | bytes 12599296 | tf_op jit(solution)/shard_map/gather | solution.py:417
  296.9 142.6 %all_to_all.10 = bf16[4,512,1536]{2,1,0:T(8,128)(2,1)} all-to-all(bf16[4,512,1536]{2,1,0:T(8,128)(2,1)S(1)} %fusion.57), channel_id=1, replica_groups=mesh['fsdp'=4,'ctx'=2,'tp'=4] {'fsdp'}, dimensions={0} | all-to-all | bytes 12582912 | tf_op jit(solution)/shard_map/all_to_all | solution.py:419
  441.5 16.6 %all_gather.15 = bf16[1,512,768]{2,1,0:T(8,128)(2,1)S(1)} all-gather(bf16[1,512,384]{2,1,0:T(8,128)(2,1)S(1)} %get-tuple-element.896), channel_id=1, replica_groups=mesh['fsdp'=4,'ctx'=2,'tp'=4] {'ctx'}, dimensions={2}, use_global_device_ids=true | all-gather | bytes 1179648 | tf_op jit(solution)/shard_map/all_gather | solution.py:521
  458.0 10.8 pad_maximum_fusion.1
  470.7 12.4 fusion.63
  483.2 14.4 %multiply_bitcast_fusion = (f32[4096,1,512]{2,0,1:T(8,128)}, f32[4096,1,512]{2,0,1:T(8,128)}) fusion(f32[4096,2,512]{2,0,1:T(8,128)} %fusion.63, bf16[1,512,768]{2,1,0:T(8,128)(2,1)S(1)} %all_gather.15, bf16[4096,1536]{1,0:T(8,128)(2,1)} %bitcast.448), kind=kOutput, calls=%fused_computation.89 | convolution fusion | flops 3246391296 | bytes 40632320 | tf_op jit(solution)/shard_map/rd,fd->rf/dot_general | solution.py:436
  505.6 15.3 %convolution_bitcast_fusion = f32[4096,768]{0,1:T(8,128)} fusion(bf16[1,768,2,512]{3,1,2,0:T(8,128)(2,1)S(1)} %copy-done.146, f32[4096,1,512]{2,0,1:T(8,128)} %get-tuple-element.879, f32[4096,1,512]{2,0,1:T(8,128)} %get-tuple-element.878), kind=kOutput, calls=%fused_computation.91 | convolution fusion | flops 6450839552 | bytes 30932992 | tf_op jit(solution)/shard_map/rgf,dgf->rd/dot_general | solution.py:442
  520.9 14.5 %pad_maximum_fusion = f32[4096,1536]{0,1:T(8,128)} fusion(f32[4096,768]{0,1:T(8,128)} %convolution_bitcast_fusion, f32[4096,768]{0,1:T(8,128)S(1)} %fusion.65), kind=kLoop, calls=%fused_computation.68 | loop fusion | flops 6291456 | bytes 50331648 | tf_op jit(solution)/shard_map/concatenate | solution.py:445
  535.5 30.0 %reshape.1340 = f32[4,1024,1536]{1,0,2:T(4,128)} reshape(f32[4096,1536]{0,1:T(8,128)} %pad_maximum_fusion) | data formatting | bytes 50331648 | tf_op jit(solution)/shard_map/reshape | solution.py:445
  565.5 18.3 %fusion.193 = (f32[4,512,1536]{1,0,2:T(4,128)}, f32[4,512,1536]{1,0,2:T(4,128)}) fusion(f32[4,1024,1536]{1,0,2:T(4,128)} %reshape.1340), kind=kLoop, calls=%fused_computation.422 | loop fusion | bytes 50331648 | tf_op jit(solution)/shard_map/slice | solution.py:448
  583.8 13.1 copy.261
  597.0 12.7 fusion.109
  616.4 13.9 fusion.49
  635.6 13.7 fusion.90
  731.8 42.5 %all-to-all-done.1 = bf16[4,512,1536]{1,2,0:T(8,128)(2,1)} async-done(((bf16[4,512,1536]{1,2,0:T(8,128)(2,1)}), bf16[4,512,1536]{1,2,0:T(8,128)(2,1)}, u32[]{:S(2)}, u32[]{:S(2)}) %all-to-all-start.1) | async-done | bytes 6291488 | tf_op jit(solution)/shard_map/all_to_all | solution.py:419
  783.0 16.9 %gather_fusion.2 = bf16[2048,1536]{1,0:T(8,128)(2,1)} fusion(bf16[2048,1536]{1,0:T(8,128)(2,1)} %bitcast.441, s32[2048]{0:T(1024)S(1)} %copy-done.120), kind=kCustom, calls=%fused_computation.2 | custom fusion | bytes 12591104 | tf_op jit(solution)/shard_map/gather | solution.py:454
  825.8 12.0 reduce_sum.549
  855.2 31.2 %multiply_reduce_fusion.2 = f32[1024,768]{1,0:T(8,128)S(1)} fusion(f32[1024,2,768]{2,1,0:T(2,128)} %reshape.1342, f32[1024,2]{1,0:T(8,128)S(1)} %copy-done.29), kind=kLoop, calls=%fused_computation.96 | loop fusion | flops 2359296 | bytes 9445376 | tf_op jit(solution)/shard_map/reduce_sum | solution.py:457
  889.1 22.7 %all-reduce.15.cloned.1.call-done = f32[1024,768]{1,0:T(8,128)} async-done(((f32[1024,768]{1,0:T(8,128)}), f32[1024,768]{1,0:T(8,128)}) %all-reduce.15.cloned.1.call-update) | async-done | bytes 3145744 | tf_op jit(solution)/shard_map/psum | solution.py:617
  921.6 77.1 %while.40 = (s32[]{:T(128)}, f32[2048,3,64]{0,2,1:T(8,128)}, f32[2048,3,64]{0,2,1:T(8,128)S(1)}, f32[1024,3,64]{0,2,1:T(8,128)}, bf16[1024,3,64]{0,2,1:T(8,128)(...) while((s32[]{:T(128)}, f32[2048,3,64]{0,2,1:T(8,128)}, ...), condition=%wide.region_26.27_spmd, body=%wide.region_24.26_spmd.sunk | while | flops 1541608448 | bytes 106823088 | solution.py:719
  930.2 8.8 multiply_reduce_fusion.22
  939.0 9.4 multiply_convert_fusion.7
  968.5 8.9 multiply_reduce_fusion.22
  977.4 9.4 multiply_convert_fusion.7
  1052.1 164.5 %shard_map.396 = f32[1792,128]{1,0:T(8,128)} custom-call(f32[4,2,1792,128]{3,2,1,0:T(8,128)} %bitcast.442), custom_call_target="tpu_custom_call" | custom-call | tf_op jit(solution)/shard_map/pallas_call | solution.py:244
  1239.0 29.6 %shard_map.397 = f32[344,128]{1,0:T(8,128)} custom-call(f32[344,128]{1,0:T(8,128)} %pad_bitcast_fusion.1.x_ref), custom_call_target="tpu_custom_call" | custom-call | tf_op jit(solution)/shard_map/pallas_call | solution.py:162
  1353.1 13.9 shard_map.398
  (676 shorter events, 526.9 us)
Async XLA Ops:
  8.0 152.1 %all-gather.7.cloned.1.call-start = ((), (), s32[]{:S(2)}) async-start(), calls=%async_computation.9 | async-start | bytes 5985792 | tf_op jit(solution)/shard_map/all_gather | solution.py:336
  49.7 41.3 %collective-permute-start.2 = (bf16[1024,3,64]{0,2,1:T(8,128)(2,1)}, bf16[1024,3,64]{0,2,1:T(8,128)(2,1)}, u32[]{:S(2)}, u32[]{:S(2)}) collective-permute-start(bf16[1024,3,64]{0,2,1:T(8,128)(2,1)} %pad_maximum_fusion.5), channel_id=1, source_target_pairs={{0,4},{1,5},{2,6},{3,7},{8,12},{9,13},{10,14},{11,15},{16,20},{17,... | collective-permute-start | bytes 1179656 | tf_op jit(solution)/shard_map/ppermute | solution.py:27
  56.1 36.1 %collective-permute-start = (bf16[1024,3,64]{0,2,1:T(8,128)(2,1)S(1)}, bf16[1024,3,64]{0,2,1:T(8,128)(2,1)}, u32[]{:S(2)}, u32[]{:S(2)}) collective-permute-start(bf16[1024,3,64]{0,2,1:T(8,128)(2,1)S(1)} %bitcast.481), channel_id=1, source_target_pairs={{0,4},{1,5},{2,6},{3,7},{8,12},{9,13},{10,14},{11,15},{16,20},{17,... | collective-permute-start | bytes 1179656 | tf_op jit(solution)/shard_map/ppermute | solution.py:27
  58.2 32.8 %collective-permute-start.1 = (bf16[1024]{0:T(1024)(128)(2,1)S(1)}, bf16[1024]{0:T(1024)(128)(2,1)S(1)}, u32[]{:S(2)}, u32[]{:S(2)}) collective-permute-start(bf16[1024]{0:T(1024)(128)(2,1)S(1)} %convert_reduce_fusion), channel_id=1, source_target_pairs={{0,4},{1,5},{2,6},{3,7},{8,12},{9,13},{10,14},{11,15},{16,20},{17,... | collective-permute-start | bytes 6152 | tf_op jit(solution)/shard_map/ppermute | solution.py:27
  68.9 167.3 %all-reduce.13.cloned.1.call-start = ((), (), s32[]{:S(2)}) async-start(), calls=%async_computation.4 | async-start | bytes 6291456 | tf_op jit(solution)/shard_map/psum | solution.py:570
  132.7 30.7 %copy-start.14 = (bf16[2048,3,64]{0,2,1:T(8,128)(2,1)}, bf16[2048,3,64]{0,2,1:T(8,128)(2,1)S(1)}, u32[]{:S(2)}) copy-start(bf16[2048,3,64]{0,2,1:T(8,128)(2,1)S(1)} %get-tuple-element.1219) | copy-start | bytes 2359300
  132.7 30.7 %copy-start.21 = (bf16[1024,3,64]{0,2,1:T(8,128)(2,1)}, bf16[1024,3,64]{0,2,1:T(8,128)(2,1)S(1)}, u32[]{:S(2)}) copy-start(bf16[1024,3,64]{0,2,1:T(8,128)(2,1)S(1)} %get-tuple-element.1220) | copy-start | bytes 1179652
  132.7 36.7 %copy-start.75 = (bf16[2048]{0:T(1024)(128)(2,1)}, bf16[2048]{0:T(1024)(128)(2,1)S(1)}, u32[]{:S(2)}) copy-start(bf16[2048]{0:T(1024)(128)(2,1)S(1)} %get-tuple-element.1245) | copy-start | bytes 12292
  132.7 36.7 %copy-start.87 = (bf16[1024]{0:T(1024)(128)(2,1)}, bf16[1024]{0:T(1024)(128)(2,1)S(1)}, u32[]{:S(2)}) copy-start(bf16[1024]{0:T(1024)(128)(2,1)S(1)} %get-tuple-element.1248) | copy-start | bytes 6148
  169.5 301.3 %all-gather.5.cloned.1.call-start = ((), (), s32[]{:S(2)}) async-start(), calls=%async_computation.5 | async-start | bytes 2359296 | tf_op jit(solution)/shard_map/all_gather | solution.py:520
  172.0 66.6 %copy-start.92 = (s32[2048]{0:T(1024)}, s32[2048]{0:T(1024)S(1)}, u32[]{:S(2)}) copy-start(s32[2048]{0:T(1024)S(1)} %fusion.147) | copy-start | bytes 24580
  190.1 49.5 %copy-start.53 = (bf16[768,4]{1,0:T(8,128)(2,1)}, bf16[768,4]{1,0:T(8,128)(2,1)S(1)}, u32[]{:S(2)}) copy-start(bf16[768,4]{1,0:T(8,128)(2,1)S(1)} %reshape_reshape.22) | copy-start | bytes 18436
  190.1 49.2 %copy-start.94 = (f32[768]{0:T(1024)S(1)}, f32[768]{0:T(1024)}, u32[]{:S(2)}) copy-start(f32[768]{0:T(1024)} %reshape.1368) | copy-start | bytes 9220
  296.9 142.6 %copy-start.18 = (f32[1,384,2,512]{3,2,1,0:T(2,128)S(1)}, f32[1,384,2,512]{3,2,1,0:T(2,128)}, u32[]{:S(2)}) copy-start(f32[1,384,2,512]{3,2,1,0:T(2,128)} %param.34) | copy-start | bytes 4718596
  439.5 18.6 %collective-permute-start.3 = (bf16[4,512,1536]{2,1,0:T(8,128)(2,1)}, bf16[4,512,1536]{2,1,0:T(8,128)(2,1)}, u32[]{:S(2)}, u32[]{:S(2)}) collective-permute-start(bf16[4,512,1536]{2,1,0:T(8,128)(2,1)} %all_to_all.10), channel_id=1, source_target_pairs={{0,1},{1,0},{2,3},{3,2},{4,5},{5,4},{6,7},{7,6},{8,9},{9,8},{10,11... | collective-permute-start | bytes 18874376 | tf_op jit(solution)/shard_map/ppermute | solution.py:421
  440.6 282.9 %reduce-scatter.5.cloned.1.call-start = ((), (), s32[]{:S(2)}) async-start(), calls=%async_computation.8 | async-start | bytes 2359296 | tf_op jit(solution)/shard_map/reduce_scatter | solution.py:663
  596.9 19.5 %collective-permute-start.4 = (f32[4,512,1536]{1,2,0:T(8,128)}, f32[4,512,1536]{1,2,0:T(8,128)}, u32[]{:S(2)}, u32[]{:S(2)}) collective-permute-start(f32[4,512,1536]{1,2,0:T(8,128)} %copy.261), channel_id=1, source_target_pairs={{0,1},{1,0},{2,3},{3,2},{4,5},{5,4},{6,7},{7,6},{8,9},{9,8},{10,11... | collective-permute-start | bytes 37748744 | tf_op jit(solution)/shard_map/ppermute | solution.py:421
  630.3 144.0 %all-to-all-start.1 = ((bf16[4,512,1536]{1,2,0:T(8,128)(2,1)}), bf16[4,512,1536]{1,2,0:T(8,128)(2,1)}, u32[]{:S(2)}, u32[]{:S(2)}) async-start(bf16[4,512,1536]{1,2,0:T(8,128)(2,1)} %fusion.49), calls=%async_computation.1 | async-start | bytes 12582912 | tf_op jit(solution)/shard_map/all_to_all | solution.py:419
  635.6 89.3 %reduce-scatter.3.cloned.1.call-start = ((), (), s32[]{:S(2)}) async-start(), calls=%async_computation.7 | async-start | bytes 4718592 | tf_op jit(solution)/shard_map/reduce_scatter | solution.py:662
  649.4 262.4 %all-reduce.15.cloned.1.call-start = ((), (), s32[]{:S(2)}) async-start(), calls=%async_computation.6 | async-start | bytes 6291456 | tf_op jit(solution)/shard_map/psum | solution.py:617
  731.8 51.1 %copy-start.120 = (s32[2048]{0:T(1024)S(1)}, s32[2048]{0:T(1024)}, u32[]{:S(2)}) copy-start(s32[2048]{0:T(1024)} %broadcast_clamp_fusion) | copy-start | bytes 24580
  844.6 386.0 %all-reduce.17.cloned.1.call-start = ((), (), s32[]{:S(2)}) async-start(), calls=%async_computation.10 | async-start | bytes 12582912 | tf_op jit(solution)/shard_map/psum | solution.py:617
  855.2 31.2 %copy-start.34 = (bf16[1024,1,512]{2,0,1:T(8,128)(2,1)S(1)}, bf16[1024,1,512]{2,0,1:T(8,128)(2,1)}, u32[]{:S(2)}) copy-start(bf16[1024,1,512]{2,0,1:T(8,128)(2,1)} %copy-done.33) | copy-start | bytes 3145732
  855.2 31.2 %copy-start.46 = (bf16[512,8,96]{0,2,1:T(8,128)(2,1)S(1)}, bf16[512,8,96]{0,2,1:T(8,128)(2,1)}, u32[]{:S(2)}) copy-start(bf16[512,8,96]{0,2,1:T(8,128)(2,1)} %copy.215) | copy-start | bytes 2359300
  1000.0 14.0 collective-permute-start.5
  1002.1 19.1 %collective-permute-start.6 = (bf16[1024,3,64]{0,2,1:T(8,128)(2,1)}, bf16[1024,3,64]{0,2,1:T(8,128)(2,1)}, u32[]{:S(2)}, u32[]{:S(2)}) collective-permute-start(bf16[1024,3,64]{0,2,1:T(8,128)(2,1)} %slice.668), channel_id=1, source_target_pairs={{4,0},{5,1},{6,2},{7,3},{12,8},{13,9},{14,10},{15,11},{20,16},{21,... | collective-permute-start | bytes 1179656 | tf_op jit(solution)/shard_map/ppermute | solution.py:27
  1225.0 43.6 %copy-start.69 = (f32[192,96]{1,0:T(8,128)}, f32[192,96]{1,0:T(8,128)S(1)}, u32[]{:S(2)}) copy-start(f32[192,96]{1,0:T(8,128)S(1)} %reshape.1352) | copy-start | bytes 221188
  1285.3 59.4 %copy-start.13 = (f32[1,384,2,512]{3,1,2,0:T(8,128)S(1)}, f32[1,384,2,512]{3,1,2,0:T(8,128)}, u32[]{:S(2)}) copy-start(f32[1,384,2,512]{3,1,2,0:T(8,128)} %reduce-scatter.3.cloned.1.call-done) | copy-start | bytes 4718596
  1285.3 85.7 %copy-start.20 = (f32[1,384,2,512]{3,2,1,0:T(2,128)S(1)}, f32[1,384,2,512]{3,2,1,0:T(2,128)}, u32[]{:S(2)}) copy-start(f32[1,384,2,512]{3,2,1,0:T(2,128)} %param.34) | copy-start | bytes 4718596
  1306.2 38.5 %copy-start.101 = (f32[2,512]{1,0:T(2,128)S(1)}, f32[2,512]{1,0:T(2,128)}, u32[]{:S(2)}) copy-start(f32[2,512]{1,0:T(2,128)} %copy-done.100) | copy-start | bytes 12292
  1306.2 40.3 %copy-start.117 = (f32[1,1,512]{2,1,0:T(1,128)S(1)}, f32[1,1,512]{2,1,0:T(1,128)}, u32[]{:S(2)}) copy-start(f32[1,1,512]{2,1,0:T(1,128)} %fusion.177) | copy-start | bytes 6148
  1308.3 62.7 %copy-start.115 = (f32[512]{0:T(512)}, f32[512]{0:T(512)S(1)}, u32[]{:S(2)}) copy-start(f32[512]{0:T(512)S(1)} %multiply_add_fusion.8) | copy-start | bytes 6148
  (139 other events, 994.4 us)
Sparse Core Ops, SparseCore 0:
  69.1 91.0 all-gather.6
  169.5 66.6 all-reduce.12
  844.7 67.0 all-reduce.14
  1025.5 119.2 all-reduce.16
Sparse Core Ops, SparseCore 1:
  440.7 30.0 all-gather.4
  609.7 24.9 reduce-scatter.4
  649.4 44.0 reduce-scatter.2

commit v8 on v7

--- a/solution.py
+++ b/solution.py
@@ -413,9 +413,13 @@
         .astype(jnp.bfloat16)
         .reshape(2 * block_len, model_width)
     )
-    send_rows = jnp.concatenate(
-        [normed_two[owner_route // 2] * fill_mask, route_grads[owner_route] * fill_mask], axis=1
-    ).reshape(experts, capacity, 2 * model_width)
+    send_rows = jnp.stack(
+        [
+            (normed_two[owner_route // 2] * fill_mask).reshape(experts, capacity, model_width),
+            (route_grads[owner_route] * fill_mask).reshape(experts, capacity, model_width),
+        ],
+        axis=1,
+    )
     exchange = lambda rows: lax.all_to_all(rows, "fsdp", split_axis=0, concat_axis=0, tiled=True)
     pair_count = lax.axis_size("tp")
     swap = lambda rows: lax.ppermute(
@@ -423,12 +427,10 @@
     )
     half = capacity // 2
     side = lax.axis_index("tp") % 2
-    mine = exchange(lax.dynamic_slice_in_dim(send_rows, side * half, half, 1))
-    received_both = jnp.concatenate([mine, swap(mine)], axis=1).reshape(
-        experts * capacity, 2 * model_width
-    )
-    received = received_both[:, :model_width]
-    grad_received = received_both[:, model_width:]
+    mine = exchange(lax.dynamic_slice_in_dim(send_rows, side * half, half, 2))
+    received_both = jnp.concatenate([mine, swap(mine)], axis=2)
+    received = received_both[:, 0].reshape(experts * capacity, model_width)
+    grad_received = received_both[:, 1].reshape(experts * capacity, model_width)
     gate_up = jnp.einsum("rd,dgf->rgf", received, expert_in_low, preferred_element_type=jnp.float32)
     act, act_back = jax.vjp(swiglu, gate_up)
     hidden = act.astype(jnp.bfloat16)
@@ -442,18 +444,22 @@
     grad_expert_rows = jnp.einsum(
         "rgf,dgf->rd", grad_gate_up, expert_in_low, preferred_element_type=jnp.float32
     )
-    results = jnp.concatenate([outs, grad_expert_rows], axis=1).reshape(
-        experts, capacity, 2 * model_width
-    )
-    pair_sum = results[:, :half] + swap(results[:, half:])
-    held = exchange(pair_sum.astype(jnp.bfloat16)).reshape(experts * half, 2 * model_width)
+    pair_sums = []
+    for rows in (outs, grad_expert_rows):
+        rows = rows.reshape(experts, capacity, model_width)
+        pair_sums.append(rows[:, :half] + swap(rows[:, half:]))
+    held = exchange(jnp.stack(pair_sums, axis=1).astype(jnp.bfloat16))
     slot_expert = slot_index // capacity
     slot_rank = slot_index % capacity
-    in_side = (slot_rank // half) == side
+    in_side = ((slot_rank // half) == side)[:, None]
     local_slot = slot_expert * half + slot_rank % half
-    returned = jnp.where(in_side[:, None], held[local_slot].astype(jnp.float32), 0.0)
-    route_out = returned[:, :model_width].reshape(block_len, 2, model_width)
-    grad_routes = returned[:, model_width:].reshape(block_len, 2, model_width)
+    picked_rows = []
+    for which in range(2):
+        rows = held[:, which].reshape(experts * half, model_width)[local_slot]
+        picked_rows.append(
+            jnp.where(in_side, rows.astype(jnp.float32), 0.0).reshape(block_len, 2, model_width)
+        )
+    route_out, grad_routes = picked_rows
     combined = jnp.sum(gate_probs[:, :, None] * route_out, axis=1)
     gate_dots = jnp.sum(grad_out[:, None, :] * route_out, axis=-1)
     grad_rows = jnp.sum(grad_routes, axis=1)

time: 1420 us -> 1350 us (0.951)
  other arithmetic: 249 us -> 200 us
  local copies, waits for them, and re-layouts: 367 us -> 340 us
  waiting for transfers between devices: 153 us -> 178 us
  matrix products: 176 us -> 155 us
    reshape x3 -> x0, local copies, waits for them, and re-layouts: 46.9 us -> none  [the longest x1 30 us: experts_routed(): jnp.concatenate([outs, grad_expert_rows], axis=1)]
    reduce_sum x1 -> x0, other arithmetic: 31.2 us -> none  [experts_routed(): combined = jnp.sum(gate_probs[:, :, None] * route_out, axis=1)]
    concatenate x3 -> x0, other arithmetic: 27.7 us -> none  [the longest x1 14.5 us: experts_routed(): jnp.concatenate([outs, grad_expert_rows], axis=1)]
    psum x2, waiting for transfers between devices: 22.7 us -> 47.9 us  [local(): lax.psum((shared_out + combined, partial_two, gate_dots), 'tp')]
    convert_element_type x0 -> x2, local copies, waits for them, and re-layouts: none -> 15.7 us  [experts_routed(): rows.astype(jnp.float32)]
    unnamed x310 -> x328, local copies, waits for them, and re-layouts: 65.4 us -> 67.2 us
  transfers between devices with their start and end apart: 15 -> 16, of which waited for: 8 -> 7; matrix products, arithmetic and copies ran while one was open for 22% -> 22% of each run, Pallas kernels for 12% -> 12%
where the time goes in v8:
time: 1350 us; the launch traced here: 1340 us
  local copies, waits for them, and re-layouts  340 us (25%)
  Pallas kernels  231 us (17%)
  other arithmetic  200 us (15%)
  waiting for transfers between devices  178 us (13%)
  blocking collectives  166 us (12%)
  matrix products  155 us (11%)
  between operations  43.1 us (3%)
  starting transfers between devices  17.1 us (1%)
    pallas_call x1, Pallas kernels, halving_scatter(): pl.pallas_call(halving_kernel, out_shape=jax.ShapeDtypeStruct((rows, 128)...  164 us
    all_to_all x1, blocking collectives, experts_routed(): lax.all_to_all(rows, 'fsdp', split_axis=0, concat_axis=0, tiled=True)  143 us
    unnamed x328, local copies, waits for them, and re-layouts  67.2 us
    psum x2, waiting for transfers between devices, local(): lax.psum((shared_out + combined, partial_two, gate_dots), 'tp')  47.9 us
    all_to_all x1, waiting for transfers between devices, experts_routed(): lax.all_to_all(rows, 'fsdp', split_axis=0, concat_axis=0, tiled=True)  46.2 us
    psum x1, waiting for transfers between devices, local(): lax.psum(jnp.dot(mixed_heads, attn_out_low, preferred_element_type=jnp.fl...  46.2 us
    pallas_call x2, Pallas kernels, butterfly_sum(): pl.pallas_call(butterfly_kernel, out_shape=jax.ShapeDtypeStruct((rows, 12...  43.6 us
    all_gather x1, waiting for transfers between devices, gather_packed(): full = lax.all_gather(flat, axes, axis=0, tiled=False)  28.3 us
  transfers between devices with their start and end apart: 16, of which 7 were waited for; matrix products, arithmetic and copies ran while one was open for 22% of the time, Pallas kernels for 12%

profile of v8, /device:TPU:0, one launch (start us, length us, event | category | flops | bytes accessed | tf_op | source)
XLA Modules:
  0.0 1337.0 jit_solution(15992893037421719289)
XLA Ops:
  12.4 22.7 %shard_map.395 = bf16[8,448,128]{2,1,0:T(8,128)(2,1)} custom-call(bf16[448,128]{1,0:T(8,128)(2,1)} %fusion.143.x_ref), custom_call_target="tpu_custom_call" | custom-call | tf_op jit(solution)/shard_map/pallas_call | solution.py:312
  83.6 8.6 mul.1199
  94.5 34.1 %while.39 = (s32[]{:T(128)}, bf16[2,512,3,64]{1,3,2,0:T(8,128)(2,1)}, f32[2,3,512,1]{2,1,3,0:T(4,128)}, s32[2]{0:T(128)S(1)}, bf16[2048,3,64]{0,2,1:T(8,128)(2,1...) while((s32[]{:T(128)}, ...), condition=%wide.region_4.5_spmd, body=%wide.region_1.4_spmd.sunk | while | flops 644092928 | bytes 33315144 | solution.py:574
  131.9 28.3 %all-gather.7.cloned.1.call-done = bf16[8,1,166272]{2,1,0:T(2,128)(2,1)} async-done(((bf16[1,1,166272]{2,1,0:T(2,128)(2,1)}), bf16[8,1,166272]{2,1,0:T(2,128)(2,1)}) %all-gather.7.cloned.1.call-update) | async-done | bytes 2660368 | tf_op jit(solution)/shard_map/all_gather | solution.py:336
  172.8 8.1 scatter_custom_fusion
  180.8 8.1 scatter_custom_fusion.1
  190.1 46.2 %all-reduce.13.cloned.1.call-done = f32[1024,768]{1,0:T(8,128)} async-done(((f32[1024,768]{1,0:T(8,128)}), f32[1024,768]{1,0:T(8,128)}) %all-reduce.13.cloned.1.call-update) | async-done | bytes 3145744 | tf_op jit(solution)/shard_map/psum | solution.py:576
  242.6 17.8 %gather_fusion = bf16[4096,768]{1,0:T(8,128)(2,1)} fusion(bf16[1024,768]{1,0:T(8,128)(2,1)S(1)} %multiply_convert_fusion.3, s32[4096]{0:T(1024)S(1)} %get-tuple-element.934), kind=kCustom, calls=%fused_computation | custom fusion | bytes 12599296 | tf_op jit(solution)/shard_map/gather | solution.py:418
  265.2 21.4 %gather_fusion.1 = bf16[4096,768]{1,0:T(8,128)(2,1)} fusion(bf16[2048,768]{1,0:T(8,128)(2,1)} %multiply_convert_fusion.2, s32[4096]{0:T(1024)S(1)} %get-tuple-element.933), kind=kCustom, calls=%fused_computation.1 | custom fusion | bytes 12599296 | tf_op jit(solution)/shard_map/gather | solution.py:419
  292.6 142.6 %all_to_all.10 = bf16[4,2,512,768]{3,2,1,0:T(8,128)(2,1)} all-to-all(bf16[4,2,512,768]{3,2,1,0:T(8,128)(2,1)S(1)} %fusion.57), channel_id=1, replica_groups=mesh['fsdp'=4,'ctx'=2,'tp'=4] {'fsdp'}, dimensions={0} | all-to-all | bytes 12582912 | tf_op jit(solution)/shard_map/all_to_all | solution.py:423
  437.3 16.6 %all_gather.15 = bf16[1,512,768]{2,1,0:T(8,128)(2,1)S(1)} all-gather(bf16[1,512,384]{2,1,0:T(8,128)(2,1)S(1)} %get-tuple-element.897), channel_id=1, replica_groups=mesh['fsdp'=4,'ctx'=2,'tp'=4] {'ctx'}, dimensions={2}, use_global_device_ids=true | all-gather | bytes 1179648 | tf_op jit(solution)/shard_map/all_gather | solution.py:527
  466.5 9.3 fusion.94
  481.6 14.2 %fusion.56 = (f32[4096,1,512]{2,0,1:T(8,128)}, f32[4096,1,512]{2,0,1:T(8,128)}) fusion(f32[4096,2,512]{2,0,1:T(8,128)} %copy-done.17, bf16[4096,768]{1,0:T(8,128)(2,1)} %bitcast.476, bf16[1,512,768]{2,1,0:T(8,128)(2,1)S(1)} %all_gather.15), kind=kOutput, calls=%fused_computation.84 | convolution fusion | flops 3246391296 | bytes 40632320 | tf_op jit(solution)/shard_map/rd,fd->rf/dot_general | solution.py:438
  505.7 9.2 add_convert_fusion
  514.9 10.0 convolution_bitcast_fusion
  563.6 12.2 convolution_bitcast_fusion.1
  656.0 46.2 %all-to-all-done.1 = bf16[4,2,512,768]{3,2,1,0:T(8,128)(2,1)} async-done(((bf16[4,2,512,768]{3,2,1,0:T(8,128)(2,1)}), bf16[4,2,512,768]{3,2,1,0:T(8,128)(2,1)}, u32[]{:S(2)}, u32[]{:S(2)}) %all-to-all-start.1) | async-done | bytes 6291488 | tf_op jit(solution)/shard_map/all_to_all | solution.py:423
  708.2 12.4 gather_fusion.2
  720.5 7.8 reshape.1408
  728.4 12.4 gather_fusion.3
  740.7 7.9 reshape.1409
  748.6 20.7 %select_reduce_fusion = (f32[1024,768]{1,0:T(8,128)S(1)}, f32[1024,768]{1,0:T(8,128)}) fusion(f32[1024,2,768]{2,1,0:T(2,128)} %reshape.1409, pred[1024,2]{1,0:T(8,128)(4,1)S(1)} %copy-done.66, f32[1024,2,768]{2,1,0:T(2,128)} %reshape.1408, f32[1024,2]{1,0:T(8,128)S(1)} %copy-done.33), kind=kLoop, calls=%fused_computation.94 | loop fusion | flops 6291456 | bytes 18884608 | tf_op jit(solution)/shard_map/reduce_sum | solution.py:465
  792.3 47.9 %all-reduce.15.cloned.1.call-done = f32[1024,768]{1,0:T(8,128)} async-done(((f32[1024,768]{1,0:T(8,128)}), f32[1024,768]{1,0:T(8,128)}) %all-reduce.15.cloned.1.call-update) | async-done | bytes 3145744 | tf_op jit(solution)/shard_map/psum | solution.py:623
  850.0 76.7 %while.40 = (s32[]{:T(128)}, f32[2048,3,64]{0,2,1:T(8,128)}, f32[2048,3,64]{0,2,1:T(8,128)S(1)}, f32[1024,3,64]{0,2,1:T(8,128)}, bf16[1024,3,64]{0,2,1:T(8,128)(...) while((s32[]{:T(128)}, f32[2048,3,64]{0,2,1:T(8,128)}, ...), condition=%wide.region_26.27_spmd, body=%wide.region_24.26_spmd.sunk | while | flops 1541608448 | bytes 106823088 | solution.py:725
  858.2 8.8 multiply_reduce_fusion.22
  867.0 9.5 multiply_convert_fusion.6
  896.5 8.8 multiply_reduce_fusion.22
  905.3 9.5 multiply_convert_fusion.6
  980.1 164.4 %shard_map.396 = f32[1792,128]{1,0:T(8,128)} custom-call(f32[4,2,1792,128]{3,2,1,0:T(8,128)} %bitcast.459), custom_call_target="tpu_custom_call" | custom-call | tf_op jit(solution)/shard_map/pallas_call | solution.py:244
  1167.1 29.7 %shard_map.397 = f32[344,128]{1,0:T(8,128)} custom-call(f32[344,128]{1,0:T(8,128)} %pad_bitcast_fusion.1.x_ref), custom_call_target="tpu_custom_call" | custom-call | tf_op jit(solution)/shard_map/pallas_call | solution.py:162
  1205.6 7.8 slice.486
  1281.2 13.9 %shard_map.398 = f32[8,128]{1,0:T(8,128)} custom-call(f32[8,128]{1,0:T(8,128)} %pad_bitcast_fusion.2.x_ref), custom_call_target="tpu_custom_call" | custom-call | tf_op jit(solution)/shard_map/pallas_call | solution.py:162
  (699 shorter events, 503.2 us)
Async XLA Ops:
  8.0 152.2 %all-gather.7.cloned.1.call-start = ((), (), s32[]{:S(2)}) async-start(), calls=%async_computation.9 | async-start | bytes 5985792 | tf_op jit(solution)/shard_map/all_gather | solution.py:336
  49.8 42.5 %collective-permute-start.2 = (bf16[1024,3,64]{0,2,1:T(8,128)(2,1)}, bf16[1024,3,64]{0,2,1:T(8,128)(2,1)}, u32[]{:S(2)}, u32[]{:S(2)}) collective-permute-start(bf16[1024,3,64]{0,2,1:T(8,128)(2,1)} %pad_maximum_fusion.4), channel_id=1, source_target_pairs={{0,4},{1,5},{2,6},{3,7},{8,12},{9,13},{10,14},{11,15},{16,20},{17,... | collective-permute-start | bytes 1179656 | tf_op jit(solution)/shard_map/ppermute | solution.py:27
  56.1 37.2 %collective-permute-start = (bf16[1024,3,64]{0,2,1:T(8,128)(2,1)S(1)}, bf16[1024,3,64]{0,2,1:T(8,128)(2,1)}, u32[]{:S(2)}, u32[]{:S(2)}) collective-permute-start(bf16[1024,3,64]{0,2,1:T(8,128)(2,1)S(1)} %bitcast.500), channel_id=1, source_target_pairs={{0,4},{1,5},{2,6},{3,7},{8,12},{9,13},{10,14},{11,15},{16,20},{17,... | collective-permute-start | bytes 1179656 | tf_op jit(solution)/shard_map/ppermute | solution.py:27
  58.2 34.0 %collective-permute-start.1 = (bf16[1024]{0:T(1024)(128)(2,1)S(1)}, bf16[1024]{0:T(1024)(128)(2,1)S(1)}, u32[]{:S(2)}, u32[]{:S(2)}) collective-permute-start(bf16[1024]{0:T(1024)(128)(2,1)S(1)} %convert_reduce_fusion), channel_id=1, source_target_pairs={{0,4},{1,5},{2,6},{3,7},{8,12},{9,13},{10,14},{11,15},{16,20},{17,... | collective-permute-start | bytes 6152 | tf_op jit(solution)/shard_map/ppermute | solution.py:27
  69.0 167.3 %all-reduce.13.cloned.1.call-start = ((), (), s32[]{:S(2)}) async-start(), calls=%async_computation.4 | async-start | bytes 6291456 | tf_op jit(solution)/shard_map/psum | solution.py:576
  128.6 40.9 %copy-start.79 = (bf16[2048]{0:T(1024)(128)(2,1)}, bf16[2048]{0:T(1024)(128)(2,1)S(1)}, u32[]{:S(2)}) copy-start(bf16[2048]{0:T(1024)(128)(2,1)S(1)} %get-tuple-element.1258) | copy-start | bytes 12292
  128.6 40.9 %copy-start.87 = (bf16[1024]{0:T(1024)(128)(2,1)}, bf16[1024]{0:T(1024)(128)(2,1)S(1)}, u32[]{:S(2)}) copy-start(bf16[1024]{0:T(1024)(128)(2,1)S(1)} %get-tuple-element.1257) | copy-start | bytes 6148
  169.5 297.0 %all-gather.5.cloned.1.call-start = ((), (), s32[]{:S(2)}) async-start(), calls=%async_computation.5 | async-start | bytes 2359296 | tf_op jit(solution)/shard_map/all_gather | solution.py:526
  172.0 66.6 %copy-start.92 = (s32[2048]{0:T(1024)}, s32[2048]{0:T(1024)S(1)}, u32[]{:S(2)}) copy-start(s32[2048]{0:T(1024)S(1)} %fusion.148) | copy-start | bytes 24580
  190.1 49.5 %copy-start.55 = (bf16[768,4]{1,0:T(8,128)(2,1)}, bf16[768,4]{1,0:T(8,128)(2,1)S(1)}, u32[]{:S(2)}) copy-start(bf16[768,4]{1,0:T(8,128)(2,1)S(1)} %reshape_reshape.22) | copy-start | bytes 18436
  190.1 49.2 %copy-start.94 = (f32[768]{0:T(1024)S(1)}, f32[768]{0:T(1024)}, u32[]{:S(2)}) copy-start(f32[768]{0:T(1024)} %reshape.1407) | copy-start | bytes 9220
  292.6 142.6 %copy-start.20 = (f32[1,384,2,512]{3,2,1,0:T(2,128)S(1)}, f32[1,384,2,512]{3,2,1,0:T(2,128)}, u32[]{:S(2)}) copy-start(f32[1,384,2,512]{3,2,1,0:T(2,128)} %param.34) | copy-start | bytes 4718596
  435.2 21.8 %collective-permute-start.3 = (bf16[4,2,512,768]{3,2,1,0:T(8,128)(2,1)}, bf16[4,2,512,768]{3,2,1,0:T(8,128)(2,1)}, u32[]{:S(2)}, u32[]{:S(2)}) collective-permute-start(bf16[4,2,512,768]{3,2,1,0:T(8,128)(2,1)} %all_to_all.10), channel_id=1, source_target_pairs={{0,1},{1,0},{2,3},{3,2},{4,5},{5,4},{6,7},{7,6},{8,9},{9,8},{10,11... | collective-permute-start | bytes 18874376 | tf_op jit(solution)/shard_map/ppermute | solution.py:425
  436.4 211.3 %reduce-scatter.5.cloned.1.call-start = ((), (), s32[]{:S(2)}) async-start(), calls=%async_computation.8 | async-start | bytes 2359296 | tf_op jit(solution)/shard_map/reduce_scatter | solution.py:669
  505.7 32.9 %collective-permute-start.4 = (f32[4,512,768]{2,1,0:T(8,128)}, f32[4,512,768]{2,1,0:T(8,128)}, u32[]{:S(2)}, u32[]{:S(2)}) collective-permute-start(f32[4,512,768]{2,1,0:T(8,128)} %slice.549), channel_id=1, source_target_pairs={{0,1},{1,0},{2,3},{3,2},{4,5},{5,4},{6,7},{7,6},{8,9},{9,8},{10,11... | collective-permute-start | bytes 18874376 | tf_op jit(solution)/shard_map/ppermute | solution.py:425
  531.3 12.7 collective-permute-start.5
  558.3 143.9 %all-to-all-start.1 = ((bf16[4,2,512,768]{3,2,1,0:T(8,128)(2,1)}), bf16[4,2,512,768]{3,2,1,0:T(8,128)(2,1)}, u32[]{:S(2)}, u32[]{:S(2)}) async-start(bf16[4,2,512,768]{3,2,1,0:T(8,128)(2,1)} %copy.229), calls=%async_computation.1 | async-start | bytes 12582912 | tf_op jit(solution)/shard_map/all_to_all | solution.py:423
  563.5 85.6 %reduce-scatter.3.cloned.1.call-start = ((), (), s32[]{:S(2)}) async-start(), calls=%async_computation.7 | async-start | bytes 4718592 | tf_op jit(solution)/shard_map/reduce_scatter | solution.py:668
  575.8 264.4 %all-reduce.15.cloned.1.call-start = ((), (), s32[]{:S(2)}) async-start(), calls=%async_computation.6 | async-start | bytes 6291456 | tf_op jit(solution)/shard_map/psum | solution.py:623
  772.9 385.7 %all-reduce.17.cloned.1.call-start = ((), (), s32[]{:S(2)}) async-start(), calls=%async_computation.10 | async-start | bytes 12582912 | tf_op jit(solution)/shard_map/psum | solution.py:623
  787.0 53.2 %copy-start.4 = (f32[1024,768]{1,0:T(8,128)S(1)}, f32[1024,768]{1,0:T(8,128)}, u32[]{:S(2)}) copy-start(f32[1024,768]{1,0:T(8,128)} %copy-done.3) | copy-start | bytes 9437188
  787.0 53.2 %copy-start.56 = (bf16[768,4]{1,0:T(8,128)(2,1)S(1)}, bf16[768,4]{1,0:T(8,128)(2,1)}, u32[]{:S(2)}) copy-start(bf16[768,4]{1,0:T(8,128)(2,1)} %copy-done.55) | copy-start | bytes 18436
  787.0 53.2 %copy-start.95 = (f32[768]{0:T(1024)S(1)}, f32[768]{0:T(1024)}, u32[]{:S(2)}) copy-start(f32[768]{0:T(1024)} %reshape.1407) | copy-start | bytes 9220
  787.0 53.2 %copy-start.97 = (f32[1024]{0:T(1024)S(1)}, f32[1024]{0:T(1024)}, u32[]{:S(2)}) copy-start(f32[1024]{0:T(1024)} %copy-done.96) | copy-start | bytes 12292
  792.3 51.7 %copy-start.106 = (f32[1024]{0:T(1024)S(1)}, f32[1024]{0:T(1024)}, u32[]{:S(2)}) copy-start(f32[1024]{0:T(1024)} %copy-done.105) | copy-start | bytes 12292
  928.0 14.0 %collective-permute-start.6 = (bf16[1024,3,64]{0,2,1:T(8,128)(2,1)S(1)}, bf16[1024,3,64]{0,2,1:T(8,128)(2,1)}, u32[]{:S(2)}, u32[]{:S(2)}) collective-permute-start(bf16[1024,3,64]{0,2,1:T(8,128)(2,1)S(1)} %slice.664), channel_id=1, source_target_pairs={{4,0},{5,1},{6,2},{7,3},{12,8},{13,9},{14,10},{15,11},{20,16},{21,... | collective-permute-start | bytes 1179656 | tf_op jit(solution)/shard_map/ppermute | solution.py:27
  930.1 19.1 %collective-permute-start.7 = (bf16[1024,3,64]{0,2,1:T(8,128)(2,1)}, bf16[1024,3,64]{0,2,1:T(8,128)(2,1)}, u32[]{:S(2)}, u32[]{:S(2)}) collective-permute-start(bf16[1024,3,64]{0,2,1:T(8,128)(2,1)} %slice.663), channel_id=1, source_target_pairs={{4,0},{5,1},{6,2},{7,3},{12,8},{13,9},{14,10},{15,11},{20,16},{21,... | collective-permute-start | bytes 1179656 | tf_op jit(solution)/shard_map/ppermute | solution.py:27
  1153.0 43.7 %copy-start.72 = (f32[192,96]{1,0:T(8,128)}, f32[192,96]{1,0:T(8,128)S(1)}, u32[]{:S(2)}) copy-start(f32[192,96]{1,0:T(8,128)S(1)} %reshape.1391) | copy-start | bytes 221188
  1213.4 59.4 %copy-start.14 = (f32[1,384,2,512]{3,1,2,0:T(8,128)S(1)}, f32[1,384,2,512]{3,1,2,0:T(8,128)}, u32[]{:S(2)}) copy-start(f32[1,384,2,512]{3,1,2,0:T(8,128)} %reduce-scatter.3.cloned.1.call-done) | copy-start | bytes 4718596
  1213.4 85.7 %copy-start.21 = (f32[1,384,2,512]{3,2,1,0:T(2,128)S(1)}, f32[1,384,2,512]{3,2,1,0:T(2,128)}, u32[]{:S(2)}) copy-start(f32[1,384,2,512]{3,2,1,0:T(2,128)} %param.34) | copy-start | bytes 4718596
  1234.2 40.4 %copy-start.119 = (f32[1,1,512]{2,1,0:T(1,128)S(1)}, f32[1,1,512]{2,1,0:T(1,128)}, u32[]{:S(2)}) copy-start(f32[1,1,512]{2,1,0:T(1,128)} %fusion.174) | copy-start | bytes 6148
  1236.3 62.8 %copy-start.115 = (f32[512]{0:T(512)}, f32[512]{0:T(512)S(1)}, u32[]{:S(2)}) copy-start(f32[512]{0:T(512)S(1)} %multiply_add_fusion.8) | copy-start | bytes 6148
  (147 other events, 1027.1 us)
Sparse Core Ops, SparseCore 0:
  69.1 91.0 all-gather.6
  169.6 66.6 all-reduce.12
  773.0 67.2 all-reduce.14
  953.5 119.1 all-reduce.16
Sparse Core Ops, SparseCore 1:
  436.5 30.0 all-gather.4
  538.6 24.8 reduce-scatter.4
  575.9 44.0 reduce-scatter.2

commit v9 on v8

--- a/solution.py
+++ b/solution.py
@@ -500,28 +500,32 @@
     ctx_count = lax.axis_size("ctx")
     base_pos = ctx_index * block_len
     low = lambda v: v.astype(jnp.bfloat16)
-    gain_low, attn_in_low = gather_packed(
-        [(low(gains), 1), (low(attention_in), 0)], ("fsdp", "ctx"), shard_count <= 8
-    )
-    later = [
+    dense_pieces = [
+        (low(gains), 1),
+        (low(attention_in), 0),
         (low(attention_out), 1),
         (low(router_weight), 0),
         (low(shared_in), 0),
         (low(shared_down), 1),
     ]
-    if dense_experts:
-        later += [(low(expert_in), 0), (low(expert_down), 0)]
-    later_full = gather_packed(later, ("fsdp", "ctx"))
-    attn_out_low, router_low, shared_in_low, shared_down_low = later_full[:4]
-    if dense_experts:
-        fe_local = expert_down.shape[1]
-        expert_in_all = later_full[4].reshape(experts, model_width, 2, fe_local)
-        expert_down_all = (
-            later_full[5]
-            .reshape(experts, ctx_count, fe_local, model_width // ctx_count)
-            .transpose(0, 2, 1, 3)
-            .reshape(experts, fe_local, model_width)
-        )
+    if shard_count <= 8:
+        dense_full = gather_packed(dense_pieces, ("fsdp", "ctx"), True)
+    else:
+        dense_full = gather_packed(dense_pieces[:2], ("fsdp", "ctx")) + gather_packed(
+            dense_pieces[2:], ("fsdp", "ctx")
+        )
+    gain_low, attn_in_low, attn_out_low, router_low, shared_in_low, shared_down_low = dense_full
+    if ctx_count == 2:
+        flip = lambda v: lax.ppermute(v, "ctx", [(0, 1), (1, 0)])
+        in_pair = [low(expert_in), flip(low(expert_in))]
+        down_pair = [low(expert_down), flip(low(expert_down))]
+        if_first = lambda pair, axis: jnp.where(
+            ctx_index == 0,
+            jnp.concatenate(pair, axis=axis),
+            jnp.concatenate(pair[::-1], axis=axis),
+        )
+        expert_in_low = if_first(in_pair, 1)[0]
+        expert_down_low = if_first(down_pair, 2)[0]
     else:
         expert_in_low = lax.all_gather(low(expert_in), "ctx", axis=1, tiled=True)[0]
         expert_down_low = lax.all_gather(low(expert_down), "ctx", axis=2, tiled=True)[0]

time: 1350 us -> 1420 us (1.052)
  Pallas kernels: 231 us -> 275 us
  blocking collectives: 166 us -> 149 us
  local copies, waits for them, and re-layouts: 340 us -> 356 us
    pallas_call x1, Pallas kernels: 22.7 us -> 66.5 us  [gather_shards(): pl.pallas_call(gather_kernel, out_shape=jax.ShapeDtypeStruct((count, rows...]
    all_gather x2 -> x0, waiting for transfers between devices: 29 us -> none  [the longest x1 28.3 us: gather_packed(): full = lax.all_gather(flat, axes, axis=0, tiled=False)]
    psum x1, waiting for transfers between devices: 46.2 us -> 65.6 us  [local(): lax.psum(jnp.dot(mixed_heads, attn_out_low, preferred_element_type=jnp.fl...]
    ppermute x0 -> x2, waiting for transfers between devices: none -> 17.5 us  [local(): flip = lambda v: lax.ppermute(v, 'ctx', [(0, 1), (1, 0)])]
    all_gather x1 -> x0, blocking collectives: 16.6 us -> none  [local(): lax.all_gather(low(expert_down), 'ctx', axis=2, tiled=True)[0]]
    unnamed x328 -> x321, local copies, waits for them, and re-layouts: 67.2 us -> 63.7 us
  transfers between devices with their start and end apart: 16 -> 16, of which waited for: 7 -> 6; matrix products, arithmetic and copies ran while one was open for 22% -> 21% of each run, Pallas kernels for 12% -> 12%
where the time goes in v9:
time: 1420 us; the launch traced here: 1400 us
  local copies, waits for them, and re-layouts  356 us (25%)
  Pallas kernels  275 us (19%)
  other arithmetic  200 us (14%)
  waiting for transfers between devices  192 us (14%)
  matrix products  159 us (11%)
  blocking collectives  149 us (10%)
  between operations  41.3 us (3%)
  starting transfers between devices  19.2 us (1%)
    pallas_call x1, Pallas kernels, halving_scatter(): pl.pallas_call(halving_kernel, out_shape=jax.ShapeDtypeStruct((rows, 128)...  164 us
    all_to_all x1, blocking collectives, experts_routed(): lax.all_to_all(rows, 'fsdp', split_axis=0, concat_axis=0, tiled=True)  143 us
    pallas_call x1, Pallas kernels, gather_shards(): pl.pallas_call(gather_kernel, out_shape=jax.ShapeDtypeStruct((count, rows...  66.5 us
    psum x1, waiting for transfers between devices, local(): lax.psum(jnp.dot(mixed_heads, attn_out_low, preferred_element_type=jnp.fl...  65.6 us
    unnamed x321, local copies, waits for them, and re-layouts  63.7 us
    all_to_all x1, waiting for transfers between devices, experts_routed(): lax.all_to_all(rows, 'fsdp', split_axis=0, concat_axis=0, tiled=True)  52.7 us
    psum x2, waiting for transfers between devices, local(): lax.psum((shared_out + combined, partial_two, gate_dots), 'tp')  47.8 us
    pallas_call x2, Pallas kernels, butterfly_sum(): pl.pallas_call(butterfly_kernel, out_shape=jax.ShapeDtypeStruct((rows, 12...  43.6 us
  transfers between devices with their start and end apart: 16, of which 6 were waited for; matrix products, arithmetic and copies ran while one was open for 21% of the time, Pallas kernels for 12%

profile of v9, /device:TPU:0, one launch (start us, length us, event | category | flops | bytes accessed | tf_op | source)
XLA Modules:
  0.0 1398.7 jit_solution(1913773041902889599)
XLA Ops:
  23.2 66.5 %shard_map.395 = bf16[8,1744,128]{2,1,0:T(8,128)(2,1)} custom-call(bf16[1744,128]{1,0:T(8,128)(2,1)} %pad_bitcast_fusion.1.x_ref), custom_call_target="tpu_custom_call" | custom-call | tf_op jit(solution)/shard_map/pallas_call | solution.py:312
  142.8 8.6 mul.1201
  153.7 34.1 %while.39 = (s32[]{:T(128)}, bf16[2,512,3,64]{1,3,2,0:T(8,128)(2,1)}, f32[2,3,512,1]{2,1,3,0:T(4,128)}, s32[2]{0:T(128)S(1)}, bf16[2048,3,64]{0,2,1:T(8,128)(2,1...) while((s32[]{:T(128)}, ...), condition=%wide.region_4.5_spmd, body=%wide.region_1.4_spmd.sunk | while | flops 644092928 | bytes 33315144 | solution.py:578
  198.1 8.5 scatter_custom_fusion
  206.6 8.1 scatter_custom_fusion.1
  214.7 65.6 %all-reduce.13.cloned.1.call-done = f32[1024,768]{1,0:T(8,128)} async-done(((f32[1024,768]{1,0:T(8,128)}), f32[1024,768]{1,0:T(8,128)}) %all-reduce.13.cloned.1.call-update) | async-done | bytes 3145744 | tf_op jit(solution)/shard_map/psum | solution.py:580
  286.2 17.8 %gather_fusion = bf16[4096,768]{1,0:T(8,128)(2,1)} fusion(bf16[1024,768]{1,0:T(8,128)(2,1)S(1)} %multiply_convert_fusion.6, s32[4096]{0:T(1024)S(1)} %get-tuple-element.938), kind=kCustom, calls=%fused_computation | custom fusion | bytes 12599296 | tf_op jit(solution)/shard_map/gather | solution.py:418
  308.8 21.4 %gather_fusion.1 = bf16[4096,768]{1,0:T(8,128)(2,1)} fusion(bf16[2048,768]{1,0:T(8,128)(2,1)} %multiply_convert_fusion.3, s32[4096]{0:T(1024)S(1)} %get-tuple-element.937), kind=kCustom, calls=%fused_computation.1 | custom fusion | bytes 12599296 | tf_op jit(solution)/shard_map/gather | solution.py:419
  336.3 142.8 %all_to_all.10 = bf16[4,2,512,768]{3,2,1,0:T(8,128)(2,1)} all-to-all(bf16[4,2,512,768]{3,2,1,0:T(8,128)(2,1)S(1)} %fusion.57), channel_id=1, replica_groups=mesh['fsdp'=4,'ctx'=2,'tp'=4] {'fsdp'}, dimensions={0} | all-to-all | bytes 12582912 | tf_op jit(solution)/shard_map/all_to_all | solution.py:423
  484.1 17.5 %collective-permute-done.4 = bf16[1,384,2,512]{3,2,1,0:T(2,128)(2,1)S(1)} collective-permute-done((bf16[1,384,2,512]{3,2,1,0:T(2,128)(2,1)S(1)}, bf16[1,384,2,512]{3,2,1,0:T(2,128)(2,1)S(1)}, u32[]{:S(2)}, u32[]{:S(2)}) %collective-permute-start.4) | collective-permute-done | bytes 786464 | tf_op jit(solution)/shard_map/ppermute | solution.py:519
  501.6 7.5 broadcast_select_fusion
  540.7 14.3 %fusion.56 = (f32[4096,1,512]{2,0,1:T(8,128)}, f32[4096,1,512]{2,0,1:T(8,128)}) fusion(f32[4096,2,512]{2,0,1:T(8,128)} %copy-done.16, bf16[4096,768]{1,0:T(8,128)(2,1)} %bitcast.471, bf16[512,384]{1,0:T(8,128)(2,1)S(1)} %bitcast.532, bf16[512,384]{1,0:T(8,128)(2,1)S(1)} %bitcast.501, pred[]{:T(512)S(6)} %eq.146), kind=kOutput, calls=%fused_computation.84 | convolution fusion | flops 3249930240 | bytes 40632320 | tf_op jit(solution)/shard_map/rd,fd->rf/dot_general | solution.py:438
  555.0 8.4 fusion.62
  577.3 9.7 convolution_bitcast_fusion
  594.3 7.9 fusion.107
  623.7 12.2 convolution_bitcast_fusion.1
  709.5 52.7 %all-to-all-done.1 = bf16[4,2,512,768]{3,2,1,0:T(8,128)(2,1)} async-done(((bf16[4,2,512,768]{3,2,1,0:T(8,128)(2,1)}), bf16[4,2,512,768]{3,2,1,0:T(8,128)(2,1)}, u32[]{:S(2)}, u32[]{:S(2)}) %all-to-all-start.1) | async-done | bytes 6291488 | tf_op jit(solution)/shard_map/all_to_all | solution.py:423
  768.2 12.4 gather_fusion.2
  780.6 7.8 reshape.1449
  788.4 12.4 gather_fusion.3
  800.8 7.9 reshape.1450
  808.7 20.7 %select_reduce_fusion = (f32[1024,768]{1,0:T(8,128)S(1)}, f32[1024,768]{1,0:T(8,128)}) fusion(f32[1024,2,768]{2,1,0:T(2,128)} %reshape.1450, pred[1024,2]{1,0:T(8,128)(4,1)S(1)} %copy-done.73, f32[1024,2,768]{2,1,0:T(2,128)} %reshape.1449, f32[1024,2]{1,0:T(8,128)S(1)} %copy-done.38), kind=kLoop, calls=%fused_computation.95 | loop fusion | flops 6291456 | bytes 18884608 | tf_op jit(solution)/shard_map/reduce_sum | solution.py:465
  852.5 47.8 %all-reduce.15.cloned.1.call-done = f32[1024,768]{1,0:T(8,128)} async-done(((f32[1024,768]{1,0:T(8,128)}), f32[1024,768]{1,0:T(8,128)}) %all-reduce.15.cloned.1.call-update) | async-done | bytes 3145744 | tf_op jit(solution)/shard_map/psum | solution.py:627
  910.1 76.7 %while.40 = (s32[]{:T(128)}, f32[2048,3,64]{0,2,1:T(8,128)}, f32[2048,3,64]{0,2,1:T(8,128)S(1)}, f32[1024,3,64]{0,2,1:T(8,128)}, bf16[1024,3,64]{0,2,1:T(8,128)(...) while((s32[]{:T(128)}, f32[2048,3,64]{0,2,1:T(8,128)}, ...), condition=%wide.region_26.27_spmd, body=%wide.region_24.26_spmd.sunk | while | flops 1541608448 | bytes 106823088 | solution.py:729
  918.2 8.8 multiply_reduce_fusion.22
  927.0 9.5 multiply_convert_fusion.9
  956.5 8.8 multiply_reduce_fusion.22
  965.4 9.5 multiply_convert_fusion.9
  1040.2 164.5 %shard_map.396 = f32[1792,128]{1,0:T(8,128)} custom-call(f32[4,2,1792,128]{3,2,1,0:T(8,128)} %bitcast.447), custom_call_target="tpu_custom_call" | custom-call | tf_op jit(solution)/shard_map/pallas_call | solution.py:244
  1249.0 29.7 %shard_map.397 = f32[344,128]{1,0:T(8,128)} custom-call(f32[344,128]{1,0:T(8,128)} %pad_bitcast_fusion.2.x_ref), custom_call_target="tpu_custom_call" | custom-call | tf_op jit(solution)/shard_map/pallas_call | solution.py:162
  1286.8 7.8 slice.490
  1342.8 13.9 shard_map.398
  (692 shorter events, 518.6 us)
Async XLA Ops:
  7.2 273.1 %all-reduce.13.cloned.1.call-start = ((), (), s32[]{:S(2)}) async-start(), calls=%async_computation.4 | async-start | bytes 6291456 | tf_op jit(solution)/shard_map/psum | solution.py:580
  110.6 40.8 %collective-permute-start.2 = (bf16[1024,3,64]{0,2,1:T(8,128)(2,1)}, bf16[1024,3,64]{0,2,1:T(8,128)(2,1)}, u32[]{:S(2)}, u32[]{:S(2)}) collective-permute-start(bf16[1024,3,64]{0,2,1:T(8,128)(2,1)} %pad_maximum_fusion.4), channel_id=1, source_target_pairs={{0,4},{1,5},{2,6},{3,7},{8,12},{9,13},{10,14},{11,15},{16,20},{17,... | collective-permute-start | bytes 1179656 | tf_op jit(solution)/shard_map/ppermute | solution.py:27
  116.9 35.6 %collective-permute-start = (bf16[1024,3,64]{0,2,1:T(8,128)(2,1)S(1)}, bf16[1024,3,64]{0,2,1:T(8,128)(2,1)}, u32[]{:S(2)}, u32[]{:S(2)}) collective-permute-start(bf16[1024,3,64]{0,2,1:T(8,128)(2,1)S(1)} %bitcast.493), channel_id=1, source_target_pairs={{0,4},{1,5},{2,6},{3,7},{8,12},{9,13},{10,14},{11,15},{16,20},{17,... | collective-permute-start | bytes 1179656 | tf_op jit(solution)/shard_map/ppermute | solution.py:27
  119.1 32.3 %collective-permute-start.1 = (bf16[1024]{0:T(1024)(128)(2,1)S(1)}, bf16[1024]{0:T(1024)(128)(2,1)S(1)}, u32[]{:S(2)}, u32[]{:S(2)}) collective-permute-start(bf16[1024]{0:T(1024)(128)(2,1)S(1)} %convert_reduce_fusion), channel_id=1, source_target_pairs={{0,4},{1,5},{2,6},{3,7},{8,12},{9,13},{10,14},{11,15},{16,20},{17,... | collective-permute-start | bytes 6152 | tf_op jit(solution)/shard_map/ppermute | solution.py:27
  187.8 95.3 %copy-start.82 = (bf16[2048]{0:T(1024)(128)(2,1)}, bf16[2048]{0:T(1024)(128)(2,1)S(1)}, u32[]{:S(2)}) copy-start(bf16[2048]{0:T(1024)(128)(2,1)S(1)} %get-tuple-element.1257) | copy-start | bytes 12292
  187.8 95.3 %copy-start.89 = (bf16[1024]{0:T(1024)(128)(2,1)}, bf16[1024]{0:T(1024)(128)(2,1)S(1)}, u32[]{:S(2)}) copy-start(bf16[1024]{0:T(1024)(128)(2,1)S(1)} %get-tuple-element.1256) | copy-start | bytes 6148
  193.7 507.6 %reduce-scatter.5.cloned.1.call-start = ((), (), s32[]{:S(2)}) async-start(), calls=%async_computation.7 | async-start | bytes 2359296 | tf_op jit(solution)/shard_map/reduce_scatter | solution.py:673
  197.4 85.3 %copy-start.93 = (s32[2048]{0:T(1024)}, s32[2048]{0:T(1024)S(1)}, u32[]{:S(2)}) copy-start(s32[2048]{0:T(1024)S(1)} %fusion.143) | copy-start | bytes 24580
  214.7 68.0 %copy-start.95 = (f32[768]{0:T(1024)S(1)}, f32[768]{0:T(1024)}, u32[]{:S(2)}) copy-start(f32[768]{0:T(1024)} %reshape.1448) | copy-start | bytes 9220
  336.2 142.8 %copy-start.35 = (f32[1,384,2,512]{3,2,1,0:T(2,128)S(1)}, f32[1,384,2,512]{3,2,1,0:T(2,128)}, u32[]{:S(2)}) copy-start(f32[1,384,2,512]{3,2,1,0:T(2,128)} %param.34) | copy-start | bytes 4718596
  336.2 146.5 %copy-start.48 = (f32[1,512,384]{2,1,0:T(8,128)S(1)}, f32[1,512,384]{2,1,0:T(8,128)}, u32[]{:S(2)}) copy-start(f32[1,512,384]{2,1,0:T(8,128)} %param.35) | copy-start | bytes 2359300
  479.0 33.9 %collective-permute-start.3 = (bf16[4,2,512,768]{3,2,1,0:T(8,128)(2,1)}, bf16[4,2,512,768]{3,2,1,0:T(8,128)(2,1)}, u32[]{:S(2)}, u32[]{:S(2)}) collective-permute-start(bf16[4,2,512,768]{3,2,1,0:T(8,128)(2,1)} %all_to_all.10), channel_id=1, source_target_pairs={{0,1},{1,0},{2,3},{3,2},{4,5},{5,4},{6,7},{7,6},{8,9},{9,8},{10,11... | collective-permute-start | bytes 18874376 | tf_op jit(solution)/shard_map/ppermute | solution.py:425
  481.3 20.3 %collective-permute-start.4 = (bf16[1,384,2,512]{3,2,1,0:T(2,128)(2,1)S(1)}, bf16[1,384,2,512]{3,2,1,0:T(2,128)(2,1)S(1)}, u32[]{:S(2)}, u32[]{:S(2)}) collective-permute-start(bf16[1,384,2,512]{3,2,1,0:T(2,128)(2,1)S(1)} %get-tuple-element.891), channel_id=1, source_target_pairs={{0,4},{4,0},{1,5},{5,1},{2,6},{6,2},{3,7},{7,3},{8,12},{12,8},{9,1... | collective-permute-start | bytes 2359304 | tf_op jit(solution)/shard_map/ppermute | solution.py:519
  483.5 57.1 %collective-permute-start.5 = (bf16[1,512,384]{2,1,0:T(8,128)(2,1)S(1)}, bf16[1,512,384]{2,1,0:T(8,128)(2,1)S(1)}, u32[]{:S(2)}, u32[]{:S(2)}) collective-permute-start(bf16[1,512,384]{2,1,0:T(8,128)(2,1)S(1)} %get-tuple-element.901), channel_id=1, source_target_pairs={{0,4},{4,0},{1,5},{5,1},{2,6},{6,2},{3,7},{7,3},{8,12},{12,8},{9,1... | collective-permute-start | bytes 1179656 | tf_op jit(solution)/shard_map/ppermute | solution.py:519
  570.1 32.2 %collective-permute-start.6 = (f32[4,512,768]{2,1,0:T(8,128)}, f32[4,512,768]{2,1,0:T(8,128)}, u32[]{:S(2)}, u32[]{:S(2)}) collective-permute-start(f32[4,512,768]{2,1,0:T(8,128)} %slice.553), channel_id=1, source_target_pairs={{0,1},{1,0},{2,3},{3,2},{4,5},{5,4},{6,7},{7,6},{8,9},{9,8},{10,11... | collective-permute-start | bytes 18874376 | tf_op jit(solution)/shard_map/ppermute | solution.py:425
  593.8 13.9 collective-permute-start.7
  618.4 143.9 %all-to-all-start.1 = ((bf16[4,2,512,768]{3,2,1,0:T(8,128)(2,1)}), bf16[4,2,512,768]{3,2,1,0:T(8,128)(2,1)}, u32[]{:S(2)}, u32[]{:S(2)}) async-start(bf16[4,2,512,768]{3,2,1,0:T(8,128)(2,1)} %copy.234), calls=%async_computation.1 | async-start | bytes 12582912 | tf_op jit(solution)/shard_map/all_to_all | solution.py:423
  623.6 79.0 %reduce-scatter.3.cloned.1.call-start = ((), (), s32[]{:S(2)}) async-start(), calls=%async_computation.6 | async-start | bytes 4718592 | tf_op jit(solution)/shard_map/reduce_scatter | solution.py:672
  635.9 264.4 %all-reduce.15.cloned.1.call-start = ((), (), s32[]{:S(2)}) async-start(), calls=%async_computation.5 | async-start | bytes 6291456 | tf_op jit(solution)/shard_map/psum | solution.py:627
  833.0 406.7 %all-reduce.17.cloned.1.call-start = ((), (), s32[]{:S(2)}) async-start(), calls=%async_computation.8 | async-start | bytes 12582912 | tf_op jit(solution)/shard_map/psum | solution.py:627
  847.2 53.1 %copy-start.4 = (f32[1024,768]{1,0:T(8,128)S(1)}, f32[1024,768]{1,0:T(8,128)}, u32[]{:S(2)}) copy-start(f32[1024,768]{1,0:T(8,128)} %copy-done.3) | copy-start | bytes 9437188
  847.2 53.1 %copy-start.60 = (bf16[768,4]{1,0:T(8,128)(2,1)S(1)}, bf16[768,4]{1,0:T(8,128)(2,1)}, u32[]{:S(2)}) copy-start(bf16[768,4]{1,0:T(8,128)(2,1)} %reshape_reshape.22) | copy-start | bytes 18436
  847.2 53.1 %copy-start.96 = (f32[768]{0:T(1024)S(1)}, f32[768]{0:T(1024)}, u32[]{:S(2)}) copy-start(f32[768]{0:T(1024)} %reshape.1448) | copy-start | bytes 9220
  847.2 53.1 %copy-start.98 = (f32[1024]{0:T(1024)S(1)}, f32[1024]{0:T(1024)}, u32[]{:S(2)}) copy-start(f32[1024]{0:T(1024)} %copy-done.97) | copy-start | bytes 12292
  852.5 51.6 %copy-start.104 = (f32[1024]{0:T(1024)S(1)}, f32[1024]{0:T(1024)}, u32[]{:S(2)}) copy-start(f32[1024]{0:T(1024)} %copy-done.103) | copy-start | bytes 12292
  988.0 14.0 %collective-permute-start.8 = (bf16[1024,3,64]{0,2,1:T(8,128)(2,1)S(1)}, bf16[1024,3,64]{0,2,1:T(8,128)(2,1)}, u32[]{:S(2)}, u32[]{:S(2)}) collective-permute-start(bf16[1024,3,64]{0,2,1:T(8,128)(2,1)S(1)} %slice.674), channel_id=1, source_target_pairs={{4,0},{5,1},{6,2},{7,3},{12,8},{13,9},{14,10},{15,11},{20,16},{21,... | collective-permute-start | bytes 1179656 | tf_op jit(solution)/shard_map/ppermute | solution.py:27
  990.1 19.1 %collective-permute-start.9 = (bf16[1024,3,64]{0,2,1:T(8,128)(2,1)}, bf16[1024,3,64]{0,2,1:T(8,128)(2,1)}, u32[]{:S(2)}, u32[]{:S(2)}) collective-permute-start(bf16[1024,3,64]{0,2,1:T(8,128)(2,1)} %slice.673), channel_id=1, source_target_pairs={{4,0},{5,1},{6,2},{7,3},{12,8},{13,9},{14,10},{15,11},{20,16},{21,... | collective-permute-start | bytes 1179656 | tf_op jit(solution)/shard_map/ppermute | solution.py:27
  1294.6 40.9 %copy-start.13 = (f32[1,384,2,512]{3,1,2,0:T(8,128)S(1)}, f32[1,384,2,512]{3,1,2,0:T(8,128)}, u32[]{:S(2)}) copy-start(f32[1,384,2,512]{3,1,2,0:T(8,128)} %reduce-scatter.3.cloned.1.call-done) | copy-start | bytes 4718596
  1294.6 42.7 %copy-start.30 = (f32[1,512,384]{2,1,0:T(8,128)S(1)}, f32[1,512,384]{2,1,0:T(8,128)}, u32[]{:S(2)}) copy-start(f32[1,512,384]{2,1,0:T(8,128)} %reduce-scatter.5.cloned.1.call-done) | copy-start | bytes 2359300
  1299.8 74.7 %copy-start.101 = (f32[3,192]{1,0:T(4,128)}, f32[3,192]{1,0:T(4,128)S(1)}, u32[]{:S(2)}) copy-start(f32[3,192]{1,0:T(4,128)S(1)} %fusion.162) | copy-start | bytes 6916
  1317.9 43.0 %copy-start.122 = (f32[384]{0:T(512)S(1)}, f32[384]{0:T(512)}, u32[]{:S(2)}) copy-start(f32[384]{0:T(512)} %get-tuple-element.933) | copy-start | bytes 4612
  1324.9 35.9 %copy-start.124 = (f32[192]{0:T(256)}, f32[192]{0:T(256)S(1)}, u32[]{:S(2)}) copy-start(f32[192]{0:T(256)S(1)} %multiply_add_fusion.9) | copy-start | bytes 2308
  (146 other events, 1127.4 us)
Sparse Core Ops, SparseCore 0:
  193.8 86.5 all-reduce.12
  602.4 24.9 reduce-scatter.4
  636.0 44.0 reduce-scatter.2
  833.1 67.1 all-reduce.14
  1013.5 119.1 all-reduce.16

commit v10 on v8

--- a/solution.py
+++ b/solution.py
@@ -180,8 +180,10 @@
     return results
 
 
-def halving_kernel(x_ref, o_ref, stage_one, stage_two, inbox_one, inbox_two, inbox_three, sems):
-    rows = o_ref.shape[0]
+def halving_kernel(
+    x_ref, o_ref, stage_a, stage_a2, stage_b, stage_b2, in_a1, in_a2, in_a3, in_b1, in_b2, in_b3, sems
+):
+    rows = o_ref.shape[0] // 2
     chunk = 64
     fsdp_here = lax.axis_index("fsdp")
     ctx_here = lax.axis_index("ctx")
@@ -197,69 +199,107 @@
     for partner in partners:
         pl.semaphore_signal(barrier, 1, device_id=partner, device_id_type=pl.DeviceIdType.MESH)
     pl.semaphore_wait(barrier, len(partners))
-
-    def swap(src, dst, number, partner):
-        copy = pltpu.make_async_remote_copy(
-            src_ref=src,
-            dst_ref=dst,
-            send_sem=sems.at[0, number],
-            recv_sem=sems.at[1, number],
-            device_id=partner,
-            device_id_type=pl.DeviceIdType.MESH,
-        )
-        copy.start()
-        copy.wait()
-
-    swap(x_ref.at[:, pl.ds(1 - ctx_here, 1)], inbox_one, 0, partners[0])
-
-    @pl.loop(0, rows // chunk)
-    def _(step):
-        part = pl.ds(pl.multiple_of(step * chunk, chunk), chunk)
+    first, second = pl.ds(0, rows), pl.ds(rows, rows)
+
+    def swap_pair(sources, targets, number, partner_pair):
+        copies = []
+        for index in range(2):
+            copy = pltpu.make_async_remote_copy(
+                src_ref=sources[index],
+                dst_ref=targets[index],
+                send_sem=sems.at[0, 2 * number + index],
+                recv_sem=sems.at[1, 2 * number + index],
+                device_id=partner_pair[index],
+                device_id_type=pl.DeviceIdType.MESH,
+            )
+            copy.start()
+            copies.append(copy)
+        for copy in copies:
+            copy.wait()
+
+    def each_chunk(body):
+        @pl.loop(0, rows // chunk)
+        def _(step):
+            body(pl.ds(pl.multiple_of(step * chunk, chunk), chunk))
+
+    swap_pair(
+        [
+            x_ref.at[:, :, pl.ds(1 - ctx_here, 1), first],
+            x_ref.at[:, pl.ds(1 - bit_low, 1), :, second],
+        ],
+        [in_a1, in_b1],
+        0,
+        [partners[0], partners[1]],
+    )
+
+    def round_one(part):
+        shifted = pl.ds(part.start + rows, chunk)
         for high in range(2):
-            for low in range(2):
-                stage_one[high, low, part] = (
-                    x_ref[2 * high + low, ctx_here, part] + inbox_one[2 * high + low, 0, part]
+            for other in range(2):
+                stage_a[high, other, part] = (
+                    x_ref[high, other, ctx_here, part] + in_a1[high, other, 0, part]
                 )
-
-    swap(stage_one.at[:, pl.ds(1 - bit_low, 1)], inbox_two, 1, partners[1])
-
-    @pl.loop(0, rows // chunk)
-    def _(step):
-        part = pl.ds(pl.multiple_of(step * chunk, chunk), chunk)
+                stage_b[high, other, part] = (
+                    x_ref[high, bit_low, other, shifted] + in_b1[high, 0, other, part]
+                )
+
+    each_chunk(round_one)
+    swap_pair(
+        [stage_a.at[:, pl.ds(1 - bit_low, 1)], stage_b.at[:, pl.ds(1 - ctx_here, 1)]],
+        [in_a2, in_b2],
+        1,
+        [partners[1], partners[0]],
+    )
+
+    def round_two(part):
         for high in range(2):
-            stage_two[high, part] = stage_one[high, bit_low, part] + inbox_two[high, 0, part]
-
-    swap(stage_two.at[pl.ds(1 - bit_high, 1)], inbox_three, 2, partners[2])
-
-    @pl.loop(0, rows // chunk)
-    def _(step):
-        part = pl.ds(pl.multiple_of(step * chunk, chunk), chunk)
-        o_ref[part] = stage_two[bit_high, part] + inbox_three[0, part]
+            stage_a2[high, part] = stage_a[high, bit_low, part] + in_a2[high, 0, part]
+            stage_b2[high, part] = stage_b[high, ctx_here, part] + in_b2[high, 0, part]
+
+    each_chunk(round_two)
+    swap_pair(
+        [stage_a2.at[pl.ds(1 - bit_high, 1)], stage_b2.at[pl.ds(1 - bit_high, 1)]],
+        [in_a3, in_b3],
+        2,
+        [partners[2], partners[2]],
+    )
+
+    def round_three(part):
+        o_ref[part] = stage_a2[bit_high, part] + in_a3[0, part]
+        o_ref[pl.ds(part.start + rows, chunk)] = stage_b2[bit_high, part] + in_b3[0, part]
+
+    each_chunk(round_three)
 
 
 def halving_scatter(packed, collective_id):
     count, width = packed.shape
-    rows = -(-width // (128 * 64)) * 64
-    block = jnp.pad(packed, ((0, 0), (0, rows * 128 - width))).reshape(count // 2, 2, rows, 128)
+    rows = -(-width // (128 * 128)) * 64
+    block = jnp.pad(packed, ((0, 0), (0, 2 * rows * 128 - width))).reshape(
+        2, 2, 2, 2 * rows, 128
+    )
     own = pl.pallas_call(
         halving_kernel,
-        out_shape=jax.ShapeDtypeStruct((rows, 128), jnp.float32),
+        out_shape=jax.ShapeDtypeStruct((2 * rows, 128), jnp.float32),
         in_specs=[pl.BlockSpec(memory_space=pltpu.VMEM)],
         out_specs=pl.BlockSpec(memory_space=pltpu.VMEM),
         scratch_shapes=[
             pltpu.VMEM((2, 2, rows, 128), jnp.float32),
             pltpu.VMEM((2, rows, 128), jnp.float32),
-            pltpu.VMEM((count // 2, 1, rows, 128), jnp.float32),
+            pltpu.VMEM((2, 2, rows, 128), jnp.float32),
+            pltpu.VMEM((2, rows, 128), jnp.float32),
+            pltpu.VMEM((2, 2, 1, rows, 128), jnp.float32),
             pltpu.VMEM((2, 1, rows, 128), jnp.float32),
             pltpu.VMEM((1, rows, 128), jnp.float32),
-            pltpu.SemaphoreType.DMA((2, 3)),
+            pltpu.VMEM((2, 1, 2, rows, 128), jnp.float32),
+            pltpu.VMEM((2, 1, rows, 128), jnp.float32),
+            pltpu.VMEM((1, rows, 128), jnp.float32),
+            pltpu.SemaphoreType.DMA((2, 6)),
         ],
         compiler_params=pltpu.CompilerParams(
             collective_id=collective_id, has_side_effects=True, vmem_limit_bytes=60 * 1024 * 1024
         ),
     )(block)
     return own.reshape(-1)[:width]
-
 
 def gather_kernel(x_ref, o_ref, inbox, send_sems, recv_sems):
     fsdp_here = lax.axis_index("fsdp")

time: 1350 us -> 1290 us (0.956)
  Pallas kernels: 231 us -> 172 us
    pallas_call x1, Pallas kernels: 164 us -> 105 us  [halving_scatter(): pl.pallas_call(halving_kernel, out_shape=jax.ShapeDtypeStruct((2 * rows,...]
  transfers between devices with their start and end apart: 16 -> 16, of which waited for: 7 -> 7; matrix products, arithmetic and copies ran while one was open for 22% -> 23% of each run, Pallas kernels for 12% -> 8%
where the time goes in v10:
time: 1290 us; the launch traced here: 1280 us
  local copies, waits for them, and re-layouts  340 us (26%)
  other arithmetic  200 us (16%)
  waiting for transfers between devices  178 us (14%)
  Pallas kernels  172 us (13%)
  blocking collectives  166 us (13%)
  matrix products  155 us (12%)
  between operations  43.1 us (3%)
  starting transfers between devices  17.1 us (1%)
    all_to_all x1, blocking collectives, experts_routed(): lax.all_to_all(rows, 'fsdp', split_axis=0, concat_axis=0, tiled=True)  143 us
    pallas_call x1, Pallas kernels, halving_scatter(): pl.pallas_call(halving_kernel, out_shape=jax.ShapeDtypeStruct((2 * rows,...  105 us
    unnamed x328, local copies, waits for them, and re-layouts  67.2 us
    psum x2, waiting for transfers between devices, local(): lax.psum((shared_out + combined, partial_two, gate_dots), 'tp')  47.9 us
    all_to_all x1, waiting for transfers between devices, experts_routed(): lax.all_to_all(rows, 'fsdp', split_axis=0, concat_axis=0, tiled=True)  46.2 us
    psum x1, waiting for transfers between devices, local(): lax.psum(jnp.dot(mixed_heads, attn_out_low, preferred_element_type=jnp.fl...  46.2 us
    pallas_call x2, Pallas kernels, butterfly_sum(): pl.pallas_call(butterfly_kernel, out_shape=jax.ShapeDtypeStruct((rows, 12...  44.6 us
    all_gather x1, waiting for transfers between devices, gather_packed(): full = lax.all_gather(flat, axes, axis=0, tiled=False)  28.3 us
  transfers between devices with their start and end apart: 16, of which 7 were waited for; matrix products, arithmetic and copies ran while one was open for 23% of the time, Pallas kernels for 8%

profile of v10, /device:TPU:0, one launch (start us, length us, event | category | flops | bytes accessed | tf_op | source)
XLA Modules:
  0.0 1278.7 jit_solution(4934906293719673892)
XLA Ops:
  12.4 22.7 %shard_map.395 = bf16[8,448,128]{2,1,0:T(8,128)(2,1)} custom-call(bf16[448,128]{1,0:T(8,128)(2,1)} %fusion.143.x_ref), custom_call_target="tpu_custom_call" | custom-call | tf_op jit(solution)/shard_map/pallas_call | solution.py:352
  83.6 8.6 mul.1199
  94.5 34.1 %while.39 = (s32[]{:T(128)}, bf16[2,512,3,64]{1,3,2,0:T(8,128)(2,1)}, f32[2,3,512,1]{2,1,3,0:T(4,128)}, s32[2]{0:T(128)S(1)}, bf16[2048,3,64]{0,2,1:T(8,128)(2,1...) while((s32[]{:T(128)}, ...), condition=%wide.region_4.5_spmd, body=%wide.region_1.4_spmd.sunk | while | flops 644092928 | bytes 33315144 | solution.py:614
  131.9 28.3 %all-gather.7.cloned.1.call-done = bf16[8,1,166272]{2,1,0:T(2,128)(2,1)} async-done(((bf16[1,1,166272]{2,1,0:T(2,128)(2,1)}), bf16[8,1,166272]{2,1,0:T(2,128)(2,1)}) %all-gather.7.cloned.1.call-update) | async-done | bytes 2660368 | tf_op jit(solution)/shard_map/all_gather | solution.py:376
  172.8 8.1 scatter_custom_fusion
  180.8 8.1 scatter_custom_fusion.1
  190.1 46.2 %all-reduce.13.cloned.1.call-done = f32[1024,768]{1,0:T(8,128)} async-done(((f32[1024,768]{1,0:T(8,128)}), f32[1024,768]{1,0:T(8,128)}) %all-reduce.13.cloned.1.call-update) | async-done | bytes 3145744 | tf_op jit(solution)/shard_map/psum | solution.py:616
  242.6 17.8 %gather_fusion = bf16[4096,768]{1,0:T(8,128)(2,1)} fusion(bf16[1024,768]{1,0:T(8,128)(2,1)S(1)} %multiply_convert_fusion.3, s32[4096]{0:T(1024)S(1)} %get-tuple-element.934), kind=kCustom, calls=%fused_computation | custom fusion | bytes 12599296 | tf_op jit(solution)/shard_map/gather | solution.py:458
  265.2 21.4 %gather_fusion.1 = bf16[4096,768]{1,0:T(8,128)(2,1)} fusion(bf16[2048,768]{1,0:T(8,128)(2,1)} %multiply_convert_fusion.2, s32[4096]{0:T(1024)S(1)} %get-tuple-element.933), kind=kCustom, calls=%fused_computation.1 | custom fusion | bytes 12599296 | tf_op jit(solution)/shard_map/gather | solution.py:459
  292.6 142.6 %all_to_all.10 = bf16[4,2,512,768]{3,2,1,0:T(8,128)(2,1)} all-to-all(bf16[4,2,512,768]{3,2,1,0:T(8,128)(2,1)S(1)} %fusion.57), channel_id=1, replica_groups=mesh['fsdp'=4,'ctx'=2,'tp'=4] {'fsdp'}, dimensions={0} | all-to-all | bytes 12582912 | tf_op jit(solution)/shard_map/all_to_all | solution.py:463
  437.3 16.6 %all_gather.15 = bf16[1,512,768]{2,1,0:T(8,128)(2,1)S(1)} all-gather(bf16[1,512,384]{2,1,0:T(8,128)(2,1)S(1)} %get-tuple-element.897), channel_id=1, replica_groups=mesh['fsdp'=4,'ctx'=2,'tp'=4] {'ctx'}, dimensions={2}, use_global_device_ids=true | all-gather | bytes 1179648 | tf_op jit(solution)/shard_map/all_gather | solution.py:567
  466.5 9.3 fusion.94
  481.6 14.2 %fusion.56 = (f32[4096,1,512]{2,0,1:T(8,128)}, f32[4096,1,512]{2,0,1:T(8,128)}) fusion(f32[4096,2,512]{2,0,1:T(8,128)} %copy-done.17, bf16[4096,768]{1,0:T(8,128)(2,1)} %bitcast.476, bf16[1,512,768]{2,1,0:T(8,128)(2,1)S(1)} %all_gather.15), kind=kOutput, calls=%fused_computation.84 | convolution fusion | flops 3246391296 | bytes 40632320 | tf_op jit(solution)/shard_map/rd,fd->rf/dot_general | solution.py:478
  505.7 9.2 add_convert_fusion
  514.9 10.0 convolution_bitcast_fusion
  563.6 12.2 convolution_bitcast_fusion.1
  656.0 46.2 %all-to-all-done.1 = bf16[4,2,512,768]{3,2,1,0:T(8,128)(2,1)} async-done(((bf16[4,2,512,768]{3,2,1,0:T(8,128)(2,1)}), bf16[4,2,512,768]{3,2,1,0:T(8,128)(2,1)}, u32[]{:S(2)}, u32[]{:S(2)}) %all-to-all-start.1) | async-done | bytes 6291488 | tf_op jit(solution)/shard_map/all_to_all | solution.py:463
  708.2 12.4 gather_fusion.2
  720.5 7.8 reshape.1408
  728.4 12.4 gather_fusion.3
  740.7 7.9 reshape.1409
  748.6 20.7 %select_reduce_fusion = (f32[1024,768]{1,0:T(8,128)S(1)}, f32[1024,768]{1,0:T(8,128)}) fusion(f32[1024,2,768]{2,1,0:T(2,128)} %reshape.1409, pred[1024,2]{1,0:T(8,128)(4,1)S(1)} %copy-done.66, f32[1024,2,768]{2,1,0:T(2,128)} %reshape.1408, f32[1024,2]{1,0:T(8,128)S(1)} %copy-done.33), kind=kLoop, calls=%fused_computation.94 | loop fusion | flops 6291456 | bytes 18884608 | tf_op jit(solution)/shard_map/reduce_sum | solution.py:505
  792.3 47.9 %all-reduce.15.cloned.1.call-done = f32[1024,768]{1,0:T(8,128)} async-done(((f32[1024,768]{1,0:T(8,128)}), f32[1024,768]{1,0:T(8,128)}) %all-reduce.15.cloned.1.call-update) | async-done | bytes 3145744 | tf_op jit(solution)/shard_map/psum | solution.py:663
  850.0 76.7 %while.40 = (s32[]{:T(128)}, f32[2048,3,64]{0,2,1:T(8,128)}, f32[2048,3,64]{0,2,1:T(8,128)S(1)}, f32[1024,3,64]{0,2,1:T(8,128)}, bf16[1024,3,64]{0,2,1:T(8,128)(...) while((s32[]{:T(128)}, f32[2048,3,64]{0,2,1:T(8,128)}, ...), condition=%wide.region_26.27_spmd, body=%wide.region_24.26_spmd.sunk | while | flops 1541608448 | bytes 106823088 | solution.py:765
  858.2 8.8 multiply_reduce_fusion.22
  867.0 9.5 multiply_convert_fusion.6
  896.5 8.8 multiply_reduce_fusion.22
  905.3 9.5 multiply_convert_fusion.6
  980.1 105.1 %shard_map.396 = f32[1792,128]{1,0:T(8,128)} custom-call(f32[2,2,2,1792,128]{4,3,2,1,0:T(8,128)} %bitcast.459), custom_call_target="tpu_custom_call" | custom-call | tf_op jit(solution)/shard_map/pallas_call | solution.py:280
  1107.7 29.1 %shard_map.397 = f32[344,128]{1,0:T(8,128)} custom-call(f32[344,128]{1,0:T(8,128)} %pad_bitcast_fusion.1.x_ref), custom_call_target="tpu_custom_call" | custom-call | tf_op jit(solution)/shard_map/pallas_call | solution.py:162
  1145.6 7.8 slice.486
  1221.2 15.6 %shard_map.398 = f32[8,128]{1,0:T(8,128)} custom-call(f32[8,128]{1,0:T(8,128)} %pad_bitcast_fusion.2.x_ref), custom_call_target="tpu_custom_call" | custom-call | tf_op jit(solution)/shard_map/pallas_call | solution.py:162
  (699 shorter events, 503.2 us)
Async XLA Ops:
  8.0 152.2 %all-gather.7.cloned.1.call-start = ((), (), s32[]{:S(2)}) async-start(), calls=%async_computation.9 | async-start | bytes 5985792 | tf_op jit(solution)/shard_map/all_gather | solution.py:376
  49.8 42.5 %collective-permute-start.2 = (bf16[1024,3,64]{0,2,1:T(8,128)(2,1)}, bf16[1024,3,64]{0,2,1:T(8,128)(2,1)}, u32[]{:S(2)}, u32[]{:S(2)}) collective-permute-start(bf16[1024,3,64]{0,2,1:T(8,128)(2,1)} %pad_maximum_fusion.4), channel_id=1, source_target_pairs={{0,4},{1,5},{2,6},{3,7},{8,12},{9,13},{10,14},{11,15},{16,20},{17,... | collective-permute-start | bytes 1179656 | tf_op jit(solution)/shard_map/ppermute | solution.py:27
  56.1 37.2 %collective-permute-start = (bf16[1024,3,64]{0,2,1:T(8,128)(2,1)S(1)}, bf16[1024,3,64]{0,2,1:T(8,128)(2,1)}, u32[]{:S(2)}, u32[]{:S(2)}) collective-permute-start(bf16[1024,3,64]{0,2,1:T(8,128)(2,1)S(1)} %bitcast.500), channel_id=1, source_target_pairs={{0,4},{1,5},{2,6},{3,7},{8,12},{9,13},{10,14},{11,15},{16,20},{17,... | collective-permute-start | bytes 1179656 | tf_op jit(solution)/shard_map/ppermute | solution.py:27
  58.2 34.0 %collective-permute-start.1 = (bf16[1024]{0:T(1024)(128)(2,1)S(1)}, bf16[1024]{0:T(1024)(128)(2,1)S(1)}, u32[]{:S(2)}, u32[]{:S(2)}) collective-permute-start(bf16[1024]{0:T(1024)(128)(2,1)S(1)} %convert_reduce_fusion), channel_id=1, source_target_pairs={{0,4},{1,5},{2,6},{3,7},{8,12},{9,13},{10,14},{11,15},{16,20},{17,... | collective-permute-start | bytes 6152 | tf_op jit(solution)/shard_map/ppermute | solution.py:27
  69.0 167.3 %all-reduce.13.cloned.1.call-start = ((), (), s32[]{:S(2)}) async-start(), calls=%async_computation.4 | async-start | bytes 6291456 | tf_op jit(solution)/shard_map/psum | solution.py:616
  128.6 40.9 %copy-start.79 = (bf16[2048]{0:T(1024)(128)(2,1)}, bf16[2048]{0:T(1024)(128)(2,1)S(1)}, u32[]{:S(2)}) copy-start(bf16[2048]{0:T(1024)(128)(2,1)S(1)} %get-tuple-element.1258) | copy-start | bytes 12292
  128.6 40.9 %copy-start.87 = (bf16[1024]{0:T(1024)(128)(2,1)}, bf16[1024]{0:T(1024)(128)(2,1)S(1)}, u32[]{:S(2)}) copy-start(bf16[1024]{0:T(1024)(128)(2,1)S(1)} %get-tuple-element.1257) | copy-start | bytes 6148
  169.5 297.0 %all-gather.5.cloned.1.call-start = ((), (), s32[]{:S(2)}) async-start(), calls=%async_computation.5 | async-start | bytes 2359296 | tf_op jit(solution)/shard_map/all_gather | solution.py:566
  172.0 66.6 %copy-start.92 = (s32[2048]{0:T(1024)}, s32[2048]{0:T(1024)S(1)}, u32[]{:S(2)}) copy-start(s32[2048]{0:T(1024)S(1)} %fusion.148) | copy-start | bytes 24580
  190.1 49.5 %copy-start.55 = (bf16[768,4]{1,0:T(8,128)(2,1)}, bf16[768,4]{1,0:T(8,128)(2,1)S(1)}, u32[]{:S(2)}) copy-start(bf16[768,4]{1,0:T(8,128)(2,1)S(1)} %reshape_reshape.22) | copy-start | bytes 18436
  190.1 49.2 %copy-start.94 = (f32[768]{0:T(1024)S(1)}, f32[768]{0:T(1024)}, u32[]{:S(2)}) copy-start(f32[768]{0:T(1024)} %reshape.1407) | copy-start | bytes 9220
  292.6 142.6 %copy-start.20 = (f32[1,384,2,512]{3,2,1,0:T(2,128)S(1)}, f32[1,384,2,512]{3,2,1,0:T(2,128)}, u32[]{:S(2)}) copy-start(f32[1,384,2,512]{3,2,1,0:T(2,128)} %param.34) | copy-start | bytes 4718596
  435.2 21.8 %collective-permute-start.3 = (bf16[4,2,512,768]{3,2,1,0:T(8,128)(2,1)}, bf16[4,2,512,768]{3,2,1,0:T(8,128)(2,1)}, u32[]{:S(2)}, u32[]{:S(2)}) collective-permute-start(bf16[4,2,512,768]{3,2,1,0:T(8,128)(2,1)} %all_to_all.10), channel_id=1, source_target_pairs={{0,1},{1,0},{2,3},{3,2},{4,5},{5,4},{6,7},{7,6},{8,9},{9,8},{10,11... | collective-permute-start | bytes 18874376 | tf_op jit(solution)/shard_map/ppermute | solution.py:465
  436.4 211.3 %reduce-scatter.5.cloned.1.call-start = ((), (), s32[]{:S(2)}) async-start(), calls=%async_computation.8 | async-start | bytes 2359296 | tf_op jit(solution)/shard_map/reduce_scatter | solution.py:709
  505.7 32.9 %collective-permute-start.4 = (f32[4,512,768]{2,1,0:T(8,128)}, f32[4,512,768]{2,1,0:T(8,128)}, u32[]{:S(2)}, u32[]{:S(2)}) collective-permute-start(f32[4,512,768]{2,1,0:T(8,128)} %slice.549), channel_id=1, source_target_pairs={{0,1},{1,0},{2,3},{3,2},{4,5},{5,4},{6,7},{7,6},{8,9},{9,8},{10,11... | collective-permute-start | bytes 18874376 | tf_op jit(solution)/shard_map/ppermute | solution.py:465
  531.3 12.7 collective-permute-start.5
  558.3 143.9 %all-to-all-start.1 = ((bf16[4,2,512,768]{3,2,1,0:T(8,128)(2,1)}), bf16[4,2,512,768]{3,2,1,0:T(8,128)(2,1)}, u32[]{:S(2)}, u32[]{:S(2)}) async-start(bf16[4,2,512,768]{3,2,1,0:T(8,128)(2,1)} %copy.229), calls=%async_computation.1 | async-start | bytes 12582912 | tf_op jit(solution)/shard_map/all_to_all | solution.py:463
  563.5 85.6 %reduce-scatter.3.cloned.1.call-start = ((), (), s32[]{:S(2)}) async-start(), calls=%async_computation.7 | async-start | bytes 4718592 | tf_op jit(solution)/shard_map/reduce_scatter | solution.py:708
  575.8 264.4 %all-reduce.15.cloned.1.call-start = ((), (), s32[]{:S(2)}) async-start(), calls=%async_computation.6 | async-start | bytes 6291456 | tf_op jit(solution)/shard_map/psum | solution.py:663
  772.9 326.3 %all-reduce.17.cloned.1.call-start = ((), (), s32[]{:S(2)}) async-start(), calls=%async_computation.10 | async-start | bytes 12582912 | tf_op jit(solution)/shard_map/psum | solution.py:663
  787.0 53.2 %copy-start.4 = (f32[1024,768]{1,0:T(8,128)S(1)}, f32[1024,768]{1,0:T(8,128)}, u32[]{:S(2)}) copy-start(f32[1024,768]{1,0:T(8,128)} %copy-done.3) | copy-start | bytes 9437188
  787.0 53.2 %copy-start.56 = (bf16[768,4]{1,0:T(8,128)(2,1)S(1)}, bf16[768,4]{1,0:T(8,128)(2,1)}, u32[]{:S(2)}) copy-start(bf16[768,4]{1,0:T(8,128)(2,1)} %copy-done.55) | copy-start | bytes 18436
  787.0 53.2 %copy-start.95 = (f32[768]{0:T(1024)S(1)}, f32[768]{0:T(1024)}, u32[]{:S(2)}) copy-start(f32[768]{0:T(1024)} %reshape.1407) | copy-start | bytes 9220
  787.0 53.2 %copy-start.97 = (f32[1024]{0:T(1024)S(1)}, f32[1024]{0:T(1024)}, u32[]{:S(2)}) copy-start(f32[1024]{0:T(1024)} %copy-done.96) | copy-start | bytes 12292
  792.3 51.7 %copy-start.106 = (f32[1024]{0:T(1024)S(1)}, f32[1024]{0:T(1024)}, u32[]{:S(2)}) copy-start(f32[1024]{0:T(1024)} %copy-done.105) | copy-start | bytes 12292
  928.0 14.0 %collective-permute-start.6 = (bf16[1024,3,64]{0,2,1:T(8,128)(2,1)S(1)}, bf16[1024,3,64]{0,2,1:T(8,128)(2,1)}, u32[]{:S(2)}, u32[]{:S(2)}) collective-permute-start(bf16[1024,3,64]{0,2,1:T(8,128)(2,1)S(1)} %slice.664), channel_id=1, source_target_pairs={{4,0},{5,1},{6,2},{7,3},{12,8},{13,9},{14,10},{15,11},{20,16},{21,... | collective-permute-start | bytes 1179656 | tf_op jit(solution)/shard_map/ppermute | solution.py:27
  930.1 19.1 %collective-permute-start.7 = (bf16[1024,3,64]{0,2,1:T(8,128)(2,1)}, bf16[1024,3,64]{0,2,1:T(8,128)(2,1)}, u32[]{:S(2)}, u32[]{:S(2)}) collective-permute-start(bf16[1024,3,64]{0,2,1:T(8,128)(2,1)} %slice.663), channel_id=1, source_target_pairs={{4,0},{5,1},{6,2},{7,3},{12,8},{13,9},{14,10},{15,11},{20,16},{21,... | collective-permute-start | bytes 1179656 | tf_op jit(solution)/shard_map/ppermute | solution.py:27
  1093.7 43.1 %copy-start.72 = (f32[192,96]{1,0:T(8,128)}, f32[192,96]{1,0:T(8,128)S(1)}, u32[]{:S(2)}) copy-start(f32[192,96]{1,0:T(8,128)S(1)} %reshape.1391) | copy-start | bytes 221188
  1153.4 59.4 %copy-start.14 = (f32[1,384,2,512]{3,1,2,0:T(8,128)S(1)}, f32[1,384,2,512]{3,1,2,0:T(8,128)}, u32[]{:S(2)}) copy-start(f32[1,384,2,512]{3,1,2,0:T(8,128)} %reduce-scatter.3.cloned.1.call-done) | copy-start | bytes 4718596
  1153.4 87.4 %copy-start.21 = (f32[1,384,2,512]{3,2,1,0:T(2,128)S(1)}, f32[1,384,2,512]{3,2,1,0:T(2,128)}, u32[]{:S(2)}) copy-start(f32[1,384,2,512]{3,2,1,0:T(2,128)} %param.34) | copy-start | bytes 4718596
  1174.2 40.4 %copy-start.119 = (f32[1,1,512]{2,1,0:T(1,128)S(1)}, f32[1,1,512]{2,1,0:T(1,128)}, u32[]{:S(2)}) copy-start(f32[1,1,512]{2,1,0:T(1,128)} %fusion.174) | copy-start | bytes 6148
  1176.3 64.5 %copy-start.115 = (f32[512]{0:T(512)}, f32[512]{0:T(512)S(1)}, u32[]{:S(2)}) copy-start(f32[512]{0:T(512)S(1)} %multiply_add_fusion.8) | copy-start | bytes 6148
  (147 other events, 1027.1 us)
Sparse Core Ops, SparseCore 0:
  69.1 91.0 all-gather.6
  169.6 66.6 all-reduce.12
  773.0 67.2 all-reduce.14
  953.5 119.1 all-reduce.16
Sparse Core Ops, SparseCore 1:
  436.5 30.0 all-gather.4
  538.6 24.8 reduce-scatter.4
  575.9 44.0 reduce-scatter.2

commit v11 on v10

--- a/solution.py
+++ b/solution.py
@@ -540,24 +540,24 @@
     ctx_count = lax.axis_size("ctx")
     base_pos = ctx_index * block_len
     low = lambda v: v.astype(jnp.bfloat16)
-    gain_low, attn_in_low = gather_packed(
-        [(low(gains), 1), (low(attention_in), 0)], ("fsdp", "ctx"), shard_count <= 8
+    gain_low, attn_in_low, attn_out_low, router_low = gather_packed(
+        [(low(gains), 1), (low(attention_in), 0), (low(attention_out), 1), (low(router_weight), 0)],
+        ("fsdp", "ctx"),
+        shard_count <= 8,
     )
     later = [
-        (low(attention_out), 1),
-        (low(router_weight), 0),
         (low(shared_in), 0),
         (low(shared_down), 1),
     ]
     if dense_experts:
         later += [(low(expert_in), 0), (low(expert_down), 0)]
     later_full = gather_packed(later, ("fsdp", "ctx"))
-    attn_out_low, router_low, shared_in_low, shared_down_low = later_full[:4]
+    shared_in_low, shared_down_low = later_full[:2]
     if dense_experts:
         fe_local = expert_down.shape[1]
-        expert_in_all = later_full[4].reshape(experts, model_width, 2, fe_local)
+        expert_in_all = later_full[2].reshape(experts, model_width, 2, fe_local)
         expert_down_all = (
-            later_full[5]
+            later_full[3]
             .reshape(experts, ctx_count, fe_local, model_width // ctx_count)
             .transpose(0, 2, 1, 3)
             .reshape(experts, fe_local, model_width)

time: 1290 us -> 1280 us (level)
    unnamed x328 -> x314, local copies, waits for them, and re-layouts: 67.2 us -> 53.9 us
  transfers between devices with their start and end apart: 16 -> 16, of which waited for: 7 -> 6; matrix products, arithmetic and copies ran while one was open for 23% -> 20% of each run, Pallas kernels for 8% -> 8%
where the time goes in v11:
time: 1280 us; the launch traced here: 1270 us
  local copies, waits for them, and re-layouts  339 us (26%)
  other arithmetic  196 us (15%)
  Pallas kernels  177 us (14%)
  blocking collectives  169 us (13%)
  waiting for transfers between devices  167 us (13%)
  matrix products  155 us (12%)
  between operations  43.2 us (3%)
  starting transfers between devices  17.8 us (1%)
    all_to_all x1, blocking collectives, experts_routed(): lax.all_to_all(rows, 'fsdp', split_axis=0, concat_axis=0, tiled=True)  143 us
    pallas_call x1, Pallas kernels, halving_scatter(): pl.pallas_call(halving_kernel, out_shape=jax.ShapeDtypeStruct((2 * rows,...  105 us
    unnamed x314, local copies, waits for them, and re-layouts  53.9 us
    psum x1, waiting for transfers between devices, local(): lax.psum(jnp.dot(mixed_heads, attn_out_low, preferred_element_type=jnp.fl...  53.2 us
    psum x2, waiting for transfers between devices, local(): lax.psum((shared_out + combined, partial_two, gate_dots), 'tp')  47.7 us
    pallas_call x2, Pallas kernels, butterfly_sum(): pl.pallas_call(butterfly_kernel, out_shape=jax.ShapeDtypeStruct((rows, 12...  44.7 us
    all_to_all x1, waiting for transfers between devices, experts_routed(): lax.all_to_all(rows, 'fsdp', split_axis=0, concat_axis=0, tiled=True)  36.5 us
    pallas_call x1, Pallas kernels, gather_shards(): pl.pallas_call(gather_kernel, out_shape=jax.ShapeDtypeStruct((count, rows...  27.6 us
  transfers between devices with their start and end apart: 16, of which 6 were waited for; matrix products, arithmetic and copies ran while one was open for 20% of the time, Pallas kernels for 8%

profile of v11, /device:TPU:0, one launch (start us, length us, event | category | flops | bytes accessed | tf_op | source)
XLA Modules:
  0.0 1272.5 jit_solution(5377680775013699726)
XLA Ops:
  17.1 27.6 %shard_map.395 = bf16[8,592,128]{2,1,0:T(8,128)(2,1)} custom-call(bf16[592,128]{1,0:T(8,128)(2,1)} %pad_bitcast_fusion.2.x_ref), custom_call_target="tpu_custom_call" | custom-call | tf_op jit(solution)/shard_map/pallas_call | solution.py:352
  92.1 8.5 mul.1199
  102.9 34.1 %while.39 = (s32[]{:T(128)}, bf16[2,512,3,64]{1,3,2,0:T(8,128)(2,1)}, f32[2,3,512,1]{2,1,3,0:T(4,128)}, s32[2]{0:T(128)S(1)}, bf16[2048,3,64]{0,2,1:T(8,128)(2,1...) while((s32[]{:T(128)}, ...), condition=%wide.region_4.5_spmd, body=%wide.region_1.4_spmd.sunk | while | flops 644092928 | bytes 33315144 | solution.py:614
  147.3 8.2 scatter_custom_fusion
  155.5 8.1 scatter_custom_fusion.1
  163.6 53.2 %all-reduce.13.cloned.1.call-done = f32[1024,768]{1,0:T(8,128)} async-done(((f32[1024,768]{1,0:T(8,128)}), f32[1024,768]{1,0:T(8,128)}) %all-reduce.13.cloned.1.call-update) | async-done | bytes 3145744 | tf_op jit(solution)/shard_map/psum | solution.py:616
  222.7 17.8 %gather_fusion = bf16[4096,768]{1,0:T(8,128)(2,1)} fusion(bf16[1024,768]{1,0:T(8,128)(2,1)S(1)} %multiply_convert_fusion.3, s32[4096]{0:T(1024)S(1)} %get-tuple-element.934), kind=kCustom, calls=%fused_computation | custom fusion | bytes 12599296 | tf_op jit(solution)/shard_map/gather | solution.py:458
  245.4 21.4 %gather_fusion.1 = bf16[4096,768]{1,0:T(8,128)(2,1)} fusion(bf16[2048,768]{1,0:T(8,128)(2,1)} %multiply_convert_fusion.2, s32[4096]{0:T(1024)S(1)} %get-tuple-element.933), kind=kCustom, calls=%fused_computation.1 | custom fusion | bytes 12599296 | tf_op jit(solution)/shard_map/gather | solution.py:459
  272.8 142.6 %all_to_all.10 = bf16[4,2,512,768]{3,2,1,0:T(8,128)(2,1)} all-to-all(bf16[4,2,512,768]{3,2,1,0:T(8,128)(2,1)S(1)} %fusion.57), channel_id=1, replica_groups=mesh['fsdp'=4,'ctx'=2,'tp'=4] {'fsdp'}, dimensions={0} | all-to-all | bytes 12582912 | tf_op jit(solution)/shard_map/all_to_all | solution.py:463
  419.5 18.9 %all_gather.15 = bf16[1,512,768]{2,1,0:T(8,128)(2,1)S(1)} all-gather(bf16[1,512,384]{2,1,0:T(8,128)(2,1)S(1)} %get-tuple-element.897), channel_id=1, replica_groups=mesh['fsdp'=4,'ctx'=2,'tp'=4] {'ctx'}, dimensions={2}, use_global_device_ids=true | all-gather | bytes 1179648 | tf_op jit(solution)/shard_map/all_gather | solution.py:567
  450.6 9.3 fusion.94
  465.7 15.7 %fusion.56 = (f32[4096,1,512]{2,0,1:T(8,128)}, f32[4096,1,512]{2,0,1:T(8,128)}) fusion(f32[4096,2,512]{2,0,1:T(8,128)} %copy-done.18, bf16[4096,768]{1,0:T(8,128)(2,1)} %bitcast.469, bf16[1,512,768]{2,1,0:T(8,128)(2,1)S(1)} %all_gather.15), kind=kOutput, calls=%fused_computation.84 | convolution fusion | flops 3246391296 | bytes 40632320 | tf_op jit(solution)/shard_map/rd,fd->rf/dot_general | solution.py:478
  513.1 8.7 fusion.106
  541.8 12.2 convolution_bitcast_fusion.1
  581.1 20.8 %all-gather.6.cloned.1.call-done = bf16[1179648]{0:T(1024)(128)(2,1)} async-done(((bf16[147456]{0:T(1024)(128)(2,1)}), bf16[1179648]{0:T(1024)(128)(2,1)}) %all-gather.6.cloned.1.call-update) | async-done | bytes 2359312 | tf_op jit(solution)/shard_map/all_gather | solution.py:376
  658.8 36.5 %all-to-all-done.1 = bf16[4,2,512,768]{3,2,1,0:T(8,128)(2,1)} async-done(((bf16[4,2,512,768]{3,2,1,0:T(8,128)(2,1)}), bf16[4,2,512,768]{3,2,1,0:T(8,128)(2,1)}, u32[]{:S(2)}, u32[]{:S(2)}) %all-to-all-start.1) | async-done | bytes 6291488 | tf_op jit(solution)/shard_map/all_to_all | solution.py:463
  701.3 12.4 gather_fusion.2
  713.7 7.8 reshape.1408
  721.5 12.4 gather_fusion.3
  733.9 7.9 reshape.1409
  741.8 20.7 %select_reduce_fusion = (f32[1024,768]{1,0:T(8,128)S(1)}, f32[1024,768]{1,0:T(8,128)}) fusion(f32[1024,2,768]{2,1,0:T(2,128)} %reshape.1409, pred[1024,2]{1,0:T(8,128)(4,1)S(1)} %copy-done.66, f32[1024,2,768]{2,1,0:T(2,128)} %reshape.1408, f32[1024,2]{1,0:T(8,128)S(1)} %copy-done.34), kind=kLoop, calls=%fused_computation.94 | loop fusion | flops 6291456 | bytes 18884608 | tf_op jit(solution)/shard_map/reduce_sum | solution.py:505
  771.8 7.5 psum.38
  786.2 47.7 %all-reduce.15.cloned.1.call-done = f32[1024,768]{1,0:T(8,128)} async-done(((f32[1024,768]{1,0:T(8,128)}), f32[1024,768]{1,0:T(8,128)}) %all-reduce.15.cloned.1.call-update) | async-done | bytes 3145744 | tf_op jit(solution)/shard_map/psum | solution.py:663
  843.7 76.7 %while.40 = (s32[]{:T(128)}, f32[2048,3,64]{0,2,1:T(8,128)}, f32[2048,3,64]{0,2,1:T(8,128)S(1)}, f32[1024,3,64]{0,2,1:T(8,128)}, bf16[1024,3,64]{0,2,1:T(8,128)(...) while((s32[]{:T(128)}, f32[2048,3,64]{0,2,1:T(8,128)}, ...), condition=%wide.region_26.27_spmd, body=%wide.region_24.26_spmd.sunk | while | flops 1541608448 | bytes 106823088 | solution.py:765
  851.8 8.8 multiply_reduce_fusion.22
  860.6 9.5 multiply_convert_fusion.6
  890.1 8.8 multiply_reduce_fusion.22
  899.0 9.5 multiply_convert_fusion.6
  973.7 105.0 %shard_map.396 = f32[1792,128]{1,0:T(8,128)} custom-call(f32[2,2,2,1792,128]{4,3,2,1,0:T(8,128)} %bitcast.456), custom_call_target="tpu_custom_call" | custom-call | tf_op jit(solution)/shard_map/pallas_call | solution.py:280
  1101.1 29.1 %shard_map.397 = f32[344,128]{1,0:T(8,128)} custom-call(f32[344,128]{1,0:T(8,128)} %pad_bitcast_fusion.1.x_ref), custom_call_target="tpu_custom_call" | custom-call | tf_op jit(solution)/shard_map/pallas_call | solution.py:162
  1139.1 7.8 slice.488
  1214.7 15.6 %shard_map.398 = f32[8,128]{1,0:T(8,128)} custom-call(f32[8,128]{1,0:T(8,128)} %pad_bitcast_fusion.3.x_ref), custom_call_target="tpu_custom_call" | custom-call | tf_op jit(solution)/shard_map/pallas_call | solution.py:162
  (687 shorter events, 501.1 us)
Async XLA Ops:
  8.0 208.8 %all-reduce.13.cloned.1.call-start = ((), (), s32[]{:S(2)}) async-start(), calls=%async_computation.4 | async-start | bytes 6291456 | tf_op jit(solution)/shard_map/psum | solution.py:616
  59.5 41.1 %collective-permute-start.2 = (bf16[1024,3,64]{0,2,1:T(8,128)(2,1)}, bf16[1024,3,64]{0,2,1:T(8,128)(2,1)}, u32[]{:S(2)}, u32[]{:S(2)}) collective-permute-start(bf16[1024,3,64]{0,2,1:T(8,128)(2,1)} %pad_maximum_fusion.4), channel_id=1, source_target_pairs={{0,4},{1,5},{2,6},{3,7},{8,12},{9,13},{10,14},{11,15},{16,20},{17,... | collective-permute-start | bytes 1179656 | tf_op jit(solution)/shard_map/ppermute | solution.py:27
  65.9 35.8 %collective-permute-start = (bf16[1024,3,64]{0,2,1:T(8,128)(2,1)S(1)}, bf16[1024,3,64]{0,2,1:T(8,128)(2,1)}, u32[]{:S(2)}, u32[]{:S(2)}) collective-permute-start(bf16[1024,3,64]{0,2,1:T(8,128)(2,1)S(1)} %bitcast.495), channel_id=1, source_target_pairs={{0,4},{1,5},{2,6},{3,7},{8,12},{9,13},{10,14},{11,15},{16,20},{17,... | collective-permute-start | bytes 1179656 | tf_op jit(solution)/shard_map/ppermute | solution.py:27
  68.1 32.5 %collective-permute-start.1 = (bf16[1024]{0:T(1024)(128)(2,1)S(1)}, bf16[1024]{0:T(1024)(128)(2,1)S(1)}, u32[]{:S(2)}, u32[]{:S(2)}) collective-permute-start(bf16[1024]{0:T(1024)(128)(2,1)S(1)} %convert_reduce_fusion), channel_id=1, source_target_pairs={{0,4},{1,5},{2,6},{3,7},{8,12},{9,13},{10,14},{11,15},{16,20},{17,... | collective-permute-start | bytes 6152 | tf_op jit(solution)/shard_map/ppermute | solution.py:27
  137.0 82.6 %copy-start.76 = (bf16[2048]{0:T(1024)(128)(2,1)}, bf16[2048]{0:T(1024)(128)(2,1)S(1)}, u32[]{:S(2)}) copy-start(bf16[2048]{0:T(1024)(128)(2,1)S(1)} %get-tuple-element.1258) | copy-start | bytes 12292
  137.0 82.6 %copy-start.84 = (bf16[1024]{0:T(1024)(128)(2,1)}, bf16[1024]{0:T(1024)(128)(2,1)S(1)}, u32[]{:S(2)}) copy-start(bf16[1024]{0:T(1024)(128)(2,1)S(1)} %get-tuple-element.1257) | copy-start | bytes 6148
  142.8 307.8 %all-gather.4.cloned.1.call-start = ((), (), s32[]{:S(2)}) async-start(), calls=%async_computation.5 | async-start | bytes 2359296 | tf_op jit(solution)/shard_map/all_gather | solution.py:566
  146.5 72.7 %copy-start.89 = (s32[2048]{0:T(1024)}, s32[2048]{0:T(1024)S(1)}, u32[]{:S(2)}) copy-start(s32[2048]{0:T(1024)S(1)} %fusion.144) | copy-start | bytes 24580
  163.6 55.6 %copy-start.91 = (f32[768]{0:T(1024)S(1)}, f32[768]{0:T(1024)}, u32[]{:S(2)}) copy-start(f32[768]{0:T(1024)} %reshape.1407) | copy-start | bytes 9220
  272.8 142.6 %copy-start.21 = (f32[1,384,2,512]{3,2,1,0:T(2,128)S(1)}, f32[1,384,2,512]{3,2,1,0:T(2,128)}, u32[]{:S(2)}) copy-start(f32[1,384,2,512]{3,2,1,0:T(2,128)} %param.34) | copy-start | bytes 4718596
  415.4 26.3 %collective-permute-start.3 = (bf16[4,2,512,768]{3,2,1,0:T(8,128)(2,1)}, bf16[4,2,512,768]{3,2,1,0:T(8,128)(2,1)}, u32[]{:S(2)}, u32[]{:S(2)}) collective-permute-start(bf16[4,2,512,768]{3,2,1,0:T(8,128)(2,1)} %all_to_all.10), channel_id=1, source_target_pairs={{0,1},{1,0},{2,3},{3,2},{4,5},{5,4},{6,7},{7,6},{8,9},{9,8},{10,11... | collective-permute-start | bytes 18874376 | tf_op jit(solution)/shard_map/ppermute | solution.py:465
  416.5 185.3 %all-gather.6.cloned.1.call-start = ((), (), s32[]{:S(2)}) async-start(), calls=%async_computation.9 | async-start | bytes 2654208 | tf_op jit(solution)/shard_map/all_gather | solution.py:376
  491.3 30.6 %collective-permute-start.4 = (f32[4,512,768]{2,1,0:T(8,128)}, f32[4,512,768]{2,1,0:T(8,128)}, u32[]{:S(2)}, u32[]{:S(2)}) collective-permute-start(f32[4,512,768]{2,1,0:T(8,128)} %slice.551), channel_id=1, source_target_pairs={{0,1},{1,0},{2,3},{3,2},{4,5},{5,4},{6,7},{7,6},{8,9},{9,8},{10,11... | collective-permute-start | bytes 18874376 | tf_op jit(solution)/shard_map/ppermute | solution.py:465
  511.4 16.1 %collective-permute-start.5 = (f32[4,512,768]{2,1,0:T(8,128)}, f32[4,512,768]{2,1,0:T(8,128)}, u32[]{:S(2)}, u32[]{:S(2)}) collective-permute-start(f32[4,512,768]{2,1,0:T(8,128)} %slice.554), channel_id=1, source_target_pairs={{0,1},{1,0},{2,3},{3,2},{4,5},{5,4},{6,7},{7,6},{8,9},{9,8},{10,11... | collective-permute-start | bytes 18874376 | tf_op jit(solution)/shard_map/ppermute | solution.py:465
  512.6 137.9 %reduce-scatter.5.cloned.1.call-start = ((), (), s32[]{:S(2)}) async-start(), calls=%async_computation.8 | async-start | bytes 2359296 | tf_op jit(solution)/shard_map/reduce_scatter | solution.py:709
  536.4 158.9 %all-to-all-start.1 = ((bf16[4,2,512,768]{3,2,1,0:T(8,128)(2,1)}), bf16[4,2,512,768]{3,2,1,0:T(8,128)(2,1)}, u32[]{:S(2)}, u32[]{:S(2)}) async-start(bf16[4,2,512,768]{3,2,1,0:T(8,128)(2,1)} %copy.229), calls=%async_computation.1 | async-start | bytes 12582912 | tf_op jit(solution)/shard_map/all_to_all | solution.py:463
  541.7 110.2 %reduce-scatter.3.cloned.1.call-start = ((), (), s32[]{:S(2)}) async-start(), calls=%async_computation.7 | async-start | bytes 4718592 | tf_op jit(solution)/shard_map/reduce_scatter | solution.py:708
  554.1 279.8 %all-reduce.15.cloned.1.call-start = ((), (), s32[]{:S(2)}) async-start(), calls=%async_computation.6 | async-start | bytes 6291456 | tf_op jit(solution)/shard_map/psum | solution.py:663
  766.1 326.7 %all-reduce.17.cloned.1.call-start = ((), (), s32[]{:S(2)}) async-start(), calls=%async_computation.10 | async-start | bytes 12582912 | tf_op jit(solution)/shard_map/psum | solution.py:663
  780.9 53.0 %copy-start.4 = (f32[1024,768]{1,0:T(8,128)S(1)}, f32[1024,768]{1,0:T(8,128)}, u32[]{:S(2)}) copy-start(f32[1024,768]{1,0:T(8,128)} %copy-done.3) | copy-start | bytes 9437188
  780.9 53.0 %copy-start.56 = (bf16[768,4]{1,0:T(8,128)(2,1)S(1)}, bf16[768,4]{1,0:T(8,128)(2,1)}, u32[]{:S(2)}) copy-start(bf16[768,4]{1,0:T(8,128)(2,1)} %reshape_reshape.22) | copy-start | bytes 18436
  780.9 53.0 %copy-start.92 = (f32[768]{0:T(1024)S(1)}, f32[768]{0:T(1024)}, u32[]{:S(2)}) copy-start(f32[768]{0:T(1024)} %reshape.1407) | copy-start | bytes 9220
  780.9 53.0 %copy-start.94 = (f32[1024]{0:T(1024)S(1)}, f32[1024]{0:T(1024)}, u32[]{:S(2)}) copy-start(f32[1024]{0:T(1024)} %copy-done.93) | copy-start | bytes 12292
  786.2 51.5 %copy-start.103 = (f32[1024]{0:T(1024)S(1)}, f32[1024]{0:T(1024)}, u32[]{:S(2)}) copy-start(f32[1024]{0:T(1024)} %copy-done.102) | copy-start | bytes 12292
  921.6 14.0 %collective-permute-start.6 = (bf16[1024,3,64]{0,2,1:T(8,128)(2,1)S(1)}, bf16[1024,3,64]{0,2,1:T(8,128)(2,1)}, u32[]{:S(2)}, u32[]{:S(2)}) collective-permute-start(bf16[1024,3,64]{0,2,1:T(8,128)(2,1)S(1)} %slice.666), channel_id=1, source_target_pairs={{4,0},{5,1},{6,2},{7,3},{12,8},{13,9},{14,10},{15,11},{20,16},{21,... | collective-permute-start | bytes 1179656 | tf_op jit(solution)/shard_map/ppermute | solution.py:27
  923.7 19.1 %collective-permute-start.7 = (bf16[1024,3,64]{0,2,1:T(8,128)(2,1)}, bf16[1024,3,64]{0,2,1:T(8,128)(2,1)}, u32[]{:S(2)}, u32[]{:S(2)}) collective-permute-start(bf16[1024,3,64]{0,2,1:T(8,128)(2,1)} %slice.665), channel_id=1, source_target_pairs={{4,0},{5,1},{6,2},{7,3},{12,8},{13,9},{14,10},{15,11},{20,16},{21,... | collective-permute-start | bytes 1179656 | tf_op jit(solution)/shard_map/ppermute | solution.py:27
  1087.2 43.1 %copy-start.72 = (f32[192,96]{1,0:T(8,128)}, f32[192,96]{1,0:T(8,128)S(1)}, u32[]{:S(2)}) copy-start(f32[192,96]{1,0:T(8,128)S(1)} %reshape.1391) | copy-start | bytes 221188
  1147.0 59.3 %copy-start.15 = (f32[1,384,2,512]{3,1,2,0:T(8,128)S(1)}, f32[1,384,2,512]{3,1,2,0:T(8,128)}, u32[]{:S(2)}) copy-start(f32[1,384,2,512]{3,1,2,0:T(8,128)} %reduce-scatter.3.cloned.1.call-done) | copy-start | bytes 4718596
  1147.0 87.5 %copy-start.22 = (f32[1,384,2,512]{3,2,1,0:T(2,128)S(1)}, f32[1,384,2,512]{3,2,1,0:T(2,128)}, u32[]{:S(2)}) copy-start(f32[1,384,2,512]{3,2,1,0:T(2,128)} %param.34) | copy-start | bytes 4718596
  1167.7 38.6 %copy-start.98 = (f32[2,512]{1,0:T(2,128)S(1)}, f32[2,512]{1,0:T(2,128)}, u32[]{:S(2)}) copy-start(f32[2,512]{1,0:T(2,128)} %copy-done.97) | copy-start | bytes 12292
  1167.7 40.4 %copy-start.115 = (f32[1,1,512]{2,1,0:T(1,128)S(1)}, f32[1,1,512]{2,1,0:T(1,128)}, u32[]{:S(2)}) copy-start(f32[1,1,512]{2,1,0:T(1,128)} %fusion.170) | copy-start | bytes 6148
  1169.8 64.6 %copy-start.112 = (f32[512]{0:T(512)}, f32[512]{0:T(512)S(1)}, u32[]{:S(2)}) copy-start(f32[512]{0:T(512)S(1)} %multiply_add_fusion.8) | copy-start | bytes 6148
  (141 other events, 849.2 us)
Sparse Core Ops, SparseCore 0:
  142.9 73.8 all-reduce.12
  512.7 89.0 all-gather.5
  766.1 67.6 all-reduce.14
  947.1 119.1 all-reduce.16
Sparse Core Ops, SparseCore 1:
  416.6 32.1 all-gather.3
  522.0 24.6 reduce-scatter.4
  554.1 44.9 reduce-scatter.2

commit v12 on v11

--- a/solution.py
+++ b/solution.py
@@ -447,16 +447,21 @@
     block_len, model_width = normed_two.shape
     experts = lax.axis_size("fsdp")
     slot_index, owner_route, filled = slot_tables(route_rows, experts, capacity)
-    fill_mask = filled.astype(jnp.bfloat16)[:, None]
-    route_grads = (
-        (gate_probs[:, :, None] * grad_out[:, None, :])
-        .astype(jnp.bfloat16)
-        .reshape(2 * block_len, model_width)
-    )
+    select = (
+        (owner_route[:, None] // 2 == jnp.arange(block_len, dtype=jnp.int32)[None, :])
+        & (filled[:, None] == 1)
+    ).astype(jnp.bfloat16)
+    token_rows = jnp.dot(select, normed_two, preferred_element_type=jnp.float32)
+    grad_rows_in = jnp.dot(
+        select, grad_out.astype(jnp.bfloat16), preferred_element_type=jnp.float32
+    )
+    slot_weights = gate_probs.reshape(-1)[owner_route][:, None]
     send_rows = jnp.stack(
         [
-            (normed_two[owner_route // 2] * fill_mask).reshape(experts, capacity, model_width),
-            (route_grads[owner_route] * fill_mask).reshape(experts, capacity, model_width),
+            token_rows.astype(jnp.bfloat16).reshape(experts, capacity, model_width),
+            (slot_weights * grad_rows_in)
+            .astype(jnp.bfloat16)
+            .reshape(experts, capacity, model_width),
         ],
         axis=1,
     )
@@ -493,12 +498,17 @@
     slot_rank = slot_index % capacity
     in_side = ((slot_rank // half) == side)[:, None]
     local_slot = slot_expert * half + slot_rank % half
+    pick = (
+        (local_slot[:, None] == jnp.arange(experts * half, dtype=jnp.int32)[None, :]) & in_side
+    ).astype(jnp.bfloat16)
     picked_rows = []
     for which in range(2):
-        rows = held[:, which].reshape(experts * half, model_width)[local_slot]
-        picked_rows.append(
-            jnp.where(in_side, rows.astype(jnp.float32), 0.0).reshape(block_len, 2, model_width)
-        )
+        rows = jnp.dot(
+            pick,
+            held[:, which].reshape(experts * half, model_width),
+            preferred_element_type=jnp.float32,
+        )
+        picked_rows.append(rows.reshape(block_len, 2, model_width))
     route_out, grad_routes = picked_rows
     combined = jnp.sum(gate_probs[:, :, None] * route_out, axis=1)
     gate_dots = jnp.sum(grad_out[:, None, :] * route_out, axis=-1)

time: 1280 us -> 1220 us (0.953)
  local copies, waits for them, and re-layouts: 339 us -> 280 us
  matrix products: 155 us -> 196 us
  other arithmetic: 196 us -> 170 us
  waiting for transfers between devices: 167 us -> 147 us
    dot_general x0 -> x4, matrix products: none -> 41.1 us  [the longest x2 20.6 us: experts_routed(): jnp.dot(pick, held[:, which].reshape(experts * half, model_width), prefer...]
    gather x4 -> x1, local copies, waits for them, and re-layouts: 63.9 us -> 23 us  [experts_routed(): slot_weights = gate_probs.reshape(-1)[owner_route][:, None]]
    reduce_sum x2 -> x0, other arithmetic: 25.1 us -> none  [the longest x1 20.7 us: experts_routed(): grad_rows = jnp.sum(grad_routes, axis=1)]
    mul x3 -> x0, local copies, waits for them, and re-layouts: 15.8 us -> none  [the longest x2 15.7 us: experts_routed(): gate_probs[:, :, None] * grad_out[:, None, :]]
    unnamed x314 -> x304, local copies, waits for them, and re-layouts: 53.9 us -> 52.9 us
  transfers between devices with their start and end apart: 16 -> 16, of which waited for: 6 -> 6; matrix products, arithmetic and copies ran while one was open for 20% -> 22% of each run, Pallas kernels for 8% -> 9%
where the time goes in v12:
time: 1220 us; the launch traced here: 1210 us
  local copies, waits for them, and re-layouts  280 us (23%)
  matrix products  196 us (16%)
  Pallas kernels  177 us (15%)
  blocking collectives  172 us (14%)
  other arithmetic  170 us (14%)
  waiting for transfers between devices  147 us (12%)
  between operations  42.9 us (4%)
  starting transfers between devices  18.4 us (2%)
    all_to_all x1, blocking collectives, experts_routed(): lax.all_to_all(rows, 'fsdp', split_axis=0, concat_axis=0, tiled=True)  143 us
    pallas_call x1, Pallas kernels, halving_scatter(): pl.pallas_call(halving_kernel, out_shape=jax.ShapeDtypeStruct((2 * rows,...  105 us
    psum x1, waiting for transfers between devices, local(): lax.psum(jnp.dot(mixed_heads, attn_out_low, preferred_element_type=jnp.fl...  54.2 us
    unnamed x304, local copies, waits for them, and re-layouts  52.9 us
    pallas_call x2, Pallas kernels, butterfly_sum(): pl.pallas_call(butterfly_kernel, out_shape=jax.ShapeDtypeStruct((rows, 12...  44.7 us
    all_to_all x1, waiting for transfers between devices, experts_routed(): lax.all_to_all(rows, 'fsdp', split_axis=0, concat_axis=0, tiled=True)  36.3 us
    psum x2, waiting for transfers between devices, local(): lax.psum((shared_out + combined, partial_two, gate_dots), 'tp')  36.2 us
    pallas_call x1, Pallas kernels, gather_shards(): pl.pallas_call(gather_kernel, out_shape=jax.ShapeDtypeStruct((count, rows...  27.6 us
  transfers between devices with their start and end apart: 16, of which 6 were waited for; matrix products, arithmetic and copies ran while one was open for 22% of the time, Pallas kernels for 9%

profile of v12, /device:TPU:0, one launch (start us, length us, event | category | flops | bytes accessed | tf_op | source)
XLA Modules:
  0.0 1211.4 jit_solution(11357143710427731690)
XLA Ops:
  17.3 27.6 %shard_map.395 = bf16[8,592,128]{2,1,0:T(8,128)(2,1)} custom-call(bf16[592,128]{1,0:T(8,128)(2,1)} %pad_bitcast_fusion.2.x_ref), custom_call_target="tpu_custom_call" | custom-call | tf_op jit(solution)/shard_map/pallas_call | solution.py:352
  88.3 39.3 %while.39 = (s32[]{:T(128)}, bf16[2,512,3,64]{1,3,2,0:T(8,128)(2,1)}, f32[2,3,512,1]{2,1,3,0:T(4,128)}, s32[2]{0:T(128)}, bf16[2048,3,64]{0,2,1:T(8,128)(2,1)S(1...) while((s32[]{:T(128)}, ...), condition=%wide.region_4.5_spmd, body=%wide.region_1.4_spmd.sunk | while | flops 644092928 | bytes 33331516 | solution.py:624
  136.8 8.3 scatter_custom_fusion
  145.1 8.1 scatter_custom_fusion.1
  153.2 54.2 %all-reduce.13.cloned.1.call-done = f32[1024,768]{1,0:T(8,128)} async-done(((f32[1024,768]{1,0:T(8,128)}), f32[1024,768]{1,0:T(8,128)}) %all-reduce.13.cloned.1.call-update) | async-done | bytes 3145744 | tf_op jit(solution)/shard_map/psum | solution.py:626
  212.7 23.0 %gather_fusion = f32[4096]{0:T(1024)S(1)} fusion(f32[2048]{0:T(1024)S(1)} %div.425, s32[4096]{0:T(1024)S(1)} %get-tuple-element.931), kind=kCustom, calls=%fused_computation | custom fusion | bytes 49152 | tf_op jit(solution)/shard_map/gather | solution.py:458
  235.8 9.6 fusion.78
  245.4 10.9 multiply_convert_fusion.1
  258.7 142.6 %all_to_all.10 = bf16[4,2,512,768]{3,2,1,0:T(8,128)(2,1)} all-to-all(bf16[4,2,512,768]{3,2,1,0:T(8,128)(2,1)S(1)} %fusion.81), channel_id=1, replica_groups=mesh['fsdp'=4,'ctx'=2,'tp'=4] {'fsdp'}, dimensions={0} | all-to-all | bytes 12582912 | tf_op jit(solution)/shard_map/all_to_all | solution.py:468
  410.2 21.0 %all_gather.15 = bf16[1,512,768]{2,1,0:T(8,128)(2,1)} all-gather(bf16[1,512,384]{2,1,0:T(8,128)(2,1)S(1)} %get-tuple-element.897), channel_id=1, replica_groups=mesh['fsdp'=4,'ctx'=2,'tp'=4] {'ctx'}, dimensions={2}, use_global_device_ids=true | all-gather | bytes 1179648 | tf_op jit(solution)/shard_map/all_gather | solution.py:577
  443.5 9.3 fusion.121
  458.7 15.7 %fusion.67 = (f32[4096,1,512]{2,0,1:T(8,128)}, f32[4096,1,512]{2,0,1:T(8,128)}) fusion(f32[4096,2,512]{2,0,1:T(8,128)} %copy-done.16, bf16[4096,768]{1,0:T(8,128)(2,1)} %bitcast.487, bf16[1,512,768]{2,1,0:T(8,128)(2,1)S(1)} %copy-done.46), kind=kOutput, calls=%fused_computation.91 | convolution fusion | flops 3246391296 | bytes 40632320 | tf_op jit(solution)/shard_map/rd,fd->rf/dot_general | solution.py:483
  484.2 6.8 add_convert_fusion
  491.0 6.8 convolution_bitcast_fusion
  505.8 8.7 fusion.134
  534.4 12.3 %convolution_bitcast_fusion.1 = f32[1,768,2,512]{3,1,2,0:T(8,128)} fusion(bf16[4096,768,1]{1,0,2:T(8,128)(2,1)} %bitcast.486, bf16[4096,2,512]{2,0,1:T(8,128)(2,1)} %copy-done.27), kind=kOutput, calls=%fused_computation.158 | convolution fusion | flops 6442450944 | bytes 17825792 | tf_op jit(solution)/shard_map/rd,rgf->dgf/dot_general | solution.py:487
  584.0 11.5 all-gather.6.cloned.1.call-done
  626.8 6.3 reshape_reshape.24
  652.1 36.3 %all-to-all-done.1 = bf16[4,2,512,768]{3,2,1,0:T(8,128)(2,1)} async-done(((bf16[4,2,512,768]{3,2,1,0:T(8,128)(2,1)}), bf16[4,2,512,768]{3,2,1,0:T(8,128)(2,1)}, u32[]{:S(2)}, u32[]{:S(2)}) %all-to-all-start.1) | async-done | bytes 6291488 | tf_op jit(solution)/shard_map/all_to_all | solution.py:468
  693.4 8.2 fusion.104
  705.9 12.3 %multiply_reduce_fusion.1 = (f32[1024,2]{0,1:T(2,128)S(1)}, f32[1024,768]{0,1:T(8,128)}) fusion(f32[1024,768]{0,1:T(8,128)} %copy.253, f32[1024,2]{0,1:T(2,128)S(1)} %copy-done.111, bf16[2048,768,1]{1,0,2:T(8,128)(2,1)} %bitcast.498, s32[1024,2]{0,1:T(2,128)S(1)} %copy-done.131, pred[1024,2]{0,1:T(4,128)(4,1)S(1)} %copy-done.139), kind=kOutput, calls=%fused_computation.109 | convolution fusion | flops 6456342528 | bytes 9463808 | tf_op jit(solution)/shard_map/dot_general | solution.py:506
  718.2 8.2 psum.38
  736.9 36.2 %all-reduce.15.cloned.1.call-done = f32[1024,768]{1,0:T(8,128)} async-done(((f32[1024,768]{1,0:T(8,128)}), f32[1024,768]{1,0:T(8,128)}) %all-reduce.15.cloned.1.call-update) | async-done | bytes 3145744 | tf_op jit(solution)/shard_map/psum | solution.py:673
  782.8 76.6 %while.40 = (s32[]{:T(128)}, f32[2048,3,64]{0,2,1:T(8,128)}, f32[2048,3,64]{0,2,1:T(8,128)S(1)}, f32[1024,3,64]{0,2,1:T(8,128)}, bf16[1024,3,64]{0,2,1:T(8,128)(...) while((s32[]{:T(128)}, f32[2048,3,64]{0,2,1:T(8,128)}, ...), condition=%wide.region_26.27_spmd, body=%wide.region_24.26_spmd.sunk | while | flops 1541608448 | bytes 106823088 | solution.py:775
  791.0 8.8 multiply_reduce_fusion.22
  799.8 9.4 multiply_convert_fusion.6
  829.3 8.9 multiply_reduce_fusion.22
  838.1 9.4 multiply_convert_fusion.6
  912.9 105.0 %shard_map.396 = f32[1792,128]{1,0:T(8,128)} custom-call(f32[2,2,2,1792,128]{4,3,2,1,0:T(8,128)} %bitcast.477), custom_call_target="tpu_custom_call" | custom-call | tf_op jit(solution)/shard_map/pallas_call | solution.py:280
  1040.3 29.1 %shard_map.397 = f32[344,128]{1,0:T(8,128)} custom-call(f32[344,128]{1,0:T(8,128)} %pad_bitcast_fusion.1.x_ref), custom_call_target="tpu_custom_call" | custom-call | tf_op jit(solution)/shard_map/pallas_call | solution.py:162
  1078.3 7.8 slice.488
  1153.8 15.6 %shard_map.398 = f32[8,128]{1,0:T(8,128)} custom-call(f32[8,128]{1,0:T(8,128)} %pad_bitcast_fusion.3.x_ref), custom_call_target="tpu_custom_call" | custom-call | tf_op jit(solution)/shard_map/pallas_call | solution.py:162
  (672 shorter events, 482.5 us)
Async XLA Ops:
  8.0 199.4 %all-reduce.13.cloned.1.call-start = ((), (), s32[]{:S(2)}) async-start(), calls=%async_computation.4 | async-start | bytes 6291456 | tf_op jit(solution)/shard_map/psum | solution.py:626
  59.8 26.3 %collective-permute-start.2 = (bf16[1024,3,64]{0,2,1:T(8,128)(2,1)}, bf16[1024,3,64]{0,2,1:T(8,128)(2,1)}, u32[]{:S(2)}, u32[]{:S(2)}) collective-permute-start(bf16[1024,3,64]{0,2,1:T(8,128)(2,1)} %pad_maximum_fusion.4), channel_id=1, source_target_pairs={{0,4},{1,5},{2,6},{3,7},{8,12},{9,13},{10,14},{11,15},{16,20},{17,... | collective-permute-start | bytes 1179656 | tf_op jit(solution)/shard_map/ppermute | solution.py:27
  66.2 20.9 %collective-permute-start = (bf16[1024,3,64]{0,2,1:T(8,128)(2,1)S(1)}, bf16[1024,3,64]{0,2,1:T(8,128)(2,1)}, u32[]{:S(2)}, u32[]{:S(2)}) collective-permute-start(bf16[1024,3,64]{0,2,1:T(8,128)(2,1)S(1)} %bitcast.517), channel_id=1, source_target_pairs={{0,4},{1,5},{2,6},{3,7},{8,12},{9,13},{10,14},{11,15},{16,20},{17,... | collective-permute-start | bytes 1179656 | tf_op jit(solution)/shard_map/ppermute | solution.py:27
  68.3 17.1 %collective-permute-start.1 = (bf16[1024]{0:T(1024)(128)(2,1)S(1)}, bf16[1024]{0:T(1024)(128)(2,1)}, u32[]{:S(2)}, u32[]{:S(2)}) collective-permute-start(bf16[1024]{0:T(1024)(128)(2,1)S(1)} %convert_reduce_fusion), channel_id=1, source_target_pairs={{0,4},{1,5},{2,6},{3,7},{8,12},{9,13},{10,14},{11,15},{16,20},{17,... | collective-permute-start | bytes 6152 | tf_op jit(solution)/shard_map/ppermute | solution.py:27
  127.6 83.1 %copy-start.72 = (bf16[2048]{0:T(1024)(128)(2,1)}, bf16[2048]{0:T(1024)(128)(2,1)S(1)}, u32[]{:S(2)}) copy-start(bf16[2048]{0:T(1024)(128)(2,1)S(1)} %get-tuple-element.1242) | copy-start | bytes 12292
  127.6 83.1 %copy-start.85 = (bf16[1024]{0:T(1024)(128)(2,1)}, bf16[1024]{0:T(1024)(128)(2,1)S(1)}, u32[]{:S(2)}) copy-start(bf16[1024]{0:T(1024)(128)(2,1)S(1)} %get-tuple-element.1245) | copy-start | bytes 6148
  133.4 310.1 %all-gather.4.cloned.1.call-start = ((), (), s32[]{:S(2)}) async-start(), calls=%async_computation.5 | async-start | bytes 2359296 | tf_op jit(solution)/shard_map/all_gather | solution.py:576
  136.8 73.0 %copy-start.88 = (s32[2048]{0:T(1024)}, s32[2048]{0:T(1024)S(1)}, u32[]{:S(2)}) copy-start(s32[2048]{0:T(1024)S(1)} %fusion.168) | copy-start | bytes 24580
  153.2 57.2 %copy-start.90 = (f32[768]{0:T(1024)S(1)}, f32[768]{0:T(1024)}, u32[]{:S(2)}) copy-start(f32[768]{0:T(1024)} %reshape.1339) | copy-start | bytes 9220
  258.7 142.6 %copy-start.19 = (f32[1,384,2,512]{3,2,1,0:T(2,128)S(1)}, f32[1,384,2,512]{3,2,1,0:T(2,128)}, u32[]{:S(2)}) copy-start(f32[1,384,2,512]{3,2,1,0:T(2,128)} %param.34) | copy-start | bytes 4718596
  401.3 33.0 %collective-permute-start.3 = (bf16[4,2,512,768]{3,2,1,0:T(8,128)(2,1)}, bf16[4,2,512,768]{3,2,1,0:T(8,128)(2,1)}, u32[]{:S(2)}, u32[]{:S(2)}) collective-permute-start(bf16[4,2,512,768]{3,2,1,0:T(8,128)(2,1)} %all_to_all.10), channel_id=1, source_target_pairs={{0,1},{1,0},{2,3},{3,2},{4,5},{5,4},{6,7},{7,6},{8,9},{9,8},{10,11... | collective-permute-start | bytes 18874376 | tf_op jit(solution)/shard_map/ppermute | solution.py:470
  402.5 193.0 %all-gather.6.cloned.1.call-start = ((), (), s32[]{:S(2)}) async-start(), calls=%async_computation.9 | async-start | bytes 2654208 | tf_op jit(solution)/shard_map/all_gather | solution.py:376
  484.2 30.3 %collective-permute-start.4 = (f32[4,512,768]{2,1,0:T(8,128)}, f32[4,512,768]{2,1,0:T(8,128)}, u32[]{:S(2)}, u32[]{:S(2)}) collective-permute-start(f32[4,512,768]{2,1,0:T(8,128)} %slice.545), channel_id=1, source_target_pairs={{0,1},{1,0},{2,3},{3,2},{4,5},{5,4},{6,7},{7,6},{8,9},{9,8},{10,11... | collective-permute-start | bytes 18874376 | tf_op jit(solution)/shard_map/ppermute | solution.py:470
  504.3 15.6 %collective-permute-start.5 = (f32[4,512,768]{2,1,0:T(8,128)}, f32[4,512,768]{2,1,0:T(8,128)}, u32[]{:S(2)}, u32[]{:S(2)}) collective-permute-start(f32[4,512,768]{2,1,0:T(8,128)} %slice.548), channel_id=1, source_target_pairs={{0,1},{1,0},{2,3},{3,2},{4,5},{5,4},{6,7},{7,6},{8,9},{9,8},{10,11... | collective-permute-start | bytes 18874376 | tf_op jit(solution)/shard_map/ppermute | solution.py:470
  505.5 138.3 %reduce-scatter.5.cloned.1.call-start = ((), (), s32[]{:S(2)}) async-start(), calls=%async_computation.8 | async-start | bytes 2359296 | tf_op jit(solution)/shard_map/reduce_scatter | solution.py:719
  528.8 159.6 %all-to-all-start.1 = ((bf16[4,2,512,768]{3,2,1,0:T(8,128)(2,1)}), bf16[4,2,512,768]{3,2,1,0:T(8,128)(2,1)}, u32[]{:S(2)}, u32[]{:S(2)}) async-start(bf16[4,2,512,768]{3,2,1,0:T(8,128)(2,1)} %copy.248), calls=%async_computation.1 | async-start | bytes 12582912 | tf_op jit(solution)/shard_map/all_to_all | solution.py:468
  534.3 110.9 %reduce-scatter.3.cloned.1.call-start = ((), (), s32[]{:S(2)}) async-start(), calls=%async_computation.7 | async-start | bytes 4718592 | tf_op jit(solution)/shard_map/reduce_scatter | solution.py:718
  546.7 226.4 %all-reduce.15.cloned.1.call-start = ((), (), s32[]{:S(2)}) async-start(), calls=%async_computation.6 | async-start | bytes 6291456 | tf_op jit(solution)/shard_map/psum | solution.py:673
  652.1 41.2 %copy-start.131 = (s32[1024,2]{0,1:T(2,128)S(1)}, s32[1024,2]{0,1:T(2,128)}, u32[]{:S(2)}) copy-start(s32[1024,2]{0,1:T(2,128)} %fusion.173) | copy-start | bytes 24580
  652.1 41.2 %copy-start.139 = (pred[1024,2]{0,1:T(4,128)(4,1)S(1)}, pred[1024,2]{0,1:T(4,128)(4,1)}, u32[]{:S(2)}) copy-start(pred[1024,2]{0,1:T(4,128)(4,1)} %fusion.179) | copy-start | bytes 6148
  705.2 326.7 %all-reduce.17.cloned.1.call-start = ((), (), s32[]{:S(2)}) async-start(), calls=%async_computation.10 | async-start | bytes 12582912 | tf_op jit(solution)/shard_map/psum | solution.py:673
  731.5 41.5 %copy-start.2 = (f32[1024,768]{1,0:T(8,128)S(1)}, f32[1024,768]{1,0:T(8,128)}, u32[]{:S(2)}) copy-start(f32[1024,768]{1,0:T(8,128)} %copy-done.1) | copy-start | bytes 9437188
  731.5 41.5 %copy-start.53 = (bf16[768,4]{1,0:T(8,128)(2,1)S(1)}, bf16[768,4]{1,0:T(8,128)(2,1)}, u32[]{:S(2)}) copy-start(bf16[768,4]{1,0:T(8,128)(2,1)} %reshape_reshape.22) | copy-start | bytes 18436
  731.5 41.5 %copy-start.91 = (f32[768]{0:T(1024)S(1)}, f32[768]{0:T(1024)}, u32[]{:S(2)}) copy-start(f32[768]{0:T(1024)} %reshape.1339) | copy-start | bytes 9220
  731.5 41.5 %copy-start.93 = (f32[1024]{0:T(1024)S(1)}, f32[1024]{0:T(1024)}, u32[]{:S(2)}) copy-start(f32[1024]{0:T(1024)} %copy-done.92) | copy-start | bytes 12292
  860.7 14.0 %collective-permute-start.6 = (bf16[1024,3,64]{0,2,1:T(8,128)(2,1)S(1)}, bf16[1024,3,64]{0,2,1:T(8,128)(2,1)}, u32[]{:S(2)}, u32[]{:S(2)}) collective-permute-start(bf16[1024,3,64]{0,2,1:T(8,128)(2,1)S(1)} %slice.660), channel_id=1, source_target_pairs={{4,0},{5,1},{6,2},{7,3},{12,8},{13,9},{14,10},{15,11},{20,16},{21,... | collective-permute-start | bytes 1179656 | tf_op jit(solution)/shard_map/ppermute | solution.py:27
  862.8 19.1 %collective-permute-start.7 = (bf16[1024,3,64]{0,2,1:T(8,128)(2,1)}, bf16[1024,3,64]{0,2,1:T(8,128)(2,1)}, u32[]{:S(2)}, u32[]{:S(2)}) collective-permute-start(bf16[1024,3,64]{0,2,1:T(8,128)(2,1)} %slice.659), channel_id=1, source_target_pairs={{4,0},{5,1},{6,2},{7,3},{12,8},{13,9},{14,10},{15,11},{20,16},{21,... | collective-permute-start | bytes 1179656 | tf_op jit(solution)/shard_map/ppermute | solution.py:27
  1026.3 43.1 %copy-start.68 = (f32[192,96]{1,0:T(8,128)}, f32[192,96]{1,0:T(8,128)S(1)}, u32[]{:S(2)}) copy-start(f32[192,96]{1,0:T(8,128)S(1)} %reshape.1323) | copy-start | bytes 221188
  1086.2 59.2 %copy-start.13 = (f32[1,384,2,512]{3,1,2,0:T(8,128)S(1)}, f32[1,384,2,512]{3,1,2,0:T(8,128)}, u32[]{:S(2)}) copy-start(f32[1,384,2,512]{3,1,2,0:T(8,128)} %reduce-scatter.3.cloned.1.call-done) | copy-start | bytes 4718596
  1086.2 87.3 %copy-start.20 = (f32[1,384,2,512]{3,2,1,0:T(2,128)S(1)}, f32[1,384,2,512]{3,2,1,0:T(2,128)}, u32[]{:S(2)}) copy-start(f32[1,384,2,512]{3,2,1,0:T(2,128)} %param.34) | copy-start | bytes 4718596
  1106.9 40.2 %copy-start.114 = (f32[1,1,512]{2,1,0:T(1,128)S(1)}, f32[1,1,512]{2,1,0:T(1,128)}, u32[]{:S(2)}) copy-start(f32[1,1,512]{2,1,0:T(1,128)} %fusion.193) | copy-start | bytes 6148
  1109.1 64.4 %copy-start.112 = (f32[512]{0:T(512)}, f32[512]{0:T(512)S(1)}, u32[]{:S(2)}) copy-start(f32[512]{0:T(512)S(1)} %multiply_add_fusion.9) | copy-start | bytes 6148
  (138 other events, 950.6 us)
Sparse Core Ops, SparseCore 0:
  133.5 73.8 all-reduce.12
  505.6 89.7 all-gather.5
  705.3 67.6 all-reduce.14
  886.2 119.1 all-reduce.16
Sparse Core Ops, SparseCore 1:
  402.6 34.4 all-gather.3
  514.6 24.8 reduce-scatter.4
  546.7 43.7 reduce-scatter.2

commit v13 on v12

--- a/solution.py
+++ b/solution.py
@@ -472,7 +472,18 @@
     )
     half = capacity // 2
     side = lax.axis_index("tp") % 2
-    mine = exchange(lax.dynamic_slice_in_dim(send_rows, side * half, half, 2))
+    if pair_count == 4 and half % 2 == 0:
+        quarter = half // 2
+        row_side = (lax.axis_index("tp") // 2) % 2
+        piece = exchange(
+            lax.dynamic_slice_in_dim(send_rows, (2 * side + row_side) * quarter, quarter, 2)
+        )
+        other = lax.ppermute(piece, "tp", [(0, 2), (1, 3), (2, 0), (3, 1)])
+        mine = lax.dynamic_slice_in_dim(
+            jnp.concatenate([piece, other, piece], axis=2), row_side * quarter, half, 2
+        )
+    else:
+        mine = exchange(lax.dynamic_slice_in_dim(send_rows, side * half, half, 2))
     received_both = jnp.concatenate([mine, swap(mine)], axis=2)
     received = received_both[:, 0].reshape(experts * capacity, model_width)
     grad_received = received_both[:, 1].reshape(experts * capacity, model_width)

time: 1220 us -> 1230 us (level)
  waiting for transfers between devices: 147 us -> 216 us
  blocking collectives: 172 us -> 105 us
  other arithmetic: 170 us -> 186 us
  local copies, waits for them, and re-layouts: 280 us -> 267 us
    ppermute x0 -> x1, waiting for transfers between devices: none -> 68 us  [experts_routed(): other = lax.ppermute(piece, 'tp', [(0, 2), (1, 3), (2, 0), (3, 1)])]
    all_to_all x1, blocking collectives: 143 us -> 75.1 us  [experts_routed(): lax.all_to_all(rows, 'fsdp', split_axis=0, concat_axis=0, tiled=True)]
    concatenate x0 -> x2, other arithmetic: none -> 18.6 us  [the longest x1 10.4 us: experts_routed(): received_both = jnp.concatenate([mine, swap(mine)], axis=2)]
    unnamed x304 -> x303, local copies, waits for them, and re-layouts: 52.9 us -> 49.7 us
  transfers between devices with their start and end apart: 16 -> 17, of which waited for: 6 -> 7; matrix products, arithmetic and copies ran while one was open for 22% -> 22% of each run, Pallas kernels for 9% -> 9%
where the time goes in v13:
time: 1230 us; the launch traced here: 1220 us
  local copies, waits for them, and re-layouts  267 us (22%)
  waiting for transfers between devices  216 us (18%)
  matrix products  196 us (16%)
  other arithmetic  186 us (15%)
  Pallas kernels  177 us (14%)
  blocking collectives  105 us (9%)
  between operations  42.9 us (3%)
  starting transfers between devices  19.2 us (2%)
    pallas_call x1, Pallas kernels, halving_scatter(): pl.pallas_call(halving_kernel, out_shape=jax.ShapeDtypeStruct((2 * rows,...  105 us
    all_to_all x1, blocking collectives, experts_routed(): lax.all_to_all(rows, 'fsdp', split_axis=0, concat_axis=0, tiled=True)  75.1 us
    ppermute x1, waiting for transfers between devices, experts_routed(): other = lax.ppermute(piece, 'tp', [(0, 2), (1, 3), (2, 0), (3, 1)])  68 us
    psum x1, waiting for transfers between devices, local(): lax.psum(jnp.dot(mixed_heads, attn_out_low, preferred_element_type=jnp.fl...  54.2 us
    unnamed x303, local copies, waits for them, and re-layouts  49.7 us
    pallas_call x2, Pallas kernels, butterfly_sum(): pl.pallas_call(butterfly_kernel, out_shape=jax.ShapeDtypeStruct((rows, 12...  44.7 us
    psum x2, waiting for transfers between devices, local(): lax.psum((shared_out + combined, partial_two, gate_dots), 'tp')  36.2 us
    all_to_all x1, waiting for transfers between devices, experts_routed(): lax.all_to_all(rows, 'fsdp', split_axis=0, concat_axis=0, tiled=True)  36.1 us
  transfers between devices with their start and end apart: 17, of which 7 were waited for; matrix products, arithmetic and copies ran while one was open for 22% of the time, Pallas kernels for 9%

profile of v13, /device:TPU:0, one launch (start us, length us, event | category | flops | bytes accessed | tf_op | source)
XLA Modules:
  0.0 1217.3 jit_solution(10708661054088248168)
XLA Ops:
  17.3 27.6 %shard_map.395 = bf16[8,592,128]{2,1,0:T(8,128)(2,1)} custom-call(bf16[592,128]{1,0:T(8,128)(2,1)} %pad_bitcast_fusion.2.x_ref), custom_call_target="tpu_custom_call" | custom-call | tf_op jit(solution)/shard_map/pallas_call | solution.py:352
  88.3 39.3 %while.39 = (s32[]{:T(128)}, bf16[2,512,3,64]{1,3,2,0:T(8,128)(2,1)}, f32[2,3,512,1]{2,1,3,0:T(4,128)}, s32[2]{0:T(128)}, bf16[2048,3,64]{0,2,1:T(8,128)(2,1)S(1...) while((s32[]{:T(128)}, ...), condition=%wide.region_4.5_spmd, body=%wide.region_1.4_spmd.sunk | while | flops 644092928 | bytes 33331516 | solution.py:635
  137.0 8.1 scatter_custom_fusion
  145.1 8.1 scatter_custom_fusion.1
  153.2 54.2 %all-reduce.13.cloned.1.call-done = f32[1024,768]{1,0:T(8,128)} async-done(((f32[1024,768]{1,0:T(8,128)}), f32[1024,768]{1,0:T(8,128)}) %all-reduce.13.cloned.1.call-update) | async-done | bytes 3145744 | tf_op jit(solution)/shard_map/psum | solution.py:637
  212.7 23.0 %gather_fusion = f32[4096]{0:T(1024)S(1)} fusion(f32[2048]{0:T(1024)S(1)} %div.433, s32[4096]{0:T(1024)S(1)} %get-tuple-element.931), kind=kCustom, calls=%fused_computation | custom fusion | bytes 49152 | tf_op jit(solution)/shard_map/gather | solution.py:458
  235.8 9.6 fusion.78
  245.4 10.2 multiply_convert_fusion.1
  255.9 75.1 %all_to_all.10 = bf16[4,2,256,768]{3,2,1,0:T(8,128)(2,1)} all-to-all(bf16[4,2,256,768]{3,2,1,0:T(8,128)(2,1)S(1)} %fusion.106), channel_id=1, replica_groups=mesh['fsdp'=4,'ctx'=2,'tp'=4] {'fsdp'}, dimensions={0} | all-to-all | bytes 6291456 | tf_op jit(solution)/shard_map/all_to_all | solution.py:468
  331.8 68.0 %collective-permute-done.3 = bf16[4,2,256,768]{3,2,1,0:T(8,128)(2,1)} collective-permute-done((bf16[4,2,256,768]{3,2,1,0:T(8,128)(2,1)}, bf16[4,2,256,768]{3,2,1,0:T(8,128)(2,1)}, u32[]{:S(2)}, u32[]{:S(2)}) %collective-permute-start.3) | collective-permute-done | bytes 3145760 | tf_op jit(solution)/shard_map/ppermute | solution.py:481
  399.8 8.2 fusion.82
  416.9 21.4 %all_gather.15 = bf16[1,512,768]{2,1,0:T(8,128)(2,1)} all-gather(bf16[1,512,384]{2,1,0:T(8,128)(2,1)S(1)} %get-tuple-element.897), channel_id=1, replica_groups=mesh['fsdp'=4,'ctx'=2,'tp'=4] {'ctx'}, dimensions={2}, use_global_device_ids=true | all-gather | bytes 1179648 | tf_op jit(solution)/shard_map/all_gather | solution.py:588
  438.3 10.4 fusion.83
  448.7 9.3 fusion.124
  463.9 15.7 %fusion.67 = (f32[4096,1,512]{2,0,1:T(8,128)}, f32[4096,1,512]{2,0,1:T(8,128)}) fusion(f32[4096,2,512]{2,0,1:T(8,128)} %copy-done.16, bf16[4096,768]{1,0:T(8,128)(2,1)} %bitcast.489, bf16[1,512,768]{2,1,0:T(8,128)(2,1)S(1)} %copy-done.46), kind=kOutput, calls=%fused_computation.96 | convolution fusion | flops 3246391296 | bytes 40632320 | tf_op jit(solution)/shard_map/rd,fd->rf/dot_general | solution.py:494
  511.0 8.7 fusion.137
  539.4 12.3 %convolution_bitcast_fusion.1 = f32[1,768,2,512]{3,1,2,0:T(8,128)} fusion(bf16[4096,768,1]{1,0,2:T(8,128)(2,1)} %bitcast.488, bf16[4096,2,512]{2,0,1:T(8,128)(2,1)} %copy-done.27), kind=kOutput, calls=%fused_computation.167 | convolution fusion | flops 6442450944 | bytes 17825792 | tf_op jit(solution)/shard_map/rd,rgf->dgf/dot_general | solution.py:498
  588.6 12.9 %all-gather.6.cloned.1.call-done = bf16[1179648]{0:T(1024)(128)(2,1)} async-done(((bf16[147456]{0:T(1024)(128)(2,1)}), bf16[1179648]{0:T(1024)(128)(2,1)}) %all-gather.6.cloned.1.call-update) | async-done | bytes 2359312 | tf_op jit(solution)/shard_map/all_gather | solution.py:376
  658.2 36.1 %all-to-all-done.1 = bf16[4,2,512,768]{3,2,1,0:T(8,128)(2,1)} async-done(((bf16[4,2,512,768]{3,2,1,0:T(8,128)(2,1)}), bf16[4,2,512,768]{3,2,1,0:T(8,128)(2,1)}, u32[]{:S(2)}, u32[]{:S(2)}) %all-to-all-start.1) | async-done | bytes 6291488 | tf_op jit(solution)/shard_map/all_to_all | solution.py:468
  699.3 8.2 fusion.107
  711.8 12.3 %multiply_reduce_fusion.1 = (f32[1024,2]{0,1:T(2,128)S(1)}, f32[1024,768]{0,1:T(8,128)}) fusion(f32[1024,768]{0,1:T(8,128)} %copy.253, f32[1024,2]{0,1:T(2,128)S(1)} %copy-done.111, bf16[2048,768,1]{1,0,2:T(8,128)(2,1)} %bitcast.498, s32[1024,2]{0,1:T(2,128)S(1)} %copy-done.131, pred[1024,2]{0,1:T(4,128)(4,1)S(1)} %copy-done.139), kind=kOutput, calls=%fused_computation.117 | convolution fusion | flops 6456342528 | bytes 9463808 | tf_op jit(solution)/shard_map/dot_general | solution.py:517
  724.1 8.2 psum.38
  742.7 36.2 %all-reduce.15.cloned.1.call-done = f32[1024,768]{1,0:T(8,128)} async-done(((f32[1024,768]{1,0:T(8,128)}), f32[1024,768]{1,0:T(8,128)}) %all-reduce.15.cloned.1.call-update) | async-done | bytes 3145744 | tf_op jit(solution)/shard_map/psum | solution.py:684
  788.8 76.7 %while.40 = (s32[]{:T(128)}, f32[2048,3,64]{0,2,1:T(8,128)}, f32[2048,3,64]{0,2,1:T(8,128)S(1)}, f32[1024,3,64]{0,2,1:T(8,128)}, bf16[1024,3,64]{0,2,1:T(8,128)(...) while((s32[]{:T(128)}, f32[2048,3,64]{0,2,1:T(8,128)}, ...), condition=%wide.region_26.27_spmd, body=%wide.region_24.26_spmd.sunk | while | flops 1541608448 | bytes 106823088 | solution.py:786
  796.9 8.8 multiply_reduce_fusion.22
  805.7 9.4 multiply_convert_fusion.6
  835.2 8.9 multiply_reduce_fusion.22
  844.1 9.4 multiply_convert_fusion.6
  918.8 105.1 %shard_map.396 = f32[1792,128]{1,0:T(8,128)} custom-call(f32[2,2,2,1792,128]{4,3,2,1,0:T(8,128)} %bitcast.477), custom_call_target="tpu_custom_call" | custom-call | tf_op jit(solution)/shard_map/pallas_call | solution.py:280
  1046.3 29.1 %shard_map.397 = f32[344,128]{1,0:T(8,128)} custom-call(f32[344,128]{1,0:T(8,128)} %pad_bitcast_fusion.1.x_ref), custom_call_target="tpu_custom_call" | custom-call | tf_op jit(solution)/shard_map/pallas_call | solution.py:162
  1084.3 7.8 slice.488
  1159.8 15.6 %shard_map.398 = f32[8,128]{1,0:T(8,128)} custom-call(f32[8,128]{1,0:T(8,128)} %pad_bitcast_fusion.3.x_ref), custom_call_target="tpu_custom_call" | custom-call | tf_op jit(solution)/shard_map/pallas_call | solution.py:162
  (673 shorter events, 488.5 us)
Async XLA Ops:
  8.0 199.4 %all-reduce.13.cloned.1.call-start = ((), (), s32[]{:S(2)}) async-start(), calls=%async_computation.4 | async-start | bytes 6291456 | tf_op jit(solution)/shard_map/psum | solution.py:637
  59.7 26.3 %collective-permute-start.2 = (bf16[1024,3,64]{0,2,1:T(8,128)(2,1)}, bf16[1024,3,64]{0,2,1:T(8,128)(2,1)}, u32[]{:S(2)}, u32[]{:S(2)}) collective-permute-start(bf16[1024,3,64]{0,2,1:T(8,128)(2,1)} %pad_maximum_fusion.5), channel_id=1, source_target_pairs={{0,4},{1,5},{2,6},{3,7},{8,12},{9,13},{10,14},{11,15},{16,20},{17,... | collective-permute-start | bytes 1179656 | tf_op jit(solution)/shard_map/ppermute | solution.py:27
  66.1 21.0 %collective-permute-start = (bf16[1024,3,64]{0,2,1:T(8,128)(2,1)S(1)}, bf16[1024,3,64]{0,2,1:T(8,128)(2,1)}, u32[]{:S(2)}, u32[]{:S(2)}) collective-permute-start(bf16[1024,3,64]{0,2,1:T(8,128)(2,1)S(1)} %bitcast.517), channel_id=1, source_target_pairs={{0,4},{1,5},{2,6},{3,7},{8,12},{9,13},{10,14},{11,15},{16,20},{17,... | collective-permute-start | bytes 1179656 | tf_op jit(solution)/shard_map/ppermute | solution.py:27
  68.2 17.1 %collective-permute-start.1 = (bf16[1024]{0:T(1024)(128)(2,1)S(1)}, bf16[1024]{0:T(1024)(128)(2,1)}, u32[]{:S(2)}, u32[]{:S(2)}) collective-permute-start(bf16[1024]{0:T(1024)(128)(2,1)S(1)} %convert_reduce_fusion), channel_id=1, source_target_pairs={{0,4},{1,5},{2,6},{3,7},{8,12},{9,13},{10,14},{11,15},{16,20},{17,... | collective-permute-start | bytes 6152 | tf_op jit(solution)/shard_map/ppermute | solution.py:27
  127.6 83.1 %copy-start.72 = (bf16[2048]{0:T(1024)(128)(2,1)}, bf16[2048]{0:T(1024)(128)(2,1)S(1)}, u32[]{:S(2)}) copy-start(bf16[2048]{0:T(1024)(128)(2,1)S(1)} %get-tuple-element.1242) | copy-start | bytes 12292
  127.6 83.1 %copy-start.85 = (bf16[1024]{0:T(1024)(128)(2,1)}, bf16[1024]{0:T(1024)(128)(2,1)S(1)}, u32[]{:S(2)}) copy-start(bf16[1024]{0:T(1024)(128)(2,1)S(1)} %get-tuple-element.1245) | copy-start | bytes 6148
  133.4 315.3 %all-gather.4.cloned.1.call-start = ((), (), s32[]{:S(2)}) async-start(), calls=%async_computation.5 | async-start | bytes 2359296 | tf_op jit(solution)/shard_map/all_gather | solution.py:587
  137.0 72.8 %copy-start.88 = (s32[2048]{0:T(1024)}, s32[2048]{0:T(1024)S(1)}, u32[]{:S(2)}) copy-start(s32[2048]{0:T(1024)S(1)} %fusion.171) | copy-start | bytes 24580
  153.2 57.2 %copy-start.90 = (f32[768]{0:T(1024)S(1)}, f32[768]{0:T(1024)}, u32[]{:S(2)}) copy-start(f32[768]{0:T(1024)} %reshape.1339) | copy-start | bytes 9220
  330.9 68.9 %collective-permute-start.3 = (bf16[4,2,256,768]{3,2,1,0:T(8,128)(2,1)}, bf16[4,2,256,768]{3,2,1,0:T(8,128)(2,1)}, u32[]{:S(2)}, u32[]{:S(2)}) collective-permute-start(bf16[4,2,256,768]{3,2,1,0:T(8,128)(2,1)} %all_to_all.10), channel_id=1, source_target_pairs={{0,2},{1,3},{2,0},{3,1},{4,6},{5,7},{6,4},{7,5},{8,10},{9,11},{10,... | collective-permute-start | bytes 9437192 | tf_op jit(solution)/shard_map/ppermute | solution.py:481
  331.8 76.2 %copy-start.19 = (f32[1,384,2,512]{3,2,1,0:T(2,128)S(1)}, f32[1,384,2,512]{3,2,1,0:T(2,128)}, u32[]{:S(2)}) copy-start(f32[1,384,2,512]{3,2,1,0:T(2,128)} %param.34) | copy-start | bytes 4718596
  408.1 30.3 %collective-permute-start.4 = (bf16[4,2,512,768]{3,2,1,0:T(8,128)(2,1)}, bf16[4,2,512,768]{3,2,1,0:T(8,128)(2,1)}, u32[]{:S(2)}, u32[]{:S(2)}) collective-permute-start(bf16[4,2,512,768]{3,2,1,0:T(8,128)(2,1)} %fusion.82), channel_id=1, source_target_pairs={{0,1},{1,0},{2,3},{3,2},{4,5},{5,4},{6,7},{7,6},{8,9},{9,8},{10,11... | collective-permute-start | bytes 18874376 | tf_op jit(solution)/shard_map/ppermute | solution.py:470
  409.2 192.4 %all-gather.6.cloned.1.call-start = ((), (), s32[]{:S(2)}) async-start(), calls=%async_computation.9 | async-start | bytes 2654208 | tf_op jit(solution)/shard_map/all_gather | solution.py:376
  489.5 30.3 %collective-permute-start.5 = (f32[4,512,768]{2,1,0:T(8,128)}, f32[4,512,768]{2,1,0:T(8,128)}, u32[]{:S(2)}, u32[]{:S(2)}) collective-permute-start(f32[4,512,768]{2,1,0:T(8,128)} %slice.546), channel_id=1, source_target_pairs={{0,1},{1,0},{2,3},{3,2},{4,5},{5,4},{6,7},{7,6},{8,9},{9,8},{10,11... | collective-permute-start | bytes 18874376 | tf_op jit(solution)/shard_map/ppermute | solution.py:470
  509.5 15.5 %collective-permute-start.6 = (f32[4,512,768]{2,1,0:T(8,128)}, f32[4,512,768]{2,1,0:T(8,128)}, u32[]{:S(2)}, u32[]{:S(2)}) collective-permute-start(f32[4,512,768]{2,1,0:T(8,128)} %slice.548), channel_id=1, source_target_pairs={{0,1},{1,0},{2,3},{3,2},{4,5},{5,4},{6,7},{7,6},{8,9},{9,8},{10,11... | collective-permute-start | bytes 18874376 | tf_op jit(solution)/shard_map/ppermute | solution.py:470
  510.8 139.2 %reduce-scatter.5.cloned.1.call-start = ((), (), s32[]{:S(2)}) async-start(), calls=%async_computation.8 | async-start | bytes 2359296 | tf_op jit(solution)/shard_map/reduce_scatter | solution.py:730
  534.1 160.2 %all-to-all-start.1 = ((bf16[4,2,512,768]{3,2,1,0:T(8,128)(2,1)}), bf16[4,2,512,768]{3,2,1,0:T(8,128)(2,1)}, u32[]{:S(2)}, u32[]{:S(2)}) async-start(bf16[4,2,512,768]{3,2,1,0:T(8,128)(2,1)} %copy.248), calls=%async_computation.1 | async-start | bytes 12582912 | tf_op jit(solution)/shard_map/all_to_all | solution.py:468
  539.3 112.0 %reduce-scatter.3.cloned.1.call-start = ((), (), s32[]{:S(2)}) async-start(), calls=%async_computation.7 | async-start | bytes 4718592 | tf_op jit(solution)/shard_map/reduce_scatter | solution.py:729
  551.7 227.2 %all-reduce.15.cloned.1.call-start = ((), (), s32[]{:S(2)}) async-start(), calls=%async_computation.6 | async-start | bytes 6291456 | tf_op jit(solution)/shard_map/psum | solution.py:684
  658.2 41.0 %copy-start.131 = (s32[1024,2]{0,1:T(2,128)S(1)}, s32[1024,2]{0,1:T(2,128)}, u32[]{:S(2)}) copy-start(s32[1024,2]{0,1:T(2,128)} %fusion.176) | copy-start | bytes 24580
  658.2 41.0 %copy-start.139 = (pred[1024,2]{0,1:T(4,128)(4,1)S(1)}, pred[1024,2]{0,1:T(4,128)(4,1)}, u32[]{:S(2)}) copy-start(pred[1024,2]{0,1:T(4,128)(4,1)} %fusion.182) | copy-start | bytes 6148
  711.1 326.8 %all-reduce.17.cloned.1.call-start = ((), (), s32[]{:S(2)}) async-start(), calls=%async_computation.10 | async-start | bytes 12582912 | tf_op jit(solution)/shard_map/psum | solution.py:684
  737.4 41.5 %copy-start.2 = (f32[1024,768]{1,0:T(8,128)S(1)}, f32[1024,768]{1,0:T(8,128)}, u32[]{:S(2)}) copy-start(f32[1024,768]{1,0:T(8,128)} %copy-done.1) | copy-start | bytes 9437188
  737.4 41.5 %copy-start.53 = (bf16[768,4]{1,0:T(8,128)(2,1)S(1)}, bf16[768,4]{1,0:T(8,128)(2,1)}, u32[]{:S(2)}) copy-start(bf16[768,4]{1,0:T(8,128)(2,1)} %reshape_reshape.22) | copy-start | bytes 18436
  737.4 41.5 %copy-start.91 = (f32[768]{0:T(1024)S(1)}, f32[768]{0:T(1024)}, u32[]{:S(2)}) copy-start(f32[768]{0:T(1024)} %reshape.1339) | copy-start | bytes 9220
  737.4 41.5 %copy-start.93 = (f32[1024]{0:T(1024)S(1)}, f32[1024]{0:T(1024)}, u32[]{:S(2)}) copy-start(f32[1024]{0:T(1024)} %copy-done.92) | copy-start | bytes 12292
  866.7 14.0 %collective-permute-start.7 = (bf16[1024,3,64]{0,2,1:T(8,128)(2,1)S(1)}, bf16[1024,3,64]{0,2,1:T(8,128)(2,1)}, u32[]{:S(2)}, u32[]{:S(2)}) collective-permute-start(bf16[1024,3,64]{0,2,1:T(8,128)(2,1)S(1)} %slice.666), channel_id=1, source_target_pairs={{4,0},{5,1},{6,2},{7,3},{12,8},{13,9},{14,10},{15,11},{20,16},{21,... | collective-permute-start | bytes 1179656 | tf_op jit(solution)/shard_map/ppermute | solution.py:27
  868.8 19.1 %collective-permute-start.8 = (bf16[1024,3,64]{0,2,1:T(8,128)(2,1)}, bf16[1024,3,64]{0,2,1:T(8,128)(2,1)}, u32[]{:S(2)}, u32[]{:S(2)}) collective-permute-start(bf16[1024,3,64]{0,2,1:T(8,128)(2,1)} %slice.665), channel_id=1, source_target_pairs={{4,0},{5,1},{6,2},{7,3},{12,8},{13,9},{14,10},{15,11},{20,16},{21,... | collective-permute-start | bytes 1179656 | tf_op jit(solution)/shard_map/ppermute | solution.py:27
  1032.3 43.1 %copy-start.68 = (f32[192,96]{1,0:T(8,128)}, f32[192,96]{1,0:T(8,128)S(1)}, u32[]{:S(2)}) copy-start(f32[192,96]{1,0:T(8,128)S(1)} %reshape.1323) | copy-start | bytes 221188
  1092.1 59.2 %copy-start.13 = (f32[1,384,2,512]{3,1,2,0:T(8,128)S(1)}, f32[1,384,2,512]{3,1,2,0:T(8,128)}, u32[]{:S(2)}) copy-start(f32[1,384,2,512]{3,1,2,0:T(8,128)} %reduce-scatter.3.cloned.1.call-done) | copy-start | bytes 4718596
  1092.1 87.3 %copy-start.20 = (f32[1,384,2,512]{3,2,1,0:T(2,128)S(1)}, f32[1,384,2,512]{3,2,1,0:T(2,128)}, u32[]{:S(2)}) copy-start(f32[1,384,2,512]{3,2,1,0:T(2,128)} %param.34) | copy-start | bytes 4718596
  1115.0 64.3 %copy-start.112 = (f32[512]{0:T(512)}, f32[512]{0:T(512)S(1)}, u32[]{:S(2)}) copy-start(f32[512]{0:T(512)S(1)} %multiply_add_fusion.9) | copy-start | bytes 6148
  (139 other events, 991.0 us)
Sparse Core Ops, SparseCore 0:
  133.5 73.8 all-reduce.12
  510.9 90.6 all-gather.5
  711.2 67.6 all-reduce.14
  892.2 119.1 all-reduce.16
Sparse Core Ops, SparseCore 1:
  409.3 35.0 all-gather.3
  519.8 25.6 reduce-scatter.4
  551.8 44.6 reduce-scatter.2

commit v14 on v13

--- a/solution.py
+++ b/solution.py
@@ -472,6 +472,36 @@
     )
     half = capacity // 2
     side = lax.axis_index("tp") % 2
+    def expert_block(block):
+        rows_in = block[:, 0].reshape(-1, model_width)
+        grads_in = block[:, 1].reshape(-1, model_width)
+        gate_up = jnp.einsum(
+            "rd,dgf->rgf", rows_in, expert_in_low, preferred_element_type=jnp.float32
+        )
+        act, act_back = jax.vjp(swiglu, gate_up)
+        hidden = act.astype(jnp.bfloat16)
+        outs = jnp.dot(hidden, expert_down_low, preferred_element_type=jnp.float32)
+        grad_hidden = jnp.einsum(
+            "rd,fd->rf", grads_in, expert_down_low, preferred_element_type=jnp.float32
+        )
+        grad_gate_up = act_back(grad_hidden)[0].astype(jnp.bfloat16)
+        grad_in = jnp.einsum(
+            "rd,rgf->dgf", rows_in, grad_gate_up, preferred_element_type=jnp.float32
+        )
+        grad_down = jnp.einsum("rf,rd->fd", hidden, grads_in, preferred_element_type=jnp.float32)
+        grad_expert_rows = jnp.einsum(
+            "rgf,dgf->rd", grad_gate_up, expert_in_low, preferred_element_type=jnp.float32
+        )
+        width = block.shape[2]
+        return (
+            [
+                outs.reshape(experts, width, model_width),
+                grad_expert_rows.reshape(experts, width, model_width),
+            ],
+            grad_in,
+            grad_down,
+        )
+
     if pair_count == 4 and half % 2 == 0:
         quarter = half // 2
         row_side = (lax.axis_index("tp") // 2) % 2
@@ -479,31 +509,27 @@
             lax.dynamic_slice_in_dim(send_rows, (2 * side + row_side) * quarter, quarter, 2)
         )
         other = lax.ppermute(piece, "tp", [(0, 2), (1, 3), (2, 0), (3, 1)])
-        mine = lax.dynamic_slice_in_dim(
-            jnp.concatenate([piece, other, piece], axis=2), row_side * quarter, half, 2
-        )
+        results_a, grad_in_a, grad_down_a = expert_block(
+            jnp.concatenate([piece, swap(piece)], axis=2)
+        )
+        results_b, grad_in_b, grad_down_b = expert_block(
+            jnp.concatenate([other, swap(other)], axis=2)
+        )
+        grad_in = grad_in_a + grad_in_b
+        grad_down = grad_down_a + grad_down_b
+        pair_sums = []
+        for rows_a, rows_b in zip(results_a, results_b):
+            sum_a = rows_a[:, :quarter] + swap(rows_a[:, quarter:])
+            sum_b = rows_b[:, :quarter] + swap(rows_b[:, quarter:])
+            pair_sums.append(
+                lax.dynamic_slice_in_dim(
+                    jnp.concatenate([sum_a, sum_b, sum_a], axis=1), row_side * quarter, half, 1
+                )
+            )
     else:
         mine = exchange(lax.dynamic_slice_in_dim(send_rows, side * half, half, 2))
-    received_both = jnp.concatenate([mine, swap(mine)], axis=2)
-    received = received_both[:, 0].reshape(experts * capacity, model_width)
-    grad_received = received_both[:, 1].reshape(experts * capacity, model_width)
-    gate_up = jnp.einsum("rd,dgf->rgf", received, expert_in_low, preferred_element_type=jnp.float32)
-    act, act_back = jax.vjp(swiglu, gate_up)
-    hidden = act.astype(jnp.bfloat16)
-    outs = jnp.dot(hidden, expert_down_low, preferred_element_type=jnp.float32)
-    grad_hidden = jnp.einsum(
-        "rd,fd->rf", grad_received, expert_down_low, preferred_element_type=jnp.float32
-    )
-    grad_gate_up = act_back(grad_hidden)[0].astype(jnp.bfloat16)
-    grad_in = jnp.einsum("rd,rgf->dgf", received, grad_gate_up, preferred_element_type=jnp.float32)
-    grad_down = jnp.einsum("rf,rd->fd", hidden, grad_received, preferred_element_type=jnp.float32)
-    grad_expert_rows = jnp.einsum(
-        "rgf,dgf->rd", grad_gate_up, expert_in_low, preferred_element_type=jnp.float32
-    )
-    pair_sums = []
-    for rows in (outs, grad_expert_rows):
-        rows = rows.reshape(experts, capacity, model_width)
-        pair_sums.append(rows[:, :half] + swap(rows[:, half:]))
+        results, grad_in, grad_down = expert_block(jnp.concatenate([mine, swap(mine)], axis=2))
+        pair_sums = [rows[:, :half] + swap(rows[:, half:]) for rows in results]
     held = exchange(jnp.stack(pair_sums, axis=1).astype(jnp.bfloat16))
     slot_expert = slot_index // capacity
     slot_rank = slot_index % capacity

time: 1230 us -> 1180 us (0.959)
  waiting for transfers between devices: 216 us -> 171 us
  other arithmetic: 186 us -> 171 us
  local copies, waits for them, and re-layouts: 267 us -> 282 us
    ppermute x1, waiting for transfers between devices: 68 us -> 37.8 us  [experts_routed(): other = lax.ppermute(piece, 'tp', [(0, 2), (1, 3), (2, 0), (3, 1)])]
    concatenate x2 -> x0, other arithmetic: 18.6 us -> none  [the longest x1 10.4 us: experts_routed(): received_both = jnp.concatenate([mine, swap(mine)], axis=2)]
    all_gather x1, waiting for transfers between devices: 12.9 us -> 0.01 us  [gather_packed(): full = lax.all_gather(flat, axes, axis=0, tiled=False)]
    unnamed x303 -> x331, local copies, waits for them, and re-layouts: 49.7 us -> 54.7 us
    dot_general x6 -> x12, matrix products: 56.3 us -> 51.7 us  [the longest x2 12.2 us: expert_block(): jnp.einsum('rd,fd->rf', grads_in, expert_down_low, preferred_element_type...]
  transfers between devices with their start and end apart: 17 -> 20, of which waited for: 7 -> 6; matrix products, arithmetic and copies ran while one was open for 22% -> 26% of each run, Pallas kernels for 9% -> 9%
where the time goes in v14:
time: 1180 us; the launch traced here: 1170 us
  local copies, waits for them, and re-layouts  282 us (24%)
  matrix products  191 us (16%)
  Pallas kernels  177 us (15%)
  other arithmetic  171 us (14%)
  waiting for transfers between devices  171 us (14%)
  blocking collectives  103 us (9%)
  between operations  43.2 us (4%)
  starting transfers between devices  19.7 us (2%)
    pallas_call x1, Pallas kernels, halving_scatter(): pl.pallas_call(halving_kernel, out_shape=jax.ShapeDtypeStruct((2 * rows,...  105 us
    all_to_all x1, blocking collectives, experts_routed(): lax.all_to_all(rows, 'fsdp', split_axis=0, concat_axis=0, tiled=True)  75.2 us
    unnamed x331, local copies, waits for them, and re-layouts  54.7 us
    psum x1, waiting for transfers between devices, local(): lax.psum(jnp.dot(mixed_heads, attn_out_low, preferred_element_type=jnp.fl...  54 us
    pallas_call x2, Pallas kernels, butterfly_sum(): pl.pallas_call(butterfly_kernel, out_shape=jax.ShapeDtypeStruct((rows, 12...  44.8 us
    ppermute x1, waiting for transfers between devices, experts_routed(): other = lax.ppermute(piece, 'tp', [(0, 2), (1, 3), (2, 0), (3, 1)])  37.8 us
    psum x2, waiting for transfers between devices, local(): lax.psum((shared_out + combined, partial_two, gate_dots), 'tp')  36.5 us
    all_to_all x1, waiting for transfers between devices, experts_routed(): lax.all_to_all(rows, 'fsdp', split_axis=0, concat_axis=0, tiled=True)  33 us
  transfers between devices with their start and end apart: 20, of which 6 were waited for; matrix products, arithmetic and copies ran while one was open for 26% of the time, Pallas kernels for 9%

profile of v14, /device:TPU:0, one launch (start us, length us, event | category | flops | bytes accessed | tf_op | source)
XLA Modules:
  0.0 1166.3 jit_solution(9290660833225618055)
XLA Ops:
  17.2 27.6 %shard_map.395 = bf16[8,592,128]{2,1,0:T(8,128)(2,1)} custom-call(bf16[592,128]{1,0:T(8,128)(2,1)} %pad_bitcast_fusion.2.x_ref), custom_call_target="tpu_custom_call" | custom-call | tf_op jit(solution)/shard_map/pallas_call | solution.py:352
  88.1 39.3 %while.39 = (s32[]{:T(128)}, bf16[2,512,3,64]{1,3,2,0:T(8,128)(2,1)}, f32[2,3,512,1]{2,1,3,0:T(4,128)}, s32[2]{0:T(128)}, bf16[2048,3,64]{0,2,1:T(8,128)(2,1)S(1...) while((s32[]{:T(128)}, ...), condition=%wide.region_4.5_spmd, body=%wide.region_1.4_spmd.sunk | while | flops 644092928 | bytes 33331516 | solution.py:661
  137.1 8.1 scatter_custom_fusion
  145.2 8.1 scatter_custom_fusion.1
  153.3 54.0 %all-reduce.15.cloned.1.call-done = f32[1024,768]{1,0:T(8,128)} async-done(((f32[1024,768]{1,0:T(8,128)}), f32[1024,768]{1,0:T(8,128)}) %all-reduce.15.cloned.1.call-update) | async-done | bytes 3145744 | tf_op jit(solution)/shard_map/psum | solution.py:663
  212.5 23.0 %gather_fusion = f32[4096]{0:T(1024)S(1)} fusion(f32[2048]{0:T(1024)S(1)} %div.441, s32[4096]{0:T(1024)S(1)} %get-tuple-element.935), kind=kCustom, calls=%fused_computation | custom fusion | bytes 49152 | tf_op jit(solution)/shard_map/gather | solution.py:458
  235.6 9.6 fusion.70
  245.3 10.2 multiply_convert_fusion.1
  255.7 75.2 %all_to_all.10 = bf16[4,2,256,768]{3,2,1,0:T(8,128)(2,1)} all-to-all(bf16[4,2,256,768]{3,2,1,0:T(8,128)(2,1)S(1)} %fusion.111), channel_id=1, replica_groups=mesh['fsdp'=4,'ctx'=2,'tp'=4] {'fsdp'}, dimensions={0} | all-to-all | bytes 6291456 | tf_op jit(solution)/shard_map/all_to_all | solution.py:468
  342.2 20.9 %all_gather.15 = bf16[1,512,768]{2,1,0:T(8,128)(2,1)} all-gather(bf16[1,512,384]{2,1,0:T(8,128)(2,1)S(1)} %get-tuple-element.901), channel_id=1, replica_groups=mesh['fsdp'=4,'ctx'=2,'tp'=4] {'ctx'}, dimensions={2}, use_global_device_ids=true | all-gather | bytes 1179648 | tf_op jit(solution)/shard_map/all_gather | solution.py:614
  370.5 37.8 %collective-permute-done.5 = bf16[4,2,256,768]{3,2,1,0:T(8,128)(2,1)} collective-permute-done((bf16[4,2,256,768]{3,2,1,0:T(8,128)(2,1)}, bf16[4,2,256,768]{3,2,1,0:T(8,128)(2,1)}, u32[]{:S(2)}, u32[]{:S(2)}) %collective-permute-start.5) | collective-permute-done | bytes 3145760 | tf_op jit(solution)/shard_map/ppermute | solution.py:511
  408.2 5.9 fusion.138
  423.5 6.0 fusion.94
  446.4 6.2 fusion.89
  503.8 6.5 fusion.244
  584.4 6.3 reshape_reshape.24
  609.8 33.0 %all-to-all-done.1 = bf16[4,2,512,768]{3,2,1,0:T(8,128)(2,1)} async-done(((bf16[4,2,512,768]{3,2,1,0:T(8,128)(2,1)}), bf16[4,2,512,768]{3,2,1,0:T(8,128)(2,1)}, u32[]{:S(2)}, u32[]{:S(2)}) %all-to-all-start.1) | async-done | bytes 6291488 | tf_op jit(solution)/shard_map/all_to_all | solution.py:468
  647.8 8.2 fusion.114
  660.2 12.4 %multiply_reduce_fusion.1 = (f32[1024,2]{0,1:T(2,128)S(1)}, f32[1024,768]{0,1:T(8,128)}) fusion(f32[1024,768]{0,1:T(8,128)} %copy.259, f32[1024,2]{0,1:T(2,128)S(1)} %copy-done.120, bf16[2048,768,1]{1,0,2:T(8,128)(2,1)} %bitcast.565, s32[1024,2]{0,1:T(2,128)S(1)} %copy-done.140, pred[1024,2]{0,1:T(4,128)(4,1)S(1)} %copy-done.148), kind=kOutput, calls=%fused_computation.103 | convolution fusion | flops 6456342528 | bytes 9463808 | tf_op jit(solution)/shard_map/dot_general | solution.py:543
  672.6 7.3 psum.38
  690.4 36.5 %all-reduce.17.cloned.1.call-done = f32[1024,768]{1,0:T(8,128)} async-done(((f32[1024,768]{1,0:T(8,128)}), f32[1024,768]{1,0:T(8,128)}) %all-reduce.17.cloned.1.call-update) | async-done | bytes 3145744 | tf_op jit(solution)/shard_map/psum | solution.py:710
  736.7 76.5 %while.40 = (s32[]{:T(128)}, f32[2048,3,64]{0,2,1:T(8,128)}, f32[2048,3,64]{0,2,1:T(8,128)S(1)}, f32[1024,3,64]{0,2,1:T(8,128)}, bf16[1024,3,64]{0,2,1:T(8,128)(...) while((s32[]{:T(128)}, f32[2048,3,64]{0,2,1:T(8,128)}, ...), condition=%wide.region_26.27_spmd, body=%wide.region_24.26_spmd.sunk | while | flops 1541608448 | bytes 106823088 | solution.py:812
  736.7 6.0 fusion.313
  744.8 8.8 multiply_reduce_fusion.22
  753.5 9.4 multiply_convert_fusion.7
  774.9 6.0 fusion.313
  783.0 8.8 multiply_reduce_fusion.22
  791.8 9.4 multiply_convert_fusion.7
  867.7 105.0 %shard_map.396 = f32[1792,128]{1,0:T(8,128)} custom-call(f32[2,2,2,1792,128]{4,3,2,1,0:T(8,128)} %bitcast.535), custom_call_target="tpu_custom_call" | custom-call | tf_op jit(solution)/shard_map/pallas_call | solution.py:280
  995.1 29.2 %shard_map.397 = f32[344,128]{1,0:T(8,128)} custom-call(f32[344,128]{1,0:T(8,128)} %pad_bitcast_fusion.1.x_ref), custom_call_target="tpu_custom_call" | custom-call | tf_op jit(solution)/shard_map/pallas_call | solution.py:162
  1033.2 7.8 slice.520
  1108.6 15.6 %shard_map.398 = f32[8,128]{1,0:T(8,128)} custom-call(f32[8,128]{1,0:T(8,128)} %pad_bitcast_fusion.3.x_ref), custom_call_target="tpu_custom_call" | custom-call | tf_op jit(solution)/shard_map/pallas_call | solution.py:162
  (725 shorter events, 506.3 us)
Async XLA Ops:
  8.0 199.2 %all-reduce.15.cloned.1.call-start = ((), (), s32[]{:S(2)}) async-start(), calls=%async_computation.4 | async-start | bytes 6291456 | tf_op jit(solution)/shard_map/psum | solution.py:663
  59.6 26.2 %collective-permute-start.2 = (bf16[1024,3,64]{0,2,1:T(8,128)(2,1)}, bf16[1024,3,64]{0,2,1:T(8,128)(2,1)}, u32[]{:S(2)}, u32[]{:S(2)}) collective-permute-start(bf16[1024,3,64]{0,2,1:T(8,128)(2,1)} %pad_maximum_fusion.4), channel_id=1, source_target_pairs={{0,4},{1,5},{2,6},{3,7},{8,12},{9,13},{10,14},{11,15},{16,20},{17,... | collective-permute-start | bytes 1179656 | tf_op jit(solution)/shard_map/ppermute | solution.py:27
  66.0 20.9 %collective-permute-start = (bf16[1024,3,64]{0,2,1:T(8,128)(2,1)S(1)}, bf16[1024,3,64]{0,2,1:T(8,128)(2,1)}, u32[]{:S(2)}, u32[]{:S(2)}) collective-permute-start(bf16[1024,3,64]{0,2,1:T(8,128)(2,1)S(1)} %bitcast.586), channel_id=1, source_target_pairs={{0,4},{1,5},{2,6},{3,7},{8,12},{9,13},{10,14},{11,15},{16,20},{17,... | collective-permute-start | bytes 1179656 | tf_op jit(solution)/shard_map/ppermute | solution.py:27
  68.1 17.1 %collective-permute-start.1 = (bf16[1024]{0:T(1024)(128)(2,1)S(1)}, bf16[1024]{0:T(1024)(128)(2,1)}, u32[]{:S(2)}, u32[]{:S(2)}) collective-permute-start(bf16[1024]{0:T(1024)(128)(2,1)S(1)} %convert_reduce_fusion), channel_id=1, source_target_pairs={{0,4},{1,5},{2,6},{3,7},{8,12},{9,13},{10,14},{11,15},{16,20},{17,... | collective-permute-start | bytes 6152 | tf_op jit(solution)/shard_map/ppermute | solution.py:27
  127.4 83.1 %copy-start.82 = (bf16[2048]{0:T(1024)(128)(2,1)}, bf16[2048]{0:T(1024)(128)(2,1)S(1)}, u32[]{:S(2)}) copy-start(bf16[2048]{0:T(1024)(128)(2,1)S(1)} %get-tuple-element.1245) | copy-start | bytes 12292
  127.5 83.1 %copy-start.94 = (bf16[1024]{0:T(1024)(128)(2,1)}, bf16[1024]{0:T(1024)(128)(2,1)S(1)}, u32[]{:S(2)}) copy-start(bf16[1024]{0:T(1024)(128)(2,1)S(1)} %get-tuple-element.1247) | copy-start | bytes 6148
  133.3 275.0 %all-gather.4.cloned.1.call-start = ((), (), s32[]{:S(2)}) async-start(), calls=%async_computation.5 | async-start | bytes 2359296 | tf_op jit(solution)/shard_map/all_gather | solution.py:613
  137.0 72.6 %copy-start.97 = (s32[2048]{0:T(1024)}, s32[2048]{0:T(1024)S(1)}, u32[]{:S(2)}) copy-start(s32[2048]{0:T(1024)S(1)} %fusion.188) | copy-start | bytes 24580
  153.3 57.0 %copy-start.99 = (f32[768]{0:T(1024)S(1)}, f32[768]{0:T(1024)}, u32[]{:S(2)}) copy-start(f32[768]{0:T(1024)} %reshape.1347) | copy-start | bytes 9220
  255.7 75.2 %copy-start.18 = (f32[1,384,2,512]{3,2,1,0:T(2,128)S(1)}, f32[1,384,2,512]{3,2,1,0:T(2,128)}, u32[]{:S(2)}) copy-start(f32[1,384,2,512]{3,2,1,0:T(2,128)} %param.34) | copy-start | bytes 4718596
  330.9 34.3 %collective-permute-start.3 = (bf16[4,2,256,768]{3,2,1,0:T(8,128)(2,1)}, bf16[4,2,256,768]{3,2,1,0:T(8,128)(2,1)}, u32[]{:S(2)}, u32[]{:S(2)}) collective-permute-start(bf16[4,2,256,768]{3,2,1,0:T(8,128)(2,1)} %all_to_all.10), channel_id=1, source_target_pairs={{0,1},{1,0},{2,3},{3,2},{4,5},{5,4},{6,7},{7,6},{8,9},{9,8},{10,11... | collective-permute-start | bytes 9437192 | tf_op jit(solution)/shard_map/ppermute | solution.py:470
  332.1 220.6 %all-gather.6.cloned.1.call-start = ((), (), s32[]{:S(2)}) async-start(), calls=%async_computation.9 | async-start | bytes 2654208 | tf_op jit(solution)/shard_map/all_gather | solution.py:376
  337.4 70.8 %collective-permute-start.5 = (bf16[4,2,256,768]{3,2,1,0:T(8,128)(2,1)}, bf16[4,2,256,768]{3,2,1,0:T(8,128)(2,1)}, u32[]{:S(2)}, u32[]{:S(2)}) collective-permute-start(bf16[4,2,256,768]{3,2,1,0:T(8,128)(2,1)} %all_to_all.10), channel_id=1, source_target_pairs={{0,2},{1,3},{2,0},{3,1},{4,6},{5,7},{6,4},{7,5},{8,10},{9,11},{10,... | collective-permute-start | bytes 9437192 | tf_op jit(solution)/shard_map/ppermute | solution.py:511
  340.0 261.6 %reduce-scatter.5.cloned.1.call-start = ((), (), s32[]{:S(2)}) async-start(), calls=%async_computation.8 | async-start | bytes 2359296 | tf_op jit(solution)/shard_map/reduce_scatter | solution.py:756
  408.2 32.1 %collective-permute-start.6 = (bf16[4,2,256,768]{3,2,1,0:T(8,128)(2,1)}, bf16[4,2,256,768]{3,2,1,0:T(8,128)(2,1)}, u32[]{:S(2)}, u32[]{:S(2)}) collective-permute-start(bf16[4,2,256,768]{3,2,1,0:T(8,128)(2,1)} %collective-permute-done.5), channel_id=1, source_target_pairs={{0,1},{1,0},{2,3},{3,2},{4,5},{5,4},{6,7},{7,6},{8,9},{9,8},{10,11... | collective-permute-start | bytes 9437192 | tf_op jit(solution)/shard_map/ppermute | solution.py:470
  423.0 52.4 %collective-permute-start.4 = (f32[4,256,768]{2,1,0:T(8,128)}, f32[4,256,768]{2,1,0:T(8,128)}, u32[]{:S(2)}, u32[]{:S(2)}) collective-permute-start(f32[4,256,768]{2,1,0:T(8,128)} %slice.577), channel_id=1, source_target_pairs={{0,1},{1,0},{2,3},{3,2},{4,5},{5,4},{6,7},{7,6},{8,9},{9,8},{10,11... | collective-permute-start | bytes 9437192 | tf_op jit(solution)/shard_map/ppermute | solution.py:470
  438.2 40.6 %collective-permute-start.8 = (f32[4,256,768]{2,1,0:T(8,128)}, f32[4,256,768]{2,1,0:T(8,128)}, u32[]{:S(2)}, u32[]{:S(2)}) collective-permute-start(f32[4,256,768]{2,1,0:T(8,128)} %slice.585), channel_id=1, source_target_pairs={{0,1},{1,0},{2,3},{3,2},{4,5},{5,4},{6,7},{7,6},{8,9},{9,8},{10,11... | collective-permute-start | bytes 9437192 | tf_op jit(solution)/shard_map/ppermute | solution.py:470
  459.6 23.0 %collective-permute-start.7 = (f32[4,256,768]{2,1,0:T(8,128)}, f32[4,256,768]{2,1,0:T(8,128)}, u32[]{:S(2)}, u32[]{:S(2)}) collective-permute-start(f32[4,256,768]{2,1,0:T(8,128)} %slice.582), channel_id=1, source_target_pairs={{0,1},{1,0},{2,3},{3,2},{4,5},{5,4},{6,7},{7,6},{8,9},{9,8},{10,11... | collective-permute-start | bytes 9437192 | tf_op jit(solution)/shard_map/ppermute | solution.py:470
  467.8 21.3 %collective-permute-start.9 = (f32[4,256,768]{2,1,0:T(8,128)}, f32[4,256,768]{2,1,0:T(8,128)}, u32[]{:S(2)}, u32[]{:S(2)}) collective-permute-start(f32[4,256,768]{2,1,0:T(8,128)} %slice.588), channel_id=1, source_target_pairs={{0,1},{1,0},{2,3},{3,2},{4,5},{5,4},{6,7},{7,6},{8,9},{9,8},{10,11... | collective-permute-start | bytes 9437192 | tf_op jit(solution)/shard_map/ppermute | solution.py:470
  498.5 144.3 %all-to-all-start.1 = ((bf16[4,2,512,768]{3,2,1,0:T(8,128)(2,1)}), bf16[4,2,512,768]{3,2,1,0:T(8,128)(2,1)}, u32[]{:S(2)}, u32[]{:S(2)}) async-start(bf16[4,2,512,768]{3,2,1,0:T(8,128)(2,1)} %copy.254), calls=%async_computation.1 | async-start | bytes 12582912 | tf_op jit(solution)/shard_map/all_to_all | solution.py:468
  503.8 99.1 %reduce-scatter.3.cloned.1.call-start = ((), (), s32[]{:S(2)}) async-start(), calls=%async_computation.7 | async-start | bytes 4718592 | tf_op jit(solution)/shard_map/reduce_scatter | solution.py:755
  515.6 211.2 %all-reduce.17.cloned.1.call-start = ((), (), s32[]{:S(2)}) async-start(), calls=%async_computation.6 | async-start | bytes 6291456 | tf_op jit(solution)/shard_map/psum | solution.py:710
  659.5 327.1 %all-reduce.19.cloned.1.call-start = ((), (), s32[]{:S(2)}) async-start(), calls=%async_computation.10 | async-start | bytes 12582912 | tf_op jit(solution)/shard_map/psum | solution.py:710
  685.0 41.8 %copy-start.62 = (bf16[768,4]{1,0:T(8,128)(2,1)S(1)}, bf16[768,4]{1,0:T(8,128)(2,1)}, u32[]{:S(2)}) copy-start(bf16[768,4]{1,0:T(8,128)(2,1)} %reshape_reshape.22) | copy-start | bytes 18436
  685.0 41.8 %copy-start.100 = (f32[768]{0:T(1024)S(1)}, f32[768]{0:T(1024)}, u32[]{:S(2)}) copy-start(f32[768]{0:T(1024)} %reshape.1347) | copy-start | bytes 9220
  685.0 41.8 %copy-start.102 = (f32[1024]{0:T(1024)S(1)}, f32[1024]{0:T(1024)}, u32[]{:S(2)}) copy-start(f32[1024]{0:T(1024)} %copy-done.101) | copy-start | bytes 12292
  815.2 14.2 %collective-permute-start.10 = (bf16[1024,3,64]{0,2,1:T(8,128)(2,1)}, bf16[1024,3,64]{0,2,1:T(8,128)(2,1)}, u32[]{:S(2)}, u32[]{:S(2)}) collective-permute-start(bf16[1024,3,64]{0,2,1:T(8,128)(2,1)} %slice.699), channel_id=1, source_target_pairs={{4,0},{5,1},{6,2},{7,3},{12,8},{13,9},{14,10},{15,11},{20,16},{21,... | collective-permute-start | bytes 1179656 | tf_op jit(solution)/shard_map/ppermute | solution.py:27
  817.3 19.3 %collective-permute-start.11 = (bf16[1024,3,64]{0,2,1:T(8,128)(2,1)}, bf16[1024,3,64]{0,2,1:T(8,128)(2,1)}, u32[]{:S(2)}, u32[]{:S(2)}) collective-permute-start(bf16[1024,3,64]{0,2,1:T(8,128)(2,1)} %slice.698), channel_id=1, source_target_pairs={{4,0},{5,1},{6,2},{7,3},{12,8},{13,9},{14,10},{15,11},{20,16},{21,... | collective-permute-start | bytes 1179656 | tf_op jit(solution)/shard_map/ppermute | solution.py:27
  981.1 43.2 %copy-start.77 = (f32[192,96]{1,0:T(8,128)}, f32[192,96]{1,0:T(8,128)S(1)}, u32[]{:S(2)}) copy-start(f32[192,96]{1,0:T(8,128)S(1)} %reshape.1331) | copy-start | bytes 221188
  1041.0 59.1 %copy-start.11 = (f32[1,384,2,512]{3,1,2,0:T(8,128)S(1)}, f32[1,384,2,512]{3,1,2,0:T(8,128)}, u32[]{:S(2)}) copy-start(f32[1,384,2,512]{3,1,2,0:T(8,128)} %reduce-scatter.3.cloned.1.call-done) | copy-start | bytes 4718596
  1041.0 87.2 %copy-start.19 = (f32[1,384,2,512]{3,2,1,0:T(2,128)S(1)}, f32[1,384,2,512]{3,2,1,0:T(2,128)}, u32[]{:S(2)}) copy-start(f32[1,384,2,512]{3,2,1,0:T(2,128)} %param.34) | copy-start | bytes 4718596
  1063.9 64.3 %copy-start.121 = (f32[512]{0:T(512)}, f32[512]{0:T(512)S(1)}, u32[]{:S(2)}) copy-start(f32[512]{0:T(512)S(1)} %multiply_add_fusion.8) | copy-start | bytes 6148
  (155 other events, 1142.0 us)
Sparse Core Ops, SparseCore 0:
  133.4 73.8 all-reduce.14
  659.7 67.1 all-reduce.16
  841.0 119.1 all-reduce.18
Sparse Core Ops, SparseCore 1:
  332.1 34.2 all-gather.3
  369.1 51.7 all-gather.5
  475.5 24.7 reduce-scatter.4
  515.7 44.1 reduce-scatter.2

commit v15 on v14

--- a/solution.py
+++ b/solution.py
@@ -442,7 +442,7 @@
 
 
 def experts_routed(
-    normed_two, grad_out, route_rows, gate_probs, expert_in_low, expert_down_low, capacity
+    normed_two, grad_out, route_rows, gate_probs, expert_in_low, expert_down_low, capacity, anchor
 ):
     block_len, model_width = normed_two.shape
     experts = lax.axis_size("fsdp")
@@ -508,7 +508,7 @@
         piece = exchange(
             lax.dynamic_slice_in_dim(send_rows, (2 * side + row_side) * quarter, quarter, 2)
         )
-        other = lax.ppermute(piece, "tp", [(0, 2), (1, 3), (2, 0), (3, 1)])
+        other = lax.ppermute(piece, "tp", [(0, 2), (1, 3), (2, 0), (3, 1)]) + 0.0 * anchor
         results_a, grad_in_a, grad_down_a = expert_block(
             jnp.concatenate([piece, swap(piece)], axis=2)
         )
@@ -675,6 +675,19 @@
     gate_probs = jax.nn.softmax(picked, axis=-1)
     upstream = cotangent[0]
     grad_out = upstream.astype(jnp.float32)
+    shared_gate_up = jnp.einsum(
+        "td,dgf->tgf", normed_two, shared_in_low, preferred_element_type=jnp.float32
+    )
+    shared_act, shared_act_back = jax.vjp(swiglu, shared_gate_up)
+    shared_hidden = shared_act.astype(jnp.bfloat16)
+    shared_out = jnp.dot(shared_hidden, shared_down_low, preferred_element_type=jnp.float32)
+    grad_shared_hidden = jnp.einsum(
+        "td,fd->tf", upstream, shared_down_low, preferred_element_type=jnp.float32
+    )
+    grad_shared_gate_up = shared_act_back(grad_shared_hidden)[0].astype(jnp.bfloat16)
+    shared_rows = jnp.einsum(
+        "tgf,dgf->td", grad_shared_gate_up, shared_in_low, preferred_element_type=jnp.float32
+    )
     if dense_experts:
         weights = jnp.sum(gate_probs[:, :, None] * onehot, axis=1)
         combined, dots_e, grad_rows, grad_expert_in, grad_expert_down = experts_dense(
@@ -690,23 +703,9 @@
             expert_in_low,
             expert_down_low,
             capacity,
-        )
-    shared_gate_up = jnp.einsum(
-        "td,dgf->tgf", normed_two, shared_in_low, preferred_element_type=jnp.float32
-    )
-    shared_act, shared_act_back = jax.vjp(swiglu, shared_gate_up)
-    shared_hidden = shared_act.astype(jnp.bfloat16)
-    shared_out = jnp.dot(shared_hidden, shared_down_low, preferred_element_type=jnp.float32)
-    grad_shared_hidden = jnp.einsum(
-        "td,fd->tf", upstream, shared_down_low, preferred_element_type=jnp.float32
-    )
-    grad_shared_gate_up = shared_act_back(grad_shared_hidden)[0].astype(jnp.bfloat16)
-    partial_two = (
-        jnp.einsum(
-            "tgf,dgf->td", grad_shared_gate_up, shared_in_low, preferred_element_type=jnp.float32
-        )
-        + grad_rows
-    )
+            (shared_rows[0, 0] + shared_out[0, 0]).astype(jnp.bfloat16),
+        )
+    partial_two = shared_rows + grad_rows
     branch_total, grad_normed_part, gate_total = lax.psum(
         (shared_out + combined, partial_two, gate_dots), "tp"
     )

time: 1180 us -> 1210 us (1.025)
  waiting for transfers between devices: 171 us -> 280 us
  blocking collectives: 103 us -> 24.7 us
  local copies, waits for them, and re-layouts: 282 us -> 267 us
  other arithmetic: 171 us -> 184 us
    all_to_all x1 -> x2, waiting for transfers between devices: 33 us -> 167 us  [experts_routed(): lax.all_to_all(rows, 'fsdp', split_axis=0, concat_axis=0, tiled=True)]
    all_to_all x1 -> x0, blocking collectives: 75.2 us -> none  [experts_routed(): lax.all_to_all(rows, 'fsdp', split_axis=0, concat_axis=0, tiled=True)]
    ppermute x1, waiting for transfers between devices: 37.8 us -> 14.3 us  [experts_routed(): lax.ppermute(piece, 'tp', [(0, 2), (1, 3), (2, 0), (3, 1)]) + 0.0 * anchor]
    unnamed x331 -> x336, local copies, waits for them, and re-layouts: 54.7 us -> 50.9 us
  transfers between devices with their start and end apart: 20 -> 21, of which waited for: 6 -> 7; matrix products, arithmetic and copies ran while one was open for 26% -> 25% of each run, Pallas kernels for 9% -> 9%
where the time goes in v15:
time: 1210 us; the launch traced here: 1200 us
  waiting for transfers between devices  280 us (23%)
  local copies, waits for them, and re-layouts  267 us (22%)
  matrix products  190 us (16%)
  other arithmetic  184 us (15%)
  Pallas kernels  177 us (15%)
  between operations  44.8 us (4%)
  blocking collectives  24.7 us (2%)
  starting transfers between devices  23.1 us (2%)
    all_to_all x2, waiting for transfers between devices, experts_routed(): lax.all_to_all(rows, 'fsdp', split_axis=0, concat_axis=0, tiled=True)  167 us
    pallas_call x1, Pallas kernels, halving_scatter(): pl.pallas_call(halving_kernel, out_shape=jax.ShapeDtypeStruct((2 * rows,...  105 us
    psum x1, waiting for transfers between devices, local(): lax.psum(jnp.dot(mixed_heads, attn_out_low, preferred_element_type=jnp.fl...  53 us
    unnamed x336, local copies, waits for them, and re-layouts  50.9 us
    pallas_call x2, Pallas kernels, butterfly_sum(): pl.pallas_call(butterfly_kernel, out_shape=jax.ShapeDtypeStruct((rows, 12...  44.7 us
    psum x2, waiting for transfers between devices, local(): lax.psum((shared_out + combined, partial_two, gate_dots), 'tp')  36.5 us
    pallas_call x1, Pallas kernels, gather_shards(): pl.pallas_call(gather_kernel, out_shape=jax.ShapeDtypeStruct((count, rows...  27.6 us
  transfers between devices with their start and end apart: 21, of which 7 were waited for; matrix products, arithmetic and copies ran while one was open for 25% of the time, Pallas kernels for 9%

profile of v15, /device:TPU:0, one launch (start us, length us, event | category | flops | bytes accessed | tf_op | source)
XLA Modules:
  0.0 1199.0 jit_solution(13718552426915885061)
XLA Ops:
  17.1 27.6 %shard_map.395 = bf16[8,592,128]{2,1,0:T(8,128)(2,1)} custom-call(bf16[592,128]{1,0:T(8,128)(2,1)} %pad_bitcast_fusion.2.x_ref), custom_call_target="tpu_custom_call" | custom-call | tf_op jit(solution)/shard_map/pallas_call | solution.py:352
  95.9 39.3 %while.39 = (s32[]{:T(128)}, bf16[2,512,3,64]{1,3,2,0:T(8,128)(2,1)}, f32[2,3,512,1]{2,1,3,0:T(4,128)}, s32[2]{0:T(128)}, bf16[2048,3,64]{0,2,1:T(8,128)(2,1)S(1...) while((s32[]{:T(128)}, ...), condition=%wide.region_4.5_spmd, body=%wide.region_1.4_spmd.sunk | while | flops 644092928 | bytes 33331516 | solution.py:661
  145.6 8.1 scatter_custom_fusion
  153.7 8.2 scatter_custom_fusion.1
  162.0 53.0 %all-reduce.15.cloned.1.call-done = f32[1024,768]{1,0:T(8,128)} async-done(((f32[1024,768]{1,0:T(8,128)}), f32[1024,768]{1,0:T(8,128)}) %all-reduce.15.cloned.1.call-update) | async-done | bytes 3145744 | tf_op jit(solution)/shard_map/psum | solution.py:663
  220.3 23.0 %gather_fusion = f32[4096]{0:T(1024)S(1)} fusion(f32[2048]{0:T(1024)S(1)} %div.441, s32[4096]{0:T(1024)S(1)} %get-tuple-element.935), kind=kCustom, calls=%fused_computation | custom fusion | bytes 49152 | tf_op jit(solution)/shard_map/gather | solution.py:458
  243.4 9.6 fusion.70
  253.0 10.2 multiply_convert_fusion.1
  270.8 98.2 %all-to-all-done = bf16[4,2,256,768]{3,2,1,0:T(8,128)(2,1)} async-done(((bf16[4,2,256,768]{3,2,1,0:T(8,128)(2,1)}), bf16[4,2,256,768]{3,2,1,0:T(8,128)(2,1)}, u32[]{:S(2)}, u32[]{:S(2)}) %all-to-all-start) | async-done | bytes 3145760 | tf_op jit(solution)/shard_map/all_to_all | solution.py:468
  372.6 17.7 %all_gather.15 = bf16[1,512,768]{2,1,0:T(8,128)(2,1)} all-gather(bf16[1,512,384]{2,1,0:T(8,128)(2,1)S(1)} %get-tuple-element.901), channel_id=1, replica_groups=mesh['fsdp'=4,'ctx'=2,'tp'=4] {'ctx'}, dimensions={2}, use_global_device_ids=true | all-gather | bytes 1179648 | tf_op jit(solution)/shard_map/all_gather | solution.py:614
  422.0 14.3 %collective-permute-done.5 = bf16[4,2,256,768]{3,2,1,0:T(8,128)(2,1)} collective-permute-done((bf16[4,2,256,768]{3,2,1,0:T(8,128)(2,1)}, bf16[4,2,256,768]{3,2,1,0:T(8,128)(2,1)}, u32[]{:S(2)}, u32[]{:S(2)}) %collective-permute-start.5) | collective-permute-done | bytes 3145760 | tf_op jit(solution)/shard_map/ppermute | solution.py:511
  445.2 5.9 fusion.139
  460.4 5.8 fusion.94
  481.3 6.0 fusion.89
  538.7 6.5 fusion.245
  609.0 68.7 %all-to-all-done.1 = bf16[4,2,512,768]{3,2,1,0:T(8,128)(2,1)} async-done(((bf16[4,2,512,768]{3,2,1,0:T(8,128)(2,1)}), bf16[4,2,512,768]{3,2,1,0:T(8,128)(2,1)}, u32[]{:S(2)}, u32[]{:S(2)}) %all-to-all-start.1) | async-done | bytes 6291488 | tf_op jit(solution)/shard_map/all_to_all | solution.py:468
  682.7 8.2 fusion.115
  693.7 12.5 %multiply_reduce_fusion.1 = (f32[1024,2]{0,1:T(2,128)S(1)}, f32[1024,768]{0,1:T(8,128)}) fusion(f32[1024,768]{0,1:T(8,128)} %copy.259, f32[1024,2]{0,1:T(2,128)S(1)} %copy-done.125, bf16[2048,768,1]{1,0,2:T(8,128)(2,1)} %bitcast.568, s32[1024,2]{0,1:T(2,128)S(1)} %copy-done.145, pred[1024,2]{0,1:T(4,128)(4,1)S(1)} %copy-done.153), kind=kOutput, calls=%fused_computation.105 | convolution fusion | flops 6456342528 | bytes 9463808 | tf_op jit(solution)/shard_map/dot_general | solution.py:543
  706.2 6.9 psum.38
  723.5 36.5 %all-reduce.17.cloned.1.call-done = f32[1024,768]{1,0:T(8,128)} async-done(((f32[1024,768]{1,0:T(8,128)}), f32[1024,768]{1,0:T(8,128)}) %all-reduce.17.cloned.1.call-update) | async-done | bytes 3145744 | tf_op jit(solution)/shard_map/psum | solution.py:709
  769.8 76.5 %while.40 = (s32[]{:T(128)}, f32[2048,3,64]{0,2,1:T(8,128)}, f32[2048,3,64]{0,2,1:T(8,128)S(1)}, f32[1024,3,64]{0,2,1:T(8,128)}, bf16[1024,3,64]{0,2,1:T(8,128)(...) while((s32[]{:T(128)}, f32[2048,3,64]{0,2,1:T(8,128)}, ...), condition=%wide.region_26.27_spmd, body=%wide.region_24.26_spmd.sunk | while | flops 1541608448 | bytes 106823088 | solution.py:811
  769.9 6.0 fusion.314
  777.9 8.8 multiply_reduce_fusion.22
  786.7 9.4 multiply_convert_fusion.7
  808.1 6.0 fusion.314
  816.2 8.8 multiply_reduce_fusion.22
  825.0 9.4 multiply_convert_fusion.7
  864.0 5.7 collective-permute-done.11
  900.8 105.0 %shard_map.396 = f32[1792,128]{1,0:T(8,128)} custom-call(f32[2,2,2,1792,128]{4,3,2,1,0:T(8,128)} %bitcast.536), custom_call_target="tpu_custom_call" | custom-call | tf_op jit(solution)/shard_map/pallas_call | solution.py:280
  1027.9 29.1 %shard_map.397 = f32[344,128]{1,0:T(8,128)} custom-call(f32[344,128]{1,0:T(8,128)} %pad_bitcast_fusion.1.x_ref), custom_call_target="tpu_custom_call" | custom-call | tf_op jit(solution)/shard_map/pallas_call | solution.py:162
  1065.9 7.8 slice.528
  1141.4 15.6 %shard_map.398 = f32[8,128]{1,0:T(8,128)} custom-call(f32[8,128]{1,0:T(8,128)} %pad_bitcast_fusion.3.x_ref), custom_call_target="tpu_custom_call" | custom-call | tf_op jit(solution)/shard_map/pallas_call | solution.py:162
  (735 shorter events, 507.3 us)
Async XLA Ops:
  8.0 207.0 %all-reduce.15.cloned.1.call-start = ((), (), s32[]{:S(2)}) async-start(), calls=%async_computation.4 | async-start | bytes 6291456 | tf_op jit(solution)/shard_map/psum | solution.py:663
  59.6 34.0 %collective-permute-start.2 = (bf16[1024,3,64]{0,2,1:T(8,128)(2,1)}, bf16[1024,3,64]{0,2,1:T(8,128)(2,1)}, u32[]{:S(2)}, u32[]{:S(2)}) collective-permute-start(bf16[1024,3,64]{0,2,1:T(8,128)(2,1)} %pad_maximum_fusion.5), channel_id=1, source_target_pairs={{0,4},{1,5},{2,6},{3,7},{8,12},{9,13},{10,14},{11,15},{16,20},{17,... | collective-permute-start | bytes 1179656 | tf_op jit(solution)/shard_map/ppermute | solution.py:27
  66.0 28.7 %collective-permute-start = (bf16[1024,3,64]{0,2,1:T(8,128)(2,1)S(1)}, bf16[1024,3,64]{0,2,1:T(8,128)(2,1)}, u32[]{:S(2)}, u32[]{:S(2)}) collective-permute-start(bf16[1024,3,64]{0,2,1:T(8,128)(2,1)S(1)} %bitcast.587), channel_id=1, source_target_pairs={{0,4},{1,5},{2,6},{3,7},{8,12},{9,13},{10,14},{11,15},{16,20},{17,... | collective-permute-start | bytes 1179656 | tf_op jit(solution)/shard_map/ppermute | solution.py:27
  68.1 24.9 %collective-permute-start.1 = (bf16[1024]{0:T(1024)(128)(2,1)S(1)}, bf16[1024]{0:T(1024)(128)(2,1)}, u32[]{:S(2)}, u32[]{:S(2)}) collective-permute-start(bf16[1024]{0:T(1024)(128)(2,1)S(1)} %convert_reduce_fusion), channel_id=1, source_target_pairs={{0,4},{1,5},{2,6},{3,7},{8,12},{9,13},{10,14},{11,15},{16,20},{17,... | collective-permute-start | bytes 6152 | tf_op jit(solution)/shard_map/ppermute | solution.py:27
  135.2 83.2 %copy-start.86 = (bf16[2048]{0:T(1024)(128)(2,1)}, bf16[2048]{0:T(1024)(128)(2,1)S(1)}, u32[]{:S(2)}) copy-start(bf16[2048]{0:T(1024)(128)(2,1)S(1)} %get-tuple-element.1247) | copy-start | bytes 12292
  135.2 83.2 %copy-start.99 = (bf16[1024]{0:T(1024)(128)(2,1)}, bf16[1024]{0:T(1024)(128)(2,1)S(1)}, u32[]{:S(2)}) copy-start(bf16[1024]{0:T(1024)(128)(2,1)S(1)} %get-tuple-element.1249) | copy-start | bytes 6148
  145.5 71.8 %copy-start.102 = (s32[2048]{0:T(1024)}, s32[2048]{0:T(1024)S(1)}, u32[]{:S(2)}) copy-start(s32[2048]{0:T(1024)S(1)} %fusion.190) | copy-start | bytes 24580
  161.9 56.0 %copy-start.104 = (f32[768]{0:T(1024)S(1)}, f32[768]{0:T(1024)}, u32[]{:S(2)}) copy-start(f32[768]{0:T(1024)} %reshape.1351) | copy-start | bytes 9220
  265.1 103.9 %copy-start.18 = (f32[1,384,2,512]{3,2,1,0:T(2,128)S(1)}, f32[1,384,2,512]{3,2,1,0:T(2,128)}, u32[]{:S(2)}) copy-start(f32[1,384,2,512]{3,2,1,0:T(2,128)} %param.34) | copy-start | bytes 4718596
  265.1 103.9 %all-to-all-start = ((bf16[4,2,256,768]{3,2,1,0:T(8,128)(2,1)}), bf16[4,2,256,768]{3,2,1,0:T(8,128)(2,1)}, u32[]{:S(2)}, u32[]{:S(2)}) async-start(bf16[4,2,256,768]{3,2,1,0:T(8,128)(2,1)} %fusion.112), calls=%async_computation | async-start | bytes 6291456 | tf_op jit(solution)/shard_map/all_to_all | solution.py:468
  269.9 120.4 %all-gather.6.cloned.1.call-start = ((), (), s32[]{:S(2)}) async-start(), calls=%async_computation.9 | async-start | bytes 2654208 | tf_op jit(solution)/shard_map/all_gather | solution.py:376
  270.7 174.5 %all-gather.4.cloned.1.call-start = ((), (), s32[]{:S(2)}) async-start(), calls=%async_computation.5 | async-start | bytes 2359296 | tf_op jit(solution)/shard_map/all_gather | solution.py:613
  369.0 67.3 %collective-permute-start.5 = (bf16[4,2,256,768]{3,2,1,0:T(8,128)(2,1)}, bf16[4,2,256,768]{3,2,1,0:T(8,128)(2,1)}, u32[]{:S(2)}, u32[]{:S(2)}) collective-permute-start(bf16[4,2,256,768]{3,2,1,0:T(8,128)(2,1)} %all-to-all-done), channel_id=1, source_target_pairs={{0,2},{1,3},{2,0},{3,1},{4,6},{5,7},{6,4},{7,5},{8,10},{9,11},{10,... | collective-permute-start | bytes 9437192 | tf_op jit(solution)/shard_map/ppermute | solution.py:511
  370.2 230.6 %reduce-scatter.5.cloned.1.call-start = ((), (), s32[]{:S(2)}) async-start(), calls=%async_computation.8 | async-start | bytes 2359296 | tf_op jit(solution)/shard_map/reduce_scatter | solution.py:755
  370.2 69.9 %collective-permute-start.3 = (bf16[4,2,256,768]{3,2,1,0:T(8,128)(2,1)}, bf16[4,2,256,768]{3,2,1,0:T(8,128)(2,1)}, u32[]{:S(2)}, u32[]{:S(2)}) collective-permute-start(bf16[4,2,256,768]{3,2,1,0:T(8,128)(2,1)} %all-to-all-done), channel_id=1, source_target_pairs={{0,1},{1,0},{2,3},{3,2},{4,5},{5,4},{6,7},{7,6},{8,9},{9,8},{10,11... | collective-permute-start | bytes 9437192 | tf_op jit(solution)/shard_map/ppermute | solution.py:470
  440.1 34.6 %collective-permute-start.6 = (bf16[4,2,256,768]{3,2,1,0:T(8,128)(2,1)}, bf16[4,2,256,768]{3,2,1,0:T(8,128)(2,1)}, u32[]{:S(2)}, u32[]{:S(2)}) collective-permute-start(bf16[4,2,256,768]{3,2,1,0:T(8,128)(2,1)} %broadcast_add_fusion), channel_id=1, source_target_pairs={{0,1},{1,0},{2,3},{3,2},{4,5},{5,4},{6,7},{7,6},{8,9},{9,8},{10,11... | collective-permute-start | bytes 9437192 | tf_op jit(solution)/shard_map/ppermute | solution.py:470
  459.9 50.3 %collective-permute-start.4 = (f32[4,256,768]{2,1,0:T(8,128)}, f32[4,256,768]{2,1,0:T(8,128)}, u32[]{:S(2)}, u32[]{:S(2)}) collective-permute-start(f32[4,256,768]{2,1,0:T(8,128)} %slice.585), channel_id=1, source_target_pairs={{0,1},{1,0},{2,3},{3,2},{4,5},{5,4},{6,7},{7,6},{8,9},{9,8},{10,11... | collective-permute-start | bytes 9437192 | tf_op jit(solution)/shard_map/ppermute | solution.py:470
  474.7 38.8 %collective-permute-start.8 = (f32[4,256,768]{2,1,0:T(8,128)}, f32[4,256,768]{2,1,0:T(8,128)}, u32[]{:S(2)}, u32[]{:S(2)}) collective-permute-start(f32[4,256,768]{2,1,0:T(8,128)} %slice.596), channel_id=1, source_target_pairs={{0,1},{1,0},{2,3},{3,2},{4,5},{5,4},{6,7},{7,6},{8,9},{9,8},{10,11... | collective-permute-start | bytes 9437192 | tf_op jit(solution)/shard_map/ppermute | solution.py:470
  494.3 22.8 %collective-permute-start.7 = (f32[4,256,768]{2,1,0:T(8,128)}, f32[4,256,768]{2,1,0:T(8,128)}, u32[]{:S(2)}, u32[]{:S(2)}) collective-permute-start(f32[4,256,768]{2,1,0:T(8,128)} %slice.593), channel_id=1, source_target_pairs={{0,1},{1,0},{2,3},{3,2},{4,5},{5,4},{6,7},{7,6},{8,9},{9,8},{10,11... | collective-permute-start | bytes 9437192 | tf_op jit(solution)/shard_map/ppermute | solution.py:470
  502.6 21.3 %collective-permute-start.9 = (f32[4,256,768]{2,1,0:T(8,128)}, f32[4,256,768]{2,1,0:T(8,128)}, u32[]{:S(2)}, u32[]{:S(2)}) collective-permute-start(f32[4,256,768]{2,1,0:T(8,128)} %slice.598), channel_id=1, source_target_pairs={{0,1},{1,0},{2,3},{3,2},{4,5},{5,4},{6,7},{7,6},{8,9},{9,8},{10,11... | collective-permute-start | bytes 9437192 | tf_op jit(solution)/shard_map/ppermute | solution.py:470
  533.3 144.4 %all-to-all-start.1 = ((bf16[4,2,512,768]{3,2,1,0:T(8,128)(2,1)}), bf16[4,2,512,768]{3,2,1,0:T(8,128)(2,1)}, u32[]{:S(2)}, u32[]{:S(2)}) async-start(bf16[4,2,512,768]{3,2,1,0:T(8,128)(2,1)} %copy.256), calls=%async_computation.1 | async-start | bytes 12582912 | tf_op jit(solution)/shard_map/all_to_all | solution.py:468
  538.6 63.5 %reduce-scatter.3.cloned.1.call-start = ((), (), s32[]{:S(2)}) async-start(), calls=%async_computation.7 | async-start | bytes 4718592 | tf_op jit(solution)/shard_map/reduce_scatter | solution.py:754
  550.4 209.6 %all-reduce.17.cloned.1.call-start = ((), (), s32[]{:S(2)}) async-start(), calls=%async_computation.6 | async-start | bytes 6291456 | tf_op jit(solution)/shard_map/psum | solution.py:709
  609.0 73.7 %copy-start.145 = (s32[1024,2]{0,1:T(2,128)S(1)}, s32[1024,2]{0,1:T(2,128)}, u32[]{:S(2)}) copy-start(s32[1024,2]{0,1:T(2,128)} %fusion.195) | copy-start | bytes 24580
  609.0 73.7 %copy-start.153 = (pred[1024,2]{0,1:T(4,128)(4,1)S(1)}, pred[1024,2]{0,1:T(4,128)(4,1)}, u32[]{:S(2)}) copy-start(pred[1024,2]{0,1:T(4,128)(4,1)} %fusion.201) | copy-start | bytes 6148
  693.0 326.7 %all-reduce.19.cloned.1.call-start = ((), (), s32[]{:S(2)}) async-start(), calls=%async_computation.10 | async-start | bytes 12582912 | tf_op jit(solution)/shard_map/psum | solution.py:709
  848.3 14.2 %collective-permute-start.10 = (bf16[1024,3,64]{0,2,1:T(8,128)(2,1)}, bf16[1024,3,64]{0,2,1:T(8,128)(2,1)}, u32[]{:S(2)}, u32[]{:S(2)}) collective-permute-start(bf16[1024,3,64]{0,2,1:T(8,128)(2,1)} %slice.715), channel_id=1, source_target_pairs={{4,0},{5,1},{6,2},{7,3},{12,8},{13,9},{14,10},{15,11},{20,16},{21,... | collective-permute-start | bytes 1179656 | tf_op jit(solution)/shard_map/ppermute | solution.py:27
  850.4 19.3 %collective-permute-start.11 = (bf16[1024,3,64]{0,2,1:T(8,128)(2,1)}, bf16[1024,3,64]{0,2,1:T(8,128)(2,1)}, u32[]{:S(2)}, u32[]{:S(2)}) collective-permute-start(bf16[1024,3,64]{0,2,1:T(8,128)(2,1)} %slice.714), channel_id=1, source_target_pairs={{4,0},{5,1},{6,2},{7,3},{12,8},{13,9},{14,10},{15,11},{20,16},{21,... | collective-permute-start | bytes 1179656 | tf_op jit(solution)/shard_map/ppermute | solution.py:27
  1014.2 42.8 %copy-start.79 = (f32[192,96]{1,0:T(8,128)}, f32[192,96]{1,0:T(8,128)S(1)}, u32[]{:S(2)}) copy-start(f32[192,96]{1,0:T(8,128)S(1)} %reshape.1335) | copy-start | bytes 221188
  1073.8 59.2 %copy-start.11 = (f32[1,384,2,512]{3,1,2,0:T(8,128)S(1)}, f32[1,384,2,512]{3,1,2,0:T(8,128)}, u32[]{:S(2)}) copy-start(f32[1,384,2,512]{3,1,2,0:T(8,128)} %reduce-scatter.3.cloned.1.call-done) | copy-start | bytes 4718596
  1073.8 87.1 %copy-start.20 = (f32[1,384,2,512]{3,2,1,0:T(2,128)S(1)}, f32[1,384,2,512]{3,2,1,0:T(2,128)}, u32[]{:S(2)}) copy-start(f32[1,384,2,512]{3,2,1,0:T(2,128)} %param.34) | copy-start | bytes 4718596
  1096.6 64.3 %copy-start.126 = (f32[512]{0:T(512)}, f32[512]{0:T(512)S(1)}, u32[]{:S(2)}) copy-start(f32[512]{0:T(512)S(1)} %multiply_add_fusion.8) | copy-start | bytes 6148
  (159 other events, 1244.9 us)
Sparse Core Ops, SparseCore 0:
  141.1 73.8 all-reduce.14
  693.1 66.8 all-reduce.16
  874.2 119.1 all-reduce.18
Sparse Core Ops, SparseCore 1:
  273.1 96.4 all-gather.5
  371.6 30.1 all-gather.3
  510.3 23.3 reduce-scatter.4
  550.5 43.6 reduce-scatter.2
